TPU v7x, 32 devices: a whole 2x2x4 slice. The times are simulated.
32 devices in a mesh: rows: 8 (over y, x, core), cols: 4 (over z).
Axes of the slice: x: 2, y: 2, z: 4, core: 2. Of those that a mesh axis runs over, the one named last changes fastest.
Arguments:
- snapshots: float32 [8192, 8192], P('rows', 'cols'), may hold values from -500 to 500, as said below
Outputs:
- updated: float32 [8192, 8192], P('rows', 'cols')
- coeffs: float32 [512, 8192], P(None, 'cols')
Inputs may be any that keep to these rules, and one draw needn't show every extreme that they name: `snapshots`: Real-valued entries.
All inputs are finite; a program needn't handle non-finite values.
Results may differ from a plain program's by a relative error of at most 0.000055.
Values sent between devices are 32-bit elements; how exact they have to be, the bound alone decides.
No kernel may reach another device: no remote copies, remote signals or barrier semaphores. Data moves between devices by JAX's collectives and lax.ppermute only.
A program may use at most 128 MiB of HBM per device.

v0:
```python
import jax
import jax.numpy as jnp
from jax import lax
from jax.sharding import PartitionSpec as P

PB = 512


def broadcast(block, axis, source):
    block = jnp.where(lax.axis_index(axis) == source, block, jnp.zeros_like(block))
    return lax.psum(block, axis)


def shards(snapshots):
    highest = lax.Precision.HIGHEST
    rows_dev, cols_dev = snapshots.shape
    total_rows = rows_dev * lax.axis_size("rows")
    panel = snapshots[:, :PB]
    local_gram = (
        jnp.dot(panel.T, panel, precision=highest, preferred_element_type=jnp.float32) / total_rows
    )
    gram = lax.psum(local_gram, "rows")
    lower = jnp.linalg.cholesky(gram)
    factor = lower.T
    basis = lax.linalg.triangular_solve(lower, panel, left_side=False, lower=True, transpose_a=True)
    basis = broadcast(basis, "cols", 0)
    partial_proj = (
        jnp.dot(basis.T, snapshots, precision=highest, preferred_element_type=jnp.float32)
        / total_rows
    )
    proj = lax.psum(partial_proj, "rows")
    column = lax.axis_index("cols") * cols_dev + jnp.arange(cols_dev, dtype=jnp.int32)
    is_panel = (column < PB)[None, :]
    coeff_fill = jnp.concatenate([factor, jnp.zeros((PB, cols_dev - PB), jnp.float32)], axis=1)
    coeffs = jnp.where(is_panel, coeff_fill, proj)
    trailing = snapshots - jnp.dot(
        basis, proj, precision=highest, preferred_element_type=jnp.float32
    )
    basis_fill = jnp.concatenate([basis, jnp.zeros((rows_dev, cols_dev - PB), jnp.float32)], axis=1)
    updated = jnp.where(is_panel, basis_fill, trailing)
    return (updated, coeffs)


def solution(mesh):
    in_specs = (P("rows", "cols"),)
    out_specs = (P("rows", "cols"), P(None, "cols"))
    return jax.shard_map(shards, mesh=mesh, in_specs=in_specs, out_specs=out_specs, check_vma=False)
```

profile of v0, /device:TPU:17, one launch (start us, length us, event | category | flops | bytes accessed | tf_op | source)
XLA Modules:
  0.0 448.2 jit_solution(13193877418435620194)
XLA Ops:
  7.2 0.0 all-reduce.7.cloned.1.call-start
  7.2 6.7 %fusion.8 = f32[512,512]{0,1:T(8,128)} fusion(f32[1024,2048]{1,0:T(8,128)} %param.1), kind=kOutput, calls=%fused_computation.14 | convolution fusion | flops 3221487616 | bytes 3145728 | tf_op jit(solution)/shard_map/dot_general | solution.py:20
  13.9 0.0 all-reduce.7.cloned.1.call-update
  14.0 0.6 all-reduce.9.cloned.1.call-start
  14.6 56.2 %all-reduce.7.cloned.1.call-done = f32[512,512]{0,1:T(8,128)} async-done(((f32[512,512]{0,1:T(8,128)}), f32[512,512]{0,1:T(8,128)}) %all-reduce.7.cloned.1.call-update) | async-done | bytes 1048592 | tf_op jit(solution)/shard_map/psum | solution.py:22
  70.7 1.6 copy.4
  72.3 1.4 fusion.17
  73.8 11.7 %cholesky.104 = f32[128,128]{1,0:T(8,128)S(1)} custom-call(f32[128,128]{1,0:T(8,128)S(1)} %cholesky.266), custom_call_target="Cholesky" | custom-call | tf_op jit(solution)/shard_map/jit(cholesky)/cholesky | solution.py:23
  85.5 9.8 %custom-call.30 = f32[1,128,128]{1,2,0:T(8,128)S(1)} custom-call(f32[1,128,128]{2,1,0:T(8,128)S(1)} %get-tuple-element.33), custom_call_target="InvertDiagBlocksLowerTriangular" | custom-call | tf_op jit(solution)/shard_map/jit(cholesky)/cholesky | solution.py:23
  95.3 0.1 cholesky.224
  95.4 0.3 constant_dynamic-update-slice_fusion.3
  95.8 0.3 convolution_subtract_fusion.2
  96.1 11.7 %cholesky.217 = f32[128,128]{1,0:T(8,128)S(1)} custom-call(f32[128,128]{1,0:T(8,128)S(1)} %cholesky.270), custom_call_target="Cholesky" | custom-call | tf_op jit(solution)/shard_map/jit(cholesky)/cholesky | solution.py:23
  107.9 10.0 %custom-call.31 = f32[1,128,128]{1,2,0:T(8,128)S(1)} custom-call(f32[1,128,128]{2,1,0:T(8,128)S(1)} %get-tuple-element.30), custom_call_target="InvertDiagBlocksLowerTriangular" | custom-call | tf_op jit(solution)/shard_map/jit(cholesky)/cholesky | solution.py:23
  117.8 0.3 convolution_dynamic-update-slice_fusion
  118.1 0.4 convolution_subtract_fusion.3
  118.5 11.7 %cholesky.238 = f32[128,128]{1,0:T(8,128)S(1)} custom-call(f32[128,128]{1,0:T(8,128)S(1)} %cholesky.275), custom_call_target="Cholesky" | custom-call | tf_op jit(solution)/shard_map/jit(cholesky)/cholesky | solution.py:23
  130.2 0.7 compare_reduce_fusion.1
  131.0 9.8 %custom-call.32 = f32[1,128,128]{1,2,0:T(8,128)S(1)} custom-call(f32[1,128,128]{2,1,0:T(8,128)S(1)} %get-tuple-element.27), custom_call_target="InvertDiagBlocksLowerTriangular" | custom-call | tf_op jit(solution)/shard_map/jit(cholesky)/cholesky | solution.py:23
  140.8 0.2 convolution_dynamic-update-slice_fusion.1
  141.0 0.4 convolution_subtract_fusion.4
  141.4 11.7 %cholesky.255 = f32[128,128]{1,0:T(8,128)S(1)} custom-call(f32[128,128]{1,0:T(8,128)S(1)} %convolution_subtract_fusion.4), custom_call_target="Cholesky" | custom-call | tf_op jit(solution)/shard_map/jit(cholesky)/cholesky | solution.py:23
  153.1 0.6 compare_reduce_fusion
  153.8 0.7 compare_reduce_fusion.2
  157.0 0.5 fusion.19
  157.4 8.5 %while.1 = (s32[]{:T(128)}, f32[512,512]{1,0:T(8,128)S(1)}, s32[4,2]{0,1:T(2,128)S(1)}, f32[4,128,128]{2,1,0:T(8,128)S(1)}, s32[]{:T(128)}) while((s32[]{:T(128)}, f32[512,512]{1,0:T(8,128)S(1)}, s32[4,2]{0,1:T(2,128)S(1)}, f32[4,128,128]{2,1,0:T(8,128)S(1)}, s32[]{:T(128)}) %tuple.33), condition=%wide.while_cond, body=%wide.while_body.sunk | while | flops 2 | bytes 131189 | solution.py:25
  157.4 0.1 constant_dynamic-slice_fusion.2
  157.5 0.6 fusion.52
  158.1 1.4 bitcast_dynamic-update-slice_fusion.2
  159.6 0.1 constant_dynamic-slice_fusion.2
  159.6 0.6 fusion.52
  160.2 1.4 bitcast_dynamic-update-slice_fusion.2
  161.7 0.1 constant_dynamic-slice_fusion.2
  161.8 0.6 fusion.52
  162.4 1.4 bitcast_dynamic-update-slice_fusion.2
  163.8 0.1 constant_dynamic-slice_fusion.2
  163.9 0.6 fusion.52
  164.5 1.4 bitcast_dynamic-update-slice_fusion.2
  165.9 39.3 %custom-call.33 = f32[4,128,128]{1,2,0:T(8,128)S(1)} custom-call(f32[4,128,128]{2,1,0:T(8,128)S(1)} %get-tuple-element.9), custom_call_target="InvertDiagBlocksLowerTriangular" | custom-call | tf_op jit(solution)/shard_map/triangular_solve | solution.py:25
  205.2 1.7 fusion.20
  206.9 2.0 convolution_subtract_fusion.1
  209.0 0.6 fusion.32
  209.6 2.9 convolution_subtract_fusion
  212.5 0.6 fusion.31
  213.1 3.8 fusion.11
  217.0 0.6 fusion.30
  217.6 1.6 maximum_select_fusion
  219.1 0.0 all-reduce.9.cloned.1.call-update
  219.2 0.3 all-reduce.11.cloned.1.call-start
  219.5 85.3 %all-reduce.9.cloned.1.call-done = f32[1024,512]{0,1:T(8,128)} async-done(((f32[1024,512]{0,1:T(8,128)}), f32[1024,512]{0,1:T(8,128)}) %all-reduce.9.cloned.1.call-update) | async-done | bytes 2097168 | tf_op jit(solution)/shard_map/psum | solution.py:11
  304.8 17.7 %convolution_multiply_fusion = f32[512,2048]{0,1:T(8,128)} fusion(f32[1024,512]{0,1:T(8,128)} %all-reduce.9.cloned.1.call-done, f32[1024,2048]{1,0:T(8,128)} %param.1), kind=kOutput, calls=%fused_computation.4 | convolution fusion | flops 12885950464 | bytes 14680064 | tf_op jit(solution)/shard_map/dot_general | solution.py:28
  322.5 0.0 all-reduce.11.cloned.1.call-update
  322.5 9.4 %copy.6 = f32[1024,2048]{0,1:T(8,128)} copy(f32[1024,2048]{1,0:T(8,128)} %param.1) | data formatting | bytes 16777216 | tf_op args[0]
  331.9 71.8 %all-reduce.11.cloned.1.call-done = f32[512,2048]{0,1:T(8,128)} async-done(((f32[512,2048]{0,1:T(8,128)}), f32[512,2048]{0,1:T(8,128)}) %all-reduce.11.cloned.1.call-update) | async-done | bytes 4194320 | tf_op jit(solution)/shard_map/psum | solution.py:31
  403.7 3.8 pad_select_fusion
  407.5 0.0 copy-start
  407.5 5.5 %copy.9 = f32[512,2048]{1,0:T(8,128)} copy(f32[512,2048]{0,1:T(8,128)} %pad_select_fusion) | data formatting | bytes 8388608
  413.0 0.0 copy-done
  413.0 19.4 %subtract_select_fusion = f32[1024,2048]{0,1:T(8,128)} fusion(f32[1024,2048]{0,1:T(8,128)} %copy.6, f32[1024,512]{0,1:T(8,128)S(1)} %copy-done, pred[2048]{0:T(1024)(128)(4,1)S(1)} %add_compare_fusion, f32[512,2048]{0,1:T(8,128)} %all-reduce.11.cloned.1.call-done), kind=kOutput, calls=%fused_computation.2 | convolution fusion | flops 12889096192 | bytes 23070720 | tf_op jit(solution)/shard_map/dot_general | solution.py:36
  432.4 9.1 %copy.8 = f32[1024,2048]{1,0:T(8,128)} copy(f32[1024,2048]{0,1:T(8,128)} %subtract_select_fusion) | data formatting | bytes 16777216
  (11 shorter events, 0.2 us)
Async XLA Ops:
  7.2 63.6 %all-reduce.7.cloned.1.call-start = ((), (), s32[]{:S(2)}) async-start(), calls=%async_computation | async-start | bytes 2097152 | tf_op jit(solution)/shard_map/psum | solution.py:22
  14.0 290.8 %all-reduce.9.cloned.1.call-start = ((), (), s32[]{:S(2)}) async-start(), calls=%async_computation.1 | async-start | bytes 4194304 | tf_op jit(solution)/shard_map/psum | solution.py:11
  219.2 184.5 %all-reduce.11.cloned.1.call-start = ((), (), s32[]{:S(2)}) async-start(), calls=%async_computation.2 | async-start | bytes 8388608 | tf_op jit(solution)/shard_map/psum | solution.py:31
  407.5 5.5 %copy-start = (f32[1024,512]{0,1:T(8,128)S(1)}, f32[1024,512]{0,1:T(8,128)}, u32[]{:S(2)}) copy-start(f32[1024,512]{0,1:T(8,128)} %all-reduce.9.cloned.1.call-done) | copy-start | bytes 6291460
Sparse Core Ops, SparseCore 0:
  14.1 56.6 all-reduce.6
  219.3 85.4 all-reduce.8
  322.6 81.0 all-reduce.10
where the time goes:
time: 454 us; the launch traced here: 448 us
  waiting for transfers between devices  213 us (47%)
  other arithmetic  125 us (28%)
  matrix products  58 us (13%)
  local copies, waits for them, and re-layouts  34.1 us (8%)
  between operations  16.6 us (4%)
    psum x1, waiting for transfers between devices, broadcast(): return lax.psum(block, axis)  85.3 us
    another operation x14, other arithmetic, shards(): lower = jnp.linalg.cholesky(gram)  78.6 us
    psum x1, waiting for transfers between devices, shards(): proj = lax.psum(partial_proj, 'rows')  71.8 us
    psum x1, waiting for transfers between devices, shards(): gram = lax.psum(local_gram, 'rows')  56.2 us
    another operation x2, other arithmetic, shards(): lax.linalg.triangular_solve(lower, panel, left_side=False, lower=True, tr...  39.3 us
    unnamed x5, local copies, waits for them, and re-layouts  24 us
    dot_general x1, matrix products, shards(): jnp.dot(basis, proj, precision=highest, preferred_element_type=jnp.float32)  19.4 us
    dot_general x1, matrix products, shards(): jnp.dot(basis.T, snapshots, precision=highest, preferred_element_type=jnp...  17.7 us
  transfers between devices with their start and end apart: 3, of which 3 were waited for; matrix products, arithmetic and copies ran while one was open for 2% of the time, Pallas kernels for 0%

commit v1 on v0

v1 whole, which is shorter than its diff:
```python
import jax
import jax.numpy as jnp
from jax import lax
from jax.experimental import pallas as pl
from jax.experimental.pallas import tpu as pltpu
from jax.sharding import PartitionSpec as P

PB = 512
NB = 128
CHUNKS = (256, 256)
F32 = jnp.float32
BF16 = jnp.bfloat16
HIGHEST = lax.Precision.HIGHEST
VMEM = pl.BlockSpec(memory_space=pltpu.VMEM)


def mm(a, b, da, db, precision=None):
    return lax.dot_general(
        a, b, (((da,), (db,)), ((), ())), precision=precision, preferred_element_type=F32
    )


def split(x):
    high = x.astype(BF16)
    return high, (x - high.astype(F32)).astype(BF16)


def diag_block(d_ref, z_ref, f_ref):
    a_all = d_ref[...]
    row = lax.broadcasted_iota(jnp.int32, (NB, NB), 0)
    col = lax.broadcasted_iota(jnp.int32, (NB, NB), 1)
    z_all = jnp.where(row == col, 1.0, 0.0).astype(F32)
    lane = lax.broadcasted_iota(jnp.int32, (1, NB), 1)
    for j in range(0, NB, 2):
        base = (j // 8) * 8
        if a_all.shape[0] != NB - base:
            a_all, z_all = a_all[8:], z_all[8:]
        i, n = j - base, NB - base
        r0, r1 = a_all[i : i + 1, :], a_all[i + 1 : i + 2, :]
        z0, z1 = z_all[i : i + 1, :], z_all[i + 1 : i + 2, :]
        c0 = jnp.broadcast_to(a_all[:, j : j + 1], (n, NB))
        c1 = jnp.broadcast_to(a_all[:, j + 1 : j + 2], (n, NB))
        a = jnp.broadcast_to(r0[:, j : j + 1], (1, NB))
        b = jnp.broadcast_to(r0[:, j + 1 : j + 2], (1, NB))
        d = jnp.broadcast_to(r1[:, j + 1 : j + 2], (1, NB))
        ra = 1.0 / a
        bra = b * ra
        s = d - b * bra
        rs = 1.0 / s
        t1 = r1 - bra * r0
        x1 = t1 * rs
        x0 = r0 * ra - bra * x1
        u1 = z1 - bra * z0
        y1 = u1 * rs
        y0 = z0 * ra - bra * y1
        qa, qs = lax.rsqrt(a), lax.rsqrt(s)
        f_ref[j : j + 1, :] = jnp.where(lane >= j, r0 * qa, 0.0)
        f_ref[j + 1 : j + 2, :] = jnp.where(lane >= j + 1, t1 * qs, 0.0)
        z_ref[j : j + 1, :] = z0 * qa
        z_ref[j + 1 : j + 2, :] = u1 * qs
        if j + 2 < NB:
            a_all = a_all - c0 * x0 - c1 * x1
            z_all = z_all - c0 * y0 - c1 * y1


def chol_kernel(g_ref, f_out, l_out, work, diag, zs, fs):
    n = g_ref.shape[0]
    nb = n // NB
    work[...] = g_ref[...]
    f_out[...] = jnp.zeros_like(f_out)
    l_out[...] = jnp.zeros_like(l_out)

    def body(k, carry):
        o = pl.multiple_of(k * NB, NB)
        diag[...] = work[pl.ds(o, NB), pl.ds(o, NB)]
        diag_block(diag, zs, fs)
        for kk in range(nb):

            @pl.when(k == kk)
            def _():
                o, e = kk * NB, kk * NB + NB
                z = zs[...]
                f_out[o:e, o:e] = fs[...]
                lk = z
                if kk > 0:
                    lk = jnp.concatenate([mm(z, l_out[o:e, :o], 1, 0, HIGHEST), z], axis=1)
                l_out[o:e, :e] = lk
                if kk < nb - 1:
                    u = mm(z, work[o:e, e:], 1, 0, HIGHEST)
                    f_out[o:e, e:] = u
                    work[e:, e:] -= mm(u, u, 0, 0, HIGHEST)
                    l_out[e:, :e] -= mm(u, lk, 0, 0, HIGHEST)

        return carry

    lax.fori_loop(0, nb, body, 0)


def chol_inv(gram):
    n = gram.shape[0]
    shape = jax.ShapeDtypeStruct((n, n), F32)
    return pl.pallas_call(
        chol_kernel,
        out_shape=(shape, shape),
        in_specs=[VMEM],
        out_specs=(VMEM, VMEM),
        scratch_shapes=[pltpu.VMEM((n, n), F32)] + [pltpu.VMEM((NB, NB), F32)] * 3,
        compiler_params=pltpu.CompilerParams(vmem_limit_bytes=16 << 20),
        cost_estimate=pl.CostEstimate(flops=10**10, bytes_accessed=3 << 20, transcendentals=0),
        name="chol_inv",
    )(gram)


def finish(info, snapshots, panel, linv, factor, pieces, layout):
    rows, cols = snapshots.shape
    tile = 256
    n_pieces = len(pieces)

    def kernel(info_ref, s_ref, p_ref, l_ref, f_ref, *rest):
        m_refs = rest[:n_pieces]
        up_ref, co_ref, bs, b3, l3, ms, m3, p3 = rest[n_pieces:]
        j = pl.program_id(0)

        @pl.when(j == 0)
        def _():
            lh, ll = split(l_ref[...])
            l3[:, :PB], l3[:, PB : 2 * PB], l3[:, 2 * PB :] = lh, lh, ll
            for r in range(0, rows, 256):
                ph, plow = split(p_ref[r : r + 256, :])
                b = mm(ph, lh, 1, 1) + (mm(ph, ll, 1, 1) + mm(plow, lh, 1, 1))
                bs[r : r + 256, :] = b
                bh, bl = split(b)
                b3[r : r + 256, :PB], b3[r : r + 256, PB : 2 * PB] = bh, bh
                b3[r : r + 256, 2 * PB :] = bl

        for ref, (base, core, chip) in zip(m_refs, layout):
            h = ref.shape[0]
            off = base + (info_ref[1] ^ core) * (h * (n_chips(layout))) + (info_ref[2] ^ chip) * h
            ms[pl.ds(pl.multiple_of(off, 8), h), :] = ref[...]
        mh, ml = split(ms[...])
        m3[:PB, :], m3[PB : 2 * PB, :], m3[2 * PB :, :] = mh, ml, mh
        proj = mm(l3[...], m3[...], 1, 0)
        ph, plow = split(proj)
        p3[:PB, :], p3[PB : 2 * PB, :], p3[2 * PB :, :] = ph, plow, ph
        co_ref[...] = proj
        for r in range(0, rows, 256):
            up_ref[r : r + 256, :] = s_ref[r : r + 256, :] - mm(b3[r : r + 256, :], p3[...], 1, 0)
        for t in range(PB // tile):

            @pl.when((info_ref[0] == 0) & (j == t))
            def _():
                co_ref[...] = f_ref[:, t * tile : (t + 1) * tile]
                up_ref[...] = bs[:, t * tile : (t + 1) * tile]

    full = lambda a: pl.BlockSpec(a.shape, lambda j, *_: (0, 0), pipeline_mode=pl.Buffered(1))
    col = lambda h: pl.BlockSpec((h, tile), lambda j, *_: (0, j))
    return pl.pallas_call(
        kernel,
        out_shape=(
            jax.ShapeDtypeStruct((rows, cols), F32),
            jax.ShapeDtypeStruct((PB, cols), F32),
        ),
        grid_spec=pltpu.PrefetchScalarGridSpec(
            num_scalar_prefetch=1,
            grid=(cols // tile,),
            in_specs=[col(rows), full(panel), full(linv), full(factor)]
            + [col(p.shape[0]) for p in pieces],
            out_specs=(col(rows), col(PB)),
            scratch_shapes=[
                pltpu.VMEM((rows, PB), F32),
                pltpu.VMEM((rows, 3 * PB), BF16),
                pltpu.VMEM((PB, 3 * PB), BF16),
                pltpu.VMEM((PB, tile), F32),
                pltpu.VMEM((3 * PB, tile), BF16),
                pltpu.VMEM((3 * PB, tile), BF16),
            ],
        ),
        compiler_params=pltpu.CompilerParams(vmem_limit_bytes=40 << 20),
        name="finish",
    )(info, snapshots, panel, linv, factor, *pieces)


def n_chips(layout):
    return 1 + max(chip for _, _, chip in layout)


def spread(x, n):
    if n == 1:
        return x
    rows = x.shape[0]
    parts = n - 1
    size = -(-rows // (8 * parts)) * 8
    starts = [min(k * size, rows - size) for k in range(parts)]
    z = lax.axis_index("cols")
    mine = None
    for k in range(parts):
        part = lax.ppermute(x[starts[k] : starts[k] + size], "cols", [(0, k + 1)])
        mine = part if mine is None else mine + part
    out = jnp.where(z == 0, x, 0.0)
    table = jnp.array(starts, jnp.int32)

    def place(out, part, owner):
        start = jnp.minimum(owner * size, rows - size)
        old = lax.dynamic_slice(out, (start, 0), part.shape)
        return lax.dynamic_update_slice(out, jnp.where(z == 0, old, part), (start, 0))

    out = place(out, mine, jnp.maximum(z - 1, 0))
    for k in range(1, parts):
        got = lax.ppermute(mine, "cols", [(1 + i, 1 + (i + k) % parts) for i in range(parts)])
        out = place(out, got, jnp.maximum(z - 1 - k, 0) + jnp.where(z - 1 - k < 0, parts + z - 1 - k, 0))
    return out


def reduce_rows(m, n):
    index = lax.axis_index("rows")
    core, chip = index & 1, index >> 1
    chips, half = n // 2, m.shape[0] // 2
    piece = half // chips
    swap = lambda k: [(i, i ^ k) for i in range(n)]
    take = lambda a, start, size: lax.dynamic_slice_in_dim(a, start, size, 0)
    other = lax.ppermute(take(m, (1 - core) * half, half), "rows", swap(1))
    mine = take(m, core * half, half) + other
    own = take(mine, chip * piece, piece)
    for k in range(1, chips):
        own = own + lax.ppermute(take(mine, (chip ^ k) * piece, piece), "rows", swap(2 * k))
    got = [own] + [lax.ppermute(own, "rows", swap(2 * k)) for k in range(1, chips)]
    pieces = [(g, 0, k) for k, g in enumerate(got)]
    pieces += [(lax.ppermute(g, "rows", swap(1)), 1, k) for k, g in enumerate(got)]
    return pieces


def shards(snapshots):
    rows_dev, cols_dev = snapshots.shape
    n_rows, n_cols = lax.axis_size("rows"), lax.axis_size("cols")
    total_rows = rows_dev * n_rows
    z = lax.axis_index("cols")
    index = lax.axis_index("rows")
    panel = snapshots[:, :PB]
    gram = mm(panel, panel, 0, 0, HIGHEST) / total_rows
    gram = lax.psum(jnp.where(z == 0, gram, 0.0), ("rows", "cols"))
    panels, pieces, layout = [], [], []
    base = 0
    for width in CHUNKS:
        part = spread(panel[:, base : base + width], n_cols)
        panels.append(part)
        m = mm(part, snapshots, 0, 0, lax.Precision.HIGH) / total_rows
        for piece, core, chip in reduce_rows(m, n_rows):
            pieces.append(piece)
            layout.append((base, core, chip))
        base += width
    factor, linv = chol_inv(gram)
    info = jnp.stack([z, index & 1, index >> 1]).astype(jnp.int32)
    panel = jnp.concatenate(panels, axis=1)
    return finish(info, snapshots, panel, linv, factor, pieces, layout)


def solution(mesh):
    in_specs = (P("rows", "cols"),)
    out_specs = (P("rows", "cols"), P(None, "cols"))
    return jax.shard_map(shards, mesh=mesh, in_specs=in_specs, out_specs=out_specs, check_vma=False)
```

time: 454 us -> 319 us (0.70)
  other arithmetic: 125 us -> 11.2 us
  waiting for transfers between devices: 213 us -> 118 us
  starting transfers between devices: 0.9 us -> 77.4 us
  Pallas kernels: 0 us -> 56 us
  matrix products: 58 us -> 19.4 us
  local copies, waits for them, and re-layouts: 34.1 us -> 17.6 us
    psum x3 -> x1, waiting for transfers between devices: 213 us -> 85.7 us  [shards(): gram = lax.psum(jnp.where(z == 0, gram, 0.0), ('rows', 'cols'))]
    another operation x16 -> x1, other arithmetic: 118 us -> 0.08 us  [shards(): info = jnp.stack([z, index & 1, index >> 1]).astype(jnp.int32)]
    ppermute x0 -> x32, starting transfers between devices: none -> 77.3 us  [the longest x4 30.8 us: spread(): lax.ppermute(mine, 'cols', [(1 + i, 1 + (i + k) % parts) for i in range(p...]
    pallas_call x0 -> x2, Pallas kernels: none -> 56 us  [the longest x1 31.8 us: chol_inv(): pl.pallas_call(chol_kernel, out_shape=(shape, shape), in_specs=[VMEM], ou...]
    ppermute x0 -> x32, waiting for transfers between devices: none -> 32.5 us  [the longest x6 13.1 us: spread(): part = lax.ppermute(x[starts[k]:starts[k] + size], 'cols', [(0, k + 1)])]
    dot_general x3, matrix products: 43.8 us -> 19.4 us  [mm(): lax.dot_general(a, b, (((da,), (db,)), ((), ())), precision=precision, pr...]
    unnamed x5 -> x18, local copies, waits for them, and re-layouts: 24 us -> 2.98 us
    another operation x13 -> x0, matrix products: 14.2 us -> none  [the longest x7 12.3 us: shards(): lax.linalg.triangular_solve(lower, panel, left_side=False, lower=True, tr...]
  transfers between devices with their start and end apart: 3 -> 33, of which waited for: 3 -> 9; matrix products, arithmetic and copies ran while one was open for 2% -> 10% of each run, Pallas kernels for 0% -> 10%
where the time goes in v1:
time: 319 us; the launch traced here: 314 us
  waiting for transfers between devices  118 us (37%)
  starting transfers between devices  77.4 us (24%)
  Pallas kernels  56 us (18%)
  matrix products  19.4 us (6%)
  local copies, waits for them, and re-layouts  17.6 us (6%)
  between operations  14.5 us (5%)
  other arithmetic  11.2 us (4%)
    psum x1, waiting for transfers between devices, shards(): gram = lax.psum(jnp.where(z == 0, gram, 0.0), ('rows', 'cols'))  85.7 us
    pallas_call x1, Pallas kernels, chol_inv(): pl.pallas_call(chol_kernel, out_shape=(shape, shape), in_specs=[VMEM], ou...  31.8 us
    ppermute x4, starting transfers between devices, spread(): lax.ppermute(mine, 'cols', [(1 + i, 1 + (i + k) % parts) for i in range(p...  30.8 us
    pallas_call x1, Pallas kernels, finish(): pl.pallas_call(kernel, out_shape=(jax.ShapeDtypeStruct((rows, cols), F32)...  24.2 us
    ppermute x8, starting transfers between devices, reduce_rows(): lax.ppermute(g, 'rows', swap(1))  23.6 us
    dot_general x3, matrix products, mm(): lax.dot_general(a, b, (((da,), (db,)), ((), ())), precision=precision, pr...  19.4 us
    ppermute x6, waiting for transfers between devices, spread(): part = lax.ppermute(x[starts[k]:starts[k] + size], 'cols', [(0, k + 1)])  13.1 us
    ppermute x6, waiting for transfers between devices, reduce_rows(): lax.ppermute(take(mine, (chip ^ k) * piece, piece), 'rows', swap(2 * k))  12.4 us
  transfers between devices with their start and end apart: 33, of which 9 were waited for; matrix products, arithmetic and copies ran while one was open for 10% of the time, Pallas kernels for 10%

profile of v1, /device:TPU:17, one launch (start us, length us, event | category | flops | bytes accessed | tf_op | source)
XLA Modules:
  0.0 314.4 jit_solution(14577909010533541923)
XLA Ops:
  7.2 2.6 fusion.8
  9.8 0.7 collective-permute-start.7
  10.5 1.3 collective-permute-start.6
  11.8 1.4 collective-permute-start.5
  13.2 1.3 collective-permute-start.1
  14.5 1.4 collective-permute-start.2
  15.9 1.7 slice_select_fusion.1
  17.6 1.4 collective-permute-start
  19.0 11.5 %collective-permute-done.6 = f32[344,256]{1,0:T(8,128)} collective-permute-done((f32[344,256]{1,0:T(8,128)S(1)}, f32[344,256]{1,0:T(8,128)}, u32[]{:S(2)}, u32[]{:S(2)}) %collective-permute-start.6) | collective-permute-done | bytes 352288 | tf_op jit(solution)/shard_map/ppermute | solution.py:197
  30.5 2.0 dynamic-slice_select_fusion.2
  32.5 1.9 collective-permute-start.8
  34.4 9.7 %collective-permute-start.9 = (f32[344,256]{1,0:T(8,128)}, f32[344,256]{1,0:T(8,128)S(1)}, u32[]{:S(2)}, u32[]{:S(2)}) collective-permute-start(f32[344,256]{1,0:T(8,128)} %get-tuple-element.9), channel_id=1, source_target_pairs={{1,3},{2,1},{3,2},{5,7},{6,5},{7,6},{9,11},{10,9},{11,10},{13,15},... | collective-permute-start | bytes 1056776 | tf_op jit(solution)/shard_map/ppermute | solution.py:209
  44.2 1.5 collective-permute-done.1
  45.7 2.1 dynamic-slice_select_fusion.5
  47.7 10.6 %collective-permute-start.3 = (f32[344,256]{1,0:T(8,128)}, f32[344,256]{1,0:T(8,128)}, u32[]{:S(2)}, u32[]{:S(2)}) collective-permute-start(f32[344,256]{1,0:T(8,128)} %get-tuple-element.7), channel_id=1, source_target_pairs={{1,2},{2,3},{3,1},{5,6},{6,7},{7,5},{9,10},{10,11},{11,9},{13,14},... | collective-permute-start | bytes 1056776 | tf_op jit(solution)/shard_map/ppermute | solution.py:209
  58.4 8.5 %collective-permute-start.4 = (f32[344,256]{1,0:T(8,128)}, f32[344,256]{1,0:T(8,128)}, u32[]{:S(2)}, u32[]{:S(2)}) collective-permute-start(f32[344,256]{1,0:T(8,128)} %get-tuple-element.7), channel_id=1, source_target_pairs={{1,3},{2,1},{3,2},{5,7},{6,5},{7,6},{9,11},{10,9},{11,10},{13,15},... | collective-permute-start | bytes 1056776 | tf_op jit(solution)/shard_map/ppermute | solution.py:209
  66.9 1.9 dynamic_update_slice.21
  68.9 1.9 dynamic_update_slice.18
  70.9 1.9 dynamic_update_slice.22
  72.9 1.4 dynamic_update_slice.23
  74.3 2.6 collective-permute-done.3
  76.9 1.0 dynamic-slice_select_fusion.4
  78.0 1.9 dynamic_update_slice.19
  79.9 1.8 collective-permute-done.4
  81.7 1.0 dynamic-slice_select_fusion.3
  82.7 1.4 dynamic_update_slice.20
  84.2 6.5 %convolution_multiply_fusion.1 = f32[256,2048]{1,0:T(8,128)S(1)} fusion(f32[1024,256]{1,0:T(8,128)S(1)} %dynamic_update_slice.20, f32[1024,2048]{1,0:T(8,128)} %s_ref.1), kind=kOutput, calls=%fused_computation.1 | convolution fusion | flops 3221749760 | bytes 11534336 | tf_op jit(solution)/shard_map/dot_general | solution.py:18
  90.7 1.2 constant_dynamic-slice_fusion.7
  91.9 0.4 copy-done.7
  92.3 1.6 collective-permute-start.10
  93.9 6.1 %convolution_multiply_fusion = f32[256,2048]{1,0:T(8,128)S(1)} fusion(f32[1024,256]{1,0:T(8,128)S(1)} %dynamic_update_slice.23, f32[1024,2048]{1,0:T(8,128)} %s_ref.1), kind=kOutput, calls=%fused_computation | convolution fusion | flops 3221749760 | bytes 11534336 | tf_op jit(solution)/shard_map/dot_general | solution.py:18
  100.0 1.3 copy-done.5
  101.5 6.8 %fusion.5 = f32[512,512]{1,0:T(8,128)} fusion(f32[1024,2048]{1,0:T(8,128)} %s_ref.1, pred[]{:T(512)S(6)} %eq.2), kind=kOutput, calls=%fused_computation.6 | convolution fusion | flops 3221749760 | bytes 3145729 | tf_op jit(solution)/shard_map/dot_general | solution.py:18
  108.4 1.5 dynamic-slice_add_fusion.1
  110.0 1.3 collective-permute-start.11
  111.2 1.2 collective-permute-start.13
  112.4 0.2 collective-permute-start.12
  112.7 1.3 dynamic-slice_add_fusion
  114.0 0.1 constant_dynamic-slice_fusion.2
  114.1 1.3 collective-permute-start.22
  115.4 1.2 collective-permute-start.24
  116.6 0.9 collective-permute-done.11
  117.5 1.2 collective-permute-start.23
  118.7 6.5 %collective-permute-done.13 = f32[32,2048]{1,0:T(8,128)S(1)} collective-permute-done((f32[32,2048]{1,0:T(8,128)S(1)}, f32[32,2048]{1,0:T(8,128)S(1)}, u32[]{:S(2)}, u32[]{:S(2)}) %collective-permute-start.13) | collective-permute-done | bytes 262176 | tf_op jit(solution)/shard_map/ppermute | solution.py:225
  125.3 4.5 %collective-permute-start.17 = (f32[32,2048]{1,0:T(8,128)S(1)}, f32[32,2048]{1,0:T(8,128)S(1)}, u32[]{:S(2)}, u32[]{:S(2)}) collective-permute-start(f32[32,2048]{1,0:T(8,128)S(1)} %add_add_fusion.3.rest_0_), channel_id=1, source_target_pairs={{0,4},{4,0},{8,12},{12,8},{16,20},{20,16},{24,28},{28,24},{1,5},{5... | collective-permute-start | bytes 786440 | tf_op jit(solution)/shard_map/ppermute | solution.py:228
  129.8 1.1 collective-permute-start.16
  130.9 1.6 collective-permute-start.15
  132.5 5.0 %collective-permute-done.24 = f32[32,2048]{1,0:T(8,128)S(1)} collective-permute-done((f32[32,2048]{1,0:T(8,128)S(1)}, f32[32,2048]{1,0:T(8,128)S(1)}, u32[]{:S(2)}, u32[]{:S(2)}) %collective-permute-start.24) | collective-permute-done | bytes 262176 | tf_op jit(solution)/shard_map/ppermute | solution.py:225
  137.5 1.3 collective-permute-start.14
  138.8 8.4 %collective-permute-start.28 = (f32[32,2048]{1,0:T(8,128)S(1)}, f32[32,2048]{1,0:T(8,128)S(1)}, u32[]{:S(2)}, u32[]{:S(2)}) collective-permute-start(f32[32,2048]{1,0:T(8,128)S(1)} %add_add_fusion.2.rest_8_), channel_id=1, source_target_pairs={{0,4},{4,0},{8,12},{12,8},{16,20},{20,16},{24,28},{28,24},{1,5},{5... | collective-permute-start | bytes 786440 | tf_op jit(solution)/shard_map/ppermute | solution.py:228
  147.2 1.2 collective-permute-start.27
  148.4 1.4 collective-permute-start.26
  149.8 0.9 collective-permute-start.25
  150.7 9.0 %collective-permute-start.20 = (f32[32,2048]{1,0:T(8,128)S(1)}, f32[32,2048]{1,0:T(8,128)S(1)}, u32[]{:S(2)}, u32[]{:S(2)}) collective-permute-start(f32[32,2048]{1,0:T(8,128)S(1)} %collective-permute-done.16.rest_3_), channel_id=1, source_target_pairs={{0,4},{4,0},{8,12},{12,8},{16,20},{20,16},{24,28},{28,24},{1,5},{5... | collective-permute-start | bytes 786440 | tf_op jit(solution)/shard_map/ppermute | solution.py:228
  159.8 0.1 pad_add_fusion.info_ref
  159.9 0.5 collective-permute-start.18
  160.4 2.6 collective-permute-done.26.rest_10_
  162.9 0.4 collective-permute-start.31
  163.3 0.8 collective-permute-start.30
  164.1 85.7 %all-reduce.2.cloned.1.call-done.g_ref = f32[512,512]{1,0:T(8,128)} async-done(((f32[512,512]{1,0:T(8,128)}), f32[512,512]{1,0:T(8,128)}) %all-reduce.2.cloned.1.call-update) | async-done | bytes 1048592 | tf_op jit(solution)/shard_map/psum | solution.py:240
  249.8 1.2 copy-done
  251.1 31.8 %chol_inv.1 = (f32[512,512]{1,0:T(8,128)S(1)}, f32[512,512]{1,0:T(8,128)S(1)}) custom-call(f32[512,512]{1,0:T(8,128)S(1)} %copy-done), custom_call_target="tpu_custom_call" | custom-call | flops 10000000000 | bytes 3145728 | tf_op jit(solution)/shard_map/chol_inv/pallas_call | solution.py:102
  282.9 0.3 pad_maximum_fusion.p_ref
  283.3 24.2 %finish.1 = (f32[1024,2048]{1,0:T(8,128)}, f32[512,2048]{1,0:T(8,128)}) custom-call(s32[3]{0:T(128)S(1)} %pad_add_fusion.info_ref, f32[1024,2048]{1,0:T(8,128)} %s_ref.1, f32[1024,512]{1,0:T(8,128)S(1)} %pad_maximum_fusion.p_ref, f32[512,512]{1,0:T(8,128)S(1)} %get-tuple-element.4.l_ref, f32[512,512]{1,0:T(8,128)S(1)} %get-tuple-element.5.f_ref, ...), custom_call_target="tpu_custom_call" | custom-call | tf_op jit(solution)/shard_map/finish/pallas_call | solution.py:157
  (50 shorter events, 0.6 us)
Async XLA Ops:
  7.2 242.7 %all-reduce.2.cloned.1.call-start = ((), (), s32[]{:S(2)}) async-start(), calls=%async_computation | async-start | bytes 2097152 | tf_op jit(solution)/shard_map/psum | solution.py:240
  9.8 7.8 %collective-permute-start.7 = (f32[344,256]{1,0:T(8,128)}, f32[344,256]{1,0:T(8,128)S(1)}, u32[]{:S(2)}, u32[]{:S(2)}) collective-permute-start(f32[344,256]{1,0:T(8,128)} %get-tuple-element.11), channel_id=1, source_target_pairs={{0,3},{4,7},{8,11},{12,15},{16,19},{20,23},{24,27},{28,31}} | collective-permute-start | bytes 1056776 | tf_op jit(solution)/shard_map/ppermute | solution.py:197
  10.5 20.1 %collective-permute-start.6 = (f32[344,256]{1,0:T(8,128)S(1)}, f32[344,256]{1,0:T(8,128)}, u32[]{:S(2)}, u32[]{:S(2)}) collective-permute-start(f32[344,256]{1,0:T(8,128)S(1)} %get-tuple-element.12), channel_id=1, source_target_pairs={{0,2},{4,6},{8,10},{12,14},{16,18},{20,22},{24,26},{28,30}} | collective-permute-start | bytes 1056776 | tf_op jit(solution)/shard_map/ppermute | solution.py:197
  11.8 18.8 %collective-permute-start.5 = (f32[344,256]{1,0:T(8,128)S(1)}, f32[344,256]{1,0:T(8,128)}, u32[]{:S(2)}, u32[]{:S(2)}) collective-permute-start(f32[344,256]{1,0:T(8,128)S(1)} %get-tuple-element.13), channel_id=1, source_target_pairs={{0,1},{4,5},{8,9},{12,13},{16,17},{20,21},{24,25},{28,29}} | collective-permute-start | bytes 1056776 | tf_op jit(solution)/shard_map/ppermute | solution.py:197
  13.2 32.5 %collective-permute-start.1 = (f32[344,256]{1,0:T(8,128)}, f32[344,256]{1,0:T(8,128)}, u32[]{:S(2)}, u32[]{:S(2)}) collective-permute-start(f32[344,256]{1,0:T(8,128)} %get-tuple-element.10), channel_id=1, source_target_pairs={{0,2},{4,6},{8,10},{12,14},{16,18},{20,22},{24,26},{28,30}} | collective-permute-start | bytes 1056776 | tf_op jit(solution)/shard_map/ppermute | solution.py:197
  14.5 31.2 %collective-permute-start.2 = (f32[344,256]{1,0:T(8,128)}, f32[344,256]{1,0:T(8,128)}, u32[]{:S(2)}, u32[]{:S(2)}) collective-permute-start(f32[344,256]{1,0:T(8,128)} %get-tuple-element.14), channel_id=1, source_target_pairs={{0,3},{4,7},{8,11},{12,15},{16,19},{20,23},{24,27},{28,31}} | collective-permute-start | bytes 1056776 | tf_op jit(solution)/shard_map/ppermute | solution.py:197
  17.6 28.1 %collective-permute-start = (f32[344,256]{1,0:T(8,128)S(1)}, f32[344,256]{1,0:T(8,128)}, u32[]{:S(2)}, u32[]{:S(2)}) collective-permute-start(f32[344,256]{1,0:T(8,128)S(1)} %get-tuple-element.15), channel_id=1, source_target_pairs={{0,1},{4,5},{8,9},{12,13},{16,17},{20,21},{24,25},{28,29}} | collective-permute-start | bytes 1056776 | tf_op jit(solution)/shard_map/ppermute | solution.py:197
  32.5 38.3 %collective-permute-start.8 = (f32[344,256]{1,0:T(8,128)}, f32[344,256]{1,0:T(8,128)S(1)}, u32[]{:S(2)}, u32[]{:S(2)}) collective-permute-start(f32[344,256]{1,0:T(8,128)} %get-tuple-element.9), channel_id=1, source_target_pairs={{1,2},{2,3},{3,1},{5,6},{6,7},{7,5},{9,10},{10,11},{11,9},{13,14},... | collective-permute-start | bytes 1056776 | tf_op jit(solution)/shard_map/ppermute | solution.py:209
  34.4 38.4 %collective-permute-start.9 = (f32[344,256]{1,0:T(8,128)}, f32[344,256]{1,0:T(8,128)S(1)}, u32[]{:S(2)}, u32[]{:S(2)}) collective-permute-start(f32[344,256]{1,0:T(8,128)} %get-tuple-element.9), channel_id=1, source_target_pairs={{1,3},{2,1},{3,2},{5,7},{6,5},{7,6},{9,11},{10,9},{11,10},{13,15},... | collective-permute-start | bytes 1056776 | tf_op jit(solution)/shard_map/ppermute | solution.py:209
  47.7 29.2 %collective-permute-start.3 = (f32[344,256]{1,0:T(8,128)}, f32[344,256]{1,0:T(8,128)}, u32[]{:S(2)}, u32[]{:S(2)}) collective-permute-start(f32[344,256]{1,0:T(8,128)} %get-tuple-element.7), channel_id=1, source_target_pairs={{1,2},{2,3},{3,1},{5,6},{6,7},{7,5},{9,10},{10,11},{11,9},{13,14},... | collective-permute-start | bytes 1056776 | tf_op jit(solution)/shard_map/ppermute | solution.py:209
  58.4 23.3 %collective-permute-start.4 = (f32[344,256]{1,0:T(8,128)}, f32[344,256]{1,0:T(8,128)}, u32[]{:S(2)}, u32[]{:S(2)}) collective-permute-start(f32[344,256]{1,0:T(8,128)} %get-tuple-element.7), channel_id=1, source_target_pairs={{1,3},{2,1},{3,2},{5,7},{6,5},{7,6},{9,11},{10,9},{11,10},{13,15},... | collective-permute-start | bytes 1056776 | tf_op jit(solution)/shard_map/ppermute | solution.py:209
  74.3 19.6 %copy-start.3 = (f32[1024,256]{1,0:T(8,128)}, f32[1024,256]{1,0:T(8,128)S(1)}, u32[]{:S(2)}) copy-start(f32[1024,256]{1,0:T(8,128)S(1)} %dynamic_update_slice.23) | copy-start | bytes 3145732
  84.2 6.5 %copy-start.1 = (f32[1024,256]{1,0:T(8,128)}, f32[1024,256]{1,0:T(8,128)S(1)}, u32[]{:S(2)}) copy-start(f32[1024,256]{1,0:T(8,128)S(1)} %dynamic_update_slice.20) | copy-start | bytes 3145732
  90.7 1.7 copy-start.7
  92.3 16.1 %collective-permute-start.10 = (f32[128,2048]{1,0:T(8,128)}, f32[128,2048]{1,0:T(8,128)}, u32[]{:S(2)}, u32[]{:S(2)}) collective-permute-start(f32[128,2048]{1,0:T(8,128)} %constant_dynamic-slice_fusion.7), channel_id=1, source_target_pairs={{0,4},{4,0},{8,12},{12,8},{16,20},{20,16},{24,28},{28,24},{1,5},{5... | collective-permute-start | bytes 3145736 | tf_op jit(solution)/shard_map/ppermute | solution.py:221
  100.0 1.3 copy-start.5
  101.4 7.0 %copy-start.8 = (f32[256,2048]{1,0:T(8,128)S(1)}, f32[256,2048]{1,0:T(8,128)}, u32[]{:S(2)}) copy-start(f32[256,2048]{1,0:T(8,128)} %copy-done.7) | copy-start | bytes 6291460
  101.4 11.3 %collective-permute-start.21 = (f32[128,2048]{1,0:T(8,128)S(1)}, f32[128,2048]{1,0:T(8,128)}, u32[]{:S(2)}, u32[]{:S(2)}) collective-permute-start(f32[128,2048]{1,0:T(8,128)S(1)} %constant_dynamic-slice_fusion.3), channel_id=1, source_target_pairs={{0,4},{4,0},{8,12},{12,8},{16,20},{20,16},{24,28},{28,24},{1,5},{5... | collective-permute-start | bytes 3145736 | tf_op jit(solution)/shard_map/ppermute | solution.py:221
  108.4 4.3 %copy-start.6 = (f32[256,2048]{1,0:T(8,128)S(1)}, f32[256,2048]{1,0:T(8,128)}, u32[]{:S(2)}) copy-start(f32[256,2048]{1,0:T(8,128)} %copy-done.5) | copy-start | bytes 6291460
  110.0 7.6 %collective-permute-start.11 = (f32[32,2048]{1,0:T(8,128)S(1)}, f32[32,2048]{1,0:T(8,128)S(1)}, u32[]{:S(2)}, u32[]{:S(2)}) collective-permute-start(f32[32,2048]{1,0:T(8,128)S(1)} %get-tuple-element.21), channel_id=1, source_target_pairs={{0,8},{4,12},{8,0},{12,4},{16,24},{20,28},{24,16},{28,20},{1,9},{5... | collective-permute-start | bytes 786440 | tf_op jit(solution)/shard_map/ppermute | solution.py:225
  111.2 14.0 %collective-permute-start.13 = (f32[32,2048]{1,0:T(8,128)S(1)}, f32[32,2048]{1,0:T(8,128)S(1)}, u32[]{:S(2)}, u32[]{:S(2)}) collective-permute-start(f32[32,2048]{1,0:T(8,128)S(1)} %get-tuple-element.22), channel_id=1, source_target_pairs={{0,24},{4,28},{8,16},{12,20},{16,8},{20,12},{24,0},{28,4},{1,25},{... | collective-permute-start | bytes 786440 | tf_op jit(solution)/shard_map/ppermute | solution.py:225
  112.4 12.8 %collective-permute-start.12 = (f32[32,2048]{1,0:T(8,128)S(1)}, f32[32,2048]{1,0:T(8,128)S(1)}, u32[]{:S(2)}, u32[]{:S(2)}) collective-permute-start(f32[32,2048]{1,0:T(8,128)S(1)} %get-tuple-element.23), channel_id=1, source_target_pairs={{0,16},{4,20},{8,24},{12,28},{16,0},{20,4},{24,8},{28,12},{1,17},{... | collective-permute-start | bytes 786440 | tf_op jit(solution)/shard_map/ppermute | solution.py:225
  114.1 16.8 %collective-permute-start.22 = (f32[32,2048]{1,0:T(8,128)S(1)}, f32[32,2048]{1,0:T(8,128)S(1)}, u32[]{:S(2)}, u32[]{:S(2)}) collective-permute-start(f32[32,2048]{1,0:T(8,128)S(1)} %get-tuple-element.18), channel_id=1, source_target_pairs={{0,8},{4,12},{8,0},{12,4},{16,24},{20,28},{24,16},{28,20},{1,9},{5... | collective-permute-start | bytes 786440 | tf_op jit(solution)/shard_map/ppermute | solution.py:225
  115.4 22.1 %collective-permute-start.24 = (f32[32,2048]{1,0:T(8,128)S(1)}, f32[32,2048]{1,0:T(8,128)S(1)}, u32[]{:S(2)}, u32[]{:S(2)}) collective-permute-start(f32[32,2048]{1,0:T(8,128)S(1)} %get-tuple-element.19), channel_id=1, source_target_pairs={{0,24},{4,28},{8,16},{12,20},{16,8},{20,12},{24,0},{28,4},{1,25},{... | collective-permute-start | bytes 786440 | tf_op jit(solution)/shard_map/ppermute | solution.py:225
  117.5 21.2 %collective-permute-start.23 = (f32[32,2048]{1,0:T(8,128)S(1)}, f32[32,2048]{1,0:T(8,128)S(1)}, u32[]{:S(2)}, u32[]{:S(2)}) collective-permute-start(f32[32,2048]{1,0:T(8,128)S(1)} %get-tuple-element.20), channel_id=1, source_target_pairs={{0,16},{4,20},{8,24},{12,28},{16,0},{20,4},{24,8},{28,12},{1,17},{... | collective-permute-start | bytes 786440 | tf_op jit(solution)/shard_map/ppermute | solution.py:225
  125.3 21.9 %collective-permute-start.17 = (f32[32,2048]{1,0:T(8,128)S(1)}, f32[32,2048]{1,0:T(8,128)S(1)}, u32[]{:S(2)}, u32[]{:S(2)}) collective-permute-start(f32[32,2048]{1,0:T(8,128)S(1)} %add_add_fusion.3.rest_0_), channel_id=1, source_target_pairs={{0,4},{4,0},{8,12},{12,8},{16,20},{20,16},{24,28},{28,24},{1,5},{5... | collective-permute-start | bytes 786440 | tf_op jit(solution)/shard_map/ppermute | solution.py:228
  129.8 18.6 %collective-permute-start.16 = (f32[32,2048]{1,0:T(8,128)S(1)}, f32[32,2048]{1,0:T(8,128)S(1)}, u32[]{:S(2)}, u32[]{:S(2)}) collective-permute-start(f32[32,2048]{1,0:T(8,128)S(1)} %add_add_fusion.3.rest_0_), channel_id=1, source_target_pairs={{0,24},{4,28},{8,16},{12,20},{16,8},{20,12},{24,0},{28,4},{1,25},{... | collective-permute-start | bytes 786440 | tf_op jit(solution)/shard_map/ppermute | solution.py:226
  130.9 18.9 %collective-permute-start.15 = (f32[32,2048]{1,0:T(8,128)S(1)}, f32[32,2048]{1,0:T(8,128)S(1)}, u32[]{:S(2)}, u32[]{:S(2)}) collective-permute-start(f32[32,2048]{1,0:T(8,128)S(1)} %add_add_fusion.3.rest_0_), channel_id=1, source_target_pairs={{0,16},{4,20},{8,24},{12,28},{16,0},{20,4},{24,8},{28,12},{1,17},{... | collective-permute-start | bytes 786440 | tf_op jit(solution)/shard_map/ppermute | solution.py:226
  137.5 13.2 %collective-permute-start.14 = (f32[32,2048]{1,0:T(8,128)S(1)}, f32[32,2048]{1,0:T(8,128)S(1)}, u32[]{:S(2)}, u32[]{:S(2)}) collective-permute-start(f32[32,2048]{1,0:T(8,128)S(1)} %add_add_fusion.3.rest_0_), channel_id=1, source_target_pairs={{0,8},{4,12},{8,0},{12,4},{16,24},{20,28},{24,16},{28,20},{1,9},{5... | collective-permute-start | bytes 786440 | tf_op jit(solution)/shard_map/ppermute | solution.py:226
  138.8 21.0 %collective-permute-start.28 = (f32[32,2048]{1,0:T(8,128)S(1)}, f32[32,2048]{1,0:T(8,128)S(1)}, u32[]{:S(2)}, u32[]{:S(2)}) collective-permute-start(f32[32,2048]{1,0:T(8,128)S(1)} %add_add_fusion.2.rest_8_), channel_id=1, source_target_pairs={{0,4},{4,0},{8,12},{12,8},{16,20},{20,16},{24,28},{28,24},{1,5},{5... | collective-permute-start | bytes 786440 | tf_op jit(solution)/shard_map/ppermute | solution.py:228
  147.2 12.7 %collective-permute-start.27 = (f32[32,2048]{1,0:T(8,128)S(1)}, f32[32,2048]{1,0:T(8,128)S(1)}, u32[]{:S(2)}, u32[]{:S(2)}) collective-permute-start(f32[32,2048]{1,0:T(8,128)S(1)} %add_add_fusion.2.rest_8_), channel_id=1, source_target_pairs={{0,24},{4,28},{8,16},{12,20},{16,8},{20,12},{24,0},{28,4},{1,25},{... | collective-permute-start | bytes 786440 | tf_op jit(solution)/shard_map/ppermute | solution.py:226
  148.4 14.5 %collective-permute-start.26 = (f32[32,2048]{1,0:T(8,128)S(1)}, f32[32,2048]{1,0:T(8,128)S(1)}, u32[]{:S(2)}, u32[]{:S(2)}) collective-permute-start(f32[32,2048]{1,0:T(8,128)S(1)} %add_add_fusion.2.rest_8_), channel_id=1, source_target_pairs={{0,16},{4,20},{8,24},{12,28},{16,0},{20,4},{24,8},{28,12},{1,17},{... | collective-permute-start | bytes 786440 | tf_op jit(solution)/shard_map/ppermute | solution.py:226
  149.8 13.5 %collective-permute-start.25 = (f32[32,2048]{1,0:T(8,128)S(1)}, f32[32,2048]{1,0:T(8,128)S(1)}, u32[]{:S(2)}, u32[]{:S(2)}) collective-permute-start(f32[32,2048]{1,0:T(8,128)S(1)} %add_add_fusion.2.rest_8_), channel_id=1, source_target_pairs={{0,8},{4,12},{8,0},{12,4},{16,24},{20,28},{24,16},{28,20},{1,9},{5... | collective-permute-start | bytes 786440 | tf_op jit(solution)/shard_map/ppermute | solution.py:226
  150.7 13.4 %collective-permute-start.20 = (f32[32,2048]{1,0:T(8,128)S(1)}, f32[32,2048]{1,0:T(8,128)S(1)}, u32[]{:S(2)}, u32[]{:S(2)}) collective-permute-start(f32[32,2048]{1,0:T(8,128)S(1)} %collective-permute-done.16.rest_3_), channel_id=1, source_target_pairs={{0,4},{4,0},{8,12},{12,8},{16,20},{20,16},{24,28},{28,24},{1,5},{5... | collective-permute-start | bytes 786440 | tf_op jit(solution)/shard_map/ppermute | solution.py:228
  159.8 123.4 %collective-permute-start.19 = (f32[32,2048]{1,0:T(8,128)S(1)}, f32[32,2048]{1,0:T(8,128)S(1)}, u32[]{:S(2)}, u32[]{:S(2)}) collective-permute-start(f32[32,2048]{1,0:T(8,128)S(1)} %collective-permute-done.15.rest_2_), channel_id=1, source_target_pairs={{0,4},{4,0},{8,12},{12,8},{16,20},{20,16},{24,28},{28,24},{1,5},{5... | collective-permute-start | bytes 786440 | tf_op jit(solution)/shard_map/ppermute | solution.py:228
  159.9 123.4 %collective-permute-start.18 = (f32[32,2048]{1,0:T(8,128)S(1)}, f32[32,2048]{1,0:T(8,128)S(1)}, u32[]{:S(2)}, u32[]{:S(2)}) collective-permute-start(f32[32,2048]{1,0:T(8,128)S(1)} %collective-permute-done.14.rest_1_), channel_id=1, source_target_pairs={{0,4},{4,0},{8,12},{12,8},{16,20},{20,16},{24,28},{28,24},{1,5},{5... | collective-permute-start | bytes 786440 | tf_op jit(solution)/shard_map/ppermute | solution.py:228
  162.9 120.4 %collective-permute-start.31 = (f32[32,2048]{1,0:T(8,128)S(1)}, f32[32,2048]{1,0:T(8,128)}, u32[]{:S(2)}, u32[]{:S(2)}) collective-permute-start(f32[32,2048]{1,0:T(8,128)S(1)} %collective-permute-done.27.rest_11_), channel_id=1, source_target_pairs={{0,4},{4,0},{8,12},{12,8},{16,20},{20,16},{24,28},{28,24},{1,5},{5... | collective-permute-start | bytes 786440 | tf_op jit(solution)/shard_map/ppermute | solution.py:228
  163.3 120.0 %collective-permute-start.30 = (f32[32,2048]{1,0:T(8,128)S(1)}, f32[32,2048]{1,0:T(8,128)}, u32[]{:S(2)}, u32[]{:S(2)}) collective-permute-start(f32[32,2048]{1,0:T(8,128)S(1)} %collective-permute-done.26.rest_10_), channel_id=1, source_target_pairs={{0,4},{4,0},{8,12},{12,8},{16,20},{20,16},{24,28},{28,24},{1,5},{5... | collective-permute-start | bytes 786440 | tf_op jit(solution)/shard_map/ppermute | solution.py:228
  164.1 119.2 %collective-permute-start.29 = (f32[32,2048]{1,0:T(8,128)S(1)}, f32[32,2048]{1,0:T(8,128)}, u32[]{:S(2)}, u32[]{:S(2)}) collective-permute-start(f32[32,2048]{1,0:T(8,128)S(1)} %collective-permute-done.25.rest_9_), channel_id=1, source_target_pairs={{0,4},{4,0},{8,12},{12,8},{16,20},{20,16},{24,28},{28,24},{1,5},{5... | collective-permute-start | bytes 786440 | tf_op jit(solution)/shard_map/ppermute | solution.py:228
  249.8 1.2 copy-start
  251.1 31.8 %copy-start.2 = (f32[1024,256]{1,0:T(8,128)S(1)}, f32[1024,256]{1,0:T(8,128)}, u32[]{:S(2)}) copy-start(f32[1024,256]{1,0:T(8,128)} %copy-done.1) | copy-start | bytes 3145732
  251.1 31.8 %copy-start.4 = (f32[1024,256]{1,0:T(8,128)S(1)}, f32[1024,256]{1,0:T(8,128)}, u32[]{:S(2)}) copy-start(f32[1024,256]{1,0:T(8,128)} %copy-done.3) | copy-start | bytes 3145732
Sparse Core Ops, SparseCore 0:
  108.5 141.3 all-reduce.1

commit v2 on v1

v2 whole, which is shorter than its diff:
```python
import jax
import jax.numpy as jnp
from jax import lax
from jax.experimental import pallas as pl
from jax.experimental.pallas import tpu as pltpu
from jax.sharding import PartitionSpec as P

PB = 512
NB = 128
F32 = jnp.float32
BF16 = jnp.bfloat16
HIGHEST = lax.Precision.HIGHEST
VMEM = pl.BlockSpec(memory_space=pltpu.VMEM)


def mm(a, b, da, db, precision=None):
    return lax.dot_general(
        a, b, (((da,), (db,)), ((), ())), precision=precision, preferred_element_type=F32
    )


def split(x):
    high = x.astype(BF16)
    return high, (x - high.astype(F32)).astype(BF16)


def diag_block(d_ref, z_ref, f_ref):
    a_all = d_ref[...]
    row = lax.broadcasted_iota(jnp.int32, (NB, NB), 0)
    col = lax.broadcasted_iota(jnp.int32, (NB, NB), 1)
    z_all = jnp.where(row == col, 1.0, 0.0).astype(F32)
    lane = lax.broadcasted_iota(jnp.int32, (1, NB), 1)
    for j in range(0, NB, 2):
        base = (j // 8) * 8
        if a_all.shape[0] != NB - base:
            a_all, z_all = a_all[8:], z_all[8:]
        i, n = j - base, NB - base
        r0, r1 = a_all[i : i + 1, :], a_all[i + 1 : i + 2, :]
        z0, z1 = z_all[i : i + 1, :], z_all[i + 1 : i + 2, :]
        c0 = jnp.broadcast_to(a_all[:, j : j + 1], (n, NB))
        c1 = jnp.broadcast_to(a_all[:, j + 1 : j + 2], (n, NB))
        a = jnp.broadcast_to(r0[:, j : j + 1], (1, NB))
        b = jnp.broadcast_to(r0[:, j + 1 : j + 2], (1, NB))
        d = jnp.broadcast_to(r1[:, j + 1 : j + 2], (1, NB))
        ra = 1.0 / a
        bra = b * ra
        s = d - b * bra
        rs = 1.0 / s
        t1 = r1 - bra * r0
        x1 = t1 * rs
        x0 = r0 * ra - bra * x1
        u1 = z1 - bra * z0
        y1 = u1 * rs
        y0 = z0 * ra - bra * y1
        qa, qs = lax.rsqrt(a), lax.rsqrt(s)
        f_ref[j : j + 1, :] = jnp.where(lane >= j, r0 * qa, 0.0)
        f_ref[j + 1 : j + 2, :] = jnp.where(lane >= j + 1, t1 * qs, 0.0)
        z_ref[j : j + 1, :] = z0 * qa
        z_ref[j + 1 : j + 2, :] = u1 * qs
        if j + 2 < NB:
            a_all = a_all - c0 * x0 - c1 * x1
            z_all = z_all - c0 * y0 - c1 * y1


def chol_part(info, first, last, pieces=None, places=None, state=None):
    fresh = pieces is not None
    arrays = pieces if fresh else state
    n = arrays[0].shape[1]
    nb = n // NB
    n_in = len(arrays)

    def kernel(info_ref, *refs):
        work, f_out, l_out = refs[n_in : n_in + 3]
        diag, zs, fs = refs[n_in + 3 :]
        if fresh:
            chips = n_in // 2
            for ref, (core, chip) in zip(refs, places):
                h = ref.shape[0]
                off = (info_ref[1] ^ core) * (h * chips) + (info_ref[2] ^ chip) * h
                work[pl.ds(pl.multiple_of(off, 8), h), :] = ref[...]
            f_out[...] = jnp.zeros_like(f_out)
            l_out[...] = jnp.zeros_like(l_out)

        def body(k, carry):
            o = pl.multiple_of(k * NB, NB)
            diag[...] = work[pl.ds(o, NB), pl.ds(o, NB)]
            diag_block(diag, zs, fs)
            for kk in range(first, last):

                @pl.when(k == kk)
                def _():
                    o, e = kk * NB, kk * NB + NB
                    z = zs[...]
                    f_out[o:e, o:e] = fs[...]
                    lk = z
                    if kk > 0:
                        lk = jnp.concatenate([mm(z, l_out[o:e, :o], 1, 0, HIGHEST), z], axis=1)
                    l_out[o:e, :e] = lk
                    if kk < nb - 1:
                        u = mm(z, work[o:e, e:], 1, 0, HIGHEST)
                        f_out[o:e, e:] = u
                        work[e:, e:] -= mm(u, u, 0, 0, HIGHEST)
                        l_out[e:, :e] -= mm(u, lk, 0, 0, HIGHEST)

            return carry

        lax.fori_loop(first, last, body, 0)

    shape = jax.ShapeDtypeStruct((n, n), F32)
    return pl.pallas_call(
        kernel,
        out_shape=(shape, shape, shape),
        in_specs=[pl.BlockSpec(memory_space=pltpu.SMEM)] + [VMEM] * n_in,
        out_specs=(VMEM, VMEM, VMEM),
        scratch_shapes=[pltpu.VMEM((NB, NB), F32)] * 3,
        input_output_aliases={} if fresh else {1: 0, 2: 1, 3: 2},
        compiler_params=pltpu.CompilerParams(vmem_limit_bytes=16 << 20),
        cost_estimate=pl.CostEstimate(
            flops=(last - first) * 8 * 10**9, bytes_accessed=3 << 20, transcendentals=0
        ),
        name="chol_part",
    )(info, *arrays)


def finish(info, snapshots, panels, linv, factor, pieces, layout, tile=256, block=1024):
    rows, cols = snapshots.shape
    n_pieces, n_panels = len(pieces), len(panels)
    chips = 1 + max(chip for _, _, chip in layout)
    bases = [sum(p.shape[1] for p in panels[:i]) for i in range(n_panels)]

    def kernel(info_ref, s_ref, l_ref, f_ref, *rest):
        p_refs, rest = rest[:n_panels], rest[n_panels:]
        m_refs = rest[:n_pieces]
        up_ref, co_ref, bs, b3, l3, ms, m3, p3 = rest[n_pieces:]
        j = pl.program_id(0)

        @pl.when(j == 0)
        def _():
            lh, ll = split(l_ref[...])
            l3[:, :PB], l3[:, PB : 2 * PB], l3[:, 2 * PB :] = lh, lh, ll
            for r in range(0, rows, 256):
                b = 0.0
                for base, p_ref in zip(bases, p_refs):
                    end = base + p_ref.shape[1]
                    ph, plow = split(p_ref[r : r + 256, :])
                    lhs = jnp.concatenate([ph, ph, plow], axis=1)
                    rhs = jnp.concatenate([lh[:, base:end], ll[:, base:end], lh[:, base:end]], axis=1)
                    b = b + mm(lhs, rhs, 1, 1)
                bs[r : r + 256, :] = b
                bh, bl = split(b)
                b3[r : r + 256, :PB], b3[r : r + 256, PB : 2 * PB] = bh, bh
                b3[r : r + 256, 2 * PB :] = bl

        for ref, (base, core, chip) in zip(m_refs, layout):
            h = ref.shape[0]
            off = base + (info_ref[1] ^ core) * (h * chips) + (info_ref[2] ^ chip) * h
            ms[pl.ds(pl.multiple_of(off, 8), h), :] = ref[...]
        mh, ml = split(ms[...])
        m3[:PB, :], m3[PB : 2 * PB, :], m3[2 * PB :, :] = mh, ml, mh
        proj = mm(l3[...], m3[...], 1, 0)
        ph, plow = split(proj)
        p3[:PB, :], p3[PB : 2 * PB, :], p3[2 * PB :, :] = ph, plow, ph
        co_ref[...] = proj
        for r in range(0, rows, block):
            up_ref[r : r + block, :] = s_ref[r : r + block, :] - mm(b3[r : r + block, :], p3[...], 1, 0)
        for t in range(PB // tile):

            @pl.when((info_ref[0] == 0) & (j == t))
            def _():
                co_ref[...] = f_ref[:, t * tile : (t + 1) * tile]
                up_ref[...] = bs[:, t * tile : (t + 1) * tile]

    full = lambda a: pl.BlockSpec(a.shape, lambda j, *_: (0, 0), pipeline_mode=pl.Buffered(1))
    col = lambda h: pl.BlockSpec((h, tile), lambda j, *_: (0, j))
    return pl.pallas_call(
        kernel,
        out_shape=(
            jax.ShapeDtypeStruct((rows, cols), F32),
            jax.ShapeDtypeStruct((PB, cols), F32),
        ),
        grid_spec=pltpu.PrefetchScalarGridSpec(
            num_scalar_prefetch=1,
            grid=(cols // tile,),
            in_specs=[col(rows), full(linv), full(factor)]
            + [full(p) for p in panels]
            + [col(p.shape[0]) for p in pieces],
            out_specs=(col(rows), col(PB)),
            scratch_shapes=[
                pltpu.VMEM((rows, PB), F32),
                pltpu.VMEM((rows, 3 * PB), BF16),
                pltpu.VMEM((PB, 3 * PB), BF16),
                pltpu.VMEM((PB, tile), F32),
                pltpu.VMEM((3 * PB, tile), BF16),
                pltpu.VMEM((3 * PB, tile), BF16),
            ],
        ),
        compiler_params=pltpu.CompilerParams(vmem_limit_bytes=58 << 20),
        cost_estimate=pl.CostEstimate(
            flops=6 * PB * cols * (rows + PB), bytes_accessed=8 * rows * cols, transcendentals=0
        ),
        name="finish",
    )(info, snapshots, linv, factor, *panels, *pieces)


def panel_dot(info, snapshots, parts, size, base, width, scale, tile=256):
    rows, cols = snapshots.shape
    half = width // 2
    n_parts = len(parts)

    def kernel(info_ref, s_ref, own_ref, *rest):
        part_refs = rest[:n_parts]
        send_ref, mine_ref, p_ref, pt3, s3, ms = rest[n_parts:]
        j = pl.program_id(0)

        @pl.when((j == 0) & (info_ref[0] == 0))
        def _():
            p_ref[...] = own_ref[...]

        if n_parts:

            @pl.when((j == 0) & (info_ref[0] != 0))
            def _():
                for k, ref in enumerate(part_refs):
                    start = pl.multiple_of(info_ref[3 + k], 8)
                    p_ref[pl.ds(start, size), :] = ref[...]

        @pl.when(j == 0)
        def _():
            for r in range(0, rows, 256):
                ph, plow = split(p_ref[r : r + 256, :])
                pt = ph.T
                pt3[:, r : r + 256], pt3[:, rows + r : rows + r + 256] = pt, pt
                pt3[:, 2 * rows + r : 2 * rows + r + 256] = plow.T

        sh, sl = split(s_ref[...])
        s3[:rows, :], s3[rows : 2 * rows, :], s3[2 * rows :, :] = sh, sl, sh
        ms[...] = mm(pt3[...], s3[...], 1, 0) * scale
        send_ref[...] = ms[pl.ds(pl.multiple_of((1 - info_ref[1]) * half, half), half), :]
        mine_ref[...] = ms[pl.ds(pl.multiple_of(info_ref[1] * half, half), half), :]

    full = lambda a: pl.BlockSpec(a.shape, lambda j, *_: (0, 0), pipeline_mode=pl.Buffered(1))
    col = lambda h: pl.BlockSpec((h, tile), lambda j, *_: (0, j))
    out = jax.ShapeDtypeStruct((half, cols), F32)
    return pl.pallas_call(
        kernel,
        out_shape=(out, out, jax.ShapeDtypeStruct((rows, width), F32)),
        grid_spec=pltpu.PrefetchScalarGridSpec(
            num_scalar_prefetch=1,
            grid=(cols // tile,),
            in_specs=[
                col(rows),
                pl.BlockSpec(
                    (rows, width), lambda j, *_: (0, base // width), pipeline_mode=pl.Buffered(1)
                ),
            ]
            + [full(p) for p in parts],
            out_specs=(col(half), col(half), pl.BlockSpec((rows, width), lambda j, *_: (0, 0))),
            scratch_shapes=[
                pltpu.VMEM((width, 3 * rows), BF16),
                pltpu.VMEM((3 * rows, tile), BF16),
                pltpu.VMEM((width, tile), F32),
            ],
        ),
        compiler_params=pltpu.CompilerParams(vmem_limit_bytes=58 << 20),
        cost_estimate=pl.CostEstimate(
            flops=6 * rows * cols * width, bytes_accessed=4 * rows * cols, transcendentals=0
        ),
        name="panel_dot",
    )(info, snapshots, snapshots, *parts)


def part_size(rows, parts):
    return -(-rows // (8 * parts)) * 8


def spread_out(x, n):
    rows, parts = x.shape[0], n - 1
    size = part_size(rows, parts)
    mine = None
    for k in reversed(range(parts)):
        start = min(k * size, rows - size)
        part = lax.ppermute(x[start : start + size], "cols", [(0, k + 1)])
        mine = part if mine is None else mine + part
    return mine


def spread_round(mine, n):
    got, parts = [mine], n - 1
    for k in range(1, parts):
        pairs = [(1 + i, 1 + (i + k) % parts) for i in range(parts)]
        got.append(lax.ppermute(mine, "cols", pairs))
    return got


def after(x, *others):
    return lax.optimization_barrier((x, others))[0]


def swap(n, k):
    return [(i, i ^ k) for i in range(n)]


def take(a, start, size):
    return lax.dynamic_slice_in_dim(a, start, size, 0)


def join_cores(send, mine, n):
    return mine + lax.ppermute(send, "rows", swap(n, 1))


def scatter_chips(mine, n):
    chips = n // 2
    chip = lax.axis_index("rows") >> 1
    piece = mine.shape[0] // chips
    own = take(mine, chip * piece, piece)
    for k in range(1, chips):
        own = own + lax.ppermute(take(mine, (chip ^ k) * piece, piece), "rows", swap(n, 2 * k))
    return own


def gather_rows(own, n):
    got = [own] + [lax.ppermute(own, "rows", swap(n, 2 * k)) for k in range(1, n // 2)]
    other = [lax.ppermute(g, "rows", swap(n, 1)) for g in got]
    return got + other, [(0, k) for k in range(n // 2)] + [(1, k) for k in range(n // 2)]


def shards(snapshots):
    rows_dev, cols_dev = snapshots.shape
    n_rows, n_cols = lax.axis_size("rows"), lax.axis_size("cols")
    total_rows = rows_dev * n_rows
    z, index = lax.axis_index("cols"), lax.axis_index("rows")
    core = index & 1
    parts = n_cols - 1
    size = part_size(rows_dev, parts)
    starts = [jnp.minimum(((z - 1 - k) % parts) * size, rows_dev - size) for k in range(parts)]
    info = jnp.stack([z, core, index >> 1] + starts).astype(jnp.int32)
    half = PB // 2
    panel = snapshots[:, :PB]
    dot = lambda got, base: panel_dot(
        info, snapshots, got, size, base, half, 1.0 / total_rows
    )

    mine_a = spread_out(panel[:, :half], n_cols)
    gram = mm(panel, panel, 0, 0, HIGHEST) / total_rows
    joined = join_cores(take(gram, (1 - core) * half, half), take(gram, core * half, half), n_rows)
    share = scatter_chips(joined, n_rows)
    far = [lax.ppermute(share, "cols", [(0, k)]) for k in reversed(range(1, n_cols))]
    share = jnp.where(z == 0, share, sum(far, jnp.zeros_like(share)))
    grams, places = gather_rows(share, n_rows)

    got_a = spread_round(mine_a, n_cols)
    mine_b = spread_out(after(panel[:, half:], mine_a, share), n_cols)
    send, keep, panel_a = dot(got_a, 0)
    grams = after(grams, send)
    state = chol_part(info, 0, 1, pieces=grams, places=places)
    joined = join_cores(send, keep, n_rows)
    own_a = scatter_chips(joined, n_rows)
    got_b = spread_round(mine_b, n_cols)
    state = chol_part(info, 1, 2, state=after(state, joined, mine_b))
    pieces_a, where = gather_rows(own_a, n_rows)
    send, keep, panel_b = dot(after(got_b, own_a), half)
    joined = join_cores(send, keep, n_rows)
    own_b = scatter_chips(joined, n_rows)
    state = chol_part(info, 2, 3, state=after(state, joined))
    pieces_b, _ = gather_rows(own_b, n_rows)
    _, factor, linv = chol_part(info, 3, 4, state=after(state, own_b))
    layout = [(base,) + w for base in (0, half) for w in where]
    return finish(
        info, snapshots, [panel_a, panel_b], linv, factor, pieces_a + pieces_b, layout
    )


def solution(mesh):
    in_specs = (P("rows", "cols"),)
    out_specs = (P("rows", "cols"), P(None, "cols"))
    return jax.shard_map(shards, mesh=mesh, in_specs=in_specs, out_specs=out_specs, check_vma=False)
```

time: 319 us -> 235 us (0.74); the launches traced: 314 us -> 234 us
  waiting for transfers between devices: 118 us -> 50.5 us
  Pallas kernels: 56 us -> 82 us
  matrix products: 19.4 us -> 5.71 us
  between operations: 14.5 us -> 1.31 us
  local copies, waits for them, and re-layouts: 17.6 us -> 9.15 us
  other arithmetic: 11.2 us -> 4.93 us
    psum x1 -> x0, waiting for transfers between devices: 85.7 us -> none  [shards(): gram = lax.psum(jnp.where(z == 0, gram, 0.0), ('rows', 'cols'))]
    pallas_call x1 -> x6, Pallas kernels: 31.8 us -> 56 us  [the longest x4 33.8 us: chol_part(): pl.pallas_call(kernel, out_shape=(shape, shape, shape), in_specs=[pl.Bloc...]
    ppermute x32 -> x46, waiting for transfers between devices: 32.5 us -> 50.5 us  [the longest x4 25 us: spread_round(): got.append(lax.ppermute(mine, 'cols', pairs))]
    dot_general x3 -> x1, matrix products: 19.4 us -> 5.71 us  [mm(): lax.dot_general(a, b, (((da,), (db,)), ((), ())), precision=precision, pr...]
    dynamic_update_slice x6 -> x0, local copies, waits for them, and re-layouts: 10.6 us -> none  [place(): lax.dynamic_update_slice(out, jnp.where(z == 0, old, part), (start, 0))]
    select_n x7 -> x1, other arithmetic: 7.88 us -> 0.04 us  [shards(): share = jnp.where(z == 0, share, sum(far, jnp.zeros_like(share)))]
    ppermute x32 -> x46, starting transfers between devices: 77.3 us -> 80.4 us  [the longest x4 39.2 us: spread_round(): got.append(lax.ppermute(mine, 'cols', pairs))]
  transfers between devices with their start and end apart: 33 -> 46, of which waited for: 9 -> 14; matrix products, arithmetic and copies ran while one was open for 10% -> 6% of each run, Pallas kernels for 10% -> 19%
where the time goes in v2:
time: 235 us; the launch traced here: 234 us
  Pallas kernels  82 us (35%)
  starting transfers between devices  80.4 us (34%)
  waiting for transfers between devices  50.5 us (21%)
  local copies, waits for them, and re-layouts  9.15 us (4%)
  matrix products  5.71 us (2%)
  other arithmetic  4.93 us (2%)
    ppermute x4, starting transfers between devices, spread_round(): got.append(lax.ppermute(mine, 'cols', pairs))  39.2 us
    pallas_call x4, Pallas kernels, chol_part(): pl.pallas_call(kernel, out_shape=(shape, shape, shape), in_specs=[pl.Bloc...  33.8 us
    pallas_call x1, Pallas kernels, finish(): pl.pallas_call(kernel, out_shape=(jax.ShapeDtypeStruct((rows, cols), F32)...  26 us
    ppermute x4, waiting for transfers between devices, spread_round(): got.append(lax.ppermute(mine, 'cols', pairs))  25 us
    pallas_call x2, Pallas kernels, panel_dot(): pl.pallas_call(kernel, out_shape=(out, out, jax.ShapeDtypeStruct((rows, w...  22.2 us
    ppermute x12, starting transfers between devices, gather_rows(): other = [lax.ppermute(g, 'rows', swap(n, 1)) for g in got]  9.38 us
    ppermute x9, starting transfers between devices, scatter_chips(): lax.ppermute(take(mine, (chip ^ k) * piece, piece), 'rows', swap(n, 2 * k))  9.09 us
    ppermute x9, starting transfers between devices, gather_rows(): lax.ppermute(own, 'rows', swap(n, 2 * k))  8.71 us
  transfers between devices with their start and end apart: 46, of which 14 were waited for; matrix products, arithmetic and copies ran while one was open for 6% of the time, Pallas kernels for 19%

profile of v2, /device:TPU:17, one launch (start us, length us, event | category | flops | bytes accessed | tf_op | source)
XLA Modules:
  0.0 234.0 jit_solution(9386565797862280372)
XLA Ops:
  0.6 2.1 fusion.5
  2.8 1.3 collective-permute-start.15
  4.7 1.4 collective-permute-start.14
  6.2 5.7 %fusion.2 = f32[512,512]{1,0:T(8,128)S(1)} fusion(f32[1024,2048]{1,0:T(8,128)} %s_ref.5), kind=kOutput, calls=%fused_computation.2 | convolution fusion | flops 3221487616 | bytes 3145728 | tf_op jit(solution)/shard_map/dot_general | solution.py:17
  11.9 0.7 collective-permute-start
  13.3 1.6 collective-permute-done.15
  14.9 1.1 add_add_fusion.1.rest_0_
  15.9 9.7 %collective-permute-start.18 = (f32[344,256]{1,0:T(8,128)S(1)}, f32[344,256]{1,0:T(8,128)S(1)}, u32[]{:S(2)}, u32[]{:S(2)}) collective-permute-start(f32[344,256]{1,0:T(8,128)S(1)} %add_add_fusion.1.rest_0_), channel_id=1, source_target_pairs={{1,3},{2,1},{3,2},{5,7},{6,5},{7,6},{9,11},{10,9},{11,10},{13,15},... | collective-permute-start | bytes 1056776 | tf_op jit(solution)/shard_map/ppermute | solution.py:291
  25.7 10.5 %collective-permute-start.17 = (f32[344,256]{1,0:T(8,128)S(1)}, f32[344,256]{1,0:T(8,128)S(1)}, u32[]{:S(2)}, u32[]{:S(2)}) collective-permute-start(f32[344,256]{1,0:T(8,128)S(1)} %add_add_fusion.1.rest_0_), channel_id=1, source_target_pairs={{1,2},{2,3},{3,1},{5,6},{6,7},{7,5},{9,10},{10,11},{11,9},{13,14},... | collective-permute-start | bytes 1056776 | tf_op jit(solution)/shard_map/ppermute | solution.py:291
  36.3 1.3 collective-permute-start.1
  37.6 1.2 collective-permute-start.3
  39.0 2.2 collective-permute-done.18.rest_2_
  41.2 9.4 %collective-permute-done.17.rest_1_ = f32[344,256]{1,0:T(8,128)S(1)} collective-permute-done((f32[344,256]{1,0:T(8,128)S(1)}, f32[344,256]{1,0:T(8,128)S(1)}, u32[]{:S(2)}, u32[]{:S(2)}) %collective-permute-start.17) | collective-permute-done | bytes 352288 | tf_op jit(solution)/shard_map/ppermute | solution.py:291
  50.6 0.8 copy-done.7
  51.4 11.1 %panel_dot.2 = (f32[128,2048]{1,0:T(8,128)}, f32[128,2048]{1,0:T(8,128)}, f32[1024,256]{1,0:T(8,128)}) custom-call(s32[6]{0:T(128)} %stack.27.info_ref, f32[1024,2048]{1,0:T(8,128)} %s_ref.5, f32[1024,2048]{1,0:T(8,128)} %s_ref.5, f32[344,256]{1,0:T(8,128)} %copy-done.3, f32[344,256]{1,0:T(8,128)} %copy-done.7, f32[344,256]{1,0:T(8,128)} %copy-done.6), custom_call_target="tpu_custom_call" | custom-call | flops 3221225472 | bytes 8388608 | tf_op jit(solution)/shard_map/panel_dot/pallas_call | solution.py:244
  62.5 1.6 collective-permute-start.19
  64.8 1.3 collective-permute-start.5
  66.8 6.8 %collective-permute-done.5 = f32[64,512]{1,0:T(8,128)S(1)} collective-permute-done((f32[64,512]{1,0:T(8,128)S(1)}, f32[64,512]{1,0:T(8,128)S(1)}, u32[]{:S(2)}, u32[]{:S(2)}) %collective-permute-start.5) | collective-permute-done | bytes 131104 | tf_op jit(solution)/shard_map/ppermute | solution.py:347
  73.6 0.8 fusion.6
  74.5 1.3 collective-permute-start.21
  75.8 1.4 collective-permute-start.22
  77.2 1.4 collective-permute-start.20
  78.6 1.3 add.122
  79.9 0.8 constant_dynamic-slice_fusion.5
  80.7 1.2 collective-permute-start.25
  81.9 1.2 collective-permute-start.27
  83.1 2.8 %collective-permute-done.21 = f32[344,256]{1,0:T(8,128)S(1)} collective-permute-done((f32[344,256]{1,0:T(8,128)}, f32[344,256]{1,0:T(8,128)S(1)}, u32[]{:S(2)}, u32[]{:S(2)}) %collective-permute-start.21) | collective-permute-done | bytes 352288 | tf_op jit(solution)/shard_map/ppermute | solution.py:282
  85.9 1.2 collective-permute-start.26
  87.2 1.2 add_add_fusion.rest_0_
  88.4 8.6 %collective-permute-start.24 = (f32[344,256]{1,0:T(8,128)S(1)}, f32[344,256]{1,0:T(8,128)S(1)}, u32[]{:S(2)}, u32[]{:S(2)}) collective-permute-start(f32[344,256]{1,0:T(8,128)S(1)} %add_add_fusion.rest_0_), channel_id=1, source_target_pairs={{1,3},{2,1},{3,2},{5,7},{6,5},{7,6},{9,11},{10,9},{11,10},{13,15},... | collective-permute-start | bytes 1056776 | tf_op jit(solution)/shard_map/ppermute | solution.py:291
  97.0 10.4 %collective-permute-start.23 = (f32[344,256]{1,0:T(8,128)S(1)}, f32[344,256]{1,0:T(8,128)S(1)}, u32[]{:S(2)}, u32[]{:S(2)}) collective-permute-start(f32[344,256]{1,0:T(8,128)S(1)} %add_add_fusion.rest_0_), channel_id=1, source_target_pairs={{1,2},{2,3},{3,1},{5,6},{6,7},{7,5},{9,10},{10,11},{11,9},{13,14},... | collective-permute-start | bytes 1056776 | tf_op jit(solution)/shard_map/ppermute | solution.py:291
  107.4 1.0 add_add_fusion.3.rest_2_
  108.4 3.4 %collective-permute-done.24.rest_2_ = f32[344,256]{1,0:T(8,128)S(1)} collective-permute-done((f32[344,256]{1,0:T(8,128)S(1)}, f32[344,256]{1,0:T(8,128)S(1)}, u32[]{:S(2)}, u32[]{:S(2)}) %collective-permute-start.24) | collective-permute-done | bytes 352288 | tf_op jit(solution)/shard_map/ppermute | solution.py:291
  111.8 10.0 %collective-permute-done.23.rest_1_ = f32[344,256]{1,0:T(8,128)S(1)} collective-permute-done((f32[344,256]{1,0:T(8,128)S(1)}, f32[344,256]{1,0:T(8,128)S(1)}, u32[]{:S(2)}, u32[]{:S(2)}) %collective-permute-start.23) | collective-permute-done | bytes 352288 | tf_op jit(solution)/shard_map/ppermute | solution.py:291
  121.8 0.7 copy-done.9
  122.6 11.1 %panel_dot.3 = (f32[128,2048]{1,0:T(8,128)}, f32[128,2048]{1,0:T(8,128)}, f32[1024,256]{1,0:T(8,128)}) custom-call(s32[6]{0:T(128)} %stack.27.info_ref, f32[1024,2048]{1,0:T(8,128)} %s_ref.5, f32[1024,2048]{1,0:T(8,128)} %s_ref.5, f32[344,256]{1,0:T(8,128)} %copy-done.4, f32[344,256]{1,0:T(8,128)} %copy-done.9, f32[344,256]{1,0:T(8,128)} %copy-done.8), custom_call_target="tpu_custom_call" | custom-call | flops 3221225472 | bytes 8388608 | tf_op jit(solution)/shard_map/panel_dot/pallas_call | solution.py:244
  133.6 1.6 collective-permute-start.28
  135.2 2.2 collective-permute-start.9
  137.9 0.9 collective-permute-start.10
  138.8 2.4 %collective-permute-done.9.refs_3_ = f32[64,512]{1,0:T(8,128)S(1)} collective-permute-done((f32[64,512]{1,0:T(8,128)S(1)}, f32[64,512]{1,0:T(8,128)S(1)}, u32[]{:S(2)}, u32[]{:S(2)}) %collective-permute-start.9) | collective-permute-done | bytes 131104 | tf_op jit(solution)/shard_map/ppermute | solution.py:322
  141.2 1.1 collective-permute-start.13
  142.4 2.0 collective-permute-done.8.refs_2_
  145.0 0.9 collective-permute-done.12.refs_6_
  146.2 8.9 %chol_part.4 = (f32[512,512]{1,0:T(8,128)S(1)}, f32[512,512]{1,0:T(8,128)S(1)}, f32[512,512]{1,0:T(8,128)S(1)}) custom-call(s32[6]{0:T(128)S(1)} %copy-done, f32[64,512]{1,0:T(8,128)S(1)} %add_select_fusion.refs_0_, f32[64,512]{1,0:T(8,128)S(1)} %collective-permute-done.7.refs_1_, f32[64,512]{1,0:T(8,128)S(1)} %collective-permute-done.8.refs_2_, ...), custom_call_target="tpu_custom_call" | custom-call | flops 8000000000 | bytes 3145728 | tf_op jit(solution)/shard_map/chol_part/pallas_call | solution.py:110
  155.2 1.5 collective-permute-start.34
  156.7 0.9 collective-permute-start.33
  158.2 1.5 collective-permute-start.31
  159.6 0.9 collective-permute-start.30
  160.6 8.5 %chol_part.5 = (f32[512,512]{1,0:T(8,128)S(1)}, f32[512,512]{1,0:T(8,128)S(1)}, f32[512,512]{1,0:T(8,128)S(1)}) custom-call(s32[6]{0:T(128)S(1)} %copy-done, f32[512,512]{1,0:T(8,128)S(1)} %get-tuple-element.54.refs_0_, f32[512,512]{1,0:T(8,128)S(1)} %get-tuple-element.55.refs_1_, ...), custom_call_target="tpu_custom_call", output_to_operand_aliasing={{0}: (1, {}), {1}: (2, {}), {2}: (3, {})} | custom-call | flops 8000000000 | bytes 3145728 | tf_op jit(solution)/shard_map/chol_part/pallas_call | solution.py:110
  169.1 1.6 collective-permute-start.35
  170.8 0.9 collective-permute-start.32
  171.7 1.0 collective-permute-start.38
  172.7 2.5 %collective-permute-done.31 = f32[32,2048]{1,0:T(8,128)S(1)} collective-permute-done((f32[32,2048]{1,0:T(8,128)S(1)}, f32[32,2048]{1,0:T(8,128)S(1)}, u32[]{:S(2)}, u32[]{:S(2)}) %collective-permute-start.31) | collective-permute-done | bytes 262176 | tf_op jit(solution)/shard_map/ppermute | solution.py:317
  175.2 1.6 collective-permute-start.37
  176.8 4.5 %collective-permute-done.30 = f32[32,2048]{1,0:T(8,128)S(1)} collective-permute-done((f32[32,2048]{1,0:T(8,128)S(1)}, f32[32,2048]{1,0:T(8,128)S(1)}, u32[]{:S(2)}, u32[]{:S(2)}) %collective-permute-start.30) | collective-permute-done | bytes 262176 | tf_op jit(solution)/shard_map/ppermute | solution.py:317
  181.3 1.5 collective-permute-start.41
  182.8 0.9 collective-permute-start.40
  184.0 8.5 %chol_part.6 = (f32[512,512]{1,0:T(8,128)S(1)}, f32[512,512]{1,0:T(8,128)S(1)}, f32[512,512]{1,0:T(8,128)S(1)}) custom-call(s32[6]{0:T(128)S(1)} %copy-done, f32[512,512]{1,0:T(8,128)S(1)} %get-tuple-element.65.refs_0_, f32[512,512]{1,0:T(8,128)S(1)} %get-tuple-element.66.refs_1_, ...), custom_call_target="tpu_custom_call", output_to_operand_aliasing={{0}: (1, {}), {1}: (2, {}), {2}: (3, {})} | custom-call | flops 8000000000 | bytes 3145728 | tf_op jit(solution)/shard_map/chol_part/pallas_call | solution.py:110
  192.6 1.4 collective-permute-start.36
  194.6 1.5 collective-permute-done.40.rest_12_
  196.7 7.9 %chol_part.7 = (f32[512,512]{1,0:T(8,128)S(1)}, f32[512,512]{1,0:T(8,128)S(1)}, f32[512,512]{1,0:T(8,128)S(1)}) custom-call(s32[6]{0:T(128)S(1)} %copy-done, f32[512,512]{1,0:T(8,128)S(1)} %get-tuple-element.71.refs_0_, f32[512,512]{1,0:T(8,128)S(1)} %get-tuple-element.72.refs_1_, ...), custom_call_target="tpu_custom_call", output_to_operand_aliasing={{0}: (1, {}), {1}: (2, {}), {2}: (3, {})} | custom-call | flops 8000000000 | bytes 3145728 | tf_op jit(solution)/shard_map/chol_part/pallas_call | solution.py:110
  204.7 1.0 copy-done.1
  205.6 1.0 copy-done.2
  207.8 26.0 %finish.1 = (f32[1024,2048]{1,0:T(8,128)}, f32[512,2048]{1,0:T(8,128)}) custom-call(s32[6]{0:T(128)} %stack.27.info_ref, f32[1024,2048]{1,0:T(8,128)} %s_ref.5, f32[512,512]{1,0:T(8,128)} %copy-done.2, f32[512,512]{1,0:T(8,128)} %copy-done.1, f32[1024,256]{1,0:T(8,128)} %get-tuple-element.76.rest_0_, f32[1024,256]{1,0:T(8,128)} %get-tuple-element.77.rest_1_, ...), custom_call_target="tpu_custom_call" | custom-call | flops 9663676416 | bytes 16777216 | tf_op jit(solution)/shard_map/finish/pallas_call | solution.py:175
  (106 shorter events, 7.8 us)
Async XLA Ops:
  2.8 12.1 %collective-permute-start.15 = (f32[344,256]{1,0:T(8,128)}, f32[344,256]{1,0:T(8,128)S(1)}, u32[]{:S(2)}, u32[]{:S(2)}) collective-permute-start(f32[344,256]{1,0:T(8,128)} %get-tuple-element.78), channel_id=1, source_target_pairs={{0,2},{4,6},{8,10},{12,14},{16,18},{20,22},{24,26},{28,30}} | collective-permute-start | bytes 1056776 | tf_op jit(solution)/shard_map/ppermute | solution.py:282
  4.1 10.8 %collective-permute-start.16 = (f32[344,256]{1,0:T(8,128)}, f32[344,256]{1,0:T(8,128)S(1)}, u32[]{:S(2)}, u32[]{:S(2)}) collective-permute-start(f32[344,256]{1,0:T(8,128)} %get-tuple-element.79), channel_id=1, source_target_pairs={{0,1},{4,5},{8,9},{12,13},{16,17},{20,21},{24,25},{28,29}} | collective-permute-start | bytes 1056776 | tf_op jit(solution)/shard_map/ppermute | solution.py:282
  4.7 10.1 %collective-permute-start.14 = (f32[344,256]{1,0:T(8,128)S(1)}, f32[344,256]{1,0:T(8,128)}, u32[]{:S(2)}, u32[]{:S(2)}) collective-permute-start(f32[344,256]{1,0:T(8,128)S(1)} %get-tuple-element.80), channel_id=1, source_target_pairs={{0,3},{4,7},{8,11},{12,15},{16,19},{20,23},{24,27},{28,31}} | collective-permute-start | bytes 1056776 | tf_op jit(solution)/shard_map/ppermute | solution.py:282
  11.9 24.2 %collective-permute-start = (f32[256,512]{1,0:T(8,128)S(1)}, f32[256,512]{1,0:T(8,128)S(1)}, u32[]{:S(2)}, u32[]{:S(2)}) collective-permute-start(f32[256,512]{1,0:T(8,128)S(1)} %constant_dynamic-slice_fusion.9), channel_id=1, source_target_pairs={{0,4},{4,0},{8,12},{12,8},{16,20},{20,16},{24,28},{28,24},{1,5},{5... | collective-permute-start | bytes 1572872 | tf_op jit(solution)/shard_map/ppermute | solution.py:308
  15.9 34.7 %copy-start.3 = (f32[344,256]{1,0:T(8,128)}, f32[344,256]{1,0:T(8,128)S(1)}, u32[]{:S(2)}) copy-start(f32[344,256]{1,0:T(8,128)S(1)} %add_add_fusion.1.rest_0_) | copy-start | bytes 1056772
  15.9 25.3 %collective-permute-start.18 = (f32[344,256]{1,0:T(8,128)S(1)}, f32[344,256]{1,0:T(8,128)S(1)}, u32[]{:S(2)}, u32[]{:S(2)}) collective-permute-start(f32[344,256]{1,0:T(8,128)S(1)} %add_add_fusion.1.rest_0_), channel_id=1, source_target_pairs={{1,3},{2,1},{3,2},{5,7},{6,5},{7,6},{9,11},{10,9},{11,10},{13,15},... | collective-permute-start | bytes 1056776 | tf_op jit(solution)/shard_map/ppermute | solution.py:291
  25.7 24.9 %collective-permute-start.17 = (f32[344,256]{1,0:T(8,128)S(1)}, f32[344,256]{1,0:T(8,128)S(1)}, u32[]{:S(2)}, u32[]{:S(2)}) collective-permute-start(f32[344,256]{1,0:T(8,128)S(1)} %add_add_fusion.1.rest_0_), channel_id=1, source_target_pairs={{1,2},{2,3},{3,1},{5,6},{6,7},{7,5},{9,10},{10,11},{11,9},{13,14},... | collective-permute-start | bytes 1056776 | tf_op jit(solution)/shard_map/ppermute | solution.py:291
  36.3 27.8 %collective-permute-start.1 = (f32[64,512]{1,0:T(8,128)S(1)}, f32[64,512]{1,0:T(8,128)S(1)}, u32[]{:S(2)}, u32[]{:S(2)}) collective-permute-start(f32[64,512]{1,0:T(8,128)S(1)} %get-tuple-element.90), channel_id=1, source_target_pairs={{0,8},{4,12},{8,0},{12,4},{16,24},{20,28},{24,16},{28,20},{1,9},{5... | collective-permute-start | bytes 393224 | tf_op jit(solution)/shard_map/ppermute | solution.py:317
  37.6 26.5 %collective-permute-start.3 = (f32[64,512]{1,0:T(8,128)S(1)}, f32[64,512]{1,0:T(8,128)S(1)}, u32[]{:S(2)}, u32[]{:S(2)}) collective-permute-start(f32[64,512]{1,0:T(8,128)S(1)} %get-tuple-element.91), channel_id=1, source_target_pairs={{0,24},{4,28},{8,16},{12,20},{16,8},{20,12},{24,0},{28,4},{1,25},{... | collective-permute-start | bytes 393224 | tf_op jit(solution)/shard_map/ppermute | solution.py:317
  38.8 34.8 %slice-start = ((f32[1024,2048]{1,0:T(8,128)}), f32[1024,256]{1,0:T(8,128)S(1)}, s32[]{:S(2)}) async-start(f32[1024,2048]{1,0:T(8,128)} %s_ref.5), calls=%async_computation | async-start | bytes 2097152 | tf_op jit(solution)/shard_map/slice | solution.py:352
  38.8 25.3 %collective-permute-start.2 = (f32[64,512]{1,0:T(8,128)S(1)}, f32[64,512]{1,0:T(8,128)S(1)}, u32[]{:S(2)}, u32[]{:S(2)}) collective-permute-start(f32[64,512]{1,0:T(8,128)S(1)} %get-tuple-element.92), channel_id=1, source_target_pairs={{0,16},{4,20},{8,24},{12,28},{16,0},{20,4},{24,8},{28,12},{1,17},{... | collective-permute-start | bytes 393224 | tf_op jit(solution)/shard_map/ppermute | solution.py:317
  41.2 9.4 %copy-start.6 = (f32[344,256]{1,0:T(8,128)}, f32[344,256]{1,0:T(8,128)S(1)}, u32[]{:S(2)}) copy-start(f32[344,256]{1,0:T(8,128)S(1)} %collective-permute-done.18.rest_2_) | copy-start | bytes 1056772
  62.5 16.1 %collective-permute-start.19 = (f32[128,2048]{1,0:T(8,128)}, f32[128,2048]{1,0:T(8,128)S(1)}, u32[]{:S(2)}, u32[]{:S(2)}) collective-permute-start(f32[128,2048]{1,0:T(8,128)} %get-tuple-element.40), channel_id=1, source_target_pairs={{0,4},{4,0},{8,12},{12,8},{16,20},{20,16},{24,28},{28,24},{1,5},{5... | collective-permute-start | bytes 3145736 | tf_op jit(solution)/shard_map/ppermute | solution.py:308
  64.1 2.7 %collective-permute-start.6 = (f32[64,512]{1,0:T(8,128)S(1)}, f32[64,512]{1,0:T(8,128)S(1)}, u32[]{:S(2)}, u32[]{:S(2)}) collective-permute-start(f32[64,512]{1,0:T(8,128)S(1)} %add_add_fusion.4), channel_id=1, source_target_pairs={{0,1},{4,5},{8,9},{12,13},{16,17},{20,21},{24,25},{28,29}} | collective-permute-start | bytes 393224 | tf_op jit(solution)/shard_map/ppermute | solution.py:347
  64.8 8.8 %collective-permute-start.5 = (f32[64,512]{1,0:T(8,128)S(1)}, f32[64,512]{1,0:T(8,128)S(1)}, u32[]{:S(2)}, u32[]{:S(2)}) collective-permute-start(f32[64,512]{1,0:T(8,128)S(1)} %add_add_fusion.4), channel_id=1, source_target_pairs={{0,2},{4,6},{8,10},{12,14},{16,18},{20,22},{24,26},{28,30}} | collective-permute-start | bytes 393224 | tf_op jit(solution)/shard_map/ppermute | solution.py:347
  66.1 7.5 %collective-permute-start.4 = (f32[64,512]{1,0:T(8,128)S(1)}, f32[64,512]{1,0:T(8,128)S(1)}, u32[]{:S(2)}, u32[]{:S(2)}) collective-permute-start(f32[64,512]{1,0:T(8,128)S(1)} %add_add_fusion.4), channel_id=1, source_target_pairs={{0,3},{4,7},{8,11},{12,15},{16,19},{20,23},{24,27},{28,31}} | collective-permute-start | bytes 393224 | tf_op jit(solution)/shard_map/ppermute | solution.py:347
  74.5 11.5 %collective-permute-start.21 = (f32[344,256]{1,0:T(8,128)}, f32[344,256]{1,0:T(8,128)S(1)}, u32[]{:S(2)}, u32[]{:S(2)}) collective-permute-start(f32[344,256]{1,0:T(8,128)} %get-tuple-element.87), channel_id=1, source_target_pairs={{0,2},{4,6},{8,10},{12,14},{16,18},{20,22},{24,26},{28,30}} | collective-permute-start | bytes 1056776 | tf_op jit(solution)/shard_map/ppermute | solution.py:282
  75.8 11.4 %collective-permute-start.22 = (f32[344,256]{1,0:T(8,128)S(1)}, f32[344,256]{1,0:T(8,128)}, u32[]{:S(2)}, u32[]{:S(2)}) collective-permute-start(f32[344,256]{1,0:T(8,128)S(1)} %get-tuple-element.88), channel_id=1, source_target_pairs={{0,1},{4,5},{8,9},{12,13},{16,17},{20,21},{24,25},{28,29}} | collective-permute-start | bytes 1056776 | tf_op jit(solution)/shard_map/ppermute | solution.py:282
  77.2 10.0 %collective-permute-start.20 = (f32[344,256]{1,0:T(8,128)S(1)}, f32[344,256]{1,0:T(8,128)}, u32[]{:S(2)}, u32[]{:S(2)}) collective-permute-start(f32[344,256]{1,0:T(8,128)S(1)} %get-tuple-element.89), channel_id=1, source_target_pairs={{0,3},{4,7},{8,11},{12,15},{16,19},{20,23},{24,27},{28,31}} | collective-permute-start | bytes 1056776 | tf_op jit(solution)/shard_map/ppermute | solution.py:282
  80.7 26.7 %collective-permute-start.25 = (f32[32,2048]{1,0:T(8,128)}, f32[32,2048]{1,0:T(8,128)S(1)}, u32[]{:S(2)}, u32[]{:S(2)}) collective-permute-start(f32[32,2048]{1,0:T(8,128)} %get-tuple-element.84), channel_id=1, source_target_pairs={{0,8},{4,12},{8,0},{12,4},{16,24},{20,28},{24,16},{28,20},{1,9},{5... | collective-permute-start | bytes 786440 | tf_op jit(solution)/shard_map/ppermute | solution.py:317
  81.9 25.5 %collective-permute-start.27 = (f32[32,2048]{1,0:T(8,128)S(1)}, f32[32,2048]{1,0:T(8,128)S(1)}, u32[]{:S(2)}, u32[]{:S(2)}) collective-permute-start(f32[32,2048]{1,0:T(8,128)S(1)} %get-tuple-element.85), channel_id=1, source_target_pairs={{0,24},{4,28},{8,16},{12,20},{16,8},{20,12},{24,0},{28,4},{1,25},{... | collective-permute-start | bytes 786440 | tf_op jit(solution)/shard_map/ppermute | solution.py:317
  85.9 21.4 %collective-permute-start.26 = (f32[32,2048]{1,0:T(8,128)S(1)}, f32[32,2048]{1,0:T(8,128)}, u32[]{:S(2)}, u32[]{:S(2)}) collective-permute-start(f32[32,2048]{1,0:T(8,128)S(1)} %get-tuple-element.86), channel_id=1, source_target_pairs={{0,16},{4,20},{8,24},{12,28},{16,0},{20,4},{24,8},{28,12},{1,17},{... | collective-permute-start | bytes 786440 | tf_op jit(solution)/shard_map/ppermute | solution.py:317
  88.4 33.5 %copy-start.4 = (f32[344,256]{1,0:T(8,128)}, f32[344,256]{1,0:T(8,128)S(1)}, u32[]{:S(2)}) copy-start(f32[344,256]{1,0:T(8,128)S(1)} %add_add_fusion.rest_0_) | copy-start | bytes 1056772
  88.4 23.4 %collective-permute-start.24 = (f32[344,256]{1,0:T(8,128)S(1)}, f32[344,256]{1,0:T(8,128)S(1)}, u32[]{:S(2)}, u32[]{:S(2)}) collective-permute-start(f32[344,256]{1,0:T(8,128)S(1)} %add_add_fusion.rest_0_), channel_id=1, source_target_pairs={{1,3},{2,1},{3,2},{5,7},{6,5},{7,6},{9,11},{10,9},{11,10},{13,15},... | collective-permute-start | bytes 1056776 | tf_op jit(solution)/shard_map/ppermute | solution.py:291
  97.0 24.8 %collective-permute-start.23 = (f32[344,256]{1,0:T(8,128)S(1)}, f32[344,256]{1,0:T(8,128)S(1)}, u32[]{:S(2)}, u32[]{:S(2)}) collective-permute-start(f32[344,256]{1,0:T(8,128)S(1)} %add_add_fusion.rest_0_), channel_id=1, source_target_pairs={{1,2},{2,3},{3,1},{5,6},{6,7},{7,5},{9,10},{10,11},{11,9},{13,14},... | collective-permute-start | bytes 1056776 | tf_op jit(solution)/shard_map/ppermute | solution.py:291
  108.4 62.4 %copy-start.10 = (f32[32,2048]{1,0:T(8,128)}, f32[32,2048]{1,0:T(8,128)S(1)}, u32[]{:S(2)}) copy-start(f32[32,2048]{1,0:T(8,128)S(1)} %add_add_fusion.3.rest_2_) | copy-start | bytes 786436
  108.4 37.8 %copy-start = (s32[6]{0:T(128)S(1)}, s32[6]{0:T(128)}, u32[]{:S(2)}) copy-start(s32[6]{0:T(128)} %stack.27.info_ref) | copy-start | bytes 76
  111.8 10.0 %copy-start.8 = (f32[344,256]{1,0:T(8,128)}, f32[344,256]{1,0:T(8,128)S(1)}, u32[]{:S(2)}) copy-start(f32[344,256]{1,0:T(8,128)S(1)} %collective-permute-done.24.rest_2_) | copy-start | bytes 1056772
  133.6 24.0 %copy-start.5 = (f32[128,2048]{1,0:T(8,128)S(1)}, f32[128,2048]{1,0:T(8,128)}, u32[]{:S(2)}) copy-start(f32[128,2048]{1,0:T(8,128)} %get-tuple-element.63) | copy-start | bytes 3145732
  133.6 24.0 %collective-permute-start.28 = (f32[128,2048]{1,0:T(8,128)}, f32[128,2048]{1,0:T(8,128)S(1)}, u32[]{:S(2)}, u32[]{:S(2)}) collective-permute-start(f32[128,2048]{1,0:T(8,128)} %get-tuple-element.64), channel_id=1, source_target_pairs={{0,4},{4,0},{8,12},{12,8},{16,20},{20,16},{24,28},{28,24},{1,5},{5... | collective-permute-start | bytes 3145736 | tf_op jit(solution)/shard_map/ppermute | solution.py:308
  135.2 6.0 %collective-permute-start.9 = (f32[64,512]{1,0:T(8,128)S(1)}, f32[64,512]{1,0:T(8,128)S(1)}, u32[]{:S(2)}, u32[]{:S(2)}) collective-permute-start(f32[64,512]{1,0:T(8,128)S(1)} %add_select_fusion.refs_0_), channel_id=1, source_target_pairs={{0,24},{4,28},{8,16},{12,20},{16,8},{20,12},{24,0},{28,4},{1,25},{... | collective-permute-start | bytes 393224 | tf_op jit(solution)/shard_map/ppermute | solution.py:322
  137.4 7.0 %collective-permute-start.8 = (f32[64,512]{1,0:T(8,128)S(1)}, f32[64,512]{1,0:T(8,128)S(1)}, u32[]{:S(2)}, u32[]{:S(2)}) collective-permute-start(f32[64,512]{1,0:T(8,128)S(1)} %add_select_fusion.refs_0_), channel_id=1, source_target_pairs={{0,16},{4,20},{8,24},{12,28},{16,0},{20,4},{24,8},{28,12},{1,17},{... | collective-permute-start | bytes 393224 | tf_op jit(solution)/shard_map/ppermute | solution.py:322
  137.7 7.2 %collective-permute-start.7 = (f32[64,512]{1,0:T(8,128)S(1)}, f32[64,512]{1,0:T(8,128)S(1)}, u32[]{:S(2)}, u32[]{:S(2)}) collective-permute-start(f32[64,512]{1,0:T(8,128)S(1)} %add_select_fusion.refs_0_), channel_id=1, source_target_pairs={{0,8},{4,12},{8,0},{12,4},{16,24},{20,28},{24,16},{28,20},{1,9},{5... | collective-permute-start | bytes 393224 | tf_op jit(solution)/shard_map/ppermute | solution.py:322
  137.9 7.1 %collective-permute-start.10 = (f32[64,512]{1,0:T(8,128)S(1)}, f32[64,512]{1,0:T(8,128)S(1)}, u32[]{:S(2)}, u32[]{:S(2)}) collective-permute-start(f32[64,512]{1,0:T(8,128)S(1)} %add_select_fusion.refs_0_), channel_id=1, source_target_pairs={{0,4},{4,0},{8,12},{12,8},{16,20},{20,16},{24,28},{28,24},{1,5},{5... | collective-permute-start | bytes 393224 | tf_op jit(solution)/shard_map/ppermute | solution.py:323
  141.2 3.8 %collective-permute-start.13 = (f32[64,512]{1,0:T(8,128)S(1)}, f32[64,512]{1,0:T(8,128)S(1)}, u32[]{:S(2)}, u32[]{:S(2)}) collective-permute-start(f32[64,512]{1,0:T(8,128)S(1)} %collective-permute-done.9.refs_3_), channel_id=1, source_target_pairs={{0,4},{4,0},{8,12},{12,8},{16,20},{20,16},{24,28},{28,24},{1,5},{5... | collective-permute-start | bytes 393224 | tf_op jit(solution)/shard_map/ppermute | solution.py:323
  144.4 1.5 collective-permute-start.12
  144.9 1.3 collective-permute-start.11
  155.2 13.9 %collective-permute-start.34 = (f32[32,2048]{1,0:T(8,128)S(1)}, f32[32,2048]{1,0:T(8,128)S(1)}, u32[]{:S(2)}, u32[]{:S(2)}) collective-permute-start(f32[32,2048]{1,0:T(8,128)S(1)} %add_add_fusion.3.rest_2_), channel_id=1, source_target_pairs={{0,24},{4,28},{8,16},{12,20},{16,8},{20,12},{24,0},{28,4},{1,25},{... | collective-permute-start | bytes 786440 | tf_op jit(solution)/shard_map/ppermute | solution.py:322
  156.7 14.1 %collective-permute-start.33 = (f32[32,2048]{1,0:T(8,128)S(1)}, f32[32,2048]{1,0:T(8,128)S(1)}, u32[]{:S(2)}, u32[]{:S(2)}) collective-permute-start(f32[32,2048]{1,0:T(8,128)S(1)} %add_add_fusion.3.rest_2_), channel_id=1, source_target_pairs={{0,16},{4,20},{8,24},{12,28},{16,0},{20,4},{24,8},{28,12},{1,17},{... | collective-permute-start | bytes 786440 | tf_op jit(solution)/shard_map/ppermute | solution.py:322
  157.9 13.8 %collective-permute-start.29 = (f32[32,2048]{1,0:T(8,128)S(1)}, f32[32,2048]{1,0:T(8,128)S(1)}, u32[]{:S(2)}, u32[]{:S(2)}) collective-permute-start(f32[32,2048]{1,0:T(8,128)S(1)} %get-tuple-element.81), channel_id=1, source_target_pairs={{0,8},{4,12},{8,0},{12,4},{16,24},{20,28},{24,16},{28,20},{1,9},{5... | collective-permute-start | bytes 786440 | tf_op jit(solution)/shard_map/ppermute | solution.py:317
  158.2 17.0 %collective-permute-start.31 = (f32[32,2048]{1,0:T(8,128)S(1)}, f32[32,2048]{1,0:T(8,128)S(1)}, u32[]{:S(2)}, u32[]{:S(2)}) collective-permute-start(f32[32,2048]{1,0:T(8,128)S(1)} %get-tuple-element.82), channel_id=1, source_target_pairs={{0,24},{4,28},{8,16},{12,20},{16,8},{20,12},{24,0},{28,4},{1,25},{... | collective-permute-start | bytes 786440 | tf_op jit(solution)/shard_map/ppermute | solution.py:317
  159.6 21.6 %collective-permute-start.30 = (f32[32,2048]{1,0:T(8,128)S(1)}, f32[32,2048]{1,0:T(8,128)S(1)}, u32[]{:S(2)}, u32[]{:S(2)}) collective-permute-start(f32[32,2048]{1,0:T(8,128)S(1)} %get-tuple-element.83), channel_id=1, source_target_pairs={{0,16},{4,20},{8,24},{12,28},{16,0},{20,4},{24,8},{28,12},{1,17},{... | collective-permute-start | bytes 786440 | tf_op jit(solution)/shard_map/ppermute | solution.py:317
  169.1 23.4 %copy-start.12 = (f32[32,2048]{1,0:T(8,128)}, f32[32,2048]{1,0:T(8,128)S(1)}, u32[]{:S(2)}) copy-start(f32[32,2048]{1,0:T(8,128)S(1)} %collective-permute-done.34.rest_5_) | copy-start | bytes 786436
  169.1 13.7 %collective-permute-start.35 = (f32[32,2048]{1,0:T(8,128)S(1)}, f32[32,2048]{1,0:T(8,128)S(1)}, u32[]{:S(2)}, u32[]{:S(2)}) collective-permute-start(f32[32,2048]{1,0:T(8,128)S(1)} %add_add_fusion.3.rest_2_), channel_id=1, source_target_pairs={{0,4},{4,0},{8,12},{12,8},{16,20},{20,16},{24,28},{28,24},{1,5},{5... | collective-permute-start | bytes 786440 | tf_op jit(solution)/shard_map/ppermute | solution.py:323
  170.8 21.8 %copy-start.13 = (f32[32,2048]{1,0:T(8,128)}, f32[32,2048]{1,0:T(8,128)S(1)}, u32[]{:S(2)}) copy-start(f32[32,2048]{1,0:T(8,128)S(1)} %collective-permute-done.33.rest_4_) | copy-start | bytes 786436
  170.8 13.0 %collective-permute-start.32 = (f32[32,2048]{1,0:T(8,128)S(1)}, f32[32,2048]{1,0:T(8,128)S(1)}, u32[]{:S(2)}, u32[]{:S(2)}) collective-permute-start(f32[32,2048]{1,0:T(8,128)S(1)} %add_add_fusion.3.rest_2_), channel_id=1, source_target_pairs={{0,8},{4,12},{8,0},{12,4},{16,24},{20,28},{24,16},{28,20},{1,9},{5... | collective-permute-start | bytes 786440 | tf_op jit(solution)/shard_map/ppermute | solution.py:322
  171.7 20.9 %collective-permute-start.38 = (f32[32,2048]{1,0:T(8,128)S(1)}, f32[32,2048]{1,0:T(8,128)S(1)}, u32[]{:S(2)}, u32[]{:S(2)}) collective-permute-start(f32[32,2048]{1,0:T(8,128)S(1)} %collective-permute-done.34.rest_5_), channel_id=1, source_target_pairs={{0,4},{4,0},{8,12},{12,8},{16,20},{20,16},{24,28},{28,24},{1,5},{5... | collective-permute-start | bytes 786440 | tf_op jit(solution)/shard_map/ppermute | solution.py:323
  175.2 18.8 %collective-permute-start.37 = (f32[32,2048]{1,0:T(8,128)S(1)}, f32[32,2048]{1,0:T(8,128)S(1)}, u32[]{:S(2)}, u32[]{:S(2)}) collective-permute-start(f32[32,2048]{1,0:T(8,128)S(1)} %collective-permute-done.33.rest_4_), channel_id=1, source_target_pairs={{0,4},{4,0},{8,12},{12,8},{16,20},{20,16},{24,28},{28,24},{1,5},{5... | collective-permute-start | bytes 786440 | tf_op jit(solution)/shard_map/ppermute | solution.py:323
  181.3 12.7 %copy-start.11 = (f32[32,2048]{1,0:T(8,128)}, f32[32,2048]{1,0:T(8,128)S(1)}, u32[]{:S(2)}) copy-start(f32[32,2048]{1,0:T(8,128)S(1)} %add_add_fusion.2.rest_10_) | copy-start | bytes 786436
  181.3 12.8 %collective-permute-start.41 = (f32[32,2048]{1,0:T(8,128)S(1)}, f32[32,2048]{1,0:T(8,128)S(1)}, u32[]{:S(2)}, u32[]{:S(2)}) collective-permute-start(f32[32,2048]{1,0:T(8,128)S(1)} %add_add_fusion.2.rest_10_), channel_id=1, source_target_pairs={{0,24},{4,28},{8,16},{12,20},{16,8},{20,12},{24,0},{28,4},{1,25},{... | collective-permute-start | bytes 786440 | tf_op jit(solution)/shard_map/ppermute | solution.py:322
  182.8 9.7 %copy-start.14 = (f32[32,2048]{1,0:T(8,128)}, f32[32,2048]{1,0:T(8,128)S(1)}, u32[]{:S(2)}) copy-start(f32[32,2048]{1,0:T(8,128)S(1)} %collective-permute-done.35.rest_6_) | copy-start | bytes 786436
  182.8 13.3 %collective-permute-start.40 = (f32[32,2048]{1,0:T(8,128)S(1)}, f32[32,2048]{1,0:T(8,128)S(1)}, u32[]{:S(2)}, u32[]{:S(2)}) collective-permute-start(f32[32,2048]{1,0:T(8,128)S(1)} %add_add_fusion.2.rest_10_), channel_id=1, source_target_pairs={{0,16},{4,20},{8,24},{12,28},{16,0},{20,4},{24,8},{28,12},{1,17},{... | collective-permute-start | bytes 786440 | tf_op jit(solution)/shard_map/ppermute | solution.py:322
  183.8 8.8 %copy-start.15 = (f32[32,2048]{1,0:T(8,128)}, f32[32,2048]{1,0:T(8,128)S(1)}, u32[]{:S(2)}) copy-start(f32[32,2048]{1,0:T(8,128)S(1)} %collective-permute-done.32.rest_3_) | copy-start | bytes 786436
  183.8 12.8 %collective-permute-start.39 = (f32[32,2048]{1,0:T(8,128)S(1)}, f32[32,2048]{1,0:T(8,128)S(1)}, u32[]{:S(2)}, u32[]{:S(2)}) collective-permute-start(f32[32,2048]{1,0:T(8,128)S(1)} %add_add_fusion.2.rest_10_), channel_id=1, source_target_pairs={{0,8},{4,12},{8,0},{12,4},{16,24},{20,28},{24,16},{28,20},{1,9},{5... | collective-permute-start | bytes 786440 | tf_op jit(solution)/shard_map/ppermute | solution.py:322
  192.6 12.0 %copy-start.16 = (f32[32,2048]{1,0:T(8,128)}, f32[32,2048]{1,0:T(8,128)S(1)}, u32[]{:S(2)}) copy-start(f32[32,2048]{1,0:T(8,128)S(1)} %collective-permute-done.38.rest_9_) | copy-start | bytes 786436
  192.6 14.0 %collective-permute-start.36 = (f32[32,2048]{1,0:T(8,128)S(1)}, f32[32,2048]{1,0:T(8,128)S(1)}, u32[]{:S(2)}, u32[]{:S(2)}) collective-permute-start(f32[32,2048]{1,0:T(8,128)S(1)} %collective-permute-done.32.rest_3_), channel_id=1, source_target_pairs={{0,4},{4,0},{8,12},{12,8},{16,20},{20,16},{24,28},{28,24},{1,5},{5... | collective-permute-start | bytes 786440 | tf_op jit(solution)/shard_map/ppermute | solution.py:323
  194.0 10.6 %copy-start.17 = (f32[32,2048]{1,0:T(8,128)}, f32[32,2048]{1,0:T(8,128)S(1)}, u32[]{:S(2)}) copy-start(f32[32,2048]{1,0:T(8,128)S(1)} %collective-permute-done.37.rest_8_) | copy-start | bytes 786436
  194.0 12.6 %collective-permute-start.42 = (f32[32,2048]{1,0:T(8,128)S(1)}, f32[32,2048]{1,0:T(8,128)S(1)}, u32[]{:S(2)}, u32[]{:S(2)}) collective-permute-start(f32[32,2048]{1,0:T(8,128)S(1)} %add_add_fusion.2.rest_10_), channel_id=1, source_target_pairs={{0,4},{4,0},{8,12},{12,8},{16,20},{20,16},{24,28},{28,24},{1,5},{5... | collective-permute-start | bytes 786440 | tf_op jit(solution)/shard_map/ppermute | solution.py:323
  194.1 10.5 %copy-start.18 = (f32[32,2048]{1,0:T(8,128)}, f32[32,2048]{1,0:T(8,128)S(1)}, u32[]{:S(2)}) copy-start(f32[32,2048]{1,0:T(8,128)S(1)} %collective-permute-done.41.rest_13_) | copy-start | bytes 786436
  194.1 12.5 %collective-permute-start.45 = (f32[32,2048]{1,0:T(8,128)S(1)}, f32[32,2048]{1,0:T(8,128)S(1)}, u32[]{:S(2)}, u32[]{:S(2)}) collective-permute-start(f32[32,2048]{1,0:T(8,128)S(1)} %collective-permute-done.41.rest_13_), channel_id=1, source_target_pairs={{0,4},{4,0},{8,12},{12,8},{16,20},{20,16},{24,28},{28,24},{1,5},{5... | collective-permute-start | bytes 786440 | tf_op jit(solution)/shard_map/ppermute | solution.py:323
  196.1 8.5 %copy-start.19 = (f32[32,2048]{1,0:T(8,128)}, f32[32,2048]{1,0:T(8,128)S(1)}, u32[]{:S(2)}) copy-start(f32[32,2048]{1,0:T(8,128)S(1)} %collective-permute-done.40.rest_12_) | copy-start | bytes 786436
  196.1 10.5 %collective-permute-start.44 = (f32[32,2048]{1,0:T(8,128)S(1)}, f32[32,2048]{1,0:T(8,128)S(1)}, u32[]{:S(2)}, u32[]{:S(2)}) collective-permute-start(f32[32,2048]{1,0:T(8,128)S(1)} %collective-permute-done.40.rest_12_), channel_id=1, source_target_pairs={{0,4},{4,0},{8,12},{12,8},{16,20},{20,16},{24,28},{28,24},{1,5},{5... | collective-permute-start | bytes 786440 | tf_op jit(solution)/shard_map/ppermute | solution.py:323
  196.6 8.0 %copy-start.20 = (f32[32,2048]{1,0:T(8,128)}, f32[32,2048]{1,0:T(8,128)S(1)}, u32[]{:S(2)}) copy-start(f32[32,2048]{1,0:T(8,128)S(1)} %collective-permute-done.39.rest_11_) | copy-start | bytes 786436
  196.6 10.1 %collective-permute-start.43 = (f32[32,2048]{1,0:T(8,128)S(1)}, f32[32,2048]{1,0:T(8,128)S(1)}, u32[]{:S(2)}, u32[]{:S(2)}) collective-permute-start(f32[32,2048]{1,0:T(8,128)S(1)} %collective-permute-done.39.rest_11_), channel_id=1, source_target_pairs={{0,4},{4,0},{8,12},{12,8},{16,20},{20,16},{24,28},{28,24},{1,5},{5... | collective-permute-start | bytes 786440 | tf_op jit(solution)/shard_map/ppermute | solution.py:323
  (9 other events, 8.1 us)

commit v3 on v2

--- a/solution.py
+++ b/solution.py
@@ -7,6 +7,7 @@
 
 PB = 512
 NB = 128
+MERGE_COST = 3 * 10**10
 F32 = jnp.float32
 BF16 = jnp.bfloat16
 HIGHEST = lax.Precision.HIGHEST
@@ -122,7 +123,7 @@
     )(info, *arrays)
 
 
-def finish(info, snapshots, panels, linv, factor, pieces, layout, tile=256, block=1024):
+def finish(info, snapshots, panels, linv, factor, pieces, layout, tile=512):
     rows, cols = snapshots.shape
     n_pieces, n_panels = len(pieces), len(panels)
     chips = 1 + max(chip for _, _, chip in layout)
@@ -161,8 +162,7 @@
         ph, plow = split(proj)
         p3[:PB, :], p3[PB : 2 * PB, :], p3[2 * PB :, :] = ph, plow, ph
         co_ref[...] = proj
-        for r in range(0, rows, block):
-            up_ref[r : r + block, :] = s_ref[r : r + block, :] - mm(b3[r : r + block, :], p3[...], 1, 0)
+        up_ref[...] = s_ref[...] - mm(b3[...], p3[...], 1, 0)
         for t in range(PB // tile):
 
             @pl.when((info_ref[0] == 0) & (j == t))
@@ -202,7 +202,7 @@
     )(info, snapshots, linv, factor, *panels, *pieces)
 
 
-def panel_dot(info, snapshots, parts, size, base, width, scale, tile=256):
+def panel_dot(info, snapshots, parts, size, base, width, scale, tile=512):
     rows, cols = snapshots.shape
     half = width // 2
     n_parts = len(parts)
@@ -273,15 +273,31 @@
     return -(-rows // (8 * parts)) * 8
 
 
+def merge(arrays):
+    def kernel(*refs):
+        total = refs[0][...]
+        for ref in refs[1:-1]:
+            total = total + ref[...]
+        refs[-1][...] = total
+
+    return pl.pallas_call(
+        kernel,
+        out_shape=jax.ShapeDtypeStruct(arrays[0].shape, F32),
+        in_specs=[VMEM] * len(arrays),
+        out_specs=VMEM,
+        cost_estimate=pl.CostEstimate(flops=MERGE_COST, bytes_accessed=1 << 20, transcendentals=0),
+        name="merge",
+    )(*arrays)
+
+
 def spread_out(x, n):
     rows, parts = x.shape[0], n - 1
     size = part_size(rows, parts)
-    mine = None
+    got = []
     for k in reversed(range(parts)):
         start = min(k * size, rows - size)
-        part = lax.ppermute(x[start : start + size], "cols", [(0, k + 1)])
-        mine = part if mine is None else mine + part
-    return mine
+        got.append(lax.ppermute(x[start : start + size], "cols", [(0, k + 1)]))
+    return merge(got)
 
 
 def spread_round(mine, n):
@@ -345,20 +361,19 @@
     joined = join_cores(take(gram, (1 - core) * half, half), take(gram, core * half, half), n_rows)
     share = scatter_chips(joined, n_rows)
     far = [lax.ppermute(share, "cols", [(0, k)]) for k in reversed(range(1, n_cols))]
+    got_a = spread_round(mine_a, n_cols)
+    mine_b = spread_out(after(panel[:, half:], mine_a), n_cols)
     share = jnp.where(z == 0, share, sum(far, jnp.zeros_like(share)))
     grams, places = gather_rows(share, n_rows)
 
-    got_a = spread_round(mine_a, n_cols)
-    mine_b = spread_out(after(panel[:, half:], mine_a, share), n_cols)
-    send, keep, panel_a = dot(got_a, 0)
-    grams = after(grams, send)
-    state = chol_part(info, 0, 1, pieces=grams, places=places)
+    send, keep, panel_a = dot(after(got_a, far), 0)
+    state = chol_part(info, 0, 1, pieces=after(grams, send, mine_b), places=places)
     joined = join_cores(send, keep, n_rows)
     own_a = scatter_chips(joined, n_rows)
     got_b = spread_round(mine_b, n_cols)
-    state = chol_part(info, 1, 2, state=after(state, joined, mine_b))
+    state = chol_part(info, 1, 2, state=after(state, joined))
     pieces_a, where = gather_rows(own_a, n_rows)
-    send, keep, panel_b = dot(after(got_b, own_a), half)
+    send, keep, panel_b = dot(after(got_b, own_a, state), half)
     joined = join_cores(send, keep, n_rows)
     own_b = scatter_chips(joined, n_rows)
     state = chol_part(info, 2, 3, state=after(state, joined))

time: 235 us -> 198 us (0.84)
  starting transfers between devices: 80.4 us -> 61.7 us
  waiting for transfers between devices: 50.5 us -> 42.6 us
  Pallas kernels: 82 us -> 75.5 us
  other arithmetic: 4.93 us -> 1.81 us
    ppermute x4, starting transfers between devices: 39.2 us -> 18.5 us  [spread_round(): got.append(lax.ppermute(mine, 'cols', pairs))]
    ppermute x4, waiting for transfers between devices: 25 us -> 6.85 us  [spread_round(): got.append(lax.ppermute(mine, 'cols', pairs))]
    ppermute x6, waiting for transfers between devices: 4.42 us -> 12.3 us  [spread_out(): got.append(lax.ppermute(x[start:start + size], 'cols', [(0, k + 1)]))]
    pallas_call x1, Pallas kernels: 26 us -> 19.2 us  [finish(): pl.pallas_call(kernel, out_shape=(jax.ShapeDtypeStruct((rows, cols), F32)...]
    pallas_call x0 -> x2, Pallas kernels: none -> 3.97 us  [merge(): pl.pallas_call(kernel, out_shape=jax.ShapeDtypeStruct(arrays[0].shape, F3...]
    pallas_call x2, Pallas kernels: 22.2 us -> 18.7 us  [panel_dot(): pl.pallas_call(kernel, out_shape=(out, out, jax.ShapeDtypeStruct((rows, w...]
    ppermute x9, waiting for transfers between devices: 7 us -> 9.99 us  [scatter_chips(): lax.ppermute(take(mine, (chip ^ k) * piece, piece), 'rows', swap(n, 2 * k))]
    ppermute x9, waiting for transfers between devices: 6.01 us -> 8.93 us  [gather_rows(): lax.ppermute(own, 'rows', swap(n, 2 * k))]
  transfers between devices with their start and end apart: 46 -> 46, of which waited for: 14 -> 10; matrix products, arithmetic and copies ran while one was open for 6% -> 2% of each run, Pallas kernels for 19% -> 24%
where the time goes in v3:
time: 198 us; the launch traced here: 196 us
  Pallas kernels  75.5 us (38%)
  starting transfers between devices  61.7 us (31%)
  waiting for transfers between devices  42.6 us (22%)
  local copies, waits for them, and re-layouts  7.62 us (4%)
  matrix products  5.72 us (3%)
    pallas_call x4, Pallas kernels, chol_part(): pl.pallas_call(kernel, out_shape=(shape, shape, shape), in_specs=[pl.Bloc...  33.6 us
    pallas_call x1, Pallas kernels, finish(): pl.pallas_call(kernel, out_shape=(jax.ShapeDtypeStruct((rows, cols), F32)...  19.2 us
    pallas_call x2, Pallas kernels, panel_dot(): pl.pallas_call(kernel, out_shape=(out, out, jax.ShapeDtypeStruct((rows, w...  18.7 us
    ppermute x4, starting transfers between devices, spread_round(): got.append(lax.ppermute(mine, 'cols', pairs))  18.5 us
    ppermute x6, waiting for transfers between devices, spread_out(): got.append(lax.ppermute(x[start:start + size], 'cols', [(0, k + 1)]))  12.3 us
    ppermute x12, starting transfers between devices, gather_rows(): other = [lax.ppermute(g, 'rows', swap(n, 1)) for g in got]  11.5 us
    ppermute x9, waiting for transfers between devices, scatter_chips(): lax.ppermute(take(mine, (chip ^ k) * piece, piece), 'rows', swap(n, 2 * k))  9.99 us
    ppermute x9, starting transfers between devices, gather_rows(): lax.ppermute(own, 'rows', swap(n, 2 * k))  9.77 us
  transfers between devices with their start and end apart: 46, of which 10 were waited for; matrix products, arithmetic and copies ran while one was open for 2% of the time, Pallas kernels for 24%

profile of v3, /device:TPU:17, one launch (start us, length us, event | category | flops | bytes accessed | tf_op | source)
XLA Modules:
  0.0 196.5 jit_solution(14500405008352452270)
XLA Ops:
  0.6 5.7 %fusion.2 = f32[512,512]{1,0:T(8,128)S(1)} fusion(f32[1024,2048]{1,0:T(8,128)} %s_ref.5), kind=kOutput, calls=%fused_computation.2 | convolution fusion | flops 3221487616 | bytes 3145728 | tf_op jit(solution)/shard_map/dot_general | solution.py:18
  6.4 0.7 collective-permute-start
  7.2 1.3 fusion.5
  8.4 1.4 collective-permute-start.16
  9.8 1.3 collective-permute-start.15
  11.1 1.4 collective-permute-start.14
  12.7 1.3 collective-permute-start.1
  14.0 1.2 collective-permute-start.3
  15.4 12.3 %collective-permute-done.15.refs_1_ = f32[344,256]{1,0:T(8,128)} collective-permute-done((f32[344,256]{1,0:T(8,128)S(1)}, f32[344,256]{1,0:T(8,128)}, u32[]{:S(2)}, u32[]{:S(2)}) %collective-permute-start.15) | collective-permute-done | bytes 352288 | tf_op jit(solution)/shard_map/ppermute | solution.py:299
  27.7 2.0 %merge.2.rest_0_ = f32[344,256]{1,0:T(8,128)} custom-call(f32[344,256]{1,0:T(8,128)} %collective-permute-done.14.refs_0_, f32[344,256]{1,0:T(8,128)} %collective-permute-done.15.refs_1_, f32[344,256]{1,0:T(8,128)} %collective-permute-done.16.refs_2_), custom_call_target="tpu_custom_call" | custom-call | flops 30000001024 | bytes 1048576 | tf_op jit(solution)/shard_map/merge/pallas_call | solution.py:283
  29.7 1.9 collective-permute-start.18
  31.6 10.6 %collective-permute-start.17 = (f32[344,256]{1,0:T(8,128)}, f32[344,256]{1,0:T(8,128)S(1)}, u32[]{:S(2)}, u32[]{:S(2)}) collective-permute-start(f32[344,256]{1,0:T(8,128)} %merge.2.rest_0_), channel_id=1, source_target_pairs={{1,2},{2,3},{3,1},{5,6},{6,7},{7,5},{9,10},{10,11},{11,9},{13,14},... | collective-permute-start | bytes 1056776 | tf_op jit(solution)/shard_map/ppermute | solution.py:307
  42.3 0.7 collective-permute-start.6
  43.0 1.3 collective-permute-start.5
  44.3 0.7 collective-permute-start.4
  45.0 0.8 fusion.6
  45.8 0.7 collective-permute-start.21
  46.6 0.6 stack.27.info_ref
  47.2 4.4 %collective-permute-done.5 = f32[64,512]{1,0:T(8,128)S(1)} collective-permute-done((f32[64,512]{1,0:T(8,128)S(1)}, f32[64,512]{1,0:T(8,128)S(1)}, u32[]{:S(2)}, u32[]{:S(2)}) %collective-permute-start.5) | collective-permute-done | bytes 131104 | tf_op jit(solution)/shard_map/ppermute | solution.py:363
  51.6 1.3 collective-permute-start.20
  52.9 0.7 collective-permute-start.19
  53.6 2.2 %collective-permute-start.9 = (f32[64,512]{1,0:T(8,128)S(1)}, f32[64,512]{1,0:T(8,128)S(1)}, u32[]{:S(2)}, u32[]{:S(2)}) collective-permute-start(f32[64,512]{1,0:T(8,128)S(1)} %add_select_fusion.refs_0_), channel_id=1, source_target_pairs={{0,24},{4,28},{8,16},{12,20},{16,8},{20,12},{24,0},{28,4},{1,25},{... | collective-permute-start | bytes 393224 | tf_op jit(solution)/shard_map/ppermute | solution.py:338
  55.8 6.8 %collective-permute-done.17.rest_1_ = f32[344,256]{1,0:T(8,128)S(1)} collective-permute-done((f32[344,256]{1,0:T(8,128)}, f32[344,256]{1,0:T(8,128)S(1)}, u32[]{:S(2)}, u32[]{:S(2)}) %collective-permute-start.17) | collective-permute-done | bytes 352288 | tf_op jit(solution)/shard_map/ppermute | solution.py:307
  62.7 1.2 collective-permute-start.8
  63.9 1.2 collective-permute-start.7
  65.1 9.2 %panel_dot.2 = (f32[128,2048]{1,0:T(8,128)}, f32[128,2048]{1,0:T(8,128)}, f32[1024,256]{1,0:T(8,128)}) custom-call(s32[6]{0:T(128)} %stack.27.info_ref, f32[1024,2048]{1,0:T(8,128)} %s_ref.5, f32[1024,2048]{1,0:T(8,128)} %s_ref.5, f32[344,256]{1,0:T(8,128)} %merge.2.rest_0_, f32[344,256]{1,0:T(8,128)} %copy-done.6, f32[344,256]{1,0:T(8,128)} %copy-done.5), custom_call_target="tpu_custom_call" | custom-call | flops 3221225472 | bytes 8388608 | tf_op jit(solution)/shard_map/panel_dot/pallas_call | solution.py:244
  74.4 3.6 %collective-permute-start.10 = (f32[64,512]{1,0:T(8,128)S(1)}, f32[64,512]{1,0:T(8,128)S(1)}, u32[]{:S(2)}, u32[]{:S(2)}) collective-permute-start(f32[64,512]{1,0:T(8,128)S(1)} %add_select_fusion.refs_0_), channel_id=1, source_target_pairs={{0,4},{4,0},{8,12},{12,8},{16,20},{20,16},{24,28},{28,24},{1,5},{5... | collective-permute-start | bytes 393224 | tf_op jit(solution)/shard_map/ppermute | solution.py:339
  78.0 0.7 copy-done.13
  78.7 0.7 collective-permute-start.22
  80.0 2.0 %merge.3.rest_0_ = f32[344,256]{1,0:T(8,128)} custom-call(f32[344,256]{1,0:T(8,128)} %copy-done.13, f32[344,256]{1,0:T(8,128)} %copy-done.12, f32[344,256]{1,0:T(8,128)} %copy-done.11), custom_call_target="tpu_custom_call" | custom-call | flops 30000001024 | bytes 1048576 | tf_op jit(solution)/shard_map/merge/pallas_call | solution.py:283
  82.0 2.0 %collective-permute-start.24 = (f32[344,256]{1,0:T(8,128)}, f32[344,256]{1,0:T(8,128)S(1)}, u32[]{:S(2)}, u32[]{:S(2)}) collective-permute-start(f32[344,256]{1,0:T(8,128)} %merge.3.rest_0_), channel_id=1, source_target_pairs={{1,3},{2,1},{3,2},{5,7},{6,5},{7,6},{9,11},{10,9},{11,10},{13,15},... | collective-permute-start | bytes 1056776 | tf_op jit(solution)/shard_map/ppermute | solution.py:307
  84.0 3.9 %collective-permute-start.23 = (f32[344,256]{1,0:T(8,128)}, f32[344,256]{1,0:T(8,128)S(1)}, u32[]{:S(2)}, u32[]{:S(2)}) collective-permute-start(f32[344,256]{1,0:T(8,128)} %merge.3.rest_0_), channel_id=1, source_target_pairs={{1,2},{2,3},{3,1},{5,6},{6,7},{7,5},{9,10},{10,11},{11,9},{13,14},... | collective-permute-start | bytes 1056776 | tf_op jit(solution)/shard_map/ppermute | solution.py:307
  88.0 8.9 %chol_part.4 = (f32[512,512]{1,0:T(8,128)S(1)}, f32[512,512]{1,0:T(8,128)S(1)}, f32[512,512]{1,0:T(8,128)S(1)}) custom-call(s32[6]{0:T(128)S(1)} %copy-done, f32[64,512]{1,0:T(8,128)S(1)} %add_select_fusion.refs_0_, f32[64,512]{1,0:T(8,128)S(1)} %collective-permute-done.7.refs_1_, f32[64,512]{1,0:T(8,128)S(1)} %collective-permute-done.8.refs_2_, ...), custom_call_target="tpu_custom_call" | custom-call | flops 8000000000 | bytes 3145728 | tf_op jit(solution)/shard_map/chol_part/pallas_call | solution.py:111
  97.2 1.3 collective-permute-start.25
  98.5 1.2 collective-permute-start.27
  99.9 8.5 %chol_part.5 = (f32[512,512]{1,0:T(8,128)S(1)}, f32[512,512]{1,0:T(8,128)S(1)}, f32[512,512]{1,0:T(8,128)S(1)}) custom-call(s32[6]{0:T(128)S(1)} %copy-done, f32[512,512]{1,0:T(8,128)S(1)} %get-tuple-element.60.refs_0_, f32[512,512]{1,0:T(8,128)S(1)} %get-tuple-element.61.refs_1_, ...), custom_call_target="tpu_custom_call", output_to_operand_aliasing={{0}: (1, {}), {1}: (2, {}), {2}: (3, {})} | custom-call | flops 8000000000 | bytes 3145728 | tf_op jit(solution)/shard_map/chol_part/pallas_call | solution.py:111
  108.5 2.5 %collective-permute-done.27 = f32[32,2048]{1,0:T(8,128)S(1)} collective-permute-done((f32[32,2048]{1,0:T(8,128)S(1)}, f32[32,2048]{1,0:T(8,128)S(1)}, u32[]{:S(2)}, u32[]{:S(2)}) %collective-permute-start.27) | collective-permute-done | bytes 262176 | tf_op jit(solution)/shard_map/ppermute | solution.py:333
  111.1 0.8 copy-done.7
  112.0 9.5 %panel_dot.3 = (f32[128,2048]{1,0:T(8,128)}, f32[128,2048]{1,0:T(8,128)}, f32[1024,256]{1,0:T(8,128)}) custom-call(s32[6]{0:T(128)} %stack.27.info_ref, f32[1024,2048]{1,0:T(8,128)} %s_ref.5, f32[1024,2048]{1,0:T(8,128)} %s_ref.5, f32[344,256]{1,0:T(8,128)} %merge.3.rest_0_, f32[344,256]{1,0:T(8,128)} %copy-done.8, f32[344,256]{1,0:T(8,128)} %copy-done.7), custom_call_target="tpu_custom_call" | custom-call | flops 3221225472 | bytes 8388608 | tf_op jit(solution)/shard_map/panel_dot/pallas_call | solution.py:244
  121.5 3.0 %collective-permute-start.28 = (f32[128,2048]{1,0:T(8,128)}, f32[128,2048]{1,0:T(8,128)S(1)}, u32[]{:S(2)}, u32[]{:S(2)}) collective-permute-start(f32[128,2048]{1,0:T(8,128)} %get-tuple-element.70), channel_id=1, source_target_pairs={{0,4},{4,0},{8,12},{12,8},{16,20},{20,16},{24,28},{28,24},{1,5},{5... | collective-permute-start | bytes 3145736 | tf_op jit(solution)/shard_map/ppermute | solution.py:324
  124.5 1.2 collective-permute-start.34
  125.7 1.2 collective-permute-start.33
  127.0 1.3 add.116
  128.5 1.3 collective-permute-start.29
  129.9 1.2 collective-permute-start.30
  131.2 2.2 %collective-permute-done.34.rest_5_ = f32[32,2048]{1,0:T(8,128)S(1)} collective-permute-done((f32[32,2048]{1,0:T(8,128)S(1)}, f32[32,2048]{1,0:T(8,128)S(1)}, u32[]{:S(2)}, u32[]{:S(2)}) %collective-permute-start.34) | collective-permute-done | bytes 262176 | tf_op jit(solution)/shard_map/ppermute | solution.py:338
  133.4 1.3 collective-permute-start.35
  134.7 5.0 %collective-permute-done.33.rest_4_ = f32[32,2048]{1,0:T(8,128)S(1)} collective-permute-done((f32[32,2048]{1,0:T(8,128)S(1)}, f32[32,2048]{1,0:T(8,128)S(1)}, u32[]{:S(2)}, u32[]{:S(2)}) %collective-permute-start.33) | collective-permute-done | bytes 262176 | tf_op jit(solution)/shard_map/ppermute | solution.py:338
  139.6 2.2 %collective-permute-start.38 = (f32[32,2048]{1,0:T(8,128)S(1)}, f32[32,2048]{1,0:T(8,128)S(1)}, u32[]{:S(2)}, u32[]{:S(2)}) collective-permute-start(f32[32,2048]{1,0:T(8,128)S(1)} %collective-permute-done.34.rest_5_), channel_id=1, source_target_pairs={{0,4},{4,0},{8,12},{12,8},{16,20},{20,16},{24,28},{28,24},{1,5},{5... | collective-permute-start | bytes 786440 | tf_op jit(solution)/shard_map/ppermute | solution.py:339
  141.8 2.8 %collective-permute-done.31 = f32[32,2048]{1,0:T(8,128)S(1)} collective-permute-done((f32[32,2048]{1,0:T(8,128)S(1)}, f32[32,2048]{1,0:T(8,128)S(1)}, u32[]{:S(2)}, u32[]{:S(2)}) %collective-permute-start.31) | collective-permute-done | bytes 262176 | tf_op jit(solution)/shard_map/ppermute | solution.py:333
  144.6 1.3 collective-permute-start.37
  145.9 4.6 %collective-permute-done.30 = f32[32,2048]{1,0:T(8,128)S(1)} collective-permute-done((f32[32,2048]{1,0:T(8,128)S(1)}, f32[32,2048]{1,0:T(8,128)S(1)}, u32[]{:S(2)}, u32[]{:S(2)}) %collective-permute-start.30) | collective-permute-done | bytes 262176 | tf_op jit(solution)/shard_map/ppermute | solution.py:333
  150.6 1.2 collective-permute-start.41
  151.9 1.5 collective-permute-start.39
  153.4 8.3 %chol_part.6 = (f32[512,512]{1,0:T(8,128)S(1)}, f32[512,512]{1,0:T(8,128)S(1)}, f32[512,512]{1,0:T(8,128)S(1)}) custom-call(s32[6]{0:T(128)S(1)} %copy-done.1, f32[512,512]{1,0:T(8,128)S(1)} %get-tuple-element.71.refs_0_, f32[512,512]{1,0:T(8,128)S(1)} %get-tuple-element.72.refs_1_, ...), custom_call_target="tpu_custom_call", output_to_operand_aliasing={{0}: (1, {}), {1}: (2, {}), {2}: (3, {})} | custom-call | flops 8000000000 | bytes 3145728 | tf_op jit(solution)/shard_map/chol_part/pallas_call | solution.py:111
  161.7 1.4 collective-permute-start.36
  163.2 0.5 collective-permute-start.45
  163.7 1.8 collective-permute-done.40.rest_12_
  165.4 0.5 collective-permute-start.44
  166.0 7.9 %chol_part.7 = (f32[512,512]{1,0:T(8,128)S(1)}, f32[512,512]{1,0:T(8,128)S(1)}, f32[512,512]{1,0:T(8,128)S(1)}) custom-call(s32[6]{0:T(128)S(1)} %copy-done.1, f32[512,512]{1,0:T(8,128)S(1)} %get-tuple-element.77.refs_0_, f32[512,512]{1,0:T(8,128)S(1)} %get-tuple-element.78.refs_1_, ...), custom_call_target="tpu_custom_call", output_to_operand_aliasing={{0}: (1, {}), {1}: (2, {}), {2}: (3, {})} | custom-call | flops 8000000000 | bytes 3145728 | tf_op jit(solution)/shard_map/chol_part/pallas_call | solution.py:111
  174.0 1.0 copy-done.2
  174.9 1.0 copy-done.3
  176.0 0.8 copy-done.27
  177.1 19.2 %finish.1 = (f32[1024,2048]{1,0:T(8,128)}, f32[512,2048]{1,0:T(8,128)}) custom-call(s32[6]{0:T(128)} %stack.27.info_ref, f32[1024,2048]{1,0:T(8,128)} %s_ref.5, f32[512,512]{1,0:T(8,128)} %copy-done.3, f32[512,512]{1,0:T(8,128)} %copy-done.2, f32[1024,256]{1,0:T(8,128)} %get-tuple-element.82.rest_0_, f32[1024,256]{1,0:T(8,128)} %get-tuple-element.83.rest_1_, ...), custom_call_target="tpu_custom_call" | custom-call | flops 9663676416 | bytes 16777216 | tf_op jit(solution)/shard_map/finish/pallas_call | solution.py:175
  (110 shorter events, 2.8 us)
Async XLA Ops:
  6.4 6.1 %collective-permute-start = (f32[256,512]{1,0:T(8,128)S(1)}, f32[256,512]{1,0:T(8,128)S(1)}, u32[]{:S(2)}, u32[]{:S(2)}) collective-permute-start(f32[256,512]{1,0:T(8,128)S(1)} %constant_dynamic-slice_fusion.9), channel_id=1, source_target_pairs={{0,4},{4,0},{8,12},{12,8},{16,20},{20,16},{24,28},{28,24},{1,5},{5... | collective-permute-start | bytes 1572872 | tf_op jit(solution)/shard_map/ppermute | solution.py:324
  8.4 6.7 %collective-permute-start.16 = (f32[344,256]{1,0:T(8,128)S(1)}, f32[344,256]{1,0:T(8,128)}, u32[]{:S(2)}, u32[]{:S(2)}) collective-permute-start(f32[344,256]{1,0:T(8,128)S(1)} %get-tuple-element.84), channel_id=1, source_target_pairs={{0,1},{4,5},{8,9},{12,13},{16,17},{20,21},{24,25},{28,29}} | collective-permute-start | bytes 1056776 | tf_op jit(solution)/shard_map/ppermute | solution.py:299
  9.8 17.9 %collective-permute-start.15 = (f32[344,256]{1,0:T(8,128)S(1)}, f32[344,256]{1,0:T(8,128)}, u32[]{:S(2)}, u32[]{:S(2)}) collective-permute-start(f32[344,256]{1,0:T(8,128)S(1)} %get-tuple-element.85), channel_id=1, source_target_pairs={{0,2},{4,6},{8,10},{12,14},{16,18},{20,22},{24,26},{28,30}} | collective-permute-start | bytes 1056776 | tf_op jit(solution)/shard_map/ppermute | solution.py:299
  11.1 16.6 %collective-permute-start.14 = (f32[344,256]{1,0:T(8,128)S(1)}, f32[344,256]{1,0:T(8,128)}, u32[]{:S(2)}, u32[]{:S(2)}) collective-permute-start(f32[344,256]{1,0:T(8,128)S(1)} %get-tuple-element.86), channel_id=1, source_target_pairs={{0,3},{4,7},{8,11},{12,15},{16,19},{20,23},{24,27},{28,31}} | collective-permute-start | bytes 1056776 | tf_op jit(solution)/shard_map/ppermute | solution.py:299
  12.7 29.6 %collective-permute-start.1 = (f32[64,512]{1,0:T(8,128)S(1)}, f32[64,512]{1,0:T(8,128)S(1)}, u32[]{:S(2)}, u32[]{:S(2)}) collective-permute-start(f32[64,512]{1,0:T(8,128)S(1)} %get-tuple-element.96), channel_id=1, source_target_pairs={{0,8},{4,12},{8,0},{12,4},{16,24},{20,28},{24,16},{28,20},{1,9},{5... | collective-permute-start | bytes 393224 | tf_op jit(solution)/shard_map/ppermute | solution.py:333
  14.0 28.3 %collective-permute-start.3 = (f32[64,512]{1,0:T(8,128)S(1)}, f32[64,512]{1,0:T(8,128)S(1)}, u32[]{:S(2)}, u32[]{:S(2)}) collective-permute-start(f32[64,512]{1,0:T(8,128)S(1)} %get-tuple-element.97), channel_id=1, source_target_pairs={{0,24},{4,28},{8,16},{12,20},{16,8},{20,12},{24,0},{28,4},{1,25},{... | collective-permute-start | bytes 393224 | tf_op jit(solution)/shard_map/ppermute | solution.py:333
  15.2 29.8 %slice-start = ((f32[1024,2048]{1,0:T(8,128)}), f32[1024,256]{1,0:T(8,128)S(1)}, s32[]{:S(2)}) async-start(f32[1024,2048]{1,0:T(8,128)} %s_ref.5), calls=%async_computation | async-start | bytes 2097152 | tf_op jit(solution)/shard_map/slice | solution.py:365
  15.2 27.1 %collective-permute-start.2 = (f32[64,512]{1,0:T(8,128)S(1)}, f32[64,512]{1,0:T(8,128)S(1)}, u32[]{:S(2)}, u32[]{:S(2)}) collective-permute-start(f32[64,512]{1,0:T(8,128)S(1)} %get-tuple-element.98), channel_id=1, source_target_pairs={{0,16},{4,20},{8,24},{12,28},{16,0},{20,4},{24,8},{28,12},{1,17},{... | collective-permute-start | bytes 393224 | tf_op jit(solution)/shard_map/ppermute | solution.py:333
  29.7 23.9 %collective-permute-start.18 = (f32[344,256]{1,0:T(8,128)}, f32[344,256]{1,0:T(8,128)S(1)}, u32[]{:S(2)}, u32[]{:S(2)}) collective-permute-start(f32[344,256]{1,0:T(8,128)} %merge.2.rest_0_), channel_id=1, source_target_pairs={{1,3},{2,1},{3,2},{5,7},{6,5},{7,6},{9,11},{10,9},{11,10},{13,15},... | collective-permute-start | bytes 1056776 | tf_op jit(solution)/shard_map/ppermute | solution.py:307
  31.6 31.1 %collective-permute-start.17 = (f32[344,256]{1,0:T(8,128)}, f32[344,256]{1,0:T(8,128)S(1)}, u32[]{:S(2)}, u32[]{:S(2)}) collective-permute-start(f32[344,256]{1,0:T(8,128)} %merge.2.rest_0_), channel_id=1, source_target_pairs={{1,2},{2,3},{3,1},{5,6},{6,7},{7,5},{9,10},{10,11},{11,9},{13,14},... | collective-permute-start | bytes 1056776 | tf_op jit(solution)/shard_map/ppermute | solution.py:307
  42.3 3.5 %collective-permute-start.6 = (f32[64,512]{1,0:T(8,128)S(1)}, f32[64,512]{1,0:T(8,128)S(1)}, u32[]{:S(2)}, u32[]{:S(2)}) collective-permute-start(f32[64,512]{1,0:T(8,128)S(1)} %add_add_fusion.2), channel_id=1, source_target_pairs={{0,1},{4,5},{8,9},{12,13},{16,17},{20,21},{24,25},{28,29}} | collective-permute-start | bytes 393224 | tf_op jit(solution)/shard_map/ppermute | solution.py:363
  43.0 8.5 %collective-permute-start.5 = (f32[64,512]{1,0:T(8,128)S(1)}, f32[64,512]{1,0:T(8,128)S(1)}, u32[]{:S(2)}, u32[]{:S(2)}) collective-permute-start(f32[64,512]{1,0:T(8,128)S(1)} %add_add_fusion.2), channel_id=1, source_target_pairs={{0,2},{4,6},{8,10},{12,14},{16,18},{20,22},{24,26},{28,30}} | collective-permute-start | bytes 393224 | tf_op jit(solution)/shard_map/ppermute | solution.py:363
  44.3 8.5 %collective-permute-start.4 = (f32[64,512]{1,0:T(8,128)S(1)}, f32[64,512]{1,0:T(8,128)S(1)}, u32[]{:S(2)}, u32[]{:S(2)}) collective-permute-start(f32[64,512]{1,0:T(8,128)S(1)} %add_add_fusion.2), channel_id=1, source_target_pairs={{0,3},{4,7},{8,11},{12,15},{16,19},{20,23},{24,27},{28,31}} | collective-permute-start | bytes 393224 | tf_op jit(solution)/shard_map/ppermute | solution.py:363
  45.8 18.1 %collective-permute-start.21 = (f32[344,256]{1,0:T(8,128)}, f32[344,256]{1,0:T(8,128)S(1)}, u32[]{:S(2)}, u32[]{:S(2)}) collective-permute-start(f32[344,256]{1,0:T(8,128)} %get-tuple-element.93), channel_id=1, source_target_pairs={{0,1},{4,5},{8,9},{12,13},{16,17},{20,21},{24,25},{28,29}} | collective-permute-start | bytes 1056776 | tf_op jit(solution)/shard_map/ppermute | solution.py:299
  51.6 22.8 %collective-permute-start.20 = (f32[344,256]{1,0:T(8,128)S(1)}, f32[344,256]{1,0:T(8,128)S(1)}, u32[]{:S(2)}, u32[]{:S(2)}) collective-permute-start(f32[344,256]{1,0:T(8,128)S(1)} %get-tuple-element.94), channel_id=1, source_target_pairs={{0,2},{4,6},{8,10},{12,14},{16,18},{20,22},{24,26},{28,30}} | collective-permute-start | bytes 1056776 | tf_op jit(solution)/shard_map/ppermute | solution.py:299
  52.9 25.1 %collective-permute-start.19 = (f32[344,256]{1,0:T(8,128)S(1)}, f32[344,256]{1,0:T(8,128)S(1)}, u32[]{:S(2)}, u32[]{:S(2)}) collective-permute-start(f32[344,256]{1,0:T(8,128)S(1)} %get-tuple-element.95), channel_id=1, source_target_pairs={{0,3},{4,7},{8,11},{12,15},{16,19},{20,23},{24,27},{28,31}} | collective-permute-start | bytes 1056776 | tf_op jit(solution)/shard_map/ppermute | solution.py:299
  53.6 11.5 %copy-start.5 = (f32[344,256]{1,0:T(8,128)}, f32[344,256]{1,0:T(8,128)S(1)}, u32[]{:S(2)}) copy-start(f32[344,256]{1,0:T(8,128)S(1)} %collective-permute-done.18.rest_2_) | copy-start | bytes 1056772
  53.6 25.8 %collective-permute-start.9 = (f32[64,512]{1,0:T(8,128)S(1)}, f32[64,512]{1,0:T(8,128)S(1)}, u32[]{:S(2)}, u32[]{:S(2)}) collective-permute-start(f32[64,512]{1,0:T(8,128)S(1)} %add_select_fusion.refs_0_), channel_id=1, source_target_pairs={{0,24},{4,28},{8,16},{12,20},{16,8},{20,12},{24,0},{28,4},{1,25},{... | collective-permute-start | bytes 393224 | tf_op jit(solution)/shard_map/ppermute | solution.py:338
  62.7 16.8 %collective-permute-start.8 = (f32[64,512]{1,0:T(8,128)S(1)}, f32[64,512]{1,0:T(8,128)S(1)}, u32[]{:S(2)}, u32[]{:S(2)}) collective-permute-start(f32[64,512]{1,0:T(8,128)S(1)} %add_select_fusion.refs_0_), channel_id=1, source_target_pairs={{0,16},{4,20},{8,24},{12,28},{16,0},{20,4},{24,8},{28,12},{1,17},{... | collective-permute-start | bytes 393224 | tf_op jit(solution)/shard_map/ppermute | solution.py:338
  63.9 10.4 %copy-start.11 = (f32[344,256]{1,0:T(8,128)}, f32[344,256]{1,0:T(8,128)S(1)}, u32[]{:S(2)}) copy-start(f32[344,256]{1,0:T(8,128)S(1)} %collective-permute-done.21.refs_2_) | copy-start | bytes 1056772
  63.9 16.0 %collective-permute-start.7 = (f32[64,512]{1,0:T(8,128)S(1)}, f32[64,512]{1,0:T(8,128)S(1)}, u32[]{:S(2)}, u32[]{:S(2)}) collective-permute-start(f32[64,512]{1,0:T(8,128)S(1)} %add_select_fusion.refs_0_), channel_id=1, source_target_pairs={{0,8},{4,12},{8,0},{12,4},{16,24},{20,28},{24,16},{28,20},{1,9},{5... | collective-permute-start | bytes 393224 | tf_op jit(solution)/shard_map/ppermute | solution.py:338
  74.4 3.6 %copy-start.12 = (f32[344,256]{1,0:T(8,128)}, f32[344,256]{1,0:T(8,128)S(1)}, u32[]{:S(2)}) copy-start(f32[344,256]{1,0:T(8,128)S(1)} %collective-permute-done.20.refs_1_) | copy-start | bytes 1056772
  74.4 7.6 %collective-permute-start.10 = (f32[64,512]{1,0:T(8,128)S(1)}, f32[64,512]{1,0:T(8,128)S(1)}, u32[]{:S(2)}, u32[]{:S(2)}) collective-permute-start(f32[64,512]{1,0:T(8,128)S(1)} %add_select_fusion.refs_0_), channel_id=1, source_target_pairs={{0,4},{4,0},{8,12},{12,8},{16,20},{20,16},{24,28},{28,24},{1,5},{5... | collective-permute-start | bytes 393224 | tf_op jit(solution)/shard_map/ppermute | solution.py:339
  78.7 9.3 %copy-start = (s32[6]{0:T(128)S(1)}, s32[6]{0:T(128)}, u32[]{:S(2)}) copy-start(s32[6]{0:T(128)} %stack.27.info_ref) | copy-start | bytes 76
  78.7 18.2 %collective-permute-start.22 = (f32[128,2048]{1,0:T(8,128)}, f32[128,2048]{1,0:T(8,128)S(1)}, u32[]{:S(2)}, u32[]{:S(2)}) collective-permute-start(f32[128,2048]{1,0:T(8,128)} %get-tuple-element.46), channel_id=1, source_target_pairs={{0,4},{4,0},{8,12},{12,8},{16,20},{20,16},{24,28},{28,24},{1,5},{5... | collective-permute-start | bytes 3145736 | tf_op jit(solution)/shard_map/ppermute | solution.py:324
  79.4 4.6 %collective-permute-start.13 = (f32[64,512]{1,0:T(8,128)S(1)}, f32[64,512]{1,0:T(8,128)S(1)}, u32[]{:S(2)}, u32[]{:S(2)}) collective-permute-start(f32[64,512]{1,0:T(8,128)S(1)} %collective-permute-done.9.refs_3_), channel_id=1, source_target_pairs={{0,4},{4,0},{8,12},{12,8},{16,20},{20,16},{24,28},{28,24},{1,5},{5... | collective-permute-start | bytes 393224 | tf_op jit(solution)/shard_map/ppermute | solution.py:339
  79.5 8.5 %collective-permute-start.12 = (f32[64,512]{1,0:T(8,128)S(1)}, f32[64,512]{1,0:T(8,128)S(1)}, u32[]{:S(2)}, u32[]{:S(2)}) collective-permute-start(f32[64,512]{1,0:T(8,128)S(1)} %collective-permute-done.8.refs_2_), channel_id=1, source_target_pairs={{0,4},{4,0},{8,12},{12,8},{16,20},{20,16},{24,28},{28,24},{1,5},{5... | collective-permute-start | bytes 393224 | tf_op jit(solution)/shard_map/ppermute | solution.py:339
  79.9 8.1 %collective-permute-start.11 = (f32[64,512]{1,0:T(8,128)S(1)}, f32[64,512]{1,0:T(8,128)S(1)}, u32[]{:S(2)}, u32[]{:S(2)}) collective-permute-start(f32[64,512]{1,0:T(8,128)S(1)} %collective-permute-done.7.refs_1_), channel_id=1, source_target_pairs={{0,4},{4,0},{8,12},{12,8},{16,20},{20,16},{24,28},{28,24},{1,5},{5... | collective-permute-start | bytes 393224 | tf_op jit(solution)/shard_map/ppermute | solution.py:339
  82.0 15.0 %copy-start.4 = (f32[128,2048]{1,0:T(8,128)S(1)}, f32[128,2048]{1,0:T(8,128)}, u32[]{:S(2)}) copy-start(f32[128,2048]{1,0:T(8,128)} %get-tuple-element.59) | copy-start | bytes 3145732
  82.0 29.1 %collective-permute-start.24 = (f32[344,256]{1,0:T(8,128)}, f32[344,256]{1,0:T(8,128)S(1)}, u32[]{:S(2)}, u32[]{:S(2)}) collective-permute-start(f32[344,256]{1,0:T(8,128)} %merge.3.rest_0_), channel_id=1, source_target_pairs={{1,3},{2,1},{3,2},{5,7},{6,5},{7,6},{9,11},{10,9},{11,10},{13,15},... | collective-permute-start | bytes 1056776 | tf_op jit(solution)/shard_map/ppermute | solution.py:307
  84.0 27.1 %collective-permute-start.23 = (f32[344,256]{1,0:T(8,128)}, f32[344,256]{1,0:T(8,128)S(1)}, u32[]{:S(2)}, u32[]{:S(2)}) collective-permute-start(f32[344,256]{1,0:T(8,128)} %merge.3.rest_0_), channel_id=1, source_target_pairs={{1,2},{2,3},{3,1},{5,6},{6,7},{7,5},{9,10},{10,11},{11,9},{13,14},... | collective-permute-start | bytes 1056776 | tf_op jit(solution)/shard_map/ppermute | solution.py:307
  97.2 11.3 %collective-permute-start.25 = (f32[32,2048]{1,0:T(8,128)S(1)}, f32[32,2048]{1,0:T(8,128)S(1)}, u32[]{:S(2)}, u32[]{:S(2)}) collective-permute-start(f32[32,2048]{1,0:T(8,128)S(1)} %get-tuple-element.90), channel_id=1, source_target_pairs={{0,8},{4,12},{8,0},{12,4},{16,24},{20,28},{24,16},{28,20},{1,9},{5... | collective-permute-start | bytes 786440 | tf_op jit(solution)/shard_map/ppermute | solution.py:333
  98.5 12.5 %collective-permute-start.27 = (f32[32,2048]{1,0:T(8,128)S(1)}, f32[32,2048]{1,0:T(8,128)S(1)}, u32[]{:S(2)}, u32[]{:S(2)}) collective-permute-start(f32[32,2048]{1,0:T(8,128)S(1)} %get-tuple-element.91), channel_id=1, source_target_pairs={{0,24},{4,28},{8,16},{12,20},{16,8},{20,12},{24,0},{28,4},{1,25},{... | collective-permute-start | bytes 786440 | tf_op jit(solution)/shard_map/ppermute | solution.py:333
  99.7 11.3 %collective-permute-start.26 = (f32[32,2048]{1,0:T(8,128)S(1)}, f32[32,2048]{1,0:T(8,128)S(1)}, u32[]{:S(2)}, u32[]{:S(2)}) collective-permute-start(f32[32,2048]{1,0:T(8,128)S(1)} %get-tuple-element.92), channel_id=1, source_target_pairs={{0,16},{4,20},{8,24},{12,28},{16,0},{20,4},{24,8},{28,12},{1,17},{... | collective-permute-start | bytes 786440 | tf_op jit(solution)/shard_map/ppermute | solution.py:333
  111.1 50.6 %copy-start.9 = (f32[32,2048]{1,0:T(8,128)}, f32[32,2048]{1,0:T(8,128)S(1)}, u32[]{:S(2)}) copy-start(f32[32,2048]{1,0:T(8,128)S(1)} %add_add_fusion.1.rest_2_) | copy-start | bytes 786436
  112.0 41.4 %copy-start.1 = (s32[6]{0:T(128)S(1)}, s32[6]{0:T(128)}, u32[]{:S(2)}) copy-start(s32[6]{0:T(128)} %stack.27.info_ref) | copy-start | bytes 76
  121.5 5.5 %collective-permute-start.28 = (f32[128,2048]{1,0:T(8,128)}, f32[128,2048]{1,0:T(8,128)S(1)}, u32[]{:S(2)}, u32[]{:S(2)}) collective-permute-start(f32[128,2048]{1,0:T(8,128)} %get-tuple-element.70), channel_id=1, source_target_pairs={{0,4},{4,0},{8,12},{12,8},{16,20},{20,16},{24,28},{28,24},{1,5},{5... | collective-permute-start | bytes 3145736 | tf_op jit(solution)/shard_map/ppermute | solution.py:324
  124.5 8.8 %collective-permute-start.34 = (f32[32,2048]{1,0:T(8,128)S(1)}, f32[32,2048]{1,0:T(8,128)S(1)}, u32[]{:S(2)}, u32[]{:S(2)}) collective-permute-start(f32[32,2048]{1,0:T(8,128)S(1)} %add_add_fusion.1.rest_2_), channel_id=1, source_target_pairs={{0,24},{4,28},{8,16},{12,20},{16,8},{20,12},{24,0},{28,4},{1,25},{... | collective-permute-start | bytes 786440 | tf_op jit(solution)/shard_map/ppermute | solution.py:338
  125.7 13.9 %collective-permute-start.33 = (f32[32,2048]{1,0:T(8,128)S(1)}, f32[32,2048]{1,0:T(8,128)S(1)}, u32[]{:S(2)}, u32[]{:S(2)}) collective-permute-start(f32[32,2048]{1,0:T(8,128)S(1)} %add_add_fusion.1.rest_2_), channel_id=1, source_target_pairs={{0,16},{4,20},{8,24},{12,28},{16,0},{20,4},{24,8},{28,12},{1,17},{... | collective-permute-start | bytes 786440 | tf_op jit(solution)/shard_map/ppermute | solution.py:338
  128.5 11.2 %collective-permute-start.29 = (f32[32,2048]{1,0:T(8,128)S(1)}, f32[32,2048]{1,0:T(8,128)S(1)}, u32[]{:S(2)}, u32[]{:S(2)}) collective-permute-start(f32[32,2048]{1,0:T(8,128)S(1)} %get-tuple-element.87), channel_id=1, source_target_pairs={{0,8},{4,12},{8,0},{12,4},{16,24},{20,28},{24,16},{28,20},{1,9},{5... | collective-permute-start | bytes 786440 | tf_op jit(solution)/shard_map/ppermute | solution.py:333
  129.7 14.9 %collective-permute-start.31 = (f32[32,2048]{1,0:T(8,128)S(1)}, f32[32,2048]{1,0:T(8,128)S(1)}, u32[]{:S(2)}, u32[]{:S(2)}) collective-permute-start(f32[32,2048]{1,0:T(8,128)S(1)} %get-tuple-element.88), channel_id=1, source_target_pairs={{0,24},{4,28},{8,16},{12,20},{16,8},{20,12},{24,0},{28,4},{1,25},{... | collective-permute-start | bytes 786440 | tf_op jit(solution)/shard_map/ppermute | solution.py:333
  129.9 20.6 %collective-permute-start.30 = (f32[32,2048]{1,0:T(8,128)S(1)}, f32[32,2048]{1,0:T(8,128)S(1)}, u32[]{:S(2)}, u32[]{:S(2)}) collective-permute-start(f32[32,2048]{1,0:T(8,128)S(1)} %get-tuple-element.89), channel_id=1, source_target_pairs={{0,16},{4,20},{8,24},{12,28},{16,0},{20,4},{24,8},{28,12},{1,17},{... | collective-permute-start | bytes 786440 | tf_op jit(solution)/shard_map/ppermute | solution.py:333
  133.4 28.3 %copy-start.14 = (f32[32,2048]{1,0:T(8,128)}, f32[32,2048]{1,0:T(8,128)S(1)}, u32[]{:S(2)}) copy-start(f32[32,2048]{1,0:T(8,128)S(1)} %collective-permute-done.34.rest_5_) | copy-start | bytes 786436
  133.4 18.5 %collective-permute-start.35 = (f32[32,2048]{1,0:T(8,128)S(1)}, f32[32,2048]{1,0:T(8,128)S(1)}, u32[]{:S(2)}, u32[]{:S(2)}) collective-permute-start(f32[32,2048]{1,0:T(8,128)S(1)} %add_add_fusion.1.rest_2_), channel_id=1, source_target_pairs={{0,4},{4,0},{8,12},{12,8},{16,20},{20,16},{24,28},{28,24},{1,5},{5... | collective-permute-start | bytes 786440 | tf_op jit(solution)/shard_map/ppermute | solution.py:339
  139.6 22.0 %copy-start.15 = (f32[32,2048]{1,0:T(8,128)}, f32[32,2048]{1,0:T(8,128)S(1)}, u32[]{:S(2)}) copy-start(f32[32,2048]{1,0:T(8,128)S(1)} %collective-permute-done.33.rest_4_) | copy-start | bytes 786436
  139.6 12.2 %collective-permute-start.32 = (f32[32,2048]{1,0:T(8,128)S(1)}, f32[32,2048]{1,0:T(8,128)S(1)}, u32[]{:S(2)}, u32[]{:S(2)}) collective-permute-start(f32[32,2048]{1,0:T(8,128)S(1)} %add_add_fusion.1.rest_2_), channel_id=1, source_target_pairs={{0,8},{4,12},{8,0},{12,4},{16,24},{20,28},{24,16},{28,20},{1,9},{5... | collective-permute-start | bytes 786440 | tf_op jit(solution)/shard_map/ppermute | solution.py:338
  139.6 22.0 %collective-permute-start.38 = (f32[32,2048]{1,0:T(8,128)S(1)}, f32[32,2048]{1,0:T(8,128)S(1)}, u32[]{:S(2)}, u32[]{:S(2)}) collective-permute-start(f32[32,2048]{1,0:T(8,128)S(1)} %collective-permute-done.34.rest_5_), channel_id=1, source_target_pairs={{0,4},{4,0},{8,12},{12,8},{16,20},{20,16},{24,28},{28,24},{1,5},{5... | collective-permute-start | bytes 786440 | tf_op jit(solution)/shard_map/ppermute | solution.py:339
  144.6 18.5 %collective-permute-start.37 = (f32[32,2048]{1,0:T(8,128)S(1)}, f32[32,2048]{1,0:T(8,128)S(1)}, u32[]{:S(2)}, u32[]{:S(2)}) collective-permute-start(f32[32,2048]{1,0:T(8,128)S(1)} %collective-permute-done.33.rest_4_), channel_id=1, source_target_pairs={{0,4},{4,0},{8,12},{12,8},{16,20},{20,16},{24,28},{28,24},{1,5},{5... | collective-permute-start | bytes 786440 | tf_op jit(solution)/shard_map/ppermute | solution.py:339
  150.6 12.5 %copy-start.10 = (f32[32,2048]{1,0:T(8,128)}, f32[32,2048]{1,0:T(8,128)S(1)}, u32[]{:S(2)}) copy-start(f32[32,2048]{1,0:T(8,128)S(1)} %add_add_fusion.rest_10_) | copy-start | bytes 786436
  150.6 12.6 %collective-permute-start.41 = (f32[32,2048]{1,0:T(8,128)S(1)}, f32[32,2048]{1,0:T(8,128)S(1)}, u32[]{:S(2)}, u32[]{:S(2)}) collective-permute-start(f32[32,2048]{1,0:T(8,128)S(1)} %add_add_fusion.rest_10_), channel_id=1, source_target_pairs={{0,24},{4,28},{8,16},{12,20},{16,8},{20,12},{24,0},{28,4},{1,25},{... | collective-permute-start | bytes 786440 | tf_op jit(solution)/shard_map/ppermute | solution.py:338
  151.8 9.8 %copy-start.16 = (f32[32,2048]{1,0:T(8,128)}, f32[32,2048]{1,0:T(8,128)S(1)}, u32[]{:S(2)}) copy-start(f32[32,2048]{1,0:T(8,128)S(1)} %collective-permute-done.35.rest_6_) | copy-start | bytes 786436
  151.8 13.6 %collective-permute-start.40 = (f32[32,2048]{1,0:T(8,128)S(1)}, f32[32,2048]{1,0:T(8,128)S(1)}, u32[]{:S(2)}, u32[]{:S(2)}) collective-permute-start(f32[32,2048]{1,0:T(8,128)S(1)} %add_add_fusion.rest_10_), channel_id=1, source_target_pairs={{0,16},{4,20},{8,24},{12,28},{16,0},{20,4},{24,8},{28,12},{1,17},{... | collective-permute-start | bytes 786440 | tf_op jit(solution)/shard_map/ppermute | solution.py:338
  151.9 9.8 %copy-start.17 = (f32[32,2048]{1,0:T(8,128)}, f32[32,2048]{1,0:T(8,128)S(1)}, u32[]{:S(2)}) copy-start(f32[32,2048]{1,0:T(8,128)S(1)} %collective-permute-done.32.rest_3_) | copy-start | bytes 786436
  151.9 14.1 %collective-permute-start.39 = (f32[32,2048]{1,0:T(8,128)S(1)}, f32[32,2048]{1,0:T(8,128)S(1)}, u32[]{:S(2)}, u32[]{:S(2)}) collective-permute-start(f32[32,2048]{1,0:T(8,128)S(1)} %add_add_fusion.rest_10_), channel_id=1, source_target_pairs={{0,8},{4,12},{8,0},{12,4},{16,24},{20,28},{24,16},{28,20},{1,9},{5... | collective-permute-start | bytes 786440 | tf_op jit(solution)/shard_map/ppermute | solution.py:338
  161.7 12.2 %copy-start.18 = (f32[32,2048]{1,0:T(8,128)}, f32[32,2048]{1,0:T(8,128)S(1)}, u32[]{:S(2)}) copy-start(f32[32,2048]{1,0:T(8,128)S(1)} %collective-permute-done.38.rest_9_) | copy-start | bytes 786436
  161.7 14.2 %collective-permute-start.36 = (f32[32,2048]{1,0:T(8,128)S(1)}, f32[32,2048]{1,0:T(8,128)S(1)}, u32[]{:S(2)}, u32[]{:S(2)}) collective-permute-start(f32[32,2048]{1,0:T(8,128)S(1)} %collective-permute-done.32.rest_3_), channel_id=1, source_target_pairs={{0,4},{4,0},{8,12},{12,8},{16,20},{20,16},{24,28},{28,24},{1,5},{5... | collective-permute-start | bytes 786440 | tf_op jit(solution)/shard_map/ppermute | solution.py:339
  163.1 10.8 %copy-start.19 = (f32[32,2048]{1,0:T(8,128)}, f32[32,2048]{1,0:T(8,128)S(1)}, u32[]{:S(2)}) copy-start(f32[32,2048]{1,0:T(8,128)S(1)} %collective-permute-done.37.rest_8_) | copy-start | bytes 786436
  163.1 12.8 %collective-permute-start.42 = (f32[32,2048]{1,0:T(8,128)S(1)}, f32[32,2048]{1,0:T(8,128)S(1)}, u32[]{:S(2)}, u32[]{:S(2)}) collective-permute-start(f32[32,2048]{1,0:T(8,128)S(1)} %add_add_fusion.rest_10_), channel_id=1, source_target_pairs={{0,4},{4,0},{8,12},{12,8},{16,20},{20,16},{24,28},{28,24},{1,5},{5... | collective-permute-start | bytes 786440 | tf_op jit(solution)/shard_map/ppermute | solution.py:339
  163.2 10.7 %copy-start.20 = (f32[32,2048]{1,0:T(8,128)}, f32[32,2048]{1,0:T(8,128)S(1)}, u32[]{:S(2)}) copy-start(f32[32,2048]{1,0:T(8,128)S(1)} %collective-permute-done.41.rest_13_) | copy-start | bytes 786436
  163.2 12.7 %collective-permute-start.45 = (f32[32,2048]{1,0:T(8,128)S(1)}, f32[32,2048]{1,0:T(8,128)S(1)}, u32[]{:S(2)}, u32[]{:S(2)}) collective-permute-start(f32[32,2048]{1,0:T(8,128)S(1)} %collective-permute-done.41.rest_13_), channel_id=1, source_target_pairs={{0,4},{4,0},{8,12},{12,8},{16,20},{20,16},{24,28},{28,24},{1,5},{5... | collective-permute-start | bytes 786440 | tf_op jit(solution)/shard_map/ppermute | solution.py:339
  165.4 8.5 %copy-start.21 = (f32[32,2048]{1,0:T(8,128)}, f32[32,2048]{1,0:T(8,128)S(1)}, u32[]{:S(2)}) copy-start(f32[32,2048]{1,0:T(8,128)S(1)} %collective-permute-done.40.rest_12_) | copy-start | bytes 786436
  165.4 10.5 %collective-permute-start.44 = (f32[32,2048]{1,0:T(8,128)S(1)}, f32[32,2048]{1,0:T(8,128)S(1)}, u32[]{:S(2)}, u32[]{:S(2)}) collective-permute-start(f32[32,2048]{1,0:T(8,128)S(1)} %collective-permute-done.40.rest_12_), channel_id=1, source_target_pairs={{0,4},{4,0},{8,12},{12,8},{16,20},{20,16},{24,28},{28,24},{1,5},{5... | collective-permute-start | bytes 786440 | tf_op jit(solution)/shard_map/ppermute | solution.py:339
  165.9 8.0 %copy-start.22 = (f32[32,2048]{1,0:T(8,128)}, f32[32,2048]{1,0:T(8,128)S(1)}, u32[]{:S(2)}) copy-start(f32[32,2048]{1,0:T(8,128)S(1)} %collective-permute-done.39.rest_11_) | copy-start | bytes 786436
  165.9 10.0 %collective-permute-start.43 = (f32[32,2048]{1,0:T(8,128)S(1)}, f32[32,2048]{1,0:T(8,128)S(1)}, u32[]{:S(2)}, u32[]{:S(2)}) collective-permute-start(f32[32,2048]{1,0:T(8,128)S(1)} %collective-permute-done.39.rest_11_), channel_id=1, source_target_pairs={{0,4},{4,0},{8,12},{12,8},{16,20},{20,16},{24,28},{28,24},{1,5},{5... | collective-permute-start | bytes 786440 | tf_op jit(solution)/shard_map/ppermute | solution.py:339
  (11 other events, 11.7 us)

commit v4 on v3

--- a/solution.py
+++ b/solution.py
@@ -7,7 +7,6 @@
 
 PB = 512
 NB = 128
-MERGE_COST = 3 * 10**10
 F32 = jnp.float32
 BF16 = jnp.bfloat16
 HIGHEST = lax.Precision.HIGHEST
@@ -31,36 +30,44 @@
     col = lax.broadcasted_iota(jnp.int32, (NB, NB), 1)
     z_all = jnp.where(row == col, 1.0, 0.0).astype(F32)
     lane = lax.broadcasted_iota(jnp.int32, (1, NB), 1)
-    for j in range(0, NB, 2):
+    for j in range(0, NB, 4):
         base = (j // 8) * 8
         if a_all.shape[0] != NB - base:
             a_all, z_all = a_all[8:], z_all[8:]
         i, n = j - base, NB - base
-        r0, r1 = a_all[i : i + 1, :], a_all[i + 1 : i + 2, :]
-        z0, z1 = z_all[i : i + 1, :], z_all[i + 1 : i + 2, :]
-        c0 = jnp.broadcast_to(a_all[:, j : j + 1], (n, NB))
-        c1 = jnp.broadcast_to(a_all[:, j + 1 : j + 2], (n, NB))
-        a = jnp.broadcast_to(r0[:, j : j + 1], (1, NB))
-        b = jnp.broadcast_to(r0[:, j + 1 : j + 2], (1, NB))
-        d = jnp.broadcast_to(r1[:, j + 1 : j + 2], (1, NB))
-        ra = 1.0 / a
-        bra = b * ra
-        s = d - b * bra
-        rs = 1.0 / s
-        t1 = r1 - bra * r0
-        x1 = t1 * rs
-        x0 = r0 * ra - bra * x1
-        u1 = z1 - bra * z0
-        y1 = u1 * rs
-        y0 = z0 * ra - bra * y1
-        qa, qs = lax.rsqrt(a), lax.rsqrt(s)
-        f_ref[j : j + 1, :] = jnp.where(lane >= j, r0 * qa, 0.0)
-        f_ref[j + 1 : j + 2, :] = jnp.where(lane >= j + 1, t1 * qs, 0.0)
-        z_ref[j : j + 1, :] = z0 * qa
-        z_ref[j + 1 : j + 2, :] = u1 * qs
-        if j + 2 < NB:
-            a_all = a_all - c0 * x0 - c1 * x1
-            z_all = z_all - c0 * y0 - c1 * y1
+        t = [a_all[i + k : i + k + 1, :] for k in range(4)]
+        u = [z_all[i + k : i + k + 1, :] for k in range(4)]
+        c = [jnp.broadcast_to(a_all[:, j + k : j + k + 1], (n, NB)) for k in range(4)]
+        e = {
+            (k, m): jnp.broadcast_to(t[k][:, j + m : j + m + 1], (1, NB))
+            for k in range(4)
+            for m in range(k, 4)
+        }
+        inv, low = [], {}
+        for k in range(4):
+            inv.append(1.0 / e[k, k])
+            for m in range(k + 1, 4):
+                low[m, k] = e[k, m] * inv[k]
+            for m in range(k + 1, 4):
+                for q in range(m, 4):
+                    e[m, q] = e[m, q] - low[m, k] * e[k, q]
+        for k in range(4):
+            for m in range(k):
+                t[k] = t[k] - low[k, m] * t[m]
+                u[k] = u[k] - low[k, m] * u[m]
+        x, y = [None] * 4, [None] * 4
+        for k in reversed(range(4)):
+            x[k], y[k] = t[k] * inv[k], u[k] * inv[k]
+            for m in range(k + 1, 4):
+                x[k] = x[k] - low[m, k] * x[m]
+                y[k] = y[k] - low[m, k] * y[m]
+        for k in range(4):
+            root = lax.rsqrt(e[k, k])
+            f_ref[j + k : j + k + 1, :] = jnp.where(lane >= j + k, t[k] * root, 0.0)
+            z_ref[j + k : j + k + 1, :] = u[k] * root
+        if j + 4 < NB:
+            a_all = a_all - ((c[0] * x[0] + c[1] * x[1]) + (c[2] * x[2] + c[3] * x[3]))
+            z_all = z_all - ((c[0] * y[0] + c[1] * y[1]) + (c[2] * y[2] + c[3] * y[3]))
 
 
 def chol_part(info, first, last, pieces=None, places=None, state=None):
@@ -170,7 +177,6 @@
                 co_ref[...] = f_ref[:, t * tile : (t + 1) * tile]
                 up_ref[...] = bs[:, t * tile : (t + 1) * tile]
 
-    full = lambda a: pl.BlockSpec(a.shape, lambda j, *_: (0, 0), pipeline_mode=pl.Buffered(1))
     col = lambda h: pl.BlockSpec((h, tile), lambda j, *_: (0, j))
     return pl.pallas_call(
         kernel,
@@ -181,8 +187,8 @@
         grid_spec=pltpu.PrefetchScalarGridSpec(
             num_scalar_prefetch=1,
             grid=(cols // tile,),
-            in_specs=[col(rows), full(linv), full(factor)]
-            + [full(p) for p in panels]
+            in_specs=[col(rows), VMEM, VMEM]
+            + [VMEM for _ in panels]
             + [col(p.shape[0]) for p in pieces],
             out_specs=(col(rows), col(PB)),
             scratch_shapes=[
@@ -273,23 +279,6 @@
     return -(-rows // (8 * parts)) * 8
 
 
-def merge(arrays):
-    def kernel(*refs):
-        total = refs[0][...]
-        for ref in refs[1:-1]:
-            total = total + ref[...]
-        refs[-1][...] = total
-
-    return pl.pallas_call(
-        kernel,
-        out_shape=jax.ShapeDtypeStruct(arrays[0].shape, F32),
-        in_specs=[VMEM] * len(arrays),
-        out_specs=VMEM,
-        cost_estimate=pl.CostEstimate(flops=MERGE_COST, bytes_accessed=1 << 20, transcendentals=0),
-        name="merge",
-    )(*arrays)
-
-
 def spread_out(x, n):
     rows, parts = x.shape[0], n - 1
     size = part_size(rows, parts)
@@ -297,7 +286,7 @@
     for k in reversed(range(parts)):
         start = min(k * size, rows - size)
         got.append(lax.ppermute(x[start : start + size], "cols", [(0, k + 1)]))
-    return merge(got)
+    return sum(got[1:], got[0])
 
 
 def spread_round(mine, n):
@@ -366,14 +355,14 @@
     share = jnp.where(z == 0, share, sum(far, jnp.zeros_like(share)))
     grams, places = gather_rows(share, n_rows)
 
-    send, keep, panel_a = dot(after(got_a, far), 0)
+    send, keep, panel_a = dot(after(got_a, far, mine_b), 0)
     state = chol_part(info, 0, 1, pieces=after(grams, send, mine_b), places=places)
     joined = join_cores(send, keep, n_rows)
     own_a = scatter_chips(joined, n_rows)
     got_b = spread_round(mine_b, n_cols)
-    state = chol_part(info, 1, 2, state=after(state, joined))
+    state = chol_part(info, 1, 2, state=after(state, own_a))
     pieces_a, where = gather_rows(own_a, n_rows)
-    send, keep, panel_b = dot(after(got_b, own_a, state), half)
+    send, keep, panel_b = dot(after(got_b, pieces_a, state), half)
     joined = join_cores(send, keep, n_rows)
     own_b = scatter_chips(joined, n_rows)
     state = chol_part(info, 2, 3, state=after(state, joined))

time: 198 us -> 207 us (1.045)
  Pallas kernels: 75.5 us -> 64.7 us
  waiting for transfers between devices: 42.6 us -> 50.2 us
  other arithmetic: 1.81 us -> 8.46 us
  starting transfers between devices: 61.7 us -> 65.7 us
  local copies, waits for them, and re-layouts: 7.62 us -> 9.86 us
    ppermute x4, waiting for transfers between devices: 6.85 us -> 22.4 us  [spread_round(): got.append(lax.ppermute(mine, 'cols', pairs))]
    ppermute x6, waiting for transfers between devices: 12.3 us -> 1.49 us  [spread_out(): got.append(lax.ppermute(x[start:start + size], 'cols', [(0, k + 1)]))]
    ppermute x4, starting transfers between devices: 18.5 us -> 26.3 us  [spread_round(): got.append(lax.ppermute(mine, 'cols', pairs))]
    pallas_call x4, Pallas kernels: 33.6 us -> 26.8 us  [chol_part(): pl.pallas_call(kernel, out_shape=(shape, shape, shape), in_specs=[pl.Bloc...]
    ppermute x9, waiting for transfers between devices: 9.99 us -> 16.6 us  [scatter_chips(): lax.ppermute(take(mine, (chip ^ k) * piece, piece), 'rows', swap(n, 2 * k))]
    ppermute x3, waiting for transfers between devices: 4.39 us -> 0.01 us  [shards(): lax.ppermute(share, 'cols', [(0, k)])]
    pallas_call x2 -> x0, Pallas kernels: 3.97 us -> none  [merge(): pl.pallas_call(kernel, out_shape=jax.ShapeDtypeStruct(arrays[0].shape, F3...]
    ppermute x9, waiting for transfers between devices: 8.93 us -> 6.28 us  [gather_rows(): lax.ppermute(own, 'rows', swap(n, 2 * k))]
  transfers between devices with their start and end apart: 46 -> 46, of which waited for: 10 -> 11; matrix products, arithmetic and copies ran while one was open for 2% -> 7% of each run, Pallas kernels for 24% -> 13%
where the time goes in v4:
time: 207 us; the launch traced here: 206 us
  starting transfers between devices  65.7 us (32%)
  Pallas kernels  64.7 us (31%)
  waiting for transfers between devices  50.2 us (24%)
  local copies, waits for them, and re-layouts  9.86 us (5%)
  other arithmetic  8.46 us (4%)
  matrix products  5.71 us (3%)
    pallas_call x4, Pallas kernels, chol_part(): pl.pallas_call(kernel, out_shape=(shape, shape, shape), in_specs=[pl.Bloc...  26.8 us
    ppermute x4, starting transfers between devices, spread_round(): got.append(lax.ppermute(mine, 'cols', pairs))  26.3 us
    ppermute x4, waiting for transfers between devices, spread_round(): got.append(lax.ppermute(mine, 'cols', pairs))  22.4 us
    pallas_call x1, Pallas kernels, finish(): pl.pallas_call(kernel, out_shape=(jax.ShapeDtypeStruct((rows, cols), F32)...  19.2 us
    pallas_call x2, Pallas kernels, panel_dot(): pl.pallas_call(kernel, out_shape=(out, out, jax.ShapeDtypeStruct((rows, w...  18.7 us
    ppermute x9, waiting for transfers between devices, scatter_chips(): lax.ppermute(take(mine, (chip ^ k) * piece, piece), 'rows', swap(n, 2 * k))  16.6 us
    ppermute x12, starting transfers between devices, gather_rows(): other = [lax.ppermute(g, 'rows', swap(n, 1)) for g in got]  9.91 us
    ppermute x9, starting transfers between devices, scatter_chips(): lax.ppermute(take(mine, (chip ^ k) * piece, piece), 'rows', swap(n, 2 * k))  8.53 us
  transfers between devices with their start and end apart: 46, of which 11 were waited for; matrix products, arithmetic and copies ran while one was open for 7% of the time, Pallas kernels for 13%

profile of v4, /device:TPU:17, one launch (start us, length us, event | category | flops | bytes accessed | tf_op | source)
XLA Modules:
  0.0 206.3 jit_solution(4236289111441999227)
XLA Ops:
  0.6 2.2 %fusion.5 = (f32[344,256]{1,0:T(8,128)}, f32[344,256]{1,0:T(8,128)}, f32[344,256]{1,0:T(8,128)S(1)}) fusion(f32[1024,2048]{1,0:T(8,128)} %s_ref.5), kind=kLoop, calls=%fused_computation.20 | loop fusion | bytes 2113536 | tf_op jit(solution)/shard_map/slice | solution.py:288
  2.9 1.3 collective-permute-start.15
  4.2 1.4 collective-permute-start.16
  5.6 1.4 collective-permute-start.14
  7.0 5.7 %fusion.2 = f32[512,512]{1,0:T(8,128)S(1)} fusion(f32[1024,2048]{1,0:T(8,128)} %s_ref.5), kind=kOutput, calls=%fused_computation.2 | convolution fusion | flops 3221487616 | bytes 3145728 | tf_op jit(solution)/shard_map/dot_general | solution.py:17
  12.8 0.7 collective-permute-start
  13.5 1.5 collective-permute-done.15
  15.0 1.2 add_add_fusion.1.rest_0_
  16.2 1.3 dynamic-slice_add_fusion
  17.5 1.3 collective-permute-start.1
  18.7 1.2 collective-permute-start.3
  20.2 0.9 fusion.6
  21.1 1.3 collective-permute-start.20
  22.4 0.7 collective-permute-start.21
  23.1 0.7 collective-permute-start.19
  24.5 9.8 %collective-permute-start.18 = (f32[344,256]{1,0:T(8,128)S(1)}, f32[344,256]{1,0:T(8,128)S(1)}, u32[]{:S(2)}, u32[]{:S(2)}) collective-permute-start(f32[344,256]{1,0:T(8,128)S(1)} %add_add_fusion.1.rest_0_), channel_id=1, source_target_pairs={{1,3},{2,1},{3,2},{5,7},{6,5},{7,6},{9,11},{10,9},{11,10},{13,15},... | collective-permute-start | bytes 1056776 | tf_op jit(solution)/shard_map/ppermute | solution.py:296
  34.3 11.0 %collective-permute-start.17 = (f32[344,256]{1,0:T(8,128)S(1)}, f32[344,256]{1,0:T(8,128)S(1)}, u32[]{:S(2)}, u32[]{:S(2)}) collective-permute-start(f32[344,256]{1,0:T(8,128)S(1)} %add_add_fusion.1.rest_0_), channel_id=1, source_target_pairs={{1,2},{2,3},{3,1},{5,6},{6,7},{7,5},{9,10},{10,11},{11,9},{13,14},... | collective-permute-start | bytes 1056776 | tf_op jit(solution)/shard_map/ppermute | solution.py:296
  45.3 1.1 add_add_fusion.4
  46.4 0.7 collective-permute-start.6
  47.1 1.3 collective-permute-start.5
  48.4 0.7 copy-done.10
  49.1 0.7 collective-permute-start.4
  49.8 1.1 add_add_fusion.rest_0_
  50.9 22.4 %collective-permute-done.17.rest_1_ = f32[344,256]{1,0:T(8,128)S(1)} collective-permute-done((f32[344,256]{1,0:T(8,128)S(1)}, f32[344,256]{1,0:T(8,128)S(1)}, u32[]{:S(2)}, u32[]{:S(2)}) %collective-permute-start.17) | collective-permute-done | bytes 352288 | tf_op jit(solution)/shard_map/ppermute | solution.py:296
  73.3 0.7 copy-done.9
  74.0 9.2 %panel_dot.2 = (f32[128,2048]{1,0:T(8,128)}, f32[128,2048]{1,0:T(8,128)}, f32[1024,256]{1,0:T(8,128)}) custom-call(s32[6]{0:T(128)} %stack.27.info_ref, f32[1024,2048]{1,0:T(8,128)} %s_ref.5, f32[1024,2048]{1,0:T(8,128)} %s_ref.5, f32[344,256]{1,0:T(8,128)} %copy-done.5, f32[344,256]{1,0:T(8,128)} %copy-done.9, f32[344,256]{1,0:T(8,128)} %copy-done.8), custom_call_target="tpu_custom_call" | custom-call | flops 3221225472 | bytes 8388608 | tf_op jit(solution)/shard_map/panel_dot/pallas_call | solution.py:250
  83.2 2.2 %collective-permute-start.22 = (f32[128,2048]{1,0:T(8,128)}, f32[128,2048]{1,0:T(8,128)S(1)}, u32[]{:S(2)}, u32[]{:S(2)}) collective-permute-start(f32[128,2048]{1,0:T(8,128)} %get-tuple-element.47), channel_id=1, source_target_pairs={{0,4},{4,0},{8,12},{12,8},{16,20},{20,16},{24,28},{28,24},{1,5},{5... | collective-permute-start | bytes 3145736 | tf_op jit(solution)/shard_map/ppermute | solution.py:313
  85.4 2.2 %collective-permute-start.9 = (f32[64,512]{1,0:T(8,128)S(1)}, f32[64,512]{1,0:T(8,128)S(1)}, u32[]{:S(2)}, u32[]{:S(2)}) collective-permute-start(f32[64,512]{1,0:T(8,128)S(1)} %add_select_fusion.refs_0_), channel_id=1, source_target_pairs={{0,24},{4,28},{8,16},{12,20},{16,8},{20,12},{24,0},{28,4},{1,25},{... | collective-permute-start | bytes 393224 | tf_op jit(solution)/shard_map/ppermute | solution.py:327
  88.6 3.0 %collective-permute-done.9.refs_3_ = f32[64,512]{1,0:T(8,128)S(1)} collective-permute-done((f32[64,512]{1,0:T(8,128)S(1)}, f32[64,512]{1,0:T(8,128)S(1)}, u32[]{:S(2)}, u32[]{:S(2)}) %collective-permute-start.9) | collective-permute-done | bytes 131104 | tf_op jit(solution)/shard_map/ppermute | solution.py:327
  91.5 0.9 collective-permute-start.13
  92.4 1.4 add.124
  93.8 0.9 constant_dynamic-slice_fusion.5
  94.6 1.5 collective-permute-start.23
  96.1 1.6 collective-permute-start.25
  98.5 0.9 collective-permute-done.12.refs_6_
  99.4 1.9 collective-permute-start.27
  101.3 3.5 %collective-permute-start.26 = (f32[344,256]{1,0:T(8,128)S(1)}, f32[344,256]{1,0:T(8,128)S(1)}, u32[]{:S(2)}, u32[]{:S(2)}) collective-permute-start(f32[344,256]{1,0:T(8,128)S(1)} %add_add_fusion.rest_0_), channel_id=1, source_target_pairs={{1,2},{2,3},{3,1},{5,6},{6,7},{7,5},{9,10},{10,11},{11,9},{13,14},... | collective-permute-start | bytes 1056776 | tf_op jit(solution)/shard_map/ppermute | solution.py:296
  104.9 5.3 %collective-permute-done.25 = f32[32,2048]{1,0:T(8,128)} collective-permute-done((f32[32,2048]{1,0:T(8,128)}, f32[32,2048]{1,0:T(8,128)}, u32[]{:S(2)}, u32[]{:S(2)}) %collective-permute-start.25) | collective-permute-done | bytes 262176 | tf_op jit(solution)/shard_map/ppermute | solution.py:322
  110.8 1.1 add_add_fusion.3.rest_2_
  111.9 0.8 collective-permute-start.30
  112.7 1.3 collective-permute-start.29
  114.6 7.2 %chol_part.4 = (f32[512,512]{1,0:T(8,128)S(1)}, f32[512,512]{1,0:T(8,128)S(1)}, f32[512,512]{1,0:T(8,128)S(1)}) custom-call(s32[6]{0:T(128)S(1)} %copy-done, f32[64,512]{1,0:T(8,128)S(1)} %add_select_fusion.refs_0_, f32[64,512]{1,0:T(8,128)S(1)} %collective-permute-done.7.refs_1_, f32[64,512]{1,0:T(8,128)S(1)} %collective-permute-done.8.refs_2_, ...), custom_call_target="tpu_custom_call" | custom-call | flops 8000000000 | bytes 3145728 | tf_op jit(solution)/shard_map/chol_part/pallas_call | solution.py:118
  121.9 2.3 %collective-permute-start.31 = (f32[32,2048]{1,0:T(8,128)S(1)}, f32[32,2048]{1,0:T(8,128)S(1)}, u32[]{:S(2)}, u32[]{:S(2)}) collective-permute-start(f32[32,2048]{1,0:T(8,128)S(1)} %add_add_fusion.3.rest_2_), channel_id=1, source_target_pairs={{0,4},{4,0},{8,12},{12,8},{16,20},{20,16},{24,28},{28,24},{1,5},{5... | collective-permute-start | bytes 786440 | tf_op jit(solution)/shard_map/ppermute | solution.py:328
  124.3 2.1 %collective-permute-done.29.rest_4_ = f32[32,2048]{1,0:T(8,128)S(1)} collective-permute-done((f32[32,2048]{1,0:T(8,128)S(1)}, f32[32,2048]{1,0:T(8,128)S(1)}, u32[]{:S(2)}, u32[]{:S(2)}) %collective-permute-start.29) | collective-permute-done | bytes 262176 | tf_op jit(solution)/shard_map/ppermute | solution.py:327
  127.1 6.8 %chol_part.5 = (f32[512,512]{1,0:T(8,128)S(1)}, f32[512,512]{1,0:T(8,128)S(1)}, f32[512,512]{1,0:T(8,128)S(1)}) custom-call(s32[6]{0:T(128)S(1)} %copy-done, f32[512,512]{1,0:T(8,128)S(1)} %get-tuple-element.60.refs_0_, f32[512,512]{1,0:T(8,128)S(1)} %get-tuple-element.61.refs_1_, ...), custom_call_target="tpu_custom_call", output_to_operand_aliasing={{0}: (1, {}), {1}: (2, {}), {2}: (3, {})} | custom-call | flops 8000000000 | bytes 3145728 | tf_op jit(solution)/shard_map/chol_part/pallas_call | solution.py:118
  134.8 9.5 %panel_dot.3 = (f32[128,2048]{1,0:T(8,128)}, f32[128,2048]{1,0:T(8,128)}, f32[1024,256]{1,0:T(8,128)}) custom-call(s32[6]{0:T(128)} %stack.27.info_ref, f32[1024,2048]{1,0:T(8,128)} %s_ref.5, f32[1024,2048]{1,0:T(8,128)} %s_ref.5, f32[344,256]{1,0:T(8,128)} %copy-done.4, f32[344,256]{1,0:T(8,128)} %copy-done.7, f32[344,256]{1,0:T(8,128)} %copy-done.6), custom_call_target="tpu_custom_call" | custom-call | flops 3221225472 | bytes 8388608 | tf_op jit(solution)/shard_map/panel_dot/pallas_call | solution.py:250
  144.8 2.5 %collective-permute-done.35 = f32[128,2048]{1,0:T(8,128)S(1)} collective-permute-done((f32[128,2048]{1,0:T(8,128)}, f32[128,2048]{1,0:T(8,128)S(1)}, u32[]{:S(2)}, u32[]{:S(2)}) %collective-permute-start.35) | collective-permute-done | bytes 1048608 | tf_op jit(solution)/shard_map/ppermute | solution.py:313
  147.3 1.3 add.132
  148.7 0.8 collective-permute-start.36
  149.5 0.9 collective-permute-start.38
  150.4 1.0 collective-permute-start.37
  151.4 4.9 %collective-permute-done.36 = f32[32,2048]{1,0:T(8,128)S(1)} collective-permute-done((f32[32,2048]{1,0:T(8,128)S(1)}, f32[32,2048]{1,0:T(8,128)S(1)}, u32[]{:S(2)}, u32[]{:S(2)}) %collective-permute-start.36) | collective-permute-done | bytes 262176 | tf_op jit(solution)/shard_map/ppermute | solution.py:322
  156.3 5.8 %collective-permute-done.38 = f32[32,2048]{1,0:T(8,128)S(1)} collective-permute-done((f32[32,2048]{1,0:T(8,128)S(1)}, f32[32,2048]{1,0:T(8,128)S(1)}, u32[]{:S(2)}, u32[]{:S(2)}) %collective-permute-start.38) | collective-permute-done | bytes 262176 | tf_op jit(solution)/shard_map/ppermute | solution.py:322
  162.2 1.5 collective-permute-start.41
  164.2 0.7 collective-permute-start.39
  164.9 6.6 %chol_part.6 = (f32[512,512]{1,0:T(8,128)S(1)}, f32[512,512]{1,0:T(8,128)S(1)}, f32[512,512]{1,0:T(8,128)S(1)}) custom-call(s32[6]{0:T(128)S(1)} %copy-done.1, f32[512,512]{1,0:T(8,128)S(1)} %get-tuple-element.71.refs_0_, f32[512,512]{1,0:T(8,128)S(1)} %get-tuple-element.72.refs_1_, ...), custom_call_target="tpu_custom_call", output_to_operand_aliasing={{0}: (1, {}), {1}: (2, {}), {2}: (3, {})} | custom-call | flops 8000000000 | bytes 3145728 | tf_op jit(solution)/shard_map/chol_part/pallas_call | solution.py:118
  171.5 3.5 %collective-permute-start.42 = (f32[32,2048]{1,0:T(8,128)S(1)}, f32[32,2048]{1,0:T(8,128)S(1)}, u32[]{:S(2)}, u32[]{:S(2)}) collective-permute-start(f32[32,2048]{1,0:T(8,128)S(1)} %add_add_fusion.2.rest_10_), channel_id=1, source_target_pairs={{0,4},{4,0},{8,12},{12,8},{16,20},{20,16},{24,28},{28,24},{1,5},{5... | collective-permute-start | bytes 786440 | tf_op jit(solution)/shard_map/ppermute | solution.py:328
  175.2 1.2 collective-permute-done.40.rest_12_
  176.3 1.2 collective-permute-start.44
  177.6 6.2 %chol_part.7 = (f32[512,512]{1,0:T(8,128)S(1)}, f32[512,512]{1,0:T(8,128)S(1)}, f32[512,512]{1,0:T(8,128)S(1)}) custom-call(s32[6]{0:T(128)S(1)} %copy-done.1, f32[512,512]{1,0:T(8,128)S(1)} %get-tuple-element.77.refs_0_, f32[512,512]{1,0:T(8,128)S(1)} %get-tuple-element.78.refs_1_, ...), custom_call_target="tpu_custom_call", output_to_operand_aliasing={{0}: (1, {}), {1}: (2, {}), {2}: (3, {})} | custom-call | flops 8000000000 | bytes 3145728 | tf_op jit(solution)/shard_map/chol_part/pallas_call | solution.py:118
  183.8 1.0 copy-done.2
  184.8 1.0 copy-done.3
  185.8 0.6 copy-done.25
  186.8 19.2 %finish.1 = (f32[1024,2048]{1,0:T(8,128)}, f32[512,2048]{1,0:T(8,128)}) custom-call(s32[6]{0:T(128)} %stack.27.info_ref, f32[1024,2048]{1,0:T(8,128)} %s_ref.5, f32[512,512]{1,0:T(8,128)} %copy-done.3, f32[512,512]{1,0:T(8,128)} %copy-done.2, f32[1024,256]{1,0:T(8,128)} %get-tuple-element.82.rest_0_, f32[1024,256]{1,0:T(8,128)} %get-tuple-element.83.rest_1_, ...), custom_call_target="tpu_custom_call" | custom-call | flops 9663676416 | bytes 16777216 | tf_op jit(solution)/shard_map/finish/pallas_call | solution.py:181
  (112 shorter events, 7.0 us)
Async XLA Ops:
  0.6 19.5 %slice-start = ((f32[1024,2048]{1,0:T(8,128)}), f32[1024,256]{1,0:T(8,128)S(1)}, s32[]{:S(2)}) async-start(f32[1024,2048]{1,0:T(8,128)} %s_ref.5), calls=%async_computation | async-start | bytes 2097152 | tf_op jit(solution)/shard_map/slice | solution.py:354
  2.9 12.1 %collective-permute-start.15 = (f32[344,256]{1,0:T(8,128)}, f32[344,256]{1,0:T(8,128)S(1)}, u32[]{:S(2)}, u32[]{:S(2)}) collective-permute-start(f32[344,256]{1,0:T(8,128)} %get-tuple-element.84), channel_id=1, source_target_pairs={{0,2},{4,6},{8,10},{12,14},{16,18},{20,22},{24,26},{28,30}} | collective-permute-start | bytes 1056776 | tf_op jit(solution)/shard_map/ppermute | solution.py:288
  4.2 10.8 %collective-permute-start.16 = (f32[344,256]{1,0:T(8,128)}, f32[344,256]{1,0:T(8,128)}, u32[]{:S(2)}, u32[]{:S(2)}) collective-permute-start(f32[344,256]{1,0:T(8,128)} %get-tuple-element.85), channel_id=1, source_target_pairs={{0,1},{4,5},{8,9},{12,13},{16,17},{20,21},{24,25},{28,29}} | collective-permute-start | bytes 1056776 | tf_op jit(solution)/shard_map/ppermute | solution.py:288
  5.6 9.4 %collective-permute-start.14 = (f32[344,256]{1,0:T(8,128)S(1)}, f32[344,256]{1,0:T(8,128)}, u32[]{:S(2)}, u32[]{:S(2)}) collective-permute-start(f32[344,256]{1,0:T(8,128)S(1)} %get-tuple-element.86), channel_id=1, source_target_pairs={{0,3},{4,7},{8,11},{12,15},{16,19},{20,23},{24,27},{28,31}} | collective-permute-start | bytes 1056776 | tf_op jit(solution)/shard_map/ppermute | solution.py:288
  12.8 3.4 %collective-permute-start = (f32[256,512]{1,0:T(8,128)S(1)}, f32[256,512]{1,0:T(8,128)}, u32[]{:S(2)}, u32[]{:S(2)}) collective-permute-start(f32[256,512]{1,0:T(8,128)S(1)} %constant_dynamic-slice_fusion.9), channel_id=1, source_target_pairs={{0,4},{4,0},{8,12},{12,8},{16,20},{20,16},{24,28},{28,24},{1,5},{5... | collective-permute-start | bytes 1572872 | tf_op jit(solution)/shard_map/ppermute | solution.py:313
  16.1 57.2 %copy-start.5 = (f32[344,256]{1,0:T(8,128)}, f32[344,256]{1,0:T(8,128)S(1)}, u32[]{:S(2)}) copy-start(f32[344,256]{1,0:T(8,128)S(1)} %add_add_fusion.1.rest_0_) | copy-start | bytes 1056772
  17.5 5.6 %collective-permute-start.1 = (f32[64,512]{1,0:T(8,128)S(1)}, f32[64,512]{1,0:T(8,128)S(1)}, u32[]{:S(2)}, u32[]{:S(2)}) collective-permute-start(f32[64,512]{1,0:T(8,128)S(1)} %get-tuple-element.96), channel_id=1, source_target_pairs={{0,8},{4,12},{8,0},{12,4},{16,24},{20,28},{24,16},{28,20},{1,9},{5... | collective-permute-start | bytes 393224 | tf_op jit(solution)/shard_map/ppermute | solution.py:322
  18.7 5.7 %collective-permute-start.3 = (f32[64,512]{1,0:T(8,128)S(1)}, f32[64,512]{1,0:T(8,128)S(1)}, u32[]{:S(2)}, u32[]{:S(2)}) collective-permute-start(f32[64,512]{1,0:T(8,128)S(1)} %get-tuple-element.97), channel_id=1, source_target_pairs={{0,24},{4,28},{8,16},{12,20},{16,8},{20,12},{24,0},{28,4},{1,25},{... | collective-permute-start | bytes 393224 | tf_op jit(solution)/shard_map/ppermute | solution.py:322
  19.9 14.4 %collective-permute-start.2 = (f32[64,512]{1,0:T(8,128)S(1)}, f32[64,512]{1,0:T(8,128)}, u32[]{:S(2)}, u32[]{:S(2)}) collective-permute-start(f32[64,512]{1,0:T(8,128)S(1)} %get-tuple-element.98), channel_id=1, source_target_pairs={{0,16},{4,20},{8,24},{12,28},{16,0},{20,4},{24,8},{28,12},{1,17},{... | collective-permute-start | bytes 393224 | tf_op jit(solution)/shard_map/ppermute | solution.py:322
  21.1 25.3 %collective-permute-start.20 = (f32[344,256]{1,0:T(8,128)}, f32[344,256]{1,0:T(8,128)S(1)}, u32[]{:S(2)}, u32[]{:S(2)}) collective-permute-start(f32[344,256]{1,0:T(8,128)} %get-tuple-element.93), channel_id=1, source_target_pairs={{0,2},{4,6},{8,10},{12,14},{16,18},{20,22},{24,26},{28,30}} | collective-permute-start | bytes 1056776 | tf_op jit(solution)/shard_map/ppermute | solution.py:288
  22.4 24.7 %collective-permute-start.21 = (f32[344,256]{1,0:T(8,128)}, f32[344,256]{1,0:T(8,128)S(1)}, u32[]{:S(2)}, u32[]{:S(2)}) collective-permute-start(f32[344,256]{1,0:T(8,128)} %get-tuple-element.94), channel_id=1, source_target_pairs={{0,1},{4,5},{8,9},{12,13},{16,17},{20,21},{24,25},{28,29}} | collective-permute-start | bytes 1056776 | tf_op jit(solution)/shard_map/ppermute | solution.py:288
  23.1 11.2 %copy-start.13 = (f32[64,512]{1,0:T(8,128)}, f32[64,512]{1,0:T(8,128)S(1)}, u32[]{:S(2)}) copy-start(f32[64,512]{1,0:T(8,128)S(1)} %collective-permute-done.1) | copy-start | bytes 393220
  23.1 25.3 %collective-permute-start.19 = (f32[344,256]{1,0:T(8,128)S(1)}, f32[344,256]{1,0:T(8,128)S(1)}, u32[]{:S(2)}, u32[]{:S(2)}) collective-permute-start(f32[344,256]{1,0:T(8,128)S(1)} %get-tuple-element.95), channel_id=1, source_target_pairs={{0,3},{4,7},{8,11},{12,15},{16,19},{20,23},{24,27},{28,31}} | collective-permute-start | bytes 1056776 | tf_op jit(solution)/shard_map/ppermute | solution.py:288
  24.5 9.8 %copy-start.14 = (f32[64,512]{1,0:T(8,128)}, f32[64,512]{1,0:T(8,128)S(1)}, u32[]{:S(2)}) copy-start(f32[64,512]{1,0:T(8,128)S(1)} %collective-permute-done.3) | copy-start | bytes 393220
  24.5 26.4 %collective-permute-start.18 = (f32[344,256]{1,0:T(8,128)S(1)}, f32[344,256]{1,0:T(8,128)S(1)}, u32[]{:S(2)}, u32[]{:S(2)}) collective-permute-start(f32[344,256]{1,0:T(8,128)S(1)} %add_add_fusion.1.rest_0_), channel_id=1, source_target_pairs={{1,3},{2,1},{3,2},{5,7},{6,5},{7,6},{9,11},{10,9},{11,10},{13,15},... | collective-permute-start | bytes 1056776 | tf_op jit(solution)/shard_map/ppermute | solution.py:296
  34.3 38.9 %collective-permute-start.17 = (f32[344,256]{1,0:T(8,128)S(1)}, f32[344,256]{1,0:T(8,128)S(1)}, u32[]{:S(2)}, u32[]{:S(2)}) collective-permute-start(f32[344,256]{1,0:T(8,128)S(1)} %add_add_fusion.1.rest_0_), channel_id=1, source_target_pairs={{1,2},{2,3},{3,1},{5,6},{6,7},{7,5},{9,10},{10,11},{11,9},{13,14},... | collective-permute-start | bytes 1056776 | tf_op jit(solution)/shard_map/ppermute | solution.py:296
  46.4 26.9 %collective-permute-start.6 = (f32[64,512]{1,0:T(8,128)S(1)}, f32[64,512]{1,0:T(8,128)S(1)}, u32[]{:S(2)}, u32[]{:S(2)}) collective-permute-start(f32[64,512]{1,0:T(8,128)S(1)} %add_add_fusion.4), channel_id=1, source_target_pairs={{0,1},{4,5},{8,9},{12,13},{16,17},{20,21},{24,25},{28,29}} | collective-permute-start | bytes 393224 | tf_op jit(solution)/shard_map/ppermute | solution.py:352
  47.1 26.2 %collective-permute-start.5 = (f32[64,512]{1,0:T(8,128)S(1)}, f32[64,512]{1,0:T(8,128)S(1)}, u32[]{:S(2)}, u32[]{:S(2)}) collective-permute-start(f32[64,512]{1,0:T(8,128)S(1)} %add_add_fusion.4), channel_id=1, source_target_pairs={{0,2},{4,6},{8,10},{12,14},{16,18},{20,22},{24,26},{28,30}} | collective-permute-start | bytes 393224 | tf_op jit(solution)/shard_map/ppermute | solution.py:352
  49.1 24.2 %collective-permute-start.4 = (f32[64,512]{1,0:T(8,128)S(1)}, f32[64,512]{1,0:T(8,128)S(1)}, u32[]{:S(2)}, u32[]{:S(2)}) collective-permute-start(f32[64,512]{1,0:T(8,128)S(1)} %add_add_fusion.4), channel_id=1, source_target_pairs={{0,3},{4,7},{8,11},{12,15},{16,19},{20,23},{24,27},{28,31}} | collective-permute-start | bytes 393224 | tf_op jit(solution)/shard_map/ppermute | solution.py:352
  50.9 50.5 %copy-start.4 = (f32[344,256]{1,0:T(8,128)}, f32[344,256]{1,0:T(8,128)S(1)}, u32[]{:S(2)}) copy-start(f32[344,256]{1,0:T(8,128)S(1)} %add_add_fusion.rest_0_) | copy-start | bytes 1056772
  50.9 63.7 %copy-start = (s32[6]{0:T(128)S(1)}, s32[6]{0:T(128)}, u32[]{:S(2)}) copy-start(s32[6]{0:T(128)} %stack.27.info_ref) | copy-start | bytes 76
  50.9 22.4 %copy-start.8 = (f32[344,256]{1,0:T(8,128)}, f32[344,256]{1,0:T(8,128)S(1)}, u32[]{:S(2)}) copy-start(f32[344,256]{1,0:T(8,128)S(1)} %collective-permute-done.18.rest_2_) | copy-start | bytes 1056772
  83.2 9.2 %collective-permute-start.22 = (f32[128,2048]{1,0:T(8,128)}, f32[128,2048]{1,0:T(8,128)S(1)}, u32[]{:S(2)}, u32[]{:S(2)}) collective-permute-start(f32[128,2048]{1,0:T(8,128)} %get-tuple-element.47), channel_id=1, source_target_pairs={{0,4},{4,0},{8,12},{12,8},{16,20},{20,16},{24,28},{28,24},{1,5},{5... | collective-permute-start | bytes 3145736 | tf_op jit(solution)/shard_map/ppermute | solution.py:313
  85.4 6.1 %collective-permute-start.9 = (f32[64,512]{1,0:T(8,128)S(1)}, f32[64,512]{1,0:T(8,128)S(1)}, u32[]{:S(2)}, u32[]{:S(2)}) collective-permute-start(f32[64,512]{1,0:T(8,128)S(1)} %add_select_fusion.refs_0_), channel_id=1, source_target_pairs={{0,24},{4,28},{8,16},{12,20},{16,8},{20,12},{24,0},{28,4},{1,25},{... | collective-permute-start | bytes 393224 | tf_op jit(solution)/shard_map/ppermute | solution.py:327
  87.7 8.5 %collective-permute-start.10 = (f32[64,512]{1,0:T(8,128)S(1)}, f32[64,512]{1,0:T(8,128)S(1)}, u32[]{:S(2)}, u32[]{:S(2)}) collective-permute-start(f32[64,512]{1,0:T(8,128)S(1)} %add_select_fusion.refs_0_), channel_id=1, source_target_pairs={{0,4},{4,0},{8,12},{12,8},{16,20},{20,16},{24,28},{28,24},{1,5},{5... | collective-permute-start | bytes 393224 | tf_op jit(solution)/shard_map/ppermute | solution.py:328
  88.0 9.8 %collective-permute-start.8 = (f32[64,512]{1,0:T(8,128)S(1)}, f32[64,512]{1,0:T(8,128)S(1)}, u32[]{:S(2)}, u32[]{:S(2)}) collective-permute-start(f32[64,512]{1,0:T(8,128)S(1)} %add_select_fusion.refs_0_), channel_id=1, source_target_pairs={{0,16},{4,20},{8,24},{12,28},{16,0},{20,4},{24,8},{28,12},{1,17},{... | collective-permute-start | bytes 393224 | tf_op jit(solution)/shard_map/ppermute | solution.py:327
  88.2 9.6 %collective-permute-start.7 = (f32[64,512]{1,0:T(8,128)S(1)}, f32[64,512]{1,0:T(8,128)S(1)}, u32[]{:S(2)}, u32[]{:S(2)}) collective-permute-start(f32[64,512]{1,0:T(8,128)S(1)} %add_select_fusion.refs_0_), channel_id=1, source_target_pairs={{0,8},{4,12},{8,0},{12,4},{16,24},{20,28},{24,16},{28,20},{1,9},{5... | collective-permute-start | bytes 393224 | tf_op jit(solution)/shard_map/ppermute | solution.py:327
  91.5 6.9 %collective-permute-start.13 = (f32[64,512]{1,0:T(8,128)S(1)}, f32[64,512]{1,0:T(8,128)S(1)}, u32[]{:S(2)}, u32[]{:S(2)}) collective-permute-start(f32[64,512]{1,0:T(8,128)S(1)} %collective-permute-done.9.refs_3_), channel_id=1, source_target_pairs={{0,4},{4,0},{8,12},{12,8},{16,20},{20,16},{24,28},{28,24},{1,5},{5... | collective-permute-start | bytes 393224 | tf_op jit(solution)/shard_map/ppermute | solution.py:328
  94.6 10.2 %collective-permute-start.23 = (f32[32,2048]{1,0:T(8,128)}, f32[32,2048]{1,0:T(8,128)S(1)}, u32[]{:S(2)}, u32[]{:S(2)}) collective-permute-start(f32[32,2048]{1,0:T(8,128)} %get-tuple-element.90), channel_id=1, source_target_pairs={{0,8},{4,12},{8,0},{12,4},{16,24},{20,28},{24,16},{28,20},{1,9},{5... | collective-permute-start | bytes 786440 | tf_op jit(solution)/shard_map/ppermute | solution.py:322
  96.1 14.1 %collective-permute-start.25 = (f32[32,2048]{1,0:T(8,128)}, f32[32,2048]{1,0:T(8,128)}, u32[]{:S(2)}, u32[]{:S(2)}) collective-permute-start(f32[32,2048]{1,0:T(8,128)} %get-tuple-element.91), channel_id=1, source_target_pairs={{0,24},{4,28},{8,16},{12,20},{16,8},{20,12},{24,0},{28,4},{1,25},{... | collective-permute-start | bytes 786440 | tf_op jit(solution)/shard_map/ppermute | solution.py:322
  97.7 13.0 %collective-permute-start.24 = (f32[32,2048]{1,0:T(8,128)S(1)}, f32[32,2048]{1,0:T(8,128)}, u32[]{:S(2)}, u32[]{:S(2)}) collective-permute-start(f32[32,2048]{1,0:T(8,128)S(1)} %get-tuple-element.92), channel_id=1, source_target_pairs={{0,16},{4,20},{8,24},{12,28},{16,0},{20,4},{24,8},{28,12},{1,17},{... | collective-permute-start | bytes 786440 | tf_op jit(solution)/shard_map/ppermute | solution.py:322
  97.8 1.6 collective-permute-start.12
  98.4 2.9 %collective-permute-start.11 = (f32[64,512]{1,0:T(8,128)S(1)}, f32[64,512]{1,0:T(8,128)S(1)}, u32[]{:S(2)}, u32[]{:S(2)}) collective-permute-start(f32[64,512]{1,0:T(8,128)S(1)} %collective-permute-done.7.refs_1_), channel_id=1, source_target_pairs={{0,4},{4,0},{8,12},{12,8},{16,20},{20,16},{24,28},{28,24},{1,5},{5... | collective-permute-start | bytes 393224 | tf_op jit(solution)/shard_map/ppermute | solution.py:328
  99.4 22.5 %collective-permute-start.27 = (f32[344,256]{1,0:T(8,128)S(1)}, f32[344,256]{1,0:T(8,128)S(1)}, u32[]{:S(2)}, u32[]{:S(2)}) collective-permute-start(f32[344,256]{1,0:T(8,128)S(1)} %add_add_fusion.rest_0_), channel_id=1, source_target_pairs={{1,3},{2,1},{3,2},{5,7},{6,5},{7,6},{9,11},{10,9},{11,10},{13,15},... | collective-permute-start | bytes 1056776 | tf_op jit(solution)/shard_map/ppermute | solution.py:296
  101.3 32.7 %collective-permute-start.26 = (f32[344,256]{1,0:T(8,128)S(1)}, f32[344,256]{1,0:T(8,128)S(1)}, u32[]{:S(2)}, u32[]{:S(2)}) collective-permute-start(f32[344,256]{1,0:T(8,128)S(1)} %add_add_fusion.rest_0_), channel_id=1, source_target_pairs={{1,2},{2,3},{3,1},{5,6},{6,7},{7,5},{9,10},{10,11},{11,9},{13,14},... | collective-permute-start | bytes 1056776 | tf_op jit(solution)/shard_map/ppermute | solution.py:296
  111.9 10.0 %copy-start.11 = (f32[32,2048]{1,0:T(8,128)}, f32[32,2048]{1,0:T(8,128)S(1)}, u32[]{:S(2)}) copy-start(f32[32,2048]{1,0:T(8,128)S(1)} %add_add_fusion.3.rest_2_) | copy-start | bytes 786436
  111.9 12.3 %collective-permute-start.30 = (f32[32,2048]{1,0:T(8,128)S(1)}, f32[32,2048]{1,0:T(8,128)S(1)}, u32[]{:S(2)}, u32[]{:S(2)}) collective-permute-start(f32[32,2048]{1,0:T(8,128)S(1)} %add_add_fusion.3.rest_2_), channel_id=1, source_target_pairs={{0,24},{4,28},{8,16},{12,20},{16,8},{20,12},{24,0},{28,4},{1,25},{... | collective-permute-start | bytes 786440 | tf_op jit(solution)/shard_map/ppermute | solution.py:327
  112.7 13.7 %collective-permute-start.29 = (f32[32,2048]{1,0:T(8,128)S(1)}, f32[32,2048]{1,0:T(8,128)S(1)}, u32[]{:S(2)}, u32[]{:S(2)}) collective-permute-start(f32[32,2048]{1,0:T(8,128)S(1)} %add_add_fusion.3.rest_2_), channel_id=1, source_target_pairs={{0,16},{4,20},{8,24},{12,28},{16,0},{20,4},{24,8},{28,12},{1,17},{... | collective-permute-start | bytes 786440 | tf_op jit(solution)/shard_map/ppermute | solution.py:327
  114.0 13.1 %collective-permute-start.28 = (f32[32,2048]{1,0:T(8,128)S(1)}, f32[32,2048]{1,0:T(8,128)S(1)}, u32[]{:S(2)}, u32[]{:S(2)}) collective-permute-start(f32[32,2048]{1,0:T(8,128)S(1)} %add_add_fusion.3.rest_2_), channel_id=1, source_target_pairs={{0,8},{4,12},{8,0},{12,4},{16,24},{20,28},{24,16},{28,20},{1,9},{5... | collective-permute-start | bytes 786440 | tf_op jit(solution)/shard_map/ppermute | solution.py:327
  121.8 12.1 %copy-start.6 = (f32[344,256]{1,0:T(8,128)}, f32[344,256]{1,0:T(8,128)S(1)}, u32[]{:S(2)}) copy-start(f32[344,256]{1,0:T(8,128)S(1)} %collective-permute-done.27.rest_2_) | copy-start | bytes 1056772
  121.9 12.2 %collective-permute-start.31 = (f32[32,2048]{1,0:T(8,128)S(1)}, f32[32,2048]{1,0:T(8,128)S(1)}, u32[]{:S(2)}, u32[]{:S(2)}) collective-permute-start(f32[32,2048]{1,0:T(8,128)S(1)} %add_add_fusion.3.rest_2_), channel_id=1, source_target_pairs={{0,4},{4,0},{8,12},{12,8},{16,20},{20,16},{24,28},{28,24},{1,5},{5... | collective-permute-start | bytes 786440 | tf_op jit(solution)/shard_map/ppermute | solution.py:328
  124.2 9.8 %copy-start.15 = (f32[32,2048]{1,0:T(8,128)}, f32[32,2048]{1,0:T(8,128)S(1)}, u32[]{:S(2)}) copy-start(f32[32,2048]{1,0:T(8,128)S(1)} %collective-permute-done.30.rest_5_) | copy-start | bytes 786436
  124.2 9.9 %collective-permute-start.34 = (f32[32,2048]{1,0:T(8,128)S(1)}, f32[32,2048]{1,0:T(8,128)S(1)}, u32[]{:S(2)}, u32[]{:S(2)}) collective-permute-start(f32[32,2048]{1,0:T(8,128)S(1)} %collective-permute-done.30.rest_5_), channel_id=1, source_target_pairs={{0,4},{4,0},{8,12},{12,8},{16,20},{20,16},{24,28},{28,24},{1,5},{5... | collective-permute-start | bytes 786440 | tf_op jit(solution)/shard_map/ppermute | solution.py:328
  126.4 7.6 %copy-start.16 = (f32[32,2048]{1,0:T(8,128)}, f32[32,2048]{1,0:T(8,128)S(1)}, u32[]{:S(2)}) copy-start(f32[32,2048]{1,0:T(8,128)S(1)} %collective-permute-done.29.rest_4_) | copy-start | bytes 786436
  126.4 7.7 %collective-permute-start.33 = (f32[32,2048]{1,0:T(8,128)S(1)}, f32[32,2048]{1,0:T(8,128)S(1)}, u32[]{:S(2)}, u32[]{:S(2)}) collective-permute-start(f32[32,2048]{1,0:T(8,128)S(1)} %collective-permute-done.29.rest_4_), channel_id=1, source_target_pairs={{0,4},{4,0},{8,12},{12,8},{16,20},{20,16},{24,28},{28,24},{1,5},{5... | collective-permute-start | bytes 786440 | tf_op jit(solution)/shard_map/ppermute | solution.py:328
  127.1 7.0 %collective-permute-start.32 = (f32[32,2048]{1,0:T(8,128)S(1)}, f32[32,2048]{1,0:T(8,128)S(1)}, u32[]{:S(2)}, u32[]{:S(2)}) collective-permute-start(f32[32,2048]{1,0:T(8,128)S(1)} %collective-permute-done.28.rest_3_), channel_id=1, source_target_pairs={{0,4},{4,0},{8,12},{12,8},{16,20},{20,16},{24,28},{28,24},{1,5},{5... | collective-permute-start | bytes 786440 | tf_op jit(solution)/shard_map/ppermute | solution.py:328
  134.0 10.2 %copy-start.18 = (f32[32,2048]{1,0:T(8,128)}, f32[32,2048]{1,0:T(8,128)S(1)}, u32[]{:S(2)}) copy-start(f32[32,2048]{1,0:T(8,128)S(1)} %collective-permute-done.31.rest_6_) | copy-start | bytes 786436
  134.1 10.2 %copy-start.19 = (f32[32,2048]{1,0:T(8,128)}, f32[32,2048]{1,0:T(8,128)S(1)}, u32[]{:S(2)}) copy-start(f32[32,2048]{1,0:T(8,128)S(1)} %collective-permute-done.34.rest_9_) | copy-start | bytes 786436
  134.1 10.2 %copy-start.20 = (f32[32,2048]{1,0:T(8,128)}, f32[32,2048]{1,0:T(8,128)S(1)}, u32[]{:S(2)}) copy-start(f32[32,2048]{1,0:T(8,128)S(1)} %collective-permute-done.33.rest_8_) | copy-start | bytes 786436
  134.1 10.2 %copy-start.21 = (f32[32,2048]{1,0:T(8,128)}, f32[32,2048]{1,0:T(8,128)S(1)}, u32[]{:S(2)}) copy-start(f32[32,2048]{1,0:T(8,128)S(1)} %collective-permute-done.32.rest_7_) | copy-start | bytes 786436
  134.8 30.2 %copy-start.1 = (s32[6]{0:T(128)S(1)}, s32[6]{0:T(128)}, u32[]{:S(2)}) copy-start(s32[6]{0:T(128)} %stack.27.info_ref) | copy-start | bytes 76
  144.3 3.0 %collective-permute-start.35 = (f32[128,2048]{1,0:T(8,128)}, f32[128,2048]{1,0:T(8,128)S(1)}, u32[]{:S(2)}, u32[]{:S(2)}) collective-permute-start(f32[128,2048]{1,0:T(8,128)} %get-tuple-element.70), channel_id=1, source_target_pairs={{0,4},{4,0},{8,12},{12,8},{16,20},{20,16},{24,28},{28,24},{1,5},{5... | collective-permute-start | bytes 3145736 | tf_op jit(solution)/shard_map/ppermute | solution.py:313
  148.7 7.6 %collective-permute-start.36 = (f32[32,2048]{1,0:T(8,128)S(1)}, f32[32,2048]{1,0:T(8,128)S(1)}, u32[]{:S(2)}, u32[]{:S(2)}) collective-permute-start(f32[32,2048]{1,0:T(8,128)S(1)} %get-tuple-element.87), channel_id=1, source_target_pairs={{0,8},{4,12},{8,0},{12,4},{16,24},{20,28},{24,16},{28,20},{1,9},{5... | collective-permute-start | bytes 786440 | tf_op jit(solution)/shard_map/ppermute | solution.py:322
  149.5 12.6 %collective-permute-start.38 = (f32[32,2048]{1,0:T(8,128)S(1)}, f32[32,2048]{1,0:T(8,128)S(1)}, u32[]{:S(2)}, u32[]{:S(2)}) collective-permute-start(f32[32,2048]{1,0:T(8,128)S(1)} %get-tuple-element.88), channel_id=1, source_target_pairs={{0,24},{4,28},{8,16},{12,20},{16,8},{20,12},{24,0},{28,4},{1,25},{... | collective-permute-start | bytes 786440 | tf_op jit(solution)/shard_map/ppermute | solution.py:322
  150.4 11.7 %collective-permute-start.37 = (f32[32,2048]{1,0:T(8,128)S(1)}, f32[32,2048]{1,0:T(8,128)S(1)}, u32[]{:S(2)}, u32[]{:S(2)}) collective-permute-start(f32[32,2048]{1,0:T(8,128)S(1)} %get-tuple-element.89), channel_id=1, source_target_pairs={{0,16},{4,20},{8,24},{12,28},{16,0},{20,4},{24,8},{28,12},{1,17},{... | collective-permute-start | bytes 786440 | tf_op jit(solution)/shard_map/ppermute | solution.py:322
  162.2 9.3 %copy-start.12 = (f32[32,2048]{1,0:T(8,128)}, f32[32,2048]{1,0:T(8,128)S(1)}, u32[]{:S(2)}) copy-start(f32[32,2048]{1,0:T(8,128)S(1)} %add_add_fusion.2.rest_10_) | copy-start | bytes 786436
  162.2 12.8 %collective-permute-start.41 = (f32[32,2048]{1,0:T(8,128)S(1)}, f32[32,2048]{1,0:T(8,128)S(1)}, u32[]{:S(2)}, u32[]{:S(2)}) collective-permute-start(f32[32,2048]{1,0:T(8,128)S(1)} %add_add_fusion.2.rest_10_), channel_id=1, source_target_pairs={{0,24},{4,28},{8,16},{12,20},{16,8},{20,12},{24,0},{28,4},{1,25},{... | collective-permute-start | bytes 786440 | tf_op jit(solution)/shard_map/ppermute | solution.py:327
  163.8 12.6 %collective-permute-start.40 = (f32[32,2048]{1,0:T(8,128)S(1)}, f32[32,2048]{1,0:T(8,128)S(1)}, u32[]{:S(2)}, u32[]{:S(2)}) collective-permute-start(f32[32,2048]{1,0:T(8,128)S(1)} %add_add_fusion.2.rest_10_), channel_id=1, source_target_pairs={{0,16},{4,20},{8,24},{12,28},{16,0},{20,4},{24,8},{28,12},{1,17},{... | collective-permute-start | bytes 786440 | tf_op jit(solution)/shard_map/ppermute | solution.py:327
  164.2 13.3 %collective-permute-start.39 = (f32[32,2048]{1,0:T(8,128)S(1)}, f32[32,2048]{1,0:T(8,128)S(1)}, u32[]{:S(2)}, u32[]{:S(2)}) collective-permute-start(f32[32,2048]{1,0:T(8,128)S(1)} %add_add_fusion.2.rest_10_), channel_id=1, source_target_pairs={{0,8},{4,12},{8,0},{12,4},{16,24},{20,28},{24,16},{28,20},{1,9},{5... | collective-permute-start | bytes 786440 | tf_op jit(solution)/shard_map/ppermute | solution.py:327
  171.5 14.2 %collective-permute-start.42 = (f32[32,2048]{1,0:T(8,128)S(1)}, f32[32,2048]{1,0:T(8,128)S(1)}, u32[]{:S(2)}, u32[]{:S(2)}) collective-permute-start(f32[32,2048]{1,0:T(8,128)S(1)} %add_add_fusion.2.rest_10_), channel_id=1, source_target_pairs={{0,4},{4,0},{8,12},{12,8},{16,20},{20,16},{24,28},{28,24},{1,5},{5... | collective-permute-start | bytes 786440 | tf_op jit(solution)/shard_map/ppermute | solution.py:328
  175.1 8.7 %copy-start.22 = (f32[32,2048]{1,0:T(8,128)}, f32[32,2048]{1,0:T(8,128)S(1)}, u32[]{:S(2)}) copy-start(f32[32,2048]{1,0:T(8,128)S(1)} %collective-permute-done.41.rest_13_) | copy-start | bytes 786436
  175.1 10.7 %collective-permute-start.45 = (f32[32,2048]{1,0:T(8,128)S(1)}, f32[32,2048]{1,0:T(8,128)S(1)}, u32[]{:S(2)}, u32[]{:S(2)}) collective-permute-start(f32[32,2048]{1,0:T(8,128)S(1)} %collective-permute-done.41.rest_13_), channel_id=1, source_target_pairs={{0,4},{4,0},{8,12},{12,8},{16,20},{20,16},{24,28},{28,24},{1,5},{5... | collective-permute-start | bytes 786440 | tf_op jit(solution)/shard_map/ppermute | solution.py:328
  176.3 9.5 %collective-permute-start.44 = (f32[32,2048]{1,0:T(8,128)S(1)}, f32[32,2048]{1,0:T(8,128)S(1)}, u32[]{:S(2)}, u32[]{:S(2)}) collective-permute-start(f32[32,2048]{1,0:T(8,128)S(1)} %collective-permute-done.40.rest_12_), channel_id=1, source_target_pairs={{0,4},{4,0},{8,12},{12,8},{16,20},{20,16},{24,28},{28,24},{1,5},{5... | collective-permute-start | bytes 786440 | tf_op jit(solution)/shard_map/ppermute | solution.py:328
  177.5 8.3 %collective-permute-start.43 = (f32[32,2048]{1,0:T(8,128)S(1)}, f32[32,2048]{1,0:T(8,128)S(1)}, u32[]{:S(2)}, u32[]{:S(2)}) collective-permute-start(f32[32,2048]{1,0:T(8,128)S(1)} %collective-permute-done.39.rest_11_), channel_id=1, source_target_pairs={{0,4},{4,0},{8,12},{12,8},{16,20},{20,16},{24,28},{28,24},{1,5},{5... | collective-permute-start | bytes 786440 | tf_op jit(solution)/shard_map/ppermute | solution.py:328
  (12 other events, 28.2 us)

commit v5 on v4

--- a/solution.py
+++ b/solution.py
@@ -11,6 +11,10 @@
 BF16 = jnp.bfloat16
 HIGHEST = lax.Precision.HIGHEST
 VMEM = pl.BlockSpec(memory_space=pltpu.VMEM)
+
+
+def cost(flops):
+    return pl.CostEstimate(flops=flops, bytes_accessed=1 << 20, transcendentals=0)
 
 
 def mm(a, b, da, db, precision=None):
@@ -123,61 +127,68 @@
         scratch_shapes=[pltpu.VMEM((NB, NB), F32)] * 3,
         input_output_aliases={} if fresh else {1: 0, 2: 1, 3: 2},
         compiler_params=pltpu.CompilerParams(vmem_limit_bytes=16 << 20),
-        cost_estimate=pl.CostEstimate(
-            flops=(last - first) * 8 * 10**9, bytes_accessed=3 << 20, transcendentals=0
-        ),
+        cost_estimate=cost((last - first) * 8 * 10**9),
         name="chol_part",
     )(info, *arrays)
 
 
-def finish(info, snapshots, panels, linv, factor, pieces, layout, tile=512):
-    rows, cols = snapshots.shape
+def finish(info, rest, panels, linv, factor, pieces, layout, half, coeffs=None, tile=512):
+    rows, cols = rest.shape
     n_pieces, n_panels = len(pieces), len(panels)
     chips = 1 + max(chip for _, _, chip in layout)
-    bases = [sum(p.shape[1] for p in panels[:i]) for i in range(n_panels)]
-
-    def kernel(info_ref, s_ref, l_ref, f_ref, *rest):
-        p_refs, rest = rest[:n_panels], rest[n_panels:]
-        m_refs = rest[:n_pieces]
-        up_ref, co_ref, bs, b3, l3, ms, m3, p3 = rest[n_pieces:]
+    width = PB // 2
+    depth = width * n_panels
+    top = half * width
+
+    def kernel(info_ref, s_ref, l_ref, f_ref, *refs):
+        p_refs, refs = refs[:n_panels], refs[n_panels:]
+        m_refs, refs = refs[:n_pieces], refs[n_pieces:]
+        up_ref, co_ref, bs, b3, l3, ms, m3, p3 = refs[-8:]
         j = pl.program_id(0)
 
         @pl.when(j == 0)
         def _():
-            lh, ll = split(l_ref[...])
-            l3[:, :PB], l3[:, PB : 2 * PB], l3[:, 2 * PB :] = lh, lh, ll
+            lh, ll = split(l_ref[top : top + width, :depth])
+            l3[:, :depth], l3[:, depth : 2 * depth], l3[:, 2 * depth :] = lh, lh, ll
             for r in range(0, rows, 256):
                 b = 0.0
-                for base, p_ref in zip(bases, p_refs):
-                    end = base + p_ref.shape[1]
+                for k, p_ref in enumerate(p_refs):
                     ph, plow = split(p_ref[r : r + 256, :])
+                    kh, kl = lh[:, k * width : (k + 1) * width], ll[:, k * width : (k + 1) * width]
                     lhs = jnp.concatenate([ph, ph, plow], axis=1)
-                    rhs = jnp.concatenate([lh[:, base:end], ll[:, base:end], lh[:, base:end]], axis=1)
-                    b = b + mm(lhs, rhs, 1, 1)
+                    b = b + mm(lhs, jnp.concatenate([kh, kl, kh], axis=1), 1, 1)
                 bs[r : r + 256, :] = b
                 bh, bl = split(b)
-                b3[r : r + 256, :PB], b3[r : r + 256, PB : 2 * PB] = bh, bh
-                b3[r : r + 256, 2 * PB :] = bl
+                b3[r : r + 256, :width], b3[r : r + 256, width : 2 * width] = bh, bh
+                b3[r : r + 256, 2 * width :] = bl
 
         for ref, (base, core, chip) in zip(m_refs, layout):
             h = ref.shape[0]
             off = base + (info_ref[1] ^ core) * (h * chips) + (info_ref[2] ^ chip) * h
             ms[pl.ds(pl.multiple_of(off, 8), h), :] = ref[...]
         mh, ml = split(ms[...])
-        m3[:PB, :], m3[PB : 2 * PB, :], m3[2 * PB :, :] = mh, ml, mh
+        m3[:depth, :], m3[depth : 2 * depth, :], m3[2 * depth :, :] = mh, ml, mh
         proj = mm(l3[...], m3[...], 1, 0)
         ph, plow = split(proj)
-        p3[:PB, :], p3[PB : 2 * PB, :], p3[2 * PB :, :] = ph, plow, ph
+        p3[:width, :], p3[width : 2 * width, :], p3[2 * width :, :] = ph, plow, ph
         co_ref[...] = proj
         up_ref[...] = s_ref[...] - mm(b3[...], p3[...], 1, 0)
-        for t in range(PB // tile):
-
-            @pl.when((info_ref[0] == 0) & (j == t))
-            def _():
-                co_ref[...] = f_ref[:, t * tile : (t + 1) * tile]
-                up_ref[...] = bs[:, t * tile : (t + 1) * tile]
+
+        @pl.when((info_ref[0] == 0) & (j == 0))
+        def _():
+            co_ref[...] = f_ref[top : top + width, :]
+            if half:
+                up_ref[:, :top] = s_ref[:, :top]
+            up_ref[:, top : top + width] = bs[...]
 
     col = lambda h: pl.BlockSpec((h, tile), lambda j, *_: (0, j))
+    operands = [rest, linv, factor, *panels, *pieces]
+    specs = [col(rows), VMEM, VMEM] + [VMEM] * n_panels + [col(p.shape[0]) for p in pieces]
+    aliases = {}
+    if half:
+        operands.append(coeffs)
+        specs.append(pl.BlockSpec(memory_space=pl.ANY))
+        aliases = {1: 0, len(operands): 1}
     return pl.pallas_call(
         kernel,
         out_shape=(
@@ -187,25 +198,22 @@
         grid_spec=pltpu.PrefetchScalarGridSpec(
             num_scalar_prefetch=1,
             grid=(cols // tile,),
-            in_specs=[col(rows), VMEM, VMEM]
-            + [VMEM for _ in panels]
-            + [col(p.shape[0]) for p in pieces],
-            out_specs=(col(rows), col(PB)),
+            in_specs=specs,
+            out_specs=(col(rows), pl.BlockSpec((width, tile), lambda j, *_: (half, j))),
             scratch_shapes=[
-                pltpu.VMEM((rows, PB), F32),
-                pltpu.VMEM((rows, 3 * PB), BF16),
-                pltpu.VMEM((PB, 3 * PB), BF16),
-                pltpu.VMEM((PB, tile), F32),
-                pltpu.VMEM((3 * PB, tile), BF16),
-                pltpu.VMEM((3 * PB, tile), BF16),
+                pltpu.VMEM((rows, width), F32),
+                pltpu.VMEM((rows, 3 * width), BF16),
+                pltpu.VMEM((width, 3 * depth), BF16),
+                pltpu.VMEM((depth, tile), F32),
+                pltpu.VMEM((3 * depth, tile), BF16),
+                pltpu.VMEM((3 * width, tile), BF16),
             ],
         ),
-        compiler_params=pltpu.CompilerParams(vmem_limit_bytes=58 << 20),
-        cost_estimate=pl.CostEstimate(
-            flops=6 * PB * cols * (rows + PB), bytes_accessed=8 * rows * cols, transcendentals=0
-        ),
+        input_output_aliases=aliases,
+        compiler_params=pltpu.CompilerParams(vmem_limit_bytes=56 << 20),
+        cost_estimate=cost(10**10),
         name="finish",
-    )(info, snapshots, linv, factor, *panels, *pieces)
+    )(info, *operands)
 
 
 def panel_dot(info, snapshots, parts, size, base, width, scale, tile=512):
@@ -268,9 +276,7 @@
             ],
         ),
         compiler_params=pltpu.CompilerParams(vmem_limit_bytes=58 << 20),
-        cost_estimate=pl.CostEstimate(
-            flops=6 * rows * cols * width, bytes_accessed=4 * rows * cols, transcendentals=0
-        ),
+        cost_estimate=cost(6 * rows * cols * width),
         name="panel_dot",
     )(info, snapshots, snapshots, *parts)
 
@@ -356,21 +362,23 @@
     grams, places = gather_rows(share, n_rows)
 
     send, keep, panel_a = dot(after(got_a, far, mine_b), 0)
-    state = chol_part(info, 0, 1, pieces=after(grams, send, mine_b), places=places)
     joined = join_cores(send, keep, n_rows)
+    got_b = spread_round(mine_b, n_cols)
     own_a = scatter_chips(joined, n_rows)
-    got_b = spread_round(mine_b, n_cols)
-    state = chol_part(info, 1, 2, state=after(state, own_a))
+    state = chol_part(info, 0, 2, pieces=after(grams, joined, mine_b), places=places)
     pieces_a, where = gather_rows(own_a, n_rows)
-    send, keep, panel_b = dot(after(got_b, pieces_a, state), half)
+    send, keep, panel_b = dot(after(got_b, own_a, state), half)
     joined = join_cores(send, keep, n_rows)
     own_b = scatter_chips(joined, n_rows)
     state = chol_part(info, 2, 3, state=after(state, joined))
+    _, factor, linv = chol_part(info, 3, 4, state=after(state, own_b))
     pieces_b, _ = gather_rows(own_b, n_rows)
-    _, factor, linv = chol_part(info, 3, 4, state=after(state, own_b))
     layout = [(base,) + w for base in (0, half) for w in where]
+    rest, coeffs = finish(
+        info, snapshots, [panel_a], linv, factor, pieces_a, layout[: len(where)], 0
+    )
     return finish(
-        info, snapshots, [panel_a, panel_b], linv, factor, pieces_a + pieces_b, layout
+        info, rest, [panel_a, panel_b], linv, factor, pieces_a + pieces_b, layout, 1, coeffs
     )
 
 

time: 207 us -> 205 us (level)
  waiting for transfers between devices: 50.2 us -> 39.1 us
  Pallas kernels: 64.7 us -> 73.1 us
    ppermute x9, waiting for transfers between devices: 16.6 us -> 5.65 us  [scatter_chips(): lax.ppermute(take(mine, (chip ^ k) * piece, piece), 'rows', swap(n, 2 * k))]
    pallas_call x1 -> x2, Pallas kernels: 19.2 us -> 28.3 us  [finish(): pl.pallas_call(kernel, out_shape=(jax.ShapeDtypeStruct((rows, cols), F32)...]
    ppermute x9, waiting for transfers between devices: 6.28 us -> 9.43 us  [gather_rows(): lax.ppermute(own, 'rows', swap(n, 2 * k))]
    ppermute x3, waiting for transfers between devices: 2.5 us -> 0.01 us  [join_cores(): return mine + lax.ppermute(send, 'rows', swap(n, 1))]
    unnamed x58 -> x60, local copies, waits for them, and re-layouts: 5.09 us -> 6 us
    pallas_call x4 -> x3, Pallas kernels: 26.8 us -> 26.3 us  [chol_part(): pl.pallas_call(kernel, out_shape=(shape, shape, shape), in_specs=[pl.Bloc...]
  transfers between devices with their start and end apart: 46 -> 46, of which waited for: 11 -> 8; matrix products, arithmetic and copies ran while one was open for 7% -> 7% of each run, Pallas kernels for 13% -> 19%
where the time goes in v5:
time: 205 us; the launch traced here: 204 us
  Pallas kernels  73.1 us (36%)
  starting transfers between devices  66.4 us (32%)
  waiting for transfers between devices  39.1 us (19%)
  local copies, waits for them, and re-layouts  9.99 us (5%)
  other arithmetic  8.35 us (4%)
  matrix products  5.71 us (3%)
    pallas_call x2, Pallas kernels, finish(): pl.pallas_call(kernel, out_shape=(jax.ShapeDtypeStruct((rows, cols), F32)...  28.3 us
    pallas_call x3, Pallas kernels, chol_part(): pl.pallas_call(kernel, out_shape=(shape, shape, shape), in_specs=[pl.Bloc...  26.3 us
    ppermute x4, starting transfers between devices, spread_round(): got.append(lax.ppermute(mine, 'cols', pairs))  26.3 us
    ppermute x4, waiting for transfers between devices, spread_round(): got.append(lax.ppermute(mine, 'cols', pairs))  22.5 us
    pallas_call x2, Pallas kernels, panel_dot(): pl.pallas_call(kernel, out_shape=(out, out, jax.ShapeDtypeStruct((rows, w...  18.5 us
    ppermute x9, starting transfers between devices, scatter_chips(): lax.ppermute(take(mine, (chip ^ k) * piece, piece), 'rows', swap(n, 2 * k))  9.64 us
    ppermute x9, waiting for transfers between devices, gather_rows(): lax.ppermute(own, 'rows', swap(n, 2 * k))  9.43 us
    ppermute x12, starting transfers between devices, gather_rows(): other = [lax.ppermute(g, 'rows', swap(n, 1)) for g in got]  8.39 us
  transfers between devices with their start and end apart: 46, of which 8 were waited for; matrix products, arithmetic and copies ran while one was open for 7% of the time, Pallas kernels for 19%

profile of v5, /device:TPU:17, one launch (start us, length us, event | category | flops | bytes accessed | tf_op | source)
XLA Modules:
  0.0 204.2 jit_solution(18132154149656599128)
XLA Ops:
  0.6 2.2 %fusion.5 = (f32[344,256]{1,0:T(8,128)}, f32[344,256]{1,0:T(8,128)}, f32[344,256]{1,0:T(8,128)S(1)}) fusion(f32[1024,2048]{1,0:T(8,128)} %s_ref.5), kind=kLoop, calls=%fused_computation.20 | loop fusion | bytes 2113536 | tf_op jit(solution)/shard_map/slice | solution.py:294
  2.9 1.3 collective-permute-start.15
  4.2 1.4 collective-permute-start.16
  5.6 1.4 collective-permute-start.14
  7.0 5.7 %fusion.2 = f32[512,512]{1,0:T(8,128)S(1)} fusion(f32[1024,2048]{1,0:T(8,128)} %s_ref.5), kind=kOutput, calls=%fused_computation.2 | convolution fusion | flops 3221487616 | bytes 3145728 | tf_op jit(solution)/shard_map/dot_general | solution.py:21
  12.7 0.7 collective-permute-start
  13.5 1.5 collective-permute-done.15
  15.0 1.2 add_add_fusion.1.rest_0_
  16.2 1.3 dynamic-slice_add_fusion
  17.5 1.3 collective-permute-start.1
  18.7 1.2 collective-permute-start.3
  20.2 0.9 fusion.6
  21.1 1.3 collective-permute-start.20
  22.4 0.7 collective-permute-start.21
  23.1 0.7 collective-permute-start.19
  24.5 9.8 %collective-permute-start.18 = (f32[344,256]{1,0:T(8,128)S(1)}, f32[344,256]{1,0:T(8,128)S(1)}, u32[]{:S(2)}, u32[]{:S(2)}) collective-permute-start(f32[344,256]{1,0:T(8,128)S(1)} %add_add_fusion.1.rest_0_), channel_id=1, source_target_pairs={{1,3},{2,1},{3,2},{5,7},{6,5},{7,6},{9,11},{10,9},{11,10},{13,15},... | collective-permute-start | bytes 1056776 | tf_op jit(solution)/shard_map/ppermute | solution.py:302
  34.3 11.0 %collective-permute-start.17 = (f32[344,256]{1,0:T(8,128)S(1)}, f32[344,256]{1,0:T(8,128)S(1)}, u32[]{:S(2)}, u32[]{:S(2)}) collective-permute-start(f32[344,256]{1,0:T(8,128)S(1)} %add_add_fusion.1.rest_0_), channel_id=1, source_target_pairs={{1,2},{2,3},{3,1},{5,6},{6,7},{7,5},{9,10},{10,11},{11,9},{13,14},... | collective-permute-start | bytes 1056776 | tf_op jit(solution)/shard_map/ppermute | solution.py:302
  45.3 1.0 add_add_fusion.4
  46.3 0.7 collective-permute-start.6
  47.0 1.3 collective-permute-start.5
  48.3 0.7 copy-done.10
  49.7 1.1 add_add_fusion.rest_0_
  50.8 22.5 %collective-permute-done.17.rest_1_ = f32[344,256]{1,0:T(8,128)S(1)} collective-permute-done((f32[344,256]{1,0:T(8,128)S(1)}, f32[344,256]{1,0:T(8,128)S(1)}, u32[]{:S(2)}, u32[]{:S(2)}) %collective-permute-start.17) | collective-permute-done | bytes 352288 | tf_op jit(solution)/shard_map/ppermute | solution.py:302
  73.3 0.7 copy-done.9
  74.0 9.2 %panel_dot.2 = (f32[128,2048]{1,0:T(8,128)}, f32[128,2048]{1,0:T(8,128)}, f32[1024,256]{1,0:T(8,128)}) custom-call(s32[6]{0:T(128)} %stack.27.info_ref, f32[1024,2048]{1,0:T(8,128)} %s_ref.5, f32[1024,2048]{1,0:T(8,128)} %s_ref.5, f32[344,256]{1,0:T(8,128)} %copy-done.4, f32[344,256]{1,0:T(8,128)} %copy-done.9, f32[344,256]{1,0:T(8,128)} %copy-done.8), custom_call_target="tpu_custom_call" | custom-call | flops 3221225472 | bytes 1048576 | tf_op jit(solution)/shard_map/panel_dot/pallas_call | solution.py:258
  83.2 2.2 %collective-permute-start.22 = (f32[128,2048]{1,0:T(8,128)}, f32[128,2048]{1,0:T(8,128)S(1)}, u32[]{:S(2)}, u32[]{:S(2)}) collective-permute-start(f32[128,2048]{1,0:T(8,128)} %get-tuple-element.44), channel_id=1, source_target_pairs={{0,4},{4,0},{8,12},{12,8},{16,20},{20,16},{24,28},{28,24},{1,5},{5... | collective-permute-start | bytes 3145736 | tf_op jit(solution)/shard_map/ppermute | solution.py:319
  85.5 1.0 add_select_fusion.refs_0_
  86.5 2.2 %collective-permute-start.9 = (f32[64,512]{1,0:T(8,128)S(1)}, f32[64,512]{1,0:T(8,128)S(1)}, u32[]{:S(2)}, u32[]{:S(2)}) collective-permute-start(f32[64,512]{1,0:T(8,128)S(1)} %add_select_fusion.refs_0_), channel_id=1, source_target_pairs={{0,24},{4,28},{8,16},{12,20},{16,8},{20,12},{24,0},{28,4},{1,25},{... | collective-permute-start | bytes 393224 | tf_op jit(solution)/shard_map/ppermute | solution.py:333
  89.3 0.7 collective-permute-start.10
  90.1 2.5 %collective-permute-done.9.refs_3_ = f32[64,512]{1,0:T(8,128)S(1)} collective-permute-done((f32[64,512]{1,0:T(8,128)S(1)}, f32[64,512]{1,0:T(8,128)S(1)}, u32[]{:S(2)}, u32[]{:S(2)}) %collective-permute-start.9) | collective-permute-done | bytes 131104 | tf_op jit(solution)/shard_map/ppermute | solution.py:333
  92.6 1.1 collective-permute-start.13
  93.7 2.1 %collective-permute-done.8.refs_2_ = f32[64,512]{1,0:T(8,128)S(1)} collective-permute-done((f32[64,512]{1,0:T(8,128)S(1)}, f32[64,512]{1,0:T(8,128)S(1)}, u32[]{:S(2)}, u32[]{:S(2)}) %collective-permute-start.8) | collective-permute-done | bytes 131104 | tf_op jit(solution)/shard_map/ppermute | solution.py:333
  96.6 1.9 collective-permute-start.24
  98.5 1.4 add.124
  100.0 3.5 %collective-permute-start.23 = (f32[344,256]{1,0:T(8,128)S(1)}, f32[344,256]{1,0:T(8,128)S(1)}, u32[]{:S(2)}, u32[]{:S(2)}) collective-permute-start(f32[344,256]{1,0:T(8,128)S(1)} %add_add_fusion.rest_0_), channel_id=1, source_target_pairs={{1,2},{2,3},{3,1},{5,6},{6,7},{7,5},{9,10},{10,11},{11,9},{13,14},... | collective-permute-start | bytes 1056776 | tf_op jit(solution)/shard_map/ppermute | solution.py:302
  103.6 0.9 collective-permute-start.25
  104.5 1.4 collective-permute-start.27
  106.3 13.6 %chol_part.3 = (f32[512,512]{1,0:T(8,128)S(1)}, f32[512,512]{1,0:T(8,128)S(1)}, f32[512,512]{1,0:T(8,128)S(1)}) custom-call(s32[6]{0:T(128)S(1)} %copy-done, f32[64,512]{1,0:T(8,128)S(1)} %add_select_fusion.refs_0_, f32[64,512]{1,0:T(8,128)S(1)} %collective-permute-done.7.refs_1_, f32[64,512]{1,0:T(8,128)S(1)} %collective-permute-done.8.refs_2_, ...), custom_call_target="tpu_custom_call" | custom-call | flops 16000000000 | bytes 1048576 | tf_op jit(solution)/shard_map/chol_part/pallas_call | solution.py:122
  120.1 0.7 copy-done.6
  120.9 9.3 %panel_dot.3 = (f32[128,2048]{1,0:T(8,128)}, f32[128,2048]{1,0:T(8,128)}, f32[1024,256]{1,0:T(8,128)}) custom-call(s32[6]{0:T(128)} %stack.27.info_ref, f32[1024,2048]{1,0:T(8,128)} %s_ref.5, f32[1024,2048]{1,0:T(8,128)} %s_ref.5, f32[344,256]{1,0:T(8,128)} %copy-done.5, f32[344,256]{1,0:T(8,128)} %copy-done.7, f32[344,256]{1,0:T(8,128)} %copy-done.6), custom_call_target="tpu_custom_call" | custom-call | flops 3221225472 | bytes 1048576 | tf_op jit(solution)/shard_map/panel_dot/pallas_call | solution.py:258
  130.2 1.5 collective-permute-start.28
  131.7 1.6 collective-permute-start.34
  133.3 0.8 collective-permute-start.33
  134.4 1.4 add.132
  135.8 1.2 collective-permute-start.29
  137.0 1.5 collective-permute-start.31
  138.5 2.0 collective-permute-done.34.refs_4_.refs_5_
  140.5 1.5 collective-permute-start.30
  142.0 6.6 %chol_part.4 = (f32[512,512]{1,0:T(8,128)S(1)}, f32[512,512]{1,0:T(8,128)S(1)}, f32[512,512]{1,0:T(8,128)S(1)}) custom-call(s32[6]{0:T(128)S(1)} %copy-done.1, f32[512,512]{1,0:T(8,128)S(1)} %get-tuple-element.61.refs_0_, f32[512,512]{1,0:T(8,128)S(1)} %get-tuple-element.62.refs_1_, ...), custom_call_target="tpu_custom_call", output_to_operand_aliasing={{0}: (1, {}), {1}: (2, {}), {2}: (3, {})} | custom-call | flops 8000000000 | bytes 1048576 | tf_op jit(solution)/shard_map/chol_part/pallas_call | solution.py:122
  148.6 1.7 collective-permute-start.35
  150.4 1.7 collective-permute-done.29
  152.0 1.3 collective-permute-start.37
  153.4 4.0 %collective-permute-done.31 = f32[32,2048]{1,0:T(8,128)S(1)} collective-permute-done((f32[32,2048]{1,0:T(8,128)S(1)}, f32[32,2048]{1,0:T(8,128)S(1)}, u32[]{:S(2)}, u32[]{:S(2)}) %collective-permute-start.31) | collective-permute-done | bytes 262176 | tf_op jit(solution)/shard_map/ppermute | solution.py:328
  157.3 0.9 collective-permute-start.36
  158.3 1.7 collective-permute-start.41
  159.9 0.8 collective-permute-start.40
  161.1 6.2 %chol_part.5 = (f32[512,512]{1,0:T(8,128)S(1)}, f32[512,512]{1,0:T(8,128)S(1)}, f32[512,512]{1,0:T(8,128)S(1)}) custom-call(s32[6]{0:T(128)S(1)} %copy-done.1, f32[512,512]{1,0:T(8,128)S(1)} %get-tuple-element.67.refs_0_, f32[512,512]{1,0:T(8,128)S(1)} %get-tuple-element.68.refs_1_, ...), custom_call_target="tpu_custom_call", output_to_operand_aliasing={{0}: (1, {}), {1}: (2, {}), {2}: (3, {})} | custom-call | flops 8000000000 | bytes 1048576 | tf_op jit(solution)/shard_map/chol_part/pallas_call | solution.py:122
  167.4 1.0 copy-done.2
  168.4 1.0 copy-done.3
  169.3 0.8 collective-permute-start.42
  170.2 2.9 %collective-permute-done.40.refs_12_ = f32[32,2048]{1,0:T(8,128)S(1)} collective-permute-done((f32[32,2048]{1,0:T(8,128)S(1)}, f32[32,2048]{1,0:T(8,128)S(1)}, u32[]{:S(2)}, u32[]{:S(2)}) %collective-permute-start.40) | collective-permute-done | bytes 262176 | tf_op jit(solution)/shard_map/ppermute | solution.py:333
  173.9 0.7 copy-done.22
  174.7 13.3 %finish.2 = (f32[1024,2048]{1,0:T(8,128)}, f32[512,2048]{1,0:T(8,128)}) custom-call(s32[6]{0:T(128)} %stack.27.info_ref, f32[1024,2048]{1,0:T(8,128)} %s_ref.5, f32[512,512]{1,0:T(8,128)} %copy-done.3, f32[512,512]{1,0:T(8,128)} %copy-done.2, f32[1024,256]{1,0:T(8,128)} %get-tuple-element.72.refs_0_, f32[32,2048]{1,0:T(8,128)} %copy-done.11, ...), custom_call_target="tpu_custom_call" | custom-call | flops 10000000000 | bytes 1048576 | tf_op jit(solution)/shard_map/finish/pallas_call | solution.py:192
  189.0 15.0 %finish.3 = (f32[1024,2048]{1,0:T(8,128)}, f32[512,2048]{1,0:T(8,128)}) custom-call(s32[6]{0:T(128)} %stack.27.info_ref, f32[1024,2048]{1,0:T(8,128)} %get-tuple-element.73.s_ref, f32[512,512]{1,0:T(8,128)} %copy-done.3, f32[512,512]{1,0:T(8,128)} %copy-done.2, ...), custom_call_target="tpu_custom_call", output_to_operand_aliasing={{0}: (1, {}), {1}: (22, {})} | custom-call | flops 10000000000 | bytes 1048576 | tf_op jit(solution)/shard_map/finish/pallas_call | solution.py:192
  (114 shorter events, 6.7 us)
Async XLA Ops:
  0.6 19.5 %slice-start = ((f32[1024,2048]{1,0:T(8,128)}), f32[1024,256]{1,0:T(8,128)S(1)}, s32[]{:S(2)}) async-start(f32[1024,2048]{1,0:T(8,128)} %s_ref.5), calls=%async_computation | async-start | bytes 2097152 | tf_op jit(solution)/shard_map/slice | solution.py:360
  2.9 12.1 %collective-permute-start.15 = (f32[344,256]{1,0:T(8,128)}, f32[344,256]{1,0:T(8,128)S(1)}, u32[]{:S(2)}, u32[]{:S(2)}) collective-permute-start(f32[344,256]{1,0:T(8,128)} %get-tuple-element.76), channel_id=1, source_target_pairs={{0,2},{4,6},{8,10},{12,14},{16,18},{20,22},{24,26},{28,30}} | collective-permute-start | bytes 1056776 | tf_op jit(solution)/shard_map/ppermute | solution.py:294
  4.2 10.8 %collective-permute-start.16 = (f32[344,256]{1,0:T(8,128)}, f32[344,256]{1,0:T(8,128)}, u32[]{:S(2)}, u32[]{:S(2)}) collective-permute-start(f32[344,256]{1,0:T(8,128)} %get-tuple-element.77), channel_id=1, source_target_pairs={{0,1},{4,5},{8,9},{12,13},{16,17},{20,21},{24,25},{28,29}} | collective-permute-start | bytes 1056776 | tf_op jit(solution)/shard_map/ppermute | solution.py:294
  5.6 9.4 %collective-permute-start.14 = (f32[344,256]{1,0:T(8,128)S(1)}, f32[344,256]{1,0:T(8,128)}, u32[]{:S(2)}, u32[]{:S(2)}) collective-permute-start(f32[344,256]{1,0:T(8,128)S(1)} %get-tuple-element.78), channel_id=1, source_target_pairs={{0,3},{4,7},{8,11},{12,15},{16,19},{20,23},{24,27},{28,31}} | collective-permute-start | bytes 1056776 | tf_op jit(solution)/shard_map/ppermute | solution.py:294
  12.7 3.4 %collective-permute-start = (f32[256,512]{1,0:T(8,128)S(1)}, f32[256,512]{1,0:T(8,128)}, u32[]{:S(2)}, u32[]{:S(2)}) collective-permute-start(f32[256,512]{1,0:T(8,128)S(1)} %constant_dynamic-slice_fusion.9), channel_id=1, source_target_pairs={{0,4},{4,0},{8,12},{12,8},{16,20},{20,16},{24,28},{28,24},{1,5},{5... | collective-permute-start | bytes 1572872 | tf_op jit(solution)/shard_map/ppermute | solution.py:319
  16.1 57.2 %copy-start.4 = (f32[344,256]{1,0:T(8,128)}, f32[344,256]{1,0:T(8,128)S(1)}, u32[]{:S(2)}) copy-start(f32[344,256]{1,0:T(8,128)S(1)} %add_add_fusion.1.rest_0_) | copy-start | bytes 1056772
  17.5 5.6 %collective-permute-start.1 = (f32[64,512]{1,0:T(8,128)S(1)}, f32[64,512]{1,0:T(8,128)S(1)}, u32[]{:S(2)}, u32[]{:S(2)}) collective-permute-start(f32[64,512]{1,0:T(8,128)S(1)} %get-tuple-element.88), channel_id=1, source_target_pairs={{0,8},{4,12},{8,0},{12,4},{16,24},{20,28},{24,16},{28,20},{1,9},{5... | collective-permute-start | bytes 393224 | tf_op jit(solution)/shard_map/ppermute | solution.py:328
  18.7 5.7 %collective-permute-start.3 = (f32[64,512]{1,0:T(8,128)S(1)}, f32[64,512]{1,0:T(8,128)S(1)}, u32[]{:S(2)}, u32[]{:S(2)}) collective-permute-start(f32[64,512]{1,0:T(8,128)S(1)} %get-tuple-element.89), channel_id=1, source_target_pairs={{0,24},{4,28},{8,16},{12,20},{16,8},{20,12},{24,0},{28,4},{1,25},{... | collective-permute-start | bytes 393224 | tf_op jit(solution)/shard_map/ppermute | solution.py:328
  19.9 14.4 %collective-permute-start.2 = (f32[64,512]{1,0:T(8,128)S(1)}, f32[64,512]{1,0:T(8,128)}, u32[]{:S(2)}, u32[]{:S(2)}) collective-permute-start(f32[64,512]{1,0:T(8,128)S(1)} %get-tuple-element.90), channel_id=1, source_target_pairs={{0,16},{4,20},{8,24},{12,28},{16,0},{20,4},{24,8},{28,12},{1,17},{... | collective-permute-start | bytes 393224 | tf_op jit(solution)/shard_map/ppermute | solution.py:328
  21.1 25.2 %collective-permute-start.20 = (f32[344,256]{1,0:T(8,128)}, f32[344,256]{1,0:T(8,128)S(1)}, u32[]{:S(2)}, u32[]{:S(2)}) collective-permute-start(f32[344,256]{1,0:T(8,128)} %get-tuple-element.85), channel_id=1, source_target_pairs={{0,2},{4,6},{8,10},{12,14},{16,18},{20,22},{24,26},{28,30}} | collective-permute-start | bytes 1056776 | tf_op jit(solution)/shard_map/ppermute | solution.py:294
  22.4 24.6 %collective-permute-start.21 = (f32[344,256]{1,0:T(8,128)}, f32[344,256]{1,0:T(8,128)S(1)}, u32[]{:S(2)}, u32[]{:S(2)}) collective-permute-start(f32[344,256]{1,0:T(8,128)} %get-tuple-element.86), channel_id=1, source_target_pairs={{0,1},{4,5},{8,9},{12,13},{16,17},{20,21},{24,25},{28,29}} | collective-permute-start | bytes 1056776 | tf_op jit(solution)/shard_map/ppermute | solution.py:294
  23.1 25.2 %collective-permute-start.19 = (f32[344,256]{1,0:T(8,128)S(1)}, f32[344,256]{1,0:T(8,128)S(1)}, u32[]{:S(2)}, u32[]{:S(2)}) collective-permute-start(f32[344,256]{1,0:T(8,128)S(1)} %get-tuple-element.87), channel_id=1, source_target_pairs={{0,3},{4,7},{8,11},{12,15},{16,19},{20,23},{24,27},{28,31}} | collective-permute-start | bytes 1056776 | tf_op jit(solution)/shard_map/ppermute | solution.py:294
  24.5 9.9 %copy-start.13 = (f32[64,512]{1,0:T(8,128)}, f32[64,512]{1,0:T(8,128)S(1)}, u32[]{:S(2)}) copy-start(f32[64,512]{1,0:T(8,128)S(1)} %collective-permute-done.3) | copy-start | bytes 393220
  24.5 26.3 %collective-permute-start.18 = (f32[344,256]{1,0:T(8,128)S(1)}, f32[344,256]{1,0:T(8,128)S(1)}, u32[]{:S(2)}, u32[]{:S(2)}) collective-permute-start(f32[344,256]{1,0:T(8,128)S(1)} %add_add_fusion.1.rest_0_), channel_id=1, source_target_pairs={{1,3},{2,1},{3,2},{5,7},{6,5},{7,6},{9,11},{10,9},{11,10},{13,15},... | collective-permute-start | bytes 1056776 | tf_op jit(solution)/shard_map/ppermute | solution.py:302
  34.3 39.0 %collective-permute-start.17 = (f32[344,256]{1,0:T(8,128)S(1)}, f32[344,256]{1,0:T(8,128)S(1)}, u32[]{:S(2)}, u32[]{:S(2)}) collective-permute-start(f32[344,256]{1,0:T(8,128)S(1)} %add_add_fusion.1.rest_0_), channel_id=1, source_target_pairs={{1,2},{2,3},{3,1},{5,6},{6,7},{7,5},{9,10},{10,11},{11,9},{13,14},... | collective-permute-start | bytes 1056776 | tf_op jit(solution)/shard_map/ppermute | solution.py:302
  46.3 27.0 %collective-permute-start.6 = (f32[64,512]{1,0:T(8,128)S(1)}, f32[64,512]{1,0:T(8,128)S(1)}, u32[]{:S(2)}, u32[]{:S(2)}) collective-permute-start(f32[64,512]{1,0:T(8,128)S(1)} %add_add_fusion.4), channel_id=1, source_target_pairs={{0,1},{4,5},{8,9},{12,13},{16,17},{20,21},{24,25},{28,29}} | collective-permute-start | bytes 393224 | tf_op jit(solution)/shard_map/ppermute | solution.py:358
  47.0 26.3 %collective-permute-start.5 = (f32[64,512]{1,0:T(8,128)S(1)}, f32[64,512]{1,0:T(8,128)S(1)}, u32[]{:S(2)}, u32[]{:S(2)}) collective-permute-start(f32[64,512]{1,0:T(8,128)S(1)} %add_add_fusion.4), channel_id=1, source_target_pairs={{0,2},{4,6},{8,10},{12,14},{16,18},{20,22},{24,26},{28,30}} | collective-permute-start | bytes 393224 | tf_op jit(solution)/shard_map/ppermute | solution.py:358
  49.1 24.2 %collective-permute-start.4 = (f32[64,512]{1,0:T(8,128)S(1)}, f32[64,512]{1,0:T(8,128)S(1)}, u32[]{:S(2)}, u32[]{:S(2)}) collective-permute-start(f32[64,512]{1,0:T(8,128)S(1)} %add_add_fusion.4), channel_id=1, source_target_pairs={{0,3},{4,7},{8,11},{12,15},{16,19},{20,23},{24,27},{28,31}} | collective-permute-start | bytes 393224 | tf_op jit(solution)/shard_map/ppermute | solution.py:358
  50.8 49.2 %copy-start.5 = (f32[344,256]{1,0:T(8,128)}, f32[344,256]{1,0:T(8,128)S(1)}, u32[]{:S(2)}) copy-start(f32[344,256]{1,0:T(8,128)S(1)} %add_add_fusion.rest_0_) | copy-start | bytes 1056772
  50.8 55.5 %copy-start = (s32[6]{0:T(128)S(1)}, s32[6]{0:T(128)}, u32[]{:S(2)}) copy-start(s32[6]{0:T(128)} %stack.27.info_ref) | copy-start | bytes 76
  50.8 22.5 %copy-start.8 = (f32[344,256]{1,0:T(8,128)}, f32[344,256]{1,0:T(8,128)S(1)}, u32[]{:S(2)}) copy-start(f32[344,256]{1,0:T(8,128)S(1)} %collective-permute-done.18.rest_2_) | copy-start | bytes 1056772
  73.3 9.9 %copy-start.14 = (f32[64,512]{1,0:T(8,128)}, f32[64,512]{1,0:T(8,128)S(1)}, u32[]{:S(2)}) copy-start(f32[64,512]{1,0:T(8,128)S(1)} %collective-permute-done.6) | copy-start | bytes 393220
  73.3 9.9 %copy-start.15 = (f32[64,512]{1,0:T(8,128)}, f32[64,512]{1,0:T(8,128)S(1)}, u32[]{:S(2)}) copy-start(f32[64,512]{1,0:T(8,128)S(1)} %collective-permute-done.5) | copy-start | bytes 393220
  83.2 13.4 %collective-permute-start.22 = (f32[128,2048]{1,0:T(8,128)}, f32[128,2048]{1,0:T(8,128)S(1)}, u32[]{:S(2)}, u32[]{:S(2)}) collective-permute-start(f32[128,2048]{1,0:T(8,128)} %get-tuple-element.44), channel_id=1, source_target_pairs={{0,4},{4,0},{8,12},{12,8},{16,20},{20,16},{24,28},{28,24},{1,5},{5... | collective-permute-start | bytes 3145736 | tf_op jit(solution)/shard_map/ppermute | solution.py:319
  86.5 6.1 %collective-permute-start.9 = (f32[64,512]{1,0:T(8,128)S(1)}, f32[64,512]{1,0:T(8,128)S(1)}, u32[]{:S(2)}, u32[]{:S(2)}) collective-permute-start(f32[64,512]{1,0:T(8,128)S(1)} %add_select_fusion.refs_0_), channel_id=1, source_target_pairs={{0,24},{4,28},{8,16},{12,20},{16,8},{20,12},{24,0},{28,4},{1,25},{... | collective-permute-start | bytes 393224 | tf_op jit(solution)/shard_map/ppermute | solution.py:333
  88.7 7.0 %collective-permute-start.8 = (f32[64,512]{1,0:T(8,128)S(1)}, f32[64,512]{1,0:T(8,128)S(1)}, u32[]{:S(2)}, u32[]{:S(2)}) collective-permute-start(f32[64,512]{1,0:T(8,128)S(1)} %add_select_fusion.refs_0_), channel_id=1, source_target_pairs={{0,16},{4,20},{8,24},{12,28},{16,0},{20,4},{24,8},{28,12},{1,17},{... | collective-permute-start | bytes 393224 | tf_op jit(solution)/shard_map/ppermute | solution.py:333
  89.0 7.2 %collective-permute-start.7 = (f32[64,512]{1,0:T(8,128)S(1)}, f32[64,512]{1,0:T(8,128)S(1)}, u32[]{:S(2)}, u32[]{:S(2)}) collective-permute-start(f32[64,512]{1,0:T(8,128)S(1)} %add_select_fusion.refs_0_), channel_id=1, source_target_pairs={{0,8},{4,12},{8,0},{12,4},{16,24},{20,28},{24,16},{28,20},{1,9},{5... | collective-permute-start | bytes 393224 | tf_op jit(solution)/shard_map/ppermute | solution.py:333
  89.3 10.6 %collective-permute-start.10 = (f32[64,512]{1,0:T(8,128)S(1)}, f32[64,512]{1,0:T(8,128)S(1)}, u32[]{:S(2)}, u32[]{:S(2)}) collective-permute-start(f32[64,512]{1,0:T(8,128)S(1)} %add_select_fusion.refs_0_), channel_id=1, source_target_pairs={{0,4},{4,0},{8,12},{12,8},{16,20},{20,16},{24,28},{28,24},{1,5},{5... | collective-permute-start | bytes 393224 | tf_op jit(solution)/shard_map/ppermute | solution.py:334
  92.6 10.9 %collective-permute-start.13 = (f32[64,512]{1,0:T(8,128)S(1)}, f32[64,512]{1,0:T(8,128)S(1)}, u32[]{:S(2)}, u32[]{:S(2)}) collective-permute-start(f32[64,512]{1,0:T(8,128)S(1)} %collective-permute-done.9.refs_3_), channel_id=1, source_target_pairs={{0,4},{4,0},{8,12},{12,8},{16,20},{20,16},{24,28},{28,24},{1,5},{5... | collective-permute-start | bytes 393224 | tf_op jit(solution)/shard_map/ppermute | solution.py:334
  95.7 7.8 %collective-permute-start.12 = (f32[64,512]{1,0:T(8,128)S(1)}, f32[64,512]{1,0:T(8,128)S(1)}, u32[]{:S(2)}, u32[]{:S(2)}) collective-permute-start(f32[64,512]{1,0:T(8,128)S(1)} %collective-permute-done.8.refs_2_), channel_id=1, source_target_pairs={{0,4},{4,0},{8,12},{12,8},{16,20},{20,16},{24,28},{28,24},{1,5},{5... | collective-permute-start | bytes 393224 | tf_op jit(solution)/shard_map/ppermute | solution.py:334
  96.2 7.3 %collective-permute-start.11 = (f32[64,512]{1,0:T(8,128)S(1)}, f32[64,512]{1,0:T(8,128)S(1)}, u32[]{:S(2)}, u32[]{:S(2)}) collective-permute-start(f32[64,512]{1,0:T(8,128)S(1)} %collective-permute-done.7.refs_1_), channel_id=1, source_target_pairs={{0,4},{4,0},{8,12},{12,8},{16,20},{20,16},{24,28},{28,24},{1,5},{5... | collective-permute-start | bytes 393224 | tf_op jit(solution)/shard_map/ppermute | solution.py:334
  96.6 23.4 %collective-permute-start.24 = (f32[344,256]{1,0:T(8,128)S(1)}, f32[344,256]{1,0:T(8,128)S(1)}, u32[]{:S(2)}, u32[]{:S(2)}) collective-permute-start(f32[344,256]{1,0:T(8,128)S(1)} %add_add_fusion.rest_0_), channel_id=1, source_target_pairs={{1,3},{2,1},{3,2},{5,7},{6,5},{7,6},{9,11},{10,9},{11,10},{13,15},... | collective-permute-start | bytes 1056776 | tf_op jit(solution)/shard_map/ppermute | solution.py:302
  100.0 20.1 %collective-permute-start.23 = (f32[344,256]{1,0:T(8,128)S(1)}, f32[344,256]{1,0:T(8,128)S(1)}, u32[]{:S(2)}, u32[]{:S(2)}) collective-permute-start(f32[344,256]{1,0:T(8,128)S(1)} %add_add_fusion.rest_0_), channel_id=1, source_target_pairs={{1,2},{2,3},{3,1},{5,6},{6,7},{7,5},{9,10},{10,11},{11,9},{13,14},... | collective-permute-start | bytes 1056776 | tf_op jit(solution)/shard_map/ppermute | solution.py:302
  103.6 16.3 %collective-permute-start.25 = (f32[32,2048]{1,0:T(8,128)S(1)}, f32[32,2048]{1,0:T(8,128)S(1)}, u32[]{:S(2)}, u32[]{:S(2)}) collective-permute-start(f32[32,2048]{1,0:T(8,128)S(1)} %get-tuple-element.82), channel_id=1, source_target_pairs={{0,8},{4,12},{8,0},{12,4},{16,24},{20,28},{24,16},{28,20},{1,9},{5... | collective-permute-start | bytes 786440 | tf_op jit(solution)/shard_map/ppermute | solution.py:328
  104.5 15.4 %collective-permute-start.27 = (f32[32,2048]{1,0:T(8,128)S(1)}, f32[32,2048]{1,0:T(8,128)S(1)}, u32[]{:S(2)}, u32[]{:S(2)}) collective-permute-start(f32[32,2048]{1,0:T(8,128)S(1)} %get-tuple-element.83), channel_id=1, source_target_pairs={{0,24},{4,28},{8,16},{12,20},{16,8},{20,12},{24,0},{28,4},{1,25},{... | collective-permute-start | bytes 786440 | tf_op jit(solution)/shard_map/ppermute | solution.py:328
  105.9 14.0 %collective-permute-start.26 = (f32[32,2048]{1,0:T(8,128)S(1)}, f32[32,2048]{1,0:T(8,128)S(1)}, u32[]{:S(2)}, u32[]{:S(2)}) collective-permute-start(f32[32,2048]{1,0:T(8,128)S(1)} %get-tuple-element.84), channel_id=1, source_target_pairs={{0,16},{4,20},{8,24},{12,28},{16,0},{20,4},{24,8},{28,12},{1,17},{... | collective-permute-start | bytes 786440 | tf_op jit(solution)/shard_map/ppermute | solution.py:328
  120.0 28.6 %copy-start.11 = (f32[32,2048]{1,0:T(8,128)}, f32[32,2048]{1,0:T(8,128)S(1)}, u32[]{:S(2)}) copy-start(f32[32,2048]{1,0:T(8,128)S(1)} %add_add_fusion.3.refs_1_.refs_2_) | copy-start | bytes 786436
  120.9 21.1 %copy-start.1 = (s32[6]{0:T(128)S(1)}, s32[6]{0:T(128)}, u32[]{:S(2)}) copy-start(s32[6]{0:T(128)} %stack.27.info_ref) | copy-start | bytes 76
  130.2 4.2 %collective-permute-start.28 = (f32[128,2048]{1,0:T(8,128)}, f32[128,2048]{1,0:T(8,128)S(1)}, u32[]{:S(2)}, u32[]{:S(2)}) collective-permute-start(f32[128,2048]{1,0:T(8,128)} %get-tuple-element.60), channel_id=1, source_target_pairs={{0,4},{4,0},{8,12},{12,8},{16,20},{20,16},{24,28},{28,24},{1,5},{5... | collective-permute-start | bytes 3145736 | tf_op jit(solution)/shard_map/ppermute | solution.py:319
  131.7 8.8 %collective-permute-start.34 = (f32[32,2048]{1,0:T(8,128)S(1)}, f32[32,2048]{1,0:T(8,128)S(1)}, u32[]{:S(2)}, u32[]{:S(2)}) collective-permute-start(f32[32,2048]{1,0:T(8,128)S(1)} %add_add_fusion.3.refs_1_.refs_2_), channel_id=1, source_target_pairs={{0,24},{4,28},{8,16},{12,20},{16,8},{20,12},{24,0},{28,4},{1,25},{... | collective-permute-start | bytes 786440 | tf_op jit(solution)/shard_map/ppermute | solution.py:333
  133.3 15.3 %collective-permute-start.33 = (f32[32,2048]{1,0:T(8,128)S(1)}, f32[32,2048]{1,0:T(8,128)S(1)}, u32[]{:S(2)}, u32[]{:S(2)}) collective-permute-start(f32[32,2048]{1,0:T(8,128)S(1)} %add_add_fusion.3.refs_1_.refs_2_), channel_id=1, source_target_pairs={{0,16},{4,20},{8,24},{12,28},{16,0},{20,4},{24,8},{28,12},{1,17},{... | collective-permute-start | bytes 786440 | tf_op jit(solution)/shard_map/ppermute | solution.py:333
  134.1 16.2 %collective-permute-start.32 = (f32[32,2048]{1,0:T(8,128)S(1)}, f32[32,2048]{1,0:T(8,128)S(1)}, u32[]{:S(2)}, u32[]{:S(2)}) collective-permute-start(f32[32,2048]{1,0:T(8,128)S(1)} %add_add_fusion.3.refs_1_.refs_2_), channel_id=1, source_target_pairs={{0,8},{4,12},{8,0},{12,4},{16,24},{20,28},{24,16},{28,20},{1,9},{5... | collective-permute-start | bytes 786440 | tf_op jit(solution)/shard_map/ppermute | solution.py:333
  135.8 16.2 %collective-permute-start.29 = (f32[32,2048]{1,0:T(8,128)S(1)}, f32[32,2048]{1,0:T(8,128)S(1)}, u32[]{:S(2)}, u32[]{:S(2)}) collective-permute-start(f32[32,2048]{1,0:T(8,128)S(1)} %get-tuple-element.79), channel_id=1, source_target_pairs={{0,8},{4,12},{8,0},{12,4},{16,24},{20,28},{24,16},{28,20},{1,9},{5... | collective-permute-start | bytes 786440 | tf_op jit(solution)/shard_map/ppermute | solution.py:328
  137.0 20.3 %collective-permute-start.31 = (f32[32,2048]{1,0:T(8,128)S(1)}, f32[32,2048]{1,0:T(8,128)S(1)}, u32[]{:S(2)}, u32[]{:S(2)}) collective-permute-start(f32[32,2048]{1,0:T(8,128)S(1)} %get-tuple-element.80), channel_id=1, source_target_pairs={{0,24},{4,28},{8,16},{12,20},{16,8},{20,12},{24,0},{28,4},{1,25},{... | collective-permute-start | bytes 786440 | tf_op jit(solution)/shard_map/ppermute | solution.py:328
  140.5 9.8 %copy-start.16 = (f32[32,2048]{1,0:T(8,128)}, f32[32,2048]{1,0:T(8,128)S(1)}, u32[]{:S(2)}) copy-start(f32[32,2048]{1,0:T(8,128)S(1)} %collective-permute-done.34.refs_4_.refs_5_) | copy-start | bytes 786436
  140.5 17.7 %collective-permute-start.30 = (f32[32,2048]{1,0:T(8,128)S(1)}, f32[32,2048]{1,0:T(8,128)S(1)}, u32[]{:S(2)}, u32[]{:S(2)}) collective-permute-start(f32[32,2048]{1,0:T(8,128)S(1)} %get-tuple-element.81), channel_id=1, source_target_pairs={{0,16},{4,20},{8,24},{12,28},{16,0},{20,4},{24,8},{28,12},{1,17},{... | collective-permute-start | bytes 786440 | tf_op jit(solution)/shard_map/ppermute | solution.py:328
  148.6 18.7 %copy-start.17 = (f32[32,2048]{1,0:T(8,128)}, f32[32,2048]{1,0:T(8,128)S(1)}, u32[]{:S(2)}) copy-start(f32[32,2048]{1,0:T(8,128)S(1)} %collective-permute-done.33.refs_3_.refs_4_) | copy-start | bytes 786436
  148.6 11.3 %collective-permute-start.35 = (f32[32,2048]{1,0:T(8,128)S(1)}, f32[32,2048]{1,0:T(8,128)S(1)}, u32[]{:S(2)}, u32[]{:S(2)}) collective-permute-start(f32[32,2048]{1,0:T(8,128)S(1)} %add_add_fusion.3.refs_1_.refs_2_), channel_id=1, source_target_pairs={{0,4},{4,0},{8,12},{12,8},{16,20},{20,16},{24,28},{28,24},{1,5},{5... | collective-permute-start | bytes 786440 | tf_op jit(solution)/shard_map/ppermute | solution.py:334
  150.3 17.0 %copy-start.18 = (f32[32,2048]{1,0:T(8,128)}, f32[32,2048]{1,0:T(8,128)S(1)}, u32[]{:S(2)}) copy-start(f32[32,2048]{1,0:T(8,128)S(1)} %collective-permute-done.32.refs_2_.refs_3_) | copy-start | bytes 786436
  150.3 10.5 %collective-permute-start.38 = (f32[32,2048]{1,0:T(8,128)S(1)}, f32[32,2048]{1,0:T(8,128)S(1)}, u32[]{:S(2)}, u32[]{:S(2)}) collective-permute-start(f32[32,2048]{1,0:T(8,128)S(1)} %collective-permute-done.34.refs_4_.refs_5_), channel_id=1, source_target_pairs={{0,4},{4,0},{8,12},{12,8},{16,20},{20,16},{24,28},{28,24},{1,5},{5... | collective-permute-start | bytes 786440 | tf_op jit(solution)/shard_map/ppermute | solution.py:334
  152.0 17.3 %collective-permute-start.37 = (f32[32,2048]{1,0:T(8,128)S(1)}, f32[32,2048]{1,0:T(8,128)S(1)}, u32[]{:S(2)}, u32[]{:S(2)}) collective-permute-start(f32[32,2048]{1,0:T(8,128)S(1)} %collective-permute-done.33.refs_3_.refs_4_), channel_id=1, source_target_pairs={{0,4},{4,0},{8,12},{12,8},{16,20},{20,16},{24,28},{28,24},{1,5},{5... | collective-permute-start | bytes 786440 | tf_op jit(solution)/shard_map/ppermute | solution.py:334
  157.3 16.6 %collective-permute-start.36 = (f32[32,2048]{1,0:T(8,128)S(1)}, f32[32,2048]{1,0:T(8,128)S(1)}, u32[]{:S(2)}, u32[]{:S(2)}) collective-permute-start(f32[32,2048]{1,0:T(8,128)S(1)} %collective-permute-done.32.refs_2_.refs_3_), channel_id=1, source_target_pairs={{0,4},{4,0},{8,12},{12,8},{16,20},{20,16},{24,28},{28,24},{1,5},{5... | collective-permute-start | bytes 786440 | tf_op jit(solution)/shard_map/ppermute | solution.py:334
  158.3 11.1 %copy-start.12 = (f32[32,2048]{1,0:T(8,128)}, f32[32,2048]{1,0:T(8,128)S(1)}, u32[]{:S(2)}) copy-start(f32[32,2048]{1,0:T(8,128)S(1)} %add_add_fusion.2.refs_10_) | copy-start | bytes 786436
  158.3 11.8 %collective-permute-start.41 = (f32[32,2048]{1,0:T(8,128)S(1)}, f32[32,2048]{1,0:T(8,128)S(1)}, u32[]{:S(2)}, u32[]{:S(2)}) collective-permute-start(f32[32,2048]{1,0:T(8,128)S(1)} %add_add_fusion.2.refs_10_), channel_id=1, source_target_pairs={{0,24},{4,28},{8,16},{12,20},{16,8},{20,12},{24,0},{28,4},{1,25},{... | collective-permute-start | bytes 786440 | tf_op jit(solution)/shard_map/ppermute | solution.py:333
  159.9 7.4 %copy-start.19 = (f32[32,2048]{1,0:T(8,128)}, f32[32,2048]{1,0:T(8,128)S(1)}, u32[]{:S(2)}) copy-start(f32[32,2048]{1,0:T(8,128)S(1)} %collective-permute-done.35.refs_5_.refs_6_) | copy-start | bytes 786436
  159.9 13.2 %collective-permute-start.40 = (f32[32,2048]{1,0:T(8,128)S(1)}, f32[32,2048]{1,0:T(8,128)S(1)}, u32[]{:S(2)}, u32[]{:S(2)}) collective-permute-start(f32[32,2048]{1,0:T(8,128)S(1)} %add_add_fusion.2.refs_10_), channel_id=1, source_target_pairs={{0,16},{4,20},{8,24},{12,28},{16,0},{20,4},{24,8},{28,12},{1,17},{... | collective-permute-start | bytes 786440 | tf_op jit(solution)/shard_map/ppermute | solution.py:333
  160.7 12.8 %collective-permute-start.39 = (f32[32,2048]{1,0:T(8,128)S(1)}, f32[32,2048]{1,0:T(8,128)S(1)}, u32[]{:S(2)}, u32[]{:S(2)}) collective-permute-start(f32[32,2048]{1,0:T(8,128)S(1)} %add_add_fusion.2.refs_10_), channel_id=1, source_target_pairs={{0,8},{4,12},{8,0},{12,4},{16,24},{20,28},{24,16},{28,20},{1,9},{5... | collective-permute-start | bytes 786440 | tf_op jit(solution)/shard_map/ppermute | solution.py:333
  169.3 18.7 %collective-permute-start.42 = (f32[32,2048]{1,0:T(8,128)S(1)}, f32[32,2048]{1,0:T(8,128)S(1)}, u32[]{:S(2)}, u32[]{:S(2)}) collective-permute-start(f32[32,2048]{1,0:T(8,128)S(1)} %add_add_fusion.2.refs_10_), channel_id=1, source_target_pairs={{0,4},{4,0},{8,12},{12,8},{16,20},{20,16},{24,28},{28,24},{1,5},{5... | collective-permute-start | bytes 786440 | tf_op jit(solution)/shard_map/ppermute | solution.py:334
  170.1 18.0 %copy-start.23 = (f32[32,2048]{1,0:T(8,128)}, f32[32,2048]{1,0:T(8,128)S(1)}, u32[]{:S(2)}) copy-start(f32[32,2048]{1,0:T(8,128)S(1)} %collective-permute-done.41.refs_13_) | copy-start | bytes 786436
  170.1 17.9 %collective-permute-start.45 = (f32[32,2048]{1,0:T(8,128)S(1)}, f32[32,2048]{1,0:T(8,128)S(1)}, u32[]{:S(2)}, u32[]{:S(2)}) collective-permute-start(f32[32,2048]{1,0:T(8,128)S(1)} %collective-permute-done.41.refs_13_), channel_id=1, source_target_pairs={{0,4},{4,0},{8,12},{12,8},{16,20},{20,16},{24,28},{28,24},{1,5},{5... | collective-permute-start | bytes 786440 | tf_op jit(solution)/shard_map/ppermute | solution.py:334
  173.1 15.0 %copy-start.24 = (f32[32,2048]{1,0:T(8,128)}, f32[32,2048]{1,0:T(8,128)S(1)}, u32[]{:S(2)}) copy-start(f32[32,2048]{1,0:T(8,128)S(1)} %collective-permute-done.40.refs_12_) | copy-start | bytes 786436
  173.1 14.9 %collective-permute-start.44 = (f32[32,2048]{1,0:T(8,128)S(1)}, f32[32,2048]{1,0:T(8,128)S(1)}, u32[]{:S(2)}, u32[]{:S(2)}) collective-permute-start(f32[32,2048]{1,0:T(8,128)S(1)} %collective-permute-done.40.refs_12_), channel_id=1, source_target_pairs={{0,4},{4,0},{8,12},{12,8},{16,20},{20,16},{24,28},{28,24},{1,5},{5... | collective-permute-start | bytes 786440 | tf_op jit(solution)/shard_map/ppermute | solution.py:334
  173.6 14.5 %copy-start.25 = (f32[32,2048]{1,0:T(8,128)}, f32[32,2048]{1,0:T(8,128)S(1)}, u32[]{:S(2)}) copy-start(f32[32,2048]{1,0:T(8,128)S(1)} %collective-permute-done.39.refs_11_) | copy-start | bytes 786436
  173.6 14.5 %collective-permute-start.43 = (f32[32,2048]{1,0:T(8,128)S(1)}, f32[32,2048]{1,0:T(8,128)S(1)}, u32[]{:S(2)}, u32[]{:S(2)}) collective-permute-start(f32[32,2048]{1,0:T(8,128)S(1)} %collective-permute-done.39.refs_11_), channel_id=1, source_target_pairs={{0,4},{4,0},{8,12},{12,8},{16,20},{20,16},{24,28},{28,24},{1,5},{5... | collective-permute-start | bytes 786440 | tf_op jit(solution)/shard_map/ppermute | solution.py:334
  (13 other events, 20.4 us)

commit v6 on v4

v6 whole, which is shorter than its diff:
```python
import jax
import jax.numpy as jnp
from jax import lax
from jax.experimental import pallas as pl
from jax.experimental.pallas import tpu as pltpu
from jax.sharding import PartitionSpec as P

PB = 512
NB = 128
F32 = jnp.float32
BF16 = jnp.bfloat16
HIGHEST = lax.Precision.HIGHEST
VMEM = pl.BlockSpec(memory_space=pltpu.VMEM)


ANY = pl.BlockSpec(memory_space=pl.ANY)
SMEM = pl.BlockSpec(memory_space=pltpu.SMEM)
TILE = 512
LIMITS = (4, 8, 6, 16)


def cost(flops):
    return pl.CostEstimate(flops=flops, bytes_accessed=1 << 20, transcendentals=0)


def vmem_limit(mib):
    return pltpu.CompilerParams(vmem_limit_bytes=mib << 20)


def mm(a, b, da, db, precision=None):
    return lax.dot_general(
        a, b, (((da,), (db,)), ((), ())), precision=precision, preferred_element_type=F32
    )


def split(x):
    high = x.astype(BF16)
    return high, (x - high.astype(F32)).astype(BF16)


def diag_block(d_ref, z_ref, f_ref):
    a_all = d_ref[...]
    row = lax.broadcasted_iota(jnp.int32, (NB, NB), 0)
    col = lax.broadcasted_iota(jnp.int32, (NB, NB), 1)
    z_all = jnp.where(row == col, 1.0, 0.0).astype(F32)
    lane = lax.broadcasted_iota(jnp.int32, (1, NB), 1)
    for j in range(0, NB, 4):
        base = (j // 8) * 8
        if a_all.shape[0] != NB - base:
            a_all, z_all = a_all[8:], z_all[8:]
        i, n = j - base, NB - base
        t = [a_all[i + k : i + k + 1, :] for k in range(4)]
        u = [z_all[i + k : i + k + 1, :] for k in range(4)]
        c = [jnp.broadcast_to(a_all[:, j + k : j + k + 1], (n, NB)) for k in range(4)]
        e = {
            (k, m): jnp.broadcast_to(t[k][:, j + m : j + m + 1], (1, NB))
            for k in range(4)
            for m in range(k, 4)
        }
        inv, low = [], {}
        for k in range(4):
            inv.append(1.0 / e[k, k])
            for m in range(k + 1, 4):
                low[m, k] = e[k, m] * inv[k]
            for m in range(k + 1, 4):
                for q in range(m, 4):
                    e[m, q] = e[m, q] - low[m, k] * e[k, q]
        for k in range(4):
            for m in range(k):
                t[k] = t[k] - low[k, m] * t[m]
                u[k] = u[k] - low[k, m] * u[m]
        x, y = [None] * 4, [None] * 4
        for k in reversed(range(4)):
            x[k], y[k] = t[k] * inv[k], u[k] * inv[k]
            for m in range(k + 1, 4):
                x[k] = x[k] - low[m, k] * x[m]
                y[k] = y[k] - low[m, k] * y[m]
        for k in range(4):
            root = lax.rsqrt(e[k, k])
            f_ref[j + k : j + k + 1, :] = jnp.where(lane >= j + k, t[k] * root, 0.0)
            z_ref[j + k : j + k + 1, :] = u[k] * root
        if j + 4 < NB:
            a_all = a_all - ((c[0] * x[0] + c[1] * x[1]) + (c[2] * x[2] + c[3] * x[3]))
            z_all = z_all - ((c[0] * y[0] + c[1] * y[1]) + (c[2] * y[2] + c[3] * y[3]))


def chol_part(info, first, last, pieces=None, places=None, state=None):
    fresh = pieces is not None
    arrays = pieces if fresh else state
    n = arrays[0].shape[1]
    nb = n // NB
    n_in = len(arrays)

    def kernel(info_ref, *refs):
        work, f_out, l_out = refs[n_in : n_in + 3]
        diag, zs, fs = refs[n_in + 3 :]
        if fresh:
            chips = n_in // 2
            for ref, (core, chip) in zip(refs, places):
                h = ref.shape[0]
                off = (info_ref[1] ^ core) * (h * chips) + (info_ref[2] ^ chip) * h
                work[pl.ds(pl.multiple_of(off, 8), h), :] = ref[...]
            f_out[...] = jnp.zeros_like(f_out)
            l_out[...] = jnp.zeros_like(l_out)

        def body(k, carry):
            o = pl.multiple_of(k * NB, NB)
            diag[...] = work[pl.ds(o, NB), pl.ds(o, NB)]
            diag_block(diag, zs, fs)
            for kk in range(first, last):

                @pl.when(k == kk)
                def _():
                    o, e = kk * NB, kk * NB + NB
                    z = zs[...]
                    f_out[o:e, o:e] = fs[...]
                    lk = z
                    if kk > 0:
                        lk = jnp.concatenate([mm(z, l_out[o:e, :o], 1, 0, HIGHEST), z], axis=1)
                    l_out[o:e, :e] = lk
                    if kk < nb - 1:
                        u = mm(z, work[o:e, e:], 1, 0, HIGHEST)
                        f_out[o:e, e:] = u
                        work[e:, e:] -= mm(u, u, 0, 0, HIGHEST)
                        l_out[e:, :e] -= mm(u, lk, 0, 0, HIGHEST)

            return carry

        lax.fori_loop(first, last, body, 0)

    shape = jax.ShapeDtypeStruct((n, n), F32)
    return pl.pallas_call(
        kernel,
        out_shape=(shape, shape, shape),
        in_specs=[SMEM] + [VMEM] * n_in,
        out_specs=(VMEM, VMEM, VMEM),
        scratch_shapes=[pltpu.VMEM((NB, NB), F32)] * 3,
        input_output_aliases={} if fresh else {1: 0, 2: 1, 3: 2},
        compiler_params=vmem_limit(LIMITS[2]),
        cost_estimate=cost(1),
        name="chol_part",
    )(info, *arrays)


def stage(snapshots):
    rows, cols = snapshots.shape

    def kernel(s_ref, h_ref, l_ref):
        for r in range(0, rows, 256):
            h_ref[r : r + 256, :], l_ref[r : r + 256, :] = split(s_ref[r : r + 256, :])

    return pl.pallas_call(
        kernel,
        out_shape=(jax.ShapeDtypeStruct((rows, cols), BF16),) * 2,
        in_specs=[VMEM],
        out_specs=(VMEM, VMEM),
        compiler_params=vmem_limit(LIMITS[0]),
        cost_estimate=cost(10**9),
        name="stage",
    )(snapshots)


def panel_dot(info, own, high, low, parts, size, first, width, scale, ready=None):
    rows, half = own.shape[0], PB // 2
    fresh = ready is None
    extra = [own, *parts] if fresh else [ready]
    n_extra = len(extra)
    tile = min(TILE, width)

    def kernel(info_ref, h_ref, l_ref, *rest):
        extra_refs, rest = rest[:n_extra], rest[n_extra:]
        send_ref, mine_ref = rest[:2]
        ms = rest[-1]
        pt = rest[3] if fresh else extra_refs[0]
        if fresh:
            p_ref = rest[2]

            @pl.when(info_ref[0] == 0)
            def _():
                p_ref[...] = extra_refs[0][...]

            if n_extra > 1:

                @pl.when(info_ref[0] != 0)
                def _():
                    for k, ref in enumerate(extra_refs[1:]):
                        start = pl.multiple_of(info_ref[3 + k], 8)
                        p_ref[pl.ds(start, size), :] = ref[...]

            def turn(i, carry):
                cut = pl.ds(pl.multiple_of(i * 256, 256), 256)
                ph, plow = split(p_ref[cut, :])
                pt[:PB, cut], pt[PB:, cut] = ph.T, plow.T
                return carry

            lax.fori_loop(0, rows // 256, turn, 0)

        def step(i, carry):
            cut = pl.ds(pl.multiple_of(i * tile, tile), tile)
            source = pl.ds(pl.multiple_of(first + i * tile, tile), tile)
            both = mm(pt[...], h_ref[:, source], 1, 0)
            ms[...] = (both[:PB] + (both[PB:] + mm(pt[:PB, :], l_ref[:, source], 1, 0))) * scale
            send_ref[:, cut] = ms[pl.ds(pl.multiple_of((1 - info_ref[1]) * half, half), half), :]
            mine_ref[:, cut] = ms[pl.ds(pl.multiple_of(info_ref[1] * half, half), half), :]
            return carry

        lax.fori_loop(0, width // tile, step, 0)

    out = [jax.ShapeDtypeStruct((half, width), F32)] * 2
    if fresh:
        out += [jax.ShapeDtypeStruct((rows, PB), F32), jax.ShapeDtypeStruct((2 * PB, rows), BF16)]
    return pl.pallas_call(
        kernel,
        out_shape=out,
        in_specs=[SMEM] + [VMEM] * (2 + n_extra),
        out_specs=[VMEM] * len(out),
        scratch_shapes=[pltpu.VMEM((PB, tile), F32)],
        compiler_params=vmem_limit(LIMITS[1]),
        cost_estimate=cost(6 * rows * PB * width),
        name="panel_dot",
    )(info, high, low, *extra)


def basis(panel, linv):
    rows = panel.shape[0]

    def kernel(p_ref, l_ref, b_ref, b3, l3):
        lh, ll = split(l_ref[...])
        l3[:, :PB], l3[:, PB : 2 * PB], l3[:, 2 * PB :] = lh, lh, ll

        def step(i, carry):
            cut = pl.ds(pl.multiple_of(i * 256, 256), 256)
            lh, ll = l3[:, :PB], l3[:, 2 * PB :]
            ph, plow = split(p_ref[cut, :])
            b = mm(ph, lh, 1, 1) + (mm(ph, ll, 1, 1) + mm(plow, lh, 1, 1))
            b_ref[cut, :] = b
            bh, bl = split(b)
            b3[cut, :PB], b3[cut, PB : 2 * PB], b3[cut, 2 * PB :] = bh, bh, bl
            return carry

        lax.fori_loop(0, rows // 256, step, 0)

    return pl.pallas_call(
        kernel,
        out_shape=(
            jax.ShapeDtypeStruct((rows, PB), F32),
            jax.ShapeDtypeStruct((rows, 3 * PB), BF16),
            jax.ShapeDtypeStruct((PB, 3 * PB), BF16),
        ),
        in_specs=[VMEM] * 2,
        out_specs=(VMEM,) * 3,
        compiler_params=vmem_limit(LIMITS[2]),
        cost_estimate=cost(6 * rows * PB * PB),
        name="basis",
    )(panel, linv)


def finish(info, snapshots, b, b3, l3, factor, pieces, places, first, width, done=None):
    rows, cols = snapshots.shape
    tile = min(TILE, width)
    n_pieces, chips = len(pieces), len(pieces) // 2
    later = [] if done is None else list(done)

    def kernel(info_ref, s_ref, b_ref, b3_ref, l3_ref, f_ref, *rest):
        m_refs, rest = rest[:n_pieces], rest[n_pieces + len(later) :]
        up_hbm, co_hbm, ms, m3, p3, up, co, sems = rest
        copies = []
        for t in range(width // tile):
            slot, cut = t % 2, pl.ds(t * tile, tile)
            goal = pl.ds(first + t * tile, tile)
            if t >= 2:
                for copy in copies[t - 2]:
                    copy.wait()
            for ref, (core, chip) in zip(m_refs, places):
                h = ref.shape[0]
                off = (info_ref[1] ^ core) * (h * chips) + (info_ref[2] ^ chip) * h
                ms[pl.ds(pl.multiple_of(off, 8), h), :] = ref[:, cut]
            mh, ml = split(ms[...])
            m3[:PB, :], m3[PB : 2 * PB, :], m3[2 * PB :, :] = mh, ml, mh
            proj = mm(l3_ref[...], m3[...], 1, 0)
            ph, plow = split(proj)
            p3[:PB, :], p3[PB : 2 * PB, :], p3[2 * PB :, :] = ph, plow, ph
            co[slot] = proj
            up[slot] = s_ref[:, goal] - mm(b3_ref[...], p3[...], 1, 0)
            if first + t * tile < PB:

                @pl.when(info_ref[0] == 0)
                def _():
                    co[slot] = f_ref[:, goal]
                    up[slot] = b_ref[:, goal]

            pair = (
                pltpu.make_async_copy(up.at[slot], up_hbm.at[:, goal], sems.at[0, slot]),
                pltpu.make_async_copy(co.at[slot], co_hbm.at[:, goal], sems.at[1, slot]),
            )
            for copy in pair:
                copy.start()
            copies.append(pair)
        for pair in copies[-2:]:
            for copy in pair:
                copy.wait()

    operands = [info, snapshots, b, b3, l3, factor, *pieces, *later]
    return pl.pallas_call(
        kernel,
        out_shape=(
            jax.ShapeDtypeStruct((rows, cols), F32),
            jax.ShapeDtypeStruct((PB, cols), F32),
        ),
        in_specs=[SMEM] + [VMEM] * (5 + n_pieces) + [ANY] * len(later),
        out_specs=(ANY, ANY),
        scratch_shapes=[
            pltpu.VMEM((PB, tile), F32),
            pltpu.VMEM((3 * PB, tile), BF16),
            pltpu.VMEM((3 * PB, tile), BF16),
            pltpu.VMEM((2, rows, tile), F32),
            pltpu.VMEM((2, PB, tile), F32),
            pltpu.SemaphoreType.DMA((2, 2)),
        ],
        input_output_aliases={len(operands) - 2: 0, len(operands) - 1: 1} if later else {},
        compiler_params=vmem_limit(LIMITS[3]),
        cost_estimate=cost(10**10),
        name="finish",
    )(*operands)


def part_size(rows, parts):
    return -(-rows // (8 * parts)) * 8


def spread_out(x, n):
    rows, parts = x.shape[0], n - 1
    size = part_size(rows, parts)
    got = []
    for k in reversed(range(parts)):
        start = min(k * size, rows - size)
        got.append(lax.ppermute(x[start : start + size], "cols", [(0, k + 1)]))
    return sum(got[1:], got[0])


def spread_round(mine, n):
    got, parts = [mine], n - 1
    for k in range(1, parts):
        pairs = [(1 + i, 1 + (i + k) % parts) for i in range(parts)]
        got.append(lax.ppermute(mine, "cols", pairs))
    return got


def after(x, *others):
    return lax.optimization_barrier((x, others))[0]


def swap(n, k):
    return [(i, i ^ k) for i in range(n)]


def take(a, start, size):
    return lax.dynamic_slice_in_dim(a, start, size, 0)


def join_cores(send, mine, n):
    return mine + lax.ppermute(send, "rows", swap(n, 1))


def scatter_chips(mine, n):
    chips = n // 2
    chip = lax.axis_index("rows") >> 1
    piece = mine.shape[0] // chips
    own = take(mine, chip * piece, piece)
    for k in range(1, chips):
        own = own + lax.ppermute(take(mine, (chip ^ k) * piece, piece), "rows", swap(n, 2 * k))
    return own


def gather_rows(own, n):
    got = [own] + [lax.ppermute(own, "rows", swap(n, 2 * k)) for k in range(1, n // 2)]
    other = [lax.ppermute(g, "rows", swap(n, 1)) for g in got]
    return got + other, [(0, k) for k in range(n // 2)] + [(1, k) for k in range(n // 2)]


def shards(snapshots):
    rows_dev, cols_dev = snapshots.shape
    n_rows, n_cols = lax.axis_size("rows"), lax.axis_size("cols")
    total_rows = rows_dev * n_rows
    z, index = lax.axis_index("cols"), lax.axis_index("rows")
    core = index & 1
    parts = n_cols - 1
    size = part_size(rows_dev, parts)
    starts = [jnp.minimum(((z - 1 - k) % parts) * size, rows_dev - size) for k in range(parts)]
    info = jnp.stack([z, core, index >> 1] + starts).astype(jnp.int32)
    half = PB // 2
    panel = snapshots[:, :PB]

    mine = spread_out(panel, n_cols)
    gram = mm(panel, panel, 0, 0, HIGHEST) / total_rows
    joined = join_cores(take(gram, (1 - core) * half, half), take(gram, core * half, half), n_rows)
    high, low = stage(after(snapshots, joined))
    share = scatter_chips(joined, n_rows)
    far = [lax.ppermute(share, "cols", [(0, k)]) for k in reversed(range(1, n_cols))]
    share = jnp.where(z == 0, share, sum(far, jnp.zeros_like(share)))
    grams, places = gather_rows(share, n_rows)
    got = spread_round(mine, n_cols)
    _, factor, linv = chol_part(info, 0, PB // NB, pieces=after(grams, mine, high), places=places)

    width = cols_dev // 2
    dot = lambda got, first, ready=None: panel_dot(
        info, panel, high, low, got, size, first, width, 1.0 / total_rows, ready
    )
    send, keep, whole, turned = dot(after(got, linv), 0)
    joined1 = join_cores(send, keep, n_rows)
    send, keep = dot(None, width, turned)
    joined2 = join_cores(send, keep, n_rows)
    own1 = scatter_chips(joined1, n_rows)
    own2 = scatter_chips(joined2, n_rows)
    b, b3, l3 = basis(after(whole, joined2), linv)
    pieces1, _ = gather_rows(own1, n_rows)
    pieces2, _ = gather_rows(own2, n_rows)
    done = finish(
        info, snapshots, b, b3, after(l3, own2), factor, pieces1, places, 0, width
    )
    return finish(info, snapshots, b, b3, l3, factor, pieces2, places, width, width, done)


def solution(mesh):
    in_specs = (P("rows", "cols"),)
    out_specs = (P("rows", "cols"), P(None, "cols"))
    return jax.shard_map(shards, mesh=mesh, in_specs=in_specs, out_specs=out_specs, check_vma=False)
```

time: 207 us -> 198 us (0.957)
  Pallas kernels: 64.7 us -> 56.6 us
  other arithmetic: 8.46 us -> 2.13 us
  starting transfers between devices: 65.7 us -> 71.5 us
    ppermute x4 -> x2, waiting for transfers between devices: 22.4 us -> 0.01 us  [spread_round(): got.append(lax.ppermute(mine, 'cols', pairs))]
    ppermute x9, waiting for transfers between devices: 16.6 us -> 31.7 us  [scatter_chips(): lax.ppermute(take(mine, (chip ^ k) * piece, piece), 'rows', swap(n, 2 * k))]
    ppermute x4 -> x2, starting transfers between devices: 26.3 us -> 34.8 us  [spread_round(): got.append(lax.ppermute(mine, 'cols', pairs))]
    ppermute x9, waiting for transfers between devices: 6.28 us -> 13.2 us  [gather_rows(): lax.ppermute(own, 'rows', swap(n, 2 * k))]
    pallas_call x6 -> x5, Pallas kernels: 45.5 us -> 41.3 us  [the longest x1 27 us: chol_part(): pl.pallas_call(kernel, out_shape=(shape, shape, shape), in_specs=[SMEM] +...]
    pallas_call x1 -> x2, Pallas kernels: 19.2 us -> 15.4 us  [finish(): pl.pallas_call(kernel, out_shape=(jax.ShapeDtypeStruct((rows, cols), F32)...]
    add x3, other arithmetic: 3.95 us -> 0.39 us  [join_cores(): return mine + lax.ppermute(send, 'rows', swap(n, 1))]
    ppermute x6 -> x3, starting transfers between devices: 6.74 us -> 4.34 us  [spread_out(): got.append(lax.ppermute(x[start:start + size], 'cols', [(0, k + 1)]))]
  transfers between devices with their start and end apart: 46 -> 41, of which waited for: 11 -> 14; matrix products, arithmetic and copies ran while one was open for 7% -> 4% of each run, Pallas kernels for 13% -> 20%
where the time goes in v6:
time: 198 us; the launch traced here: 196 us
  starting transfers between devices  71.5 us (36%)
  Pallas kernels  56.6 us (29%)
  waiting for transfers between devices  49.1 us (25%)
  local copies, waits for them, and re-layouts  9.58 us (5%)
  matrix products  5.72 us (3%)
  other arithmetic  2.13 us (1%)
    ppermute x2, starting transfers between devices, spread_round(): got.append(lax.ppermute(mine, 'cols', pairs))  34.8 us
    ppermute x9, waiting for transfers between devices, scatter_chips(): lax.ppermute(take(mine, (chip ^ k) * piece, piece), 'rows', swap(n, 2 * k))  31.7 us
    pallas_call x1, Pallas kernels, chol_part(): pl.pallas_call(kernel, out_shape=(shape, shape, shape), in_specs=[SMEM] +...  27 us
    pallas_call x2, Pallas kernels, finish(): pl.pallas_call(kernel, out_shape=(jax.ShapeDtypeStruct((rows, cols), F32)...  15.4 us
    ppermute x9, waiting for transfers between devices, gather_rows(): lax.ppermute(own, 'rows', swap(n, 2 * k))  13.2 us
    ppermute x12, starting transfers between devices, gather_rows(): other = [lax.ppermute(g, 'rows', swap(n, 1)) for g in got]  10.6 us
    pallas_call x2, Pallas kernels, panel_dot(): pl.pallas_call(kernel, out_shape=out, in_specs=[SMEM] + [VMEM] * (2 + n_e...  10.3 us
    ppermute x9, starting transfers between devices, scatter_chips(): lax.ppermute(take(mine, (chip ^ k) * piece, piece), 'rows', swap(n, 2 * k))  10.2 us
  transfers between devices with their start and end apart: 41, of which 14 were waited for; matrix products, arithmetic and copies ran while one was open for 4% of the time, Pallas kernels for 20%

profile of v6, /device:TPU:17, one launch (start us, length us, event | category | flops | bytes accessed | tf_op | source)
XLA Modules:
  0.0 195.8 jit_solution(2865949806472507177)
XLA Ops:
  0.6 5.7 %convolution_multiply_fusion = f32[512,512]{1,0:T(8,128)S(1)} fusion(f32[1024,2048]{1,0:T(8,128)} %s_ref.4), kind=kOutput, calls=%fused_computation | convolution fusion | flops 3221487616 | bytes 3145728 | tf_op jit(solution)/shard_map/dot_general | solution.py:31
  6.4 0.7 collective-permute-start
  7.2 2.8 %fusion.1 = (f32[344,512]{1,0:T(8,128)}, f32[344,512]{1,0:T(8,128)}, f32[344,512]{1,0:T(8,128)S(1)}) fusion(f32[1024,2048]{1,0:T(8,128)} %s_ref.4), kind=kLoop, calls=%fused_computation.18 | loop fusion | bytes 4227072 | tf_op jit(solution)/shard_map/slice | solution.py:337
  9.9 1.3 collective-permute-start.2
  11.2 1.5 collective-permute-start.3
  12.8 1.5 collective-permute-start.1
  14.4 1.3 collective-permute-start.6
  15.7 1.2 collective-permute-start.8
  16.9 2.7 %collective-permute-done.6 = f32[64,512]{1,0:T(8,128)S(1)} collective-permute-done((f32[64,512]{1,0:T(8,128)S(1)}, f32[64,512]{1,0:T(8,128)S(1)}, u32[]{:S(2)}, u32[]{:S(2)}) %collective-permute-start.6) | collective-permute-done | bytes 131104 | tf_op jit(solution)/shard_map/ppermute | solution.py:371
  19.6 1.2 collective-permute-start.7
  20.9 2.5 %collective-permute-done.8 = f32[64,512]{1,0:T(8,128)S(1)} collective-permute-done((f32[64,512]{1,0:T(8,128)S(1)}, f32[64,512]{1,0:T(8,128)S(1)}, u32[]{:S(2)}, u32[]{:S(2)}) %collective-permute-start.8) | collective-permute-done | bytes 131104 | tf_op jit(solution)/shard_map/ppermute | solution.py:371
  23.4 3.0 %collective-permute-done.7 = f32[64,512]{1,0:T(8,128)S(1)} collective-permute-done((f32[64,512]{1,0:T(8,128)S(1)}, f32[64,512]{1,0:T(8,128)S(1)}, u32[]{:S(2)}, u32[]{:S(2)}) %collective-permute-start.7) | collective-permute-done | bytes 131104 | tf_op jit(solution)/shard_map/ppermute | solution.py:371
  26.4 0.7 collective-permute-start.11
  27.1 1.3 collective-permute-start.10
  28.4 1.9 collective-permute-done.2
  30.3 0.7 collective-permute-start.9
  31.0 1.5 add_add_fusion.rest_1_
  32.6 16.7 %collective-permute-start.5 = (f32[344,512]{1,0:T(8,128)S(1)}, f32[344,512]{1,0:T(8,128)S(1)}, u32[]{:S(2)}, u32[]{:S(2)}) collective-permute-start(f32[344,512]{1,0:T(8,128)S(1)} %add_add_fusion.rest_1_), channel_id=1, source_target_pairs={{1,3},{2,1},{3,2},{5,7},{6,5},{7,6},{9,11},{10,9},{11,10},{13,15},... | collective-permute-start | bytes 2113544 | tf_op jit(solution)/shard_map/ppermute | solution.py:345
  49.3 18.1 %collective-permute-start.4 = (f32[344,512]{1,0:T(8,128)S(1)}, f32[344,512]{1,0:T(8,128)}, u32[]{:S(2)}, u32[]{:S(2)}) collective-permute-start(f32[344,512]{1,0:T(8,128)S(1)} %add_add_fusion.rest_1_), channel_id=1, source_target_pairs={{1,2},{2,3},{3,1},{5,6},{6,7},{7,5},{9,10},{10,11},{11,9},{13,14},... | collective-permute-start | bytes 2113544 | tf_op jit(solution)/shard_map/ppermute | solution.py:345
  67.5 1.5 collective-permute-start.15
  69.0 2.2 %collective-permute-start.14 = (f32[64,512]{1,0:T(8,128)S(1)}, f32[64,512]{1,0:T(8,128)}, u32[]{:S(2)}, u32[]{:S(2)}) collective-permute-start(f32[64,512]{1,0:T(8,128)S(1)} %add_select_fusion.refs_0_), channel_id=1, source_target_pairs={{0,24},{4,28},{8,16},{12,20},{16,8},{20,12},{24,0},{28,4},{1,25},{... | collective-permute-start | bytes 393224 | tf_op jit(solution)/shard_map/ppermute | solution.py:376
  71.2 0.2 collective-permute-start.13
  71.4 0.7 copy-done.3
  72.1 0.3 collective-permute-start.12
  72.3 0.7 copy-done.1
  73.0 2.1 %collective-permute-done.14.refs_3_ = f32[64,512]{1,0:T(8,128)} collective-permute-done((f32[64,512]{1,0:T(8,128)S(1)}, f32[64,512]{1,0:T(8,128)}, u32[]{:S(2)}, u32[]{:S(2)}) %collective-permute-start.14) | collective-permute-done | bytes 131104 | tf_op jit(solution)/shard_map/ppermute | solution.py:376
  75.1 1.0 collective-permute-start.18
  76.0 2.2 %collective-permute-done.13.refs_2_ = f32[64,512]{1,0:T(8,128)} collective-permute-done((f32[64,512]{1,0:T(8,128)S(1)}, f32[64,512]{1,0:T(8,128)}, u32[]{:S(2)}, u32[]{:S(2)}) %collective-permute-start.13) | collective-permute-done | bytes 131104 | tf_op jit(solution)/shard_map/ppermute | solution.py:376
  78.3 0.5 collective-permute-start.17
  78.8 1.8 slice.15.rest_0_
  80.7 3.4 %copy-done = f32[1024,2048]{1,0:T(8,128)S(1)} copy-done((f32[1024,2048]{1,0:T(8,128)S(1)}, f32[1024,2048]{1,0:T(8,128)}, u32[]{:S(2)}) %copy-start) | copy-done | bytes 8388632
  84.1 1.2 stage.1
  85.4 27.0 %chol_part.1 = (f32[512,512]{1,0:T(8,128)}, f32[512,512]{1,0:T(8,128)S(1)}, f32[512,512]{1,0:T(8,128)S(1)}) custom-call(s32[6]{0:T(128)S(1)} %stack.27.info_ref, f32[64,512]{1,0:T(8,128)S(1)} %copy-done.2, f32[64,512]{1,0:T(8,128)} %collective-permute-done.12.refs_1_, f32[64,512]{1,0:T(8,128)} %collective-permute-done.13.refs_2_, ...), custom_call_target="tpu_custom_call" | custom-call | flops 1 | bytes 1048576 | tf_op jit(solution)/shard_map/chol_part/pallas_call | solution.py:132
  112.4 6.1 %panel_dot.2 = (f32[256,1024]{1,0:T(8,128)S(1)}, f32[256,1024]{1,0:T(8,128)S(1)}, f32[1024,512]{1,0:T(8,128)S(1)}, bf16[1024,1024]{1,0:T(8,128)(2,1)S(1)}) custom-call(s32[6]{0:T(128)S(1)} %stack.27.info_ref, bf16[1024,2048]{1,0:T(8,128)(2,1)S(1)} %get-tuple-element.32.h_ref, bf16[1024,2048]{1,0:T(8,128)(2,1)S(1)} %get-tuple-element.33.l_ref, ...), custom_call_target="tpu_custom_call" | custom-call | flops 3221225472 | bytes 1048576 | tf_op jit(solution)/shard_map/panel_dot/pallas_call | solution.py:212
  118.4 4.3 %panel_dot.3 = (f32[256,1024]{1,0:T(8,128)S(1)}, f32[256,1024]{1,0:T(8,128)S(1)}) custom-call(s32[6]{0:T(128)S(1)} %stack.27.info_ref, bf16[1024,2048]{1,0:T(8,128)(2,1)S(1)} %get-tuple-element.32.h_ref, bf16[1024,2048]{1,0:T(8,128)(2,1)S(1)} %get-tuple-element.33.l_ref, bf16[1024,1024]{1,0:T(8,128)(2,1)S(1)} %get-tuple-element.47.rest_0_), custom_call_target="tpu_custom_call" | custom-call | flops 3221225472 | bytes 1048576 | tf_op jit(solution)/shard_map/panel_dot/pallas_call | solution.py:212
  122.7 0.5 collective-permute-start.19
  123.3 2.2 %collective-permute-done.19 = f32[256,1024]{1,0:T(8,128)S(1)} collective-permute-done((f32[256,1024]{1,0:T(8,128)S(1)}, f32[256,1024]{1,0:T(8,128)S(1)}, u32[]{:S(2)}, u32[]{:S(2)}) %collective-permute-start.19) | collective-permute-done | bytes 1048608 | tf_op jit(solution)/shard_map/ppermute | solution.py:362
  125.5 0.2 add.108
  125.7 1.3 collective-permute-start.20
  127.0 1.2 collective-permute-start.22
  128.2 0.2 collective-permute-start.21
  128.7 1.3 collective-permute-start.31
  130.0 1.2 collective-permute-start.33
  131.2 2.1 %collective-permute-done.20 = f32[64,1024]{1,0:T(8,128)S(1)} collective-permute-done((f32[64,1024]{1,0:T(8,128)S(1)}, f32[64,1024]{1,0:T(8,128)S(1)}, u32[]{:S(2)}, u32[]{:S(2)}) %collective-permute-start.20) | collective-permute-done | bytes 262176 | tf_op jit(solution)/shard_map/ppermute | solution.py:371
  133.3 1.2 collective-permute-start.32
  134.6 5.4 %collective-permute-done.22 = f32[64,1024]{1,0:T(8,128)S(1)} collective-permute-done((f32[64,1024]{1,0:T(8,128)S(1)}, f32[64,1024]{1,0:T(8,128)S(1)}, u32[]{:S(2)}, u32[]{:S(2)}) %collective-permute-start.22) | collective-permute-done | bytes 262176 | tf_op jit(solution)/shard_map/ppermute | solution.py:371
  140.0 1.2 collective-permute-start.25
  141.2 0.5 collective-permute-start.24
  141.8 2.8 %collective-permute-done.31 = f32[64,1024]{1,0:T(8,128)S(1)} collective-permute-done((f32[64,1024]{1,0:T(8,128)S(1)}, f32[64,1024]{1,0:T(8,128)S(1)}, u32[]{:S(2)}, u32[]{:S(2)}) %collective-permute-start.31) | collective-permute-done | bytes 262176 | tf_op jit(solution)/shard_map/ppermute | solution.py:371
  144.6 6.6 %collective-permute-done.33 = f32[64,1024]{1,0:T(8,128)S(1)} collective-permute-done((f32[64,1024]{1,0:T(8,128)S(1)}, f32[64,1024]{1,0:T(8,128)S(1)}, u32[]{:S(2)}, u32[]{:S(2)}) %collective-permute-start.33) | collective-permute-done | bytes 262176 | tf_op jit(solution)/shard_map/ppermute | solution.py:371
  151.2 6.5 %collective-permute-done.32 = f32[64,1024]{1,0:T(8,128)S(1)} collective-permute-done((f32[64,1024]{1,0:T(8,128)S(1)}, f32[64,1024]{1,0:T(8,128)S(1)}, u32[]{:S(2)}, u32[]{:S(2)}) %collective-permute-start.32) | collective-permute-done | bytes 262176 | tf_op jit(solution)/shard_map/ppermute | solution.py:371
  157.8 1.2 collective-permute-start.36
  159.0 0.5 collective-permute-start.35
  159.6 1.0 collective-permute-start.34
  160.5 0.5 collective-permute-start.23
  161.0 6.3 %collective-permute-done.24.rest_2_ = f32[64,1024]{1,0:T(8,128)S(1)} collective-permute-done((f32[64,1024]{1,0:T(8,128)S(1)}, f32[64,1024]{1,0:T(8,128)S(1)}, u32[]{:S(2)}, u32[]{:S(2)}) %collective-permute-start.24) | collective-permute-done | bytes 262176 | tf_op jit(solution)/shard_map/ppermute | solution.py:376
  167.3 4.7 %collective-permute-start.37 = (f32[64,1024]{1,0:T(8,128)S(1)}, f32[64,1024]{1,0:T(8,128)S(1)}, u32[]{:S(2)}, u32[]{:S(2)}) collective-permute-start(f32[64,1024]{1,0:T(8,128)S(1)} %add_add_fusion.1.rest_0_), channel_id=1, source_target_pairs={{0,4},{4,0},{8,12},{12,8},{16,20},{20,16},{24,28},{28,24},{1,5},{5... | collective-permute-start | bytes 786440 | tf_op jit(solution)/shard_map/ppermute | solution.py:377
  172.0 2.6 %collective-permute-done.35.rest_2_ = f32[64,1024]{1,0:T(8,128)S(1)} collective-permute-done((f32[64,1024]{1,0:T(8,128)S(1)}, f32[64,1024]{1,0:T(8,128)S(1)}, u32[]{:S(2)}, u32[]{:S(2)}) %collective-permute-start.35) | collective-permute-done | bytes 262176 | tf_op jit(solution)/shard_map/ppermute | solution.py:376
  174.6 1.7 collective-permute-start.39
  176.3 2.7 %basis.1 = (f32[1024,512]{1,0:T(8,128)S(1)}, bf16[1024,1536]{1,0:T(8,128)(2,1)S(1)}, bf16[512,1536]{1,0:T(8,128)(2,1)S(1)}) custom-call(f32[1024,512]{1,0:T(8,128)S(1)} %get-tuple-element.50.p_ref, f32[512,512]{1,0:T(8,128)S(1)} %get-tuple-element.42.l_ref), custom_call_target="tpu_custom_call" | custom-call | flops 1610612736 | bytes 1048576 | tf_op jit(solution)/shard_map/basis/pallas_call | solution.py:243
  179.0 0.6 collective-permute-start.26
  179.7 0.4 collective-permute-start.28
  180.2 7.8 %finish.2 = (f32[1024,2048]{1,0:T(8,128)}, f32[512,2048]{1,0:T(8,128)}) custom-call(s32[6]{0:T(128)S(1)} %stack.27.info_ref, f32[1024,2048]{1,0:T(8,128)S(1)} %bitcast.7, f32[1024,512]{1,0:T(8,128)S(1)} %get-tuple-element.51.b_ref, bf16[1024,1536]{1,0:T(8,128)(2,1)S(1)} %get-tuple-element.52.b3_ref, bf16[512,1536]{1,0:T(8,128)(2,1)S(1)} %get-tuple-element.55.l3_ref, ...), custom_call_target="tpu_custom_call" | custom-call | flops 10000000000 | bytes 1048576 | tf_op jit(solution)/shard_map/finish/pallas_call | solution.py:304
  188.1 7.6 %finish.3 = (f32[1024,2048]{1,0:T(8,128)}, f32[512,2048]{1,0:T(8,128)}) custom-call(s32[6]{0:T(128)S(1)} %stack.27.info_ref, f32[1024,2048]{1,0:T(8,128)S(1)} %bitcast.7, f32[1024,512]{1,0:T(8,128)S(1)} %get-tuple-element.51.b_ref, bf16[1024,1536]{1,0:T(8,128)(2,1)S(1)} %get-tuple-element.52.b3_ref, ...), custom_call_target="tpu_custom_call", output_to_operand_aliasing={{0}: (14, {}), {1}: (15, {})} | custom-call | flops 10000000000 | bytes 1048576 | tf_op jit(solution)/shard_map/finish/pallas_call | solution.py:304
  (56 shorter events, 1.2 us)
Async XLA Ops:
  6.4 7.9 %collective-permute-start = (f32[256,512]{1,0:T(8,128)S(1)}, f32[256,512]{1,0:T(8,128)S(1)}, u32[]{:S(2)}, u32[]{:S(2)}) collective-permute-start(f32[256,512]{1,0:T(8,128)S(1)} %constant_dynamic-slice_fusion.9), channel_id=1, source_target_pairs={{0,4},{4,0},{8,12},{12,8},{16,20},{20,16},{24,28},{28,24},{1,5},{5... | collective-permute-start | bytes 1572872 | tf_op jit(solution)/shard_map/ppermute | solution.py:362
  9.9 20.4 %collective-permute-start.2 = (f32[344,512]{1,0:T(8,128)}, f32[344,512]{1,0:T(8,128)S(1)}, u32[]{:S(2)}, u32[]{:S(2)}) collective-permute-start(f32[344,512]{1,0:T(8,128)} %get-tuple-element.60), channel_id=1, source_target_pairs={{0,2},{4,6},{8,10},{12,14},{16,18},{20,22},{24,26},{28,30}} | collective-permute-start | bytes 2113544 | tf_op jit(solution)/shard_map/ppermute | solution.py:337
  11.2 19.8 %collective-permute-start.3 = (f32[344,512]{1,0:T(8,128)}, f32[344,512]{1,0:T(8,128)}, u32[]{:S(2)}, u32[]{:S(2)}) collective-permute-start(f32[344,512]{1,0:T(8,128)} %get-tuple-element.61), channel_id=1, source_target_pairs={{0,1},{4,5},{8,9},{12,13},{16,17},{20,21},{24,25},{28,29}} | collective-permute-start | bytes 2113544 | tf_op jit(solution)/shard_map/ppermute | solution.py:337
  12.8 18.2 %collective-permute-start.1 = (f32[344,512]{1,0:T(8,128)S(1)}, f32[344,512]{1,0:T(8,128)}, u32[]{:S(2)}, u32[]{:S(2)}) collective-permute-start(f32[344,512]{1,0:T(8,128)S(1)} %get-tuple-element.62), channel_id=1, source_target_pairs={{0,3},{4,7},{8,11},{12,15},{16,19},{20,23},{24,27},{28,31}} | collective-permute-start | bytes 2113544 | tf_op jit(solution)/shard_map/ppermute | solution.py:337
  14.4 5.2 %collective-permute-start.6 = (f32[64,512]{1,0:T(8,128)S(1)}, f32[64,512]{1,0:T(8,128)S(1)}, u32[]{:S(2)}, u32[]{:S(2)}) collective-permute-start(f32[64,512]{1,0:T(8,128)S(1)} %get-tuple-element.69), channel_id=1, source_target_pairs={{0,8},{4,12},{8,0},{12,4},{16,24},{20,28},{24,16},{28,20},{1,9},{5... | collective-permute-start | bytes 393224 | tf_op jit(solution)/shard_map/ppermute | solution.py:371
  15.7 7.7 %collective-permute-start.8 = (f32[64,512]{1,0:T(8,128)S(1)}, f32[64,512]{1,0:T(8,128)S(1)}, u32[]{:S(2)}, u32[]{:S(2)}) collective-permute-start(f32[64,512]{1,0:T(8,128)S(1)} %get-tuple-element.70), channel_id=1, source_target_pairs={{0,24},{4,28},{8,16},{12,20},{16,8},{20,12},{24,0},{28,4},{1,25},{... | collective-permute-start | bytes 393224 | tf_op jit(solution)/shard_map/ppermute | solution.py:371
  19.6 6.8 %collective-permute-start.7 = (f32[64,512]{1,0:T(8,128)S(1)}, f32[64,512]{1,0:T(8,128)S(1)}, u32[]{:S(2)}, u32[]{:S(2)}) collective-permute-start(f32[64,512]{1,0:T(8,128)S(1)} %get-tuple-element.71), channel_id=1, source_target_pairs={{0,16},{4,20},{8,24},{12,28},{16,0},{20,4},{24,8},{28,12},{1,17},{... | collective-permute-start | bytes 393224 | tf_op jit(solution)/shard_map/ppermute | solution.py:371
  26.4 41.0 %collective-permute-start.11 = (f32[64,512]{1,0:T(8,128)S(1)}, f32[64,512]{1,0:T(8,128)S(1)}, u32[]{:S(2)}, u32[]{:S(2)}) collective-permute-start(f32[64,512]{1,0:T(8,128)S(1)} %add_add_fusion.3), channel_id=1, source_target_pairs={{0,1},{4,5},{8,9},{12,13},{16,17},{20,21},{24,25},{28,29}} | collective-permute-start | bytes 393224 | tf_op jit(solution)/shard_map/ppermute | solution.py:399
  27.1 40.3 %collective-permute-start.10 = (f32[64,512]{1,0:T(8,128)S(1)}, f32[64,512]{1,0:T(8,128)S(1)}, u32[]{:S(2)}, u32[]{:S(2)}) collective-permute-start(f32[64,512]{1,0:T(8,128)S(1)} %add_add_fusion.3), channel_id=1, source_target_pairs={{0,2},{4,6},{8,10},{12,14},{16,18},{20,22},{24,26},{28,30}} | collective-permute-start | bytes 393224 | tf_op jit(solution)/shard_map/ppermute | solution.py:399
  30.3 37.1 %collective-permute-start.9 = (f32[64,512]{1,0:T(8,128)S(1)}, f32[64,512]{1,0:T(8,128)S(1)}, u32[]{:S(2)}, u32[]{:S(2)}) collective-permute-start(f32[64,512]{1,0:T(8,128)S(1)} %add_add_fusion.3), channel_id=1, source_target_pairs={{0,3},{4,7},{8,11},{12,15},{16,19},{20,23},{24,27},{28,31}} | collective-permute-start | bytes 393224 | tf_op jit(solution)/shard_map/ppermute | solution.py:399
  32.6 79.8 %collective-permute-start.5 = (f32[344,512]{1,0:T(8,128)S(1)}, f32[344,512]{1,0:T(8,128)S(1)}, u32[]{:S(2)}, u32[]{:S(2)}) collective-permute-start(f32[344,512]{1,0:T(8,128)S(1)} %add_add_fusion.rest_1_), channel_id=1, source_target_pairs={{1,3},{2,1},{3,2},{5,7},{6,5},{7,6},{9,11},{10,9},{11,10},{13,15},... | collective-permute-start | bytes 2113544 | tf_op jit(solution)/shard_map/ppermute | solution.py:345
  49.3 63.1 %collective-permute-start.4 = (f32[344,512]{1,0:T(8,128)S(1)}, f32[344,512]{1,0:T(8,128)}, u32[]{:S(2)}, u32[]{:S(2)}) collective-permute-start(f32[344,512]{1,0:T(8,128)S(1)} %add_add_fusion.rest_1_), channel_id=1, source_target_pairs={{1,2},{2,3},{3,1},{5,6},{6,7},{7,5},{9,10},{10,11},{11,9},{13,14},... | collective-permute-start | bytes 2113544 | tf_op jit(solution)/shard_map/ppermute | solution.py:345
  67.5 4.0 %collective-permute-start.15 = (f32[64,512]{1,0:T(8,128)S(1)}, f32[64,512]{1,0:T(8,128)S(1)}, u32[]{:S(2)}, u32[]{:S(2)}) collective-permute-start(f32[64,512]{1,0:T(8,128)S(1)} %add_select_fusion.refs_0_), channel_id=1, source_target_pairs={{0,4},{4,0},{8,12},{12,8},{16,20},{20,16},{24,28},{28,24},{1,5},{5... | collective-permute-start | bytes 393224 | tf_op jit(solution)/shard_map/ppermute | solution.py:377
  69.0 6.1 %collective-permute-start.14 = (f32[64,512]{1,0:T(8,128)S(1)}, f32[64,512]{1,0:T(8,128)}, u32[]{:S(2)}, u32[]{:S(2)}) collective-permute-start(f32[64,512]{1,0:T(8,128)S(1)} %add_select_fusion.refs_0_), channel_id=1, source_target_pairs={{0,24},{4,28},{8,16},{12,20},{16,8},{20,12},{24,0},{28,4},{1,25},{... | collective-permute-start | bytes 393224 | tf_op jit(solution)/shard_map/ppermute | solution.py:376
  71.2 7.1 %collective-permute-start.13 = (f32[64,512]{1,0:T(8,128)S(1)}, f32[64,512]{1,0:T(8,128)}, u32[]{:S(2)}, u32[]{:S(2)}) collective-permute-start(f32[64,512]{1,0:T(8,128)S(1)} %add_select_fusion.refs_0_), channel_id=1, source_target_pairs={{0,16},{4,20},{8,24},{12,28},{16,0},{20,4},{24,8},{28,12},{1,17},{... | collective-permute-start | bytes 393224 | tf_op jit(solution)/shard_map/ppermute | solution.py:376
  71.4 0.7 copy-start.3
  72.1 6.7 %collective-permute-start.12 = (f32[64,512]{1,0:T(8,128)S(1)}, f32[64,512]{1,0:T(8,128)}, u32[]{:S(2)}, u32[]{:S(2)}) collective-permute-start(f32[64,512]{1,0:T(8,128)S(1)} %add_select_fusion.refs_0_), channel_id=1, source_target_pairs={{0,8},{4,12},{8,0},{12,4},{16,24},{20,28},{24,16},{28,20},{1,9},{5... | collective-permute-start | bytes 393224 | tf_op jit(solution)/shard_map/ppermute | solution.py:376
  72.3 0.7 copy-start.1
  75.1 10.2 %collective-permute-start.18 = (f32[64,512]{1,0:T(8,128)}, f32[64,512]{1,0:T(8,128)}, u32[]{:S(2)}, u32[]{:S(2)}) collective-permute-start(f32[64,512]{1,0:T(8,128)} %collective-permute-done.14.refs_3_), channel_id=1, source_target_pairs={{0,4},{4,0},{8,12},{12,8},{16,20},{20,16},{24,28},{28,24},{1,5},{5... | collective-permute-start | bytes 393224 | tf_op jit(solution)/shard_map/ppermute | solution.py:377
  78.3 7.0 %collective-permute-start.17 = (f32[64,512]{1,0:T(8,128)}, f32[64,512]{1,0:T(8,128)}, u32[]{:S(2)}, u32[]{:S(2)}) collective-permute-start(f32[64,512]{1,0:T(8,128)} %collective-permute-done.13.refs_2_), channel_id=1, source_target_pairs={{0,4},{4,0},{8,12},{12,8},{16,20},{20,16},{24,28},{28,24},{1,5},{5... | collective-permute-start | bytes 393224 | tf_op jit(solution)/shard_map/ppermute | solution.py:377
  78.8 6.6 %collective-permute-start.16 = (f32[64,512]{1,0:T(8,128)}, f32[64,512]{1,0:T(8,128)}, u32[]{:S(2)}, u32[]{:S(2)}) collective-permute-start(f32[64,512]{1,0:T(8,128)} %collective-permute-done.12.refs_1_), channel_id=1, source_target_pairs={{0,4},{4,0},{8,12},{12,8},{16,20},{20,16},{24,28},{28,24},{1,5},{5... | collective-permute-start | bytes 393224 | tf_op jit(solution)/shard_map/ppermute | solution.py:377
  80.7 3.4 %copy-start = (f32[1024,2048]{1,0:T(8,128)S(1)}, f32[1024,2048]{1,0:T(8,128)}, u32[]{:S(2)}) copy-start(f32[1024,2048]{1,0:T(8,128)} %s_ref.4) | copy-start | bytes 25165828
  84.1 1.2 copy-start.2
  84.1 1.2 copy-start.4
  122.7 2.8 %collective-permute-start.19 = (f32[256,1024]{1,0:T(8,128)S(1)}, f32[256,1024]{1,0:T(8,128)S(1)}, u32[]{:S(2)}, u32[]{:S(2)}) collective-permute-start(f32[256,1024]{1,0:T(8,128)S(1)} %get-tuple-element.49), channel_id=1, source_target_pairs={{0,4},{4,0},{8,12},{12,8},{16,20},{20,16},{24,28},{28,24},{1,5},{5... | collective-permute-start | bytes 3145736 | tf_op jit(solution)/shard_map/ppermute | solution.py:362
  123.2 5.3 %collective-permute-start.30 = (f32[256,1024]{1,0:T(8,128)S(1)}, f32[256,1024]{1,0:T(8,128)S(1)}, u32[]{:S(2)}, u32[]{:S(2)}) collective-permute-start(f32[256,1024]{1,0:T(8,128)S(1)} %get-tuple-element.57), channel_id=1, source_target_pairs={{0,4},{4,0},{8,12},{12,8},{16,20},{20,16},{24,28},{28,24},{1,5},{5... | collective-permute-start | bytes 3145736 | tf_op jit(solution)/shard_map/ppermute | solution.py:362
  125.5 54.7 %slice-start = ((s8[8388608]{0:T(1024)(128)(4,1)}), s8[4194304]{0:T(1024)(128)(4,1)S(1)}, s32[]{:S(2)}) async-start(s8[8388608]{0:T(1024)(128)(4,1)} %bitcast.6), calls=%async_computation | async-start | bytes 8388608
  125.7 7.6 %collective-permute-start.20 = (f32[64,1024]{1,0:T(8,128)S(1)}, f32[64,1024]{1,0:T(8,128)S(1)}, u32[]{:S(2)}, u32[]{:S(2)}) collective-permute-start(f32[64,1024]{1,0:T(8,128)S(1)} %get-tuple-element.66), channel_id=1, source_target_pairs={{0,8},{4,12},{8,0},{12,4},{16,24},{20,28},{24,16},{28,20},{1,9},{5... | collective-permute-start | bytes 786440 | tf_op jit(solution)/shard_map/ppermute | solution.py:371
  127.0 12.9 %collective-permute-start.22 = (f32[64,1024]{1,0:T(8,128)S(1)}, f32[64,1024]{1,0:T(8,128)S(1)}, u32[]{:S(2)}, u32[]{:S(2)}) collective-permute-start(f32[64,1024]{1,0:T(8,128)S(1)} %get-tuple-element.67), channel_id=1, source_target_pairs={{0,24},{4,28},{8,16},{12,20},{16,8},{20,12},{24,0},{28,4},{1,25},{... | collective-permute-start | bytes 786440 | tf_op jit(solution)/shard_map/ppermute | solution.py:371
  128.2 11.7 %collective-permute-start.21 = (f32[64,1024]{1,0:T(8,128)S(1)}, f32[64,1024]{1,0:T(8,128)S(1)}, u32[]{:S(2)}, u32[]{:S(2)}) collective-permute-start(f32[64,1024]{1,0:T(8,128)S(1)} %get-tuple-element.68), channel_id=1, source_target_pairs={{0,16},{4,20},{8,24},{12,28},{16,0},{20,4},{24,8},{28,12},{1,17},{... | collective-permute-start | bytes 786440 | tf_op jit(solution)/shard_map/ppermute | solution.py:371
  128.6 51.6 %slice-start.1 = ((s8[8388608]{0:T(1024)(128)(4,1)}), s8[4194304]{0:T(1024)(128)(4,1)S(1)}, s32[]{:S(2)}) async-start(s8[8388608]{0:T(1024)(128)(4,1)} %bitcast.6), calls=%async_computation.1 | async-start | bytes 8388608
  128.7 15.9 %collective-permute-start.31 = (f32[64,1024]{1,0:T(8,128)S(1)}, f32[64,1024]{1,0:T(8,128)S(1)}, u32[]{:S(2)}, u32[]{:S(2)}) collective-permute-start(f32[64,1024]{1,0:T(8,128)S(1)} %get-tuple-element.63), channel_id=1, source_target_pairs={{0,8},{4,12},{8,0},{12,4},{16,24},{20,28},{24,16},{28,20},{1,9},{5... | collective-permute-start | bytes 786440 | tf_op jit(solution)/shard_map/ppermute | solution.py:371
  130.0 21.2 %collective-permute-start.33 = (f32[64,1024]{1,0:T(8,128)S(1)}, f32[64,1024]{1,0:T(8,128)S(1)}, u32[]{:S(2)}, u32[]{:S(2)}) collective-permute-start(f32[64,1024]{1,0:T(8,128)S(1)} %get-tuple-element.64), channel_id=1, source_target_pairs={{0,24},{4,28},{8,16},{12,20},{16,8},{20,12},{24,0},{28,4},{1,25},{... | collective-permute-start | bytes 786440 | tf_op jit(solution)/shard_map/ppermute | solution.py:371
  133.3 24.4 %collective-permute-start.32 = (f32[64,1024]{1,0:T(8,128)S(1)}, f32[64,1024]{1,0:T(8,128)S(1)}, u32[]{:S(2)}, u32[]{:S(2)}) collective-permute-start(f32[64,1024]{1,0:T(8,128)S(1)} %get-tuple-element.65), channel_id=1, source_target_pairs={{0,16},{4,20},{8,24},{12,28},{16,0},{20,4},{24,8},{28,12},{1,17},{... | collective-permute-start | bytes 786440 | tf_op jit(solution)/shard_map/ppermute | solution.py:371
  140.0 20.5 %collective-permute-start.25 = (f32[64,1024]{1,0:T(8,128)S(1)}, f32[64,1024]{1,0:T(8,128)S(1)}, u32[]{:S(2)}, u32[]{:S(2)}) collective-permute-start(f32[64,1024]{1,0:T(8,128)S(1)} %add_add_fusion.2.rest_0_), channel_id=1, source_target_pairs={{0,24},{4,28},{8,16},{12,20},{16,8},{20,12},{24,0},{28,4},{1,25},{... | collective-permute-start | bytes 786440 | tf_op jit(solution)/shard_map/ppermute | solution.py:376
  141.2 26.0 %collective-permute-start.24 = (f32[64,1024]{1,0:T(8,128)S(1)}, f32[64,1024]{1,0:T(8,128)S(1)}, u32[]{:S(2)}, u32[]{:S(2)}) collective-permute-start(f32[64,1024]{1,0:T(8,128)S(1)} %add_add_fusion.2.rest_0_), channel_id=1, source_target_pairs={{0,16},{4,20},{8,24},{12,28},{16,0},{20,4},{24,8},{28,12},{1,17},{... | collective-permute-start | bytes 786440 | tf_op jit(solution)/shard_map/ppermute | solution.py:376
  157.8 14.2 %collective-permute-start.36 = (f32[64,1024]{1,0:T(8,128)S(1)}, f32[64,1024]{1,0:T(8,128)S(1)}, u32[]{:S(2)}, u32[]{:S(2)}) collective-permute-start(f32[64,1024]{1,0:T(8,128)S(1)} %add_add_fusion.1.rest_0_), channel_id=1, source_target_pairs={{0,24},{4,28},{8,16},{12,20},{16,8},{20,12},{24,0},{28,4},{1,25},{... | collective-permute-start | bytes 786440 | tf_op jit(solution)/shard_map/ppermute | solution.py:376
  159.0 15.5 %collective-permute-start.35 = (f32[64,1024]{1,0:T(8,128)S(1)}, f32[64,1024]{1,0:T(8,128)S(1)}, u32[]{:S(2)}, u32[]{:S(2)}) collective-permute-start(f32[64,1024]{1,0:T(8,128)S(1)} %add_add_fusion.1.rest_0_), channel_id=1, source_target_pairs={{0,16},{4,20},{8,24},{12,28},{16,0},{20,4},{24,8},{28,12},{1,17},{... | collective-permute-start | bytes 786440 | tf_op jit(solution)/shard_map/ppermute | solution.py:376
  159.6 16.7 %collective-permute-start.34 = (f32[64,1024]{1,0:T(8,128)S(1)}, f32[64,1024]{1,0:T(8,128)S(1)}, u32[]{:S(2)}, u32[]{:S(2)}) collective-permute-start(f32[64,1024]{1,0:T(8,128)S(1)} %add_add_fusion.1.rest_0_), channel_id=1, source_target_pairs={{0,8},{4,12},{8,0},{12,4},{16,24},{20,28},{24,16},{28,20},{1,9},{5... | collective-permute-start | bytes 786440 | tf_op jit(solution)/shard_map/ppermute | solution.py:376
  160.5 18.5 %collective-permute-start.23 = (f32[64,1024]{1,0:T(8,128)S(1)}, f32[64,1024]{1,0:T(8,128)S(1)}, u32[]{:S(2)}, u32[]{:S(2)}) collective-permute-start(f32[64,1024]{1,0:T(8,128)S(1)} %add_add_fusion.2.rest_0_), channel_id=1, source_target_pairs={{0,8},{4,12},{8,0},{12,4},{16,24},{20,28},{24,16},{28,20},{1,9},{5... | collective-permute-start | bytes 786440 | tf_op jit(solution)/shard_map/ppermute | solution.py:376
  167.3 12.3 %collective-permute-start.37 = (f32[64,1024]{1,0:T(8,128)S(1)}, f32[64,1024]{1,0:T(8,128)S(1)}, u32[]{:S(2)}, u32[]{:S(2)}) collective-permute-start(f32[64,1024]{1,0:T(8,128)S(1)} %add_add_fusion.1.rest_0_), channel_id=1, source_target_pairs={{0,4},{4,0},{8,12},{12,8},{16,20},{20,16},{24,28},{28,24},{1,5},{5... | collective-permute-start | bytes 786440 | tf_op jit(solution)/shard_map/ppermute | solution.py:377
  172.0 7.7 %collective-permute-start.40 = (f32[64,1024]{1,0:T(8,128)S(1)}, f32[64,1024]{1,0:T(8,128)S(1)}, u32[]{:S(2)}, u32[]{:S(2)}) collective-permute-start(f32[64,1024]{1,0:T(8,128)S(1)} %collective-permute-done.36.rest_3_), channel_id=1, source_target_pairs={{0,4},{4,0},{8,12},{12,8},{16,20},{20,16},{24,28},{28,24},{1,5},{5... | collective-permute-start | bytes 786440 | tf_op jit(solution)/shard_map/ppermute | solution.py:377
  174.6 5.6 %collective-permute-start.39 = (f32[64,1024]{1,0:T(8,128)S(1)}, f32[64,1024]{1,0:T(8,128)S(1)}, u32[]{:S(2)}, u32[]{:S(2)}) collective-permute-start(f32[64,1024]{1,0:T(8,128)S(1)} %collective-permute-done.35.rest_2_), channel_id=1, source_target_pairs={{0,4},{4,0},{8,12},{12,8},{16,20},{20,16},{24,28},{28,24},{1,5},{5... | collective-permute-start | bytes 786440 | tf_op jit(solution)/shard_map/ppermute | solution.py:377
  176.3 3.9 %collective-permute-start.38 = (f32[64,1024]{1,0:T(8,128)S(1)}, f32[64,1024]{1,0:T(8,128)S(1)}, u32[]{:S(2)}, u32[]{:S(2)}) collective-permute-start(f32[64,1024]{1,0:T(8,128)S(1)} %collective-permute-done.34.rest_1_), channel_id=1, source_target_pairs={{0,4},{4,0},{8,12},{12,8},{16,20},{20,16},{24,28},{28,24},{1,5},{5... | collective-permute-start | bytes 786440 | tf_op jit(solution)/shard_map/ppermute | solution.py:377
  179.0 9.0 %collective-permute-start.26 = (f32[64,1024]{1,0:T(8,128)S(1)}, f32[64,1024]{1,0:T(8,128)S(1)}, u32[]{:S(2)}, u32[]{:S(2)}) collective-permute-start(f32[64,1024]{1,0:T(8,128)S(1)} %add_add_fusion.2.rest_0_), channel_id=1, source_target_pairs={{0,4},{4,0},{8,12},{12,8},{16,20},{20,16},{24,28},{28,24},{1,5},{5... | collective-permute-start | bytes 786440 | tf_op jit(solution)/shard_map/ppermute | solution.py:377
  179.6 8.5 %collective-permute-start.29 = (f32[64,1024]{1,0:T(8,128)S(1)}, f32[64,1024]{1,0:T(8,128)S(1)}, u32[]{:S(2)}, u32[]{:S(2)}) collective-permute-start(f32[64,1024]{1,0:T(8,128)S(1)} %collective-permute-done.25.rest_3_), channel_id=1, source_target_pairs={{0,4},{4,0},{8,12},{12,8},{16,20},{20,16},{24,28},{28,24},{1,5},{5... | collective-permute-start | bytes 786440 | tf_op jit(solution)/shard_map/ppermute | solution.py:377
  179.7 8.4 %collective-permute-start.28 = (f32[64,1024]{1,0:T(8,128)S(1)}, f32[64,1024]{1,0:T(8,128)S(1)}, u32[]{:S(2)}, u32[]{:S(2)}) collective-permute-start(f32[64,1024]{1,0:T(8,128)S(1)} %collective-permute-done.24.rest_2_), channel_id=1, source_target_pairs={{0,4},{4,0},{8,12},{12,8},{16,20},{20,16},{24,28},{28,24},{1,5},{5... | collective-permute-start | bytes 786440 | tf_op jit(solution)/shard_map/ppermute | solution.py:377
  180.1 8.0 %collective-permute-start.27 = (f32[64,1024]{1,0:T(8,128)S(1)}, f32[64,1024]{1,0:T(8,128)S(1)}, u32[]{:S(2)}, u32[]{:S(2)}) collective-permute-start(f32[64,1024]{1,0:T(8,128)S(1)} %collective-permute-done.23.rest_1_), channel_id=1, source_target_pairs={{0,4},{4,0},{8,12},{12,8},{16,20},{20,16},{24,28},{28,24},{1,5},{5... | collective-permute-start | bytes 786440 | tf_op jit(solution)/shard_map/ppermute | solution.py:377

commit v7 on v6

--- a/solution.py
+++ b/solution.py
@@ -137,7 +137,7 @@
         scratch_shapes=[pltpu.VMEM((NB, NB), F32)] * 3,
         input_output_aliases={} if fresh else {1: 0, 2: 1, 3: 2},
         compiler_params=vmem_limit(LIMITS[2]),
-        cost_estimate=cost(1),
+        cost_estimate=cost((last - first) * 8 * 10**9),
         name="chol_part",
     )(info, *arrays)
 
@@ -160,78 +160,18 @@
     )(snapshots)
 
 
-def panel_dot(info, own, high, low, parts, size, first, width, scale, ready=None):
-    rows, half = own.shape[0], PB // 2
-    fresh = ready is None
-    extra = [own, *parts] if fresh else [ready]
-    n_extra = len(extra)
-    tile = min(TILE, width)
-
-    def kernel(info_ref, h_ref, l_ref, *rest):
-        extra_refs, rest = rest[:n_extra], rest[n_extra:]
-        send_ref, mine_ref = rest[:2]
-        ms = rest[-1]
-        pt = rest[3] if fresh else extra_refs[0]
-        if fresh:
-            p_ref = rest[2]
-
-            @pl.when(info_ref[0] == 0)
-            def _():
-                p_ref[...] = extra_refs[0][...]
-
-            if n_extra > 1:
-
-                @pl.when(info_ref[0] != 0)
-                def _():
-                    for k, ref in enumerate(extra_refs[1:]):
-                        start = pl.multiple_of(info_ref[3 + k], 8)
-                        p_ref[pl.ds(start, size), :] = ref[...]
-
-            def turn(i, carry):
-                cut = pl.ds(pl.multiple_of(i * 256, 256), 256)
-                ph, plow = split(p_ref[cut, :])
-                pt[:PB, cut], pt[PB:, cut] = ph.T, plow.T
-                return carry
-
-            lax.fori_loop(0, rows // 256, turn, 0)
-
-        def step(i, carry):
-            cut = pl.ds(pl.multiple_of(i * tile, tile), tile)
-            source = pl.ds(pl.multiple_of(first + i * tile, tile), tile)
-            both = mm(pt[...], h_ref[:, source], 1, 0)
-            ms[...] = (both[:PB] + (both[PB:] + mm(pt[:PB, :], l_ref[:, source], 1, 0))) * scale
-            send_ref[:, cut] = ms[pl.ds(pl.multiple_of((1 - info_ref[1]) * half, half), half), :]
-            mine_ref[:, cut] = ms[pl.ds(pl.multiple_of(info_ref[1] * half, half), half), :]
-            return carry
-
-        lax.fori_loop(0, width // tile, step, 0)
-
-    out = [jax.ShapeDtypeStruct((half, width), F32)] * 2
-    if fresh:
-        out += [jax.ShapeDtypeStruct((rows, PB), F32), jax.ShapeDtypeStruct((2 * PB, rows), BF16)]
-    return pl.pallas_call(
-        kernel,
-        out_shape=out,
-        in_specs=[SMEM] + [VMEM] * (2 + n_extra),
-        out_specs=[VMEM] * len(out),
-        scratch_shapes=[pltpu.VMEM((PB, tile), F32)],
-        compiler_params=vmem_limit(LIMITS[1]),
-        cost_estimate=cost(6 * rows * PB * width),
-        name="panel_dot",
-    )(info, high, low, *extra)
-
-
-def basis(panel, linv):
-    rows = panel.shape[0]
-
-    def kernel(p_ref, l_ref, b_ref, b3, l3):
+def basis(panels, linv):
+    rows, n_panels = panels[0].shape[0], len(panels)
+
+    def kernel(*refs):
+        p_refs, (l_ref, b_ref, b3, l3) = refs[:n_panels], refs[n_panels:]
         lh, ll = split(l_ref[...])
         l3[:, :PB], l3[:, PB : 2 * PB], l3[:, 2 * PB :] = lh, lh, ll
 
         def step(i, carry):
             cut = pl.ds(pl.multiple_of(i * 256, 256), 256)
             lh, ll = l3[:, :PB], l3[:, 2 * PB :]
-            ph, plow = split(p_ref[cut, :])
+            ph, plow = split(jnp.concatenate([p[cut, :] for p in p_refs], axis=1))
             b = mm(ph, lh, 1, 1) + (mm(ph, ll, 1, 1) + mm(plow, lh, 1, 1))
             b_ref[cut, :] = b
             bh, bl = split(b)
@@ -247,33 +187,32 @@
             jax.ShapeDtypeStruct((rows, 3 * PB), BF16),
             jax.ShapeDtypeStruct((PB, 3 * PB), BF16),
         ),
-        in_specs=[VMEM] * 2,
+        in_specs=[VMEM] * (n_panels + 1),
         out_specs=(VMEM,) * 3,
         compiler_params=vmem_limit(LIMITS[2]),
         cost_estimate=cost(6 * rows * PB * PB),
         name="basis",
-    )(panel, linv)
-
-
-def finish(info, snapshots, b, b3, l3, factor, pieces, places, first, width, done=None):
+    )(*panels, linv)
+
+
+def finish(info, snapshots, b, b3, l3, factor, pieces, layout):
     rows, cols = snapshots.shape
-    tile = min(TILE, width)
-    n_pieces, chips = len(pieces), len(pieces) // 2
-    later = [] if done is None else list(done)
+    tile = min(TILE, cols)
+    n_pieces = len(pieces)
+    chips = 1 + max(chip for _, _, chip in layout)
 
     def kernel(info_ref, s_ref, b_ref, b3_ref, l3_ref, f_ref, *rest):
-        m_refs, rest = rest[:n_pieces], rest[n_pieces + len(later) :]
-        up_hbm, co_hbm, ms, m3, p3, up, co, sems = rest
+        m_refs = rest[:n_pieces]
+        up_hbm, co_hbm, ms, m3, p3, up, co, sems = rest[n_pieces:]
         copies = []
-        for t in range(width // tile):
+        for t in range(cols // tile):
             slot, cut = t % 2, pl.ds(t * tile, tile)
-            goal = pl.ds(first + t * tile, tile)
             if t >= 2:
                 for copy in copies[t - 2]:
                     copy.wait()
-            for ref, (core, chip) in zip(m_refs, places):
+            for ref, (base, core, chip) in zip(m_refs, layout):
                 h = ref.shape[0]
-                off = (info_ref[1] ^ core) * (h * chips) + (info_ref[2] ^ chip) * h
+                off = base + (info_ref[1] ^ core) * (h * chips) + (info_ref[2] ^ chip) * h
                 ms[pl.ds(pl.multiple_of(off, 8), h), :] = ref[:, cut]
             mh, ml = split(ms[...])
             m3[:PB, :], m3[PB : 2 * PB, :], m3[2 * PB :, :] = mh, ml, mh
@@ -281,17 +220,17 @@
             ph, plow = split(proj)
             p3[:PB, :], p3[PB : 2 * PB, :], p3[2 * PB :, :] = ph, plow, ph
             co[slot] = proj
-            up[slot] = s_ref[:, goal] - mm(b3_ref[...], p3[...], 1, 0)
-            if first + t * tile < PB:
+            up[slot] = s_ref[:, cut] - mm(b3_ref[...], p3[...], 1, 0)
+            if t * tile < PB:
 
                 @pl.when(info_ref[0] == 0)
                 def _():
-                    co[slot] = f_ref[:, goal]
-                    up[slot] = b_ref[:, goal]
+                    co[slot] = f_ref[:, cut]
+                    up[slot] = b_ref[:, cut]
 
             pair = (
-                pltpu.make_async_copy(up.at[slot], up_hbm.at[:, goal], sems.at[0, slot]),
-                pltpu.make_async_copy(co.at[slot], co_hbm.at[:, goal], sems.at[1, slot]),
+                pltpu.make_async_copy(up.at[slot], up_hbm.at[:, cut], sems.at[0, slot]),
+                pltpu.make_async_copy(co.at[slot], co_hbm.at[:, cut], sems.at[1, slot]),
             )
             for copy in pair:
                 copy.start()
@@ -300,14 +239,13 @@
             for copy in pair:
                 copy.wait()
 
-    operands = [info, snapshots, b, b3, l3, factor, *pieces, *later]
     return pl.pallas_call(
         kernel,
         out_shape=(
             jax.ShapeDtypeStruct((rows, cols), F32),
             jax.ShapeDtypeStruct((PB, cols), F32),
         ),
-        in_specs=[SMEM] + [VMEM] * (5 + n_pieces) + [ANY] * len(later),
+        in_specs=[SMEM] + [VMEM] * (5 + n_pieces),
         out_specs=(ANY, ANY),
         scratch_shapes=[
             pltpu.VMEM((PB, tile), F32),
@@ -317,11 +255,62 @@
             pltpu.VMEM((2, PB, tile), F32),
             pltpu.SemaphoreType.DMA((2, 2)),
         ],
-        input_output_aliases={len(operands) - 2: 0, len(operands) - 1: 1} if later else {},
         compiler_params=vmem_limit(LIMITS[3]),
         cost_estimate=cost(10**10),
         name="finish",
-    )(*operands)
+    )(info, snapshots, b, b3, l3, factor, *pieces)
+
+
+def panel_dot(info, own, high, low, parts, size, scale):
+    rows, width = own.shape
+    cols, half = high.shape[1], width // 2
+    n_parts = len(parts)
+    tile = min(TILE, cols)
+
+    def kernel(info_ref, h_ref, l_ref, own_ref, *rest):
+        part_refs = rest[:n_parts]
+        send_ref, mine_ref, p_ref, pt, ms = rest[n_parts:]
+
+        @pl.when(info_ref[0] == 0)
+        def _():
+            p_ref[...] = own_ref[...]
+
+        if n_parts:
+
+            @pl.when(info_ref[0] != 0)
+            def _():
+                for k, ref in enumerate(part_refs):
+                    start = pl.multiple_of(info_ref[3 + k], 8)
+                    p_ref[pl.ds(start, size), :] = ref[...]
+
+        for r in range(0, rows, 256):
+            ph, plow = split(p_ref[r : r + 256, :])
+            pt[:width, r : r + 256], pt[width:, r : r + 256] = ph.T, plow.T
+
+        def step(i, carry):
+            cut = pl.ds(pl.multiple_of(i * tile, tile), tile)
+            both = mm(pt[...], h_ref[:, cut], 1, 0)
+            ms[...] = (both[:width] + (both[width:] + mm(pt[:width, :], l_ref[:, cut], 1, 0))) * scale
+            send_ref[:, cut] = ms[pl.ds(pl.multiple_of((1 - info_ref[1]) * half, half), half), :]
+            mine_ref[:, cut] = ms[pl.ds(pl.multiple_of(info_ref[1] * half, half), half), :]
+            return carry
+
+        lax.fori_loop(0, cols // tile, step, 0)
+
+    out = jax.ShapeDtypeStruct((half, cols), F32)
+    return pl.pallas_call(
+        kernel,
+        out_shape=(out, out, jax.ShapeDtypeStruct((rows, width), F32)),
+        in_specs=[SMEM] + [VMEM] * (3 + n_parts),
+        out_specs=(VMEM, VMEM, VMEM),
+        scratch_shapes=[
+            pltpu.VMEM((2 * width, rows), BF16),
+            pltpu.VMEM((width, tile), F32),
+        ],
+        compiler_params=vmem_limit(LIMITS[1]),
+        cost_estimate=cost(6 * rows * cols * width),
+        name="panel_dot",
+    )(info, high, low, own, *parts)
 
 
 def part_size(rows, parts):
@@ -391,34 +380,36 @@
     half = PB // 2
     panel = snapshots[:, :PB]
 
-    mine = spread_out(panel, n_cols)
+    dot = lambda got, base: panel_dot(
+        info, panel[:, base : base + half], high, low, got, size, 1.0 / total_rows
+    )
+
+    mine_a = spread_out(panel[:, :half], n_cols)
     gram = mm(panel, panel, 0, 0, HIGHEST) / total_rows
     joined = join_cores(take(gram, (1 - core) * half, half), take(gram, core * half, half), n_rows)
-    high, low = stage(after(snapshots, joined))
+    high, low = stage(snapshots)
     share = scatter_chips(joined, n_rows)
     far = [lax.ppermute(share, "cols", [(0, k)]) for k in reversed(range(1, n_cols))]
+    got_a = spread_round(mine_a, n_cols)
+    mine_b = spread_out(after(panel[:, half:], got_a), n_cols)
     share = jnp.where(z == 0, share, sum(far, jnp.zeros_like(share)))
     grams, places = gather_rows(share, n_rows)
-    got = spread_round(mine, n_cols)
-    _, factor, linv = chol_part(info, 0, PB // NB, pieces=after(grams, mine, high), places=places)
-
-    width = cols_dev // 2
-    dot = lambda got, first, ready=None: panel_dot(
-        info, panel, high, low, got, size, first, width, 1.0 / total_rows, ready
-    )
-    send, keep, whole, turned = dot(after(got, linv), 0)
-    joined1 = join_cores(send, keep, n_rows)
-    send, keep = dot(None, width, turned)
-    joined2 = join_cores(send, keep, n_rows)
-    own1 = scatter_chips(joined1, n_rows)
-    own2 = scatter_chips(joined2, n_rows)
-    b, b3, l3 = basis(after(whole, joined2), linv)
-    pieces1, _ = gather_rows(own1, n_rows)
-    pieces2, _ = gather_rows(own2, n_rows)
-    done = finish(
-        info, snapshots, b, b3, after(l3, own2), factor, pieces1, places, 0, width
-    )
-    return finish(info, snapshots, b, b3, l3, factor, pieces2, places, width, width, done)
+
+    send, keep, panel_a = dot(after(got_a, far, high), 0)
+    joined = join_cores(send, keep, n_rows)
+    got_b = spread_round(mine_b, n_cols)
+    own_a = scatter_chips(joined, n_rows)
+    state = chol_part(info, 0, 2, pieces=after(grams, joined, mine_b), places=places)
+    pieces_a, where = gather_rows(own_a, n_rows)
+    send, keep, panel_b = dot(after(got_b, own_a, state), half)
+    joined = join_cores(send, keep, n_rows)
+    own_b = scatter_chips(joined, n_rows)
+    state = chol_part(info, 2, 3, state=after(state, joined))
+    pieces_b, _ = gather_rows(after(own_b, state), n_rows)
+    _, factor, linv = chol_part(info, 3, 4, state=after(state, own_b))
+    b, b3, l3 = basis([panel_a, panel_b], linv)
+    layout = [(base,) + w for base in (0, half) for w in where]
+    return finish(info, snapshots, b, b3, l3, factor, pieces_a + pieces_b, layout)
 
 
 def solution(mesh):

time: 198 us -> 202 us (1.020)
  starting transfers between devices: 71.5 us -> 81.9 us
  waiting for transfers between devices: 49.1 us -> 39.3 us
  local copies, waits for them, and re-layouts: 9.58 us -> 12.6 us
  other arithmetic: 2.13 us -> 4.67 us
    ppermute x9, waiting for transfers between devices: 31.7 us -> 7.01 us  [scatter_chips(): lax.ppermute(take(mine, (chip ^ k) * piece, piece), 'rows', swap(n, 2 * k))]
    ppermute x2 -> x4, waiting for transfers between devices: 0.01 us -> 9.35 us  [spread_round(): got.append(lax.ppermute(mine, 'cols', pairs))]
    ppermute x3 -> x6, waiting for transfers between devices: 1.94 us -> 6.84 us  [spread_out(): got.append(lax.ppermute(x[start:start + size], 'cols', [(0, k + 1)]))]
    ppermute x3 -> x6, starting transfers between devices: 4.34 us -> 7.48 us  [spread_out(): got.append(lax.ppermute(x[start:start + size], 'cols', [(0, k + 1)]))]
    unnamed x14 -> x38, local copies, waits for them, and re-layouts: 4.71 us -> 7.63 us
    ppermute x2 -> x4, starting transfers between devices: 34.8 us -> 37.4 us  [spread_round(): got.append(lax.ppermute(mine, 'cols', pairs))]
    ppermute x3, starting transfers between devices: 1.32 us -> 3.68 us  [join_cores(): return mine + lax.ppermute(send, 'rows', swap(n, 1))]
    ppermute x12, starting transfers between devices: 10.6 us -> 12.7 us  [gather_rows(): other = [lax.ppermute(g, 'rows', swap(n, 1)) for g in got]]
  transfers between devices with their start and end apart: 41 -> 46, of which waited for: 14 -> 10; matrix products, arithmetic and copies ran while one was open for 4% -> 5% of each run, Pallas kernels for 20% -> 15%
where the time goes in v7:
time: 202 us; the launch traced here: 200 us
  starting transfers between devices  81.9 us (41%)
  Pallas kernels  54.9 us (27%)
  waiting for transfers between devices  39.3 us (19%)
  local copies, waits for them, and re-layouts  12.6 us (6%)
  matrix products  5.72 us (3%)
  other arithmetic  4.67 us (2%)
    ppermute x4, starting transfers between devices, spread_round(): got.append(lax.ppermute(mine, 'cols', pairs))  37.4 us
    pallas_call x3, Pallas kernels, chol_part(): pl.pallas_call(kernel, out_shape=(shape, shape, shape), in_specs=[SMEM] +...  26.3 us
    ppermute x9, waiting for transfers between devices, gather_rows(): lax.ppermute(own, 'rows', swap(n, 2 * k))  15.2 us
    pallas_call x1, Pallas kernels, finish(): pl.pallas_call(kernel, out_shape=(jax.ShapeDtypeStruct((rows, cols), F32)...  13.6 us
    ppermute x12, starting transfers between devices, gather_rows(): other = [lax.ppermute(g, 'rows', swap(n, 1)) for g in got]  12.7 us
    pallas_call x2, Pallas kernels, panel_dot(): pl.pallas_call(kernel, out_shape=(out, out, jax.ShapeDtypeStruct((rows, w...  11.1 us
    ppermute x4, waiting for transfers between devices, spread_round(): got.append(lax.ppermute(mine, 'cols', pairs))  9.35 us
    ppermute x9, starting transfers between devices, scatter_chips(): lax.ppermute(take(mine, (chip ^ k) * piece, piece), 'rows', swap(n, 2 * k))  9.15 us
  transfers between devices with their start and end apart: 46, of which 10 were waited for; matrix products, arithmetic and copies ran while one was open for 5% of the time, Pallas kernels for 15%

profile of v7, /device:TPU:17, one launch (start us, length us, event | category | flops | bytes accessed | tf_op | source)
XLA Modules:
  0.0 200.4 jit_solution(4322810323483968021)
XLA Ops:
  0.6 5.7 %fusion.2 = f32[512,512]{1,0:T(8,128)S(1)} fusion(f32[1024,2048]{1,0:T(8,128)} %s_ref.3), kind=kOutput, calls=%fused_computation.2 | convolution fusion | flops 3221487616 | bytes 3145728 | tf_op jit(solution)/shard_map/dot_general | solution.py:31
  6.4 0.7 collective-permute-start.5
  7.2 2.0 %fusion.6 = (f32[344,256]{1,0:T(8,128)}, f32[344,256]{1,0:T(8,128)S(1)}, f32[344,256]{1,0:T(8,128)S(1)}) fusion(f32[1024,2048]{1,0:T(8,128)} %s_ref.3), kind=kLoop, calls=%fused_computation.21 | loop fusion | bytes 2113536 | tf_op jit(solution)/shard_map/slice | solution.py:326
  9.2 1.3 collective-permute-start.1
  10.5 0.7 collective-permute-start.2
  11.2 1.4 collective-permute-start
  12.7 1.3 collective-permute-start.6
  14.0 1.2 collective-permute-start.8
  15.2 6.8 %collective-permute-done.1 = f32[344,256]{1,0:T(8,128)S(1)} collective-permute-done((f32[344,256]{1,0:T(8,128)}, f32[344,256]{1,0:T(8,128)S(1)}, u32[]{:S(2)}, u32[]{:S(2)}) %collective-permute-start.1) | collective-permute-done | bytes 352288 | tf_op jit(solution)/shard_map/ppermute | solution.py:326
  22.0 1.2 collective-permute-start.7
  23.3 1.1 add_add_fusion.1.rest_0_
  24.3 8.5 %collective-permute-start.4 = (f32[344,256]{1,0:T(8,128)S(1)}, f32[344,256]{1,0:T(8,128)S(1)}, u32[]{:S(2)}, u32[]{:S(2)}) collective-permute-start(f32[344,256]{1,0:T(8,128)S(1)} %add_add_fusion.1.rest_0_), channel_id=1, source_target_pairs={{1,3},{2,1},{3,2},{5,7},{6,5},{7,6},{9,11},{10,9},{11,10},{13,15},... | collective-permute-start | bytes 1056776 | tf_op jit(solution)/shard_map/ppermute | solution.py:334
  32.8 10.5 %collective-permute-start.3 = (f32[344,256]{1,0:T(8,128)S(1)}, f32[344,256]{1,0:T(8,128)S(1)}, u32[]{:S(2)}, u32[]{:S(2)}) collective-permute-start(f32[344,256]{1,0:T(8,128)S(1)} %add_add_fusion.1.rest_0_), channel_id=1, source_target_pairs={{1,2},{2,3},{3,1},{5,6},{6,7},{7,5},{9,10},{10,11},{11,9},{13,14},... | collective-permute-start | bytes 1056776 | tf_op jit(solution)/shard_map/ppermute | solution.py:334
  43.3 0.7 add_add_fusion.4
  44.0 0.7 collective-permute-start.11
  44.7 1.3 collective-permute-start.10
  46.0 0.7 collective-permute-start.9
  46.7 1.7 fusion.5
  48.5 3.4 %copy-done = f32[1024,2048]{1,0:T(8,128)S(1)} copy-done((f32[1024,2048]{1,0:T(8,128)S(1)}, f32[1024,2048]{1,0:T(8,128)}, u32[]{:S(2)}) %copy-start) | copy-done | bytes 8388632
  51.9 1.2 stage.1
  53.1 0.8 copy-done.5
  53.9 9.3 %collective-permute-done.3.rest_1_ = f32[344,256]{1,0:T(8,128)S(1)} collective-permute-done((f32[344,256]{1,0:T(8,128)S(1)}, f32[344,256]{1,0:T(8,128)S(1)}, u32[]{:S(2)}, u32[]{:S(2)}) %collective-permute-start.3) | collective-permute-done | bytes 352288 | tf_op jit(solution)/shard_map/ppermute | solution.py:334
  63.2 0.7 copy-done.7
  64.7 1.0 copy-done.6
  65.7 1.0 copy-done.8
  66.7 6.0 %panel_dot.2 = (f32[128,2048]{1,0:T(8,128)}, f32[128,2048]{1,0:T(8,128)S(1)}, f32[1024,256]{1,0:T(8,128)S(1)}) custom-call(s32[6]{0:T(128)S(1)} %stack.27.info_ref, bf16[1024,2048]{1,0:T(8,128)(2,1)S(1)} %get-tuple-element.43.h_ref, bf16[1024,2048]{1,0:T(8,128)(2,1)S(1)} %get-tuple-element.44.l_ref, f32[1024,256]{1,0:T(8,128)S(1)} %get-tuple-element.85.own_ref, ...), custom_call_target="tpu_custom_call" | custom-call | flops 3221225472 | bytes 1048576 | tf_op jit(solution)/shard_map/panel_dot/pallas_call | solution.py:301
  72.8 1.8 collective-permute-start.17
  74.6 2.2 %collective-permute-start.23 = (f32[64,512]{1,0:T(8,128)S(1)}, f32[64,512]{1,0:T(8,128)S(1)}, u32[]{:S(2)}, u32[]{:S(2)}) collective-permute-start(f32[64,512]{1,0:T(8,128)S(1)} %add_select_fusion.refs_0_), channel_id=1, source_target_pairs={{0,24},{4,28},{8,16},{12,20},{16,8},{20,12},{24,0},{28,4},{1,25},{... | collective-permute-start | bytes 393224 | tf_op jit(solution)/shard_map/ppermute | solution.py:365
  76.8 0.9 fusion.7
  77.7 1.3 collective-permute-start.13
  79.0 1.4 collective-permute-start.14
  80.4 1.4 collective-permute-start.12
  82.1 4.5 %collective-permute-done.22.refs_2_ = f32[64,512]{1,0:T(8,128)S(1)} collective-permute-done((f32[64,512]{1,0:T(8,128)S(1)}, f32[64,512]{1,0:T(8,128)S(1)}, u32[]{:S(2)}, u32[]{:S(2)}) %collective-permute-start.22) | collective-permute-done | bytes 131104 | tf_op jit(solution)/shard_map/ppermute | solution.py:365
  86.6 4.1 %collective-permute-done.21.refs_1_ = f32[64,512]{1,0:T(8,128)S(1)} collective-permute-done((f32[64,512]{1,0:T(8,128)S(1)}, f32[64,512]{1,0:T(8,128)S(1)}, u32[]{:S(2)}, u32[]{:S(2)}) %collective-permute-start.21) | collective-permute-done | bytes 131104 | tf_op jit(solution)/shard_map/ppermute | solution.py:365
  90.7 2.0 collective-permute-start.24
  93.3 1.2 add_add_fusion.rest_0_
  94.5 8.6 %collective-permute-start.16 = (f32[344,256]{1,0:T(8,128)S(1)}, f32[344,256]{1,0:T(8,128)S(1)}, u32[]{:S(2)}, u32[]{:S(2)}) collective-permute-start(f32[344,256]{1,0:T(8,128)S(1)} %add_add_fusion.rest_0_), channel_id=1, source_target_pairs={{1,3},{2,1},{3,2},{5,7},{6,5},{7,6},{9,11},{10,9},{11,10},{13,15},... | collective-permute-start | bytes 1056776 | tf_op jit(solution)/shard_map/ppermute | solution.py:334
  103.1 1.4 add.122
  104.5 9.8 %collective-permute-start.15 = (f32[344,256]{1,0:T(8,128)S(1)}, f32[344,256]{1,0:T(8,128)S(1)}, u32[]{:S(2)}, u32[]{:S(2)}) collective-permute-start(f32[344,256]{1,0:T(8,128)S(1)} %add_add_fusion.rest_0_), channel_id=1, source_target_pairs={{1,2},{2,3},{3,1},{5,6},{6,7},{7,5},{9,10},{10,11},{11,9},{13,14},... | collective-permute-start | bytes 1056776 | tf_op jit(solution)/shard_map/ppermute | solution.py:334
  114.8 1.2 collective-permute-start.20
  115.9 1.2 collective-permute-start.19
  117.2 13.6 %chol_part.3 = (f32[512,512]{1,0:T(8,128)S(1)}, f32[512,512]{1,0:T(8,128)S(1)}, f32[512,512]{1,0:T(8,128)S(1)}) custom-call(s32[6]{0:T(128)S(1)} %stack.27.info_ref, f32[64,512]{1,0:T(8,128)S(1)} %add_select_fusion.refs_0_, f32[64,512]{1,0:T(8,128)S(1)} %collective-permute-done.21.refs_1_, f32[64,512]{1,0:T(8,128)S(1)} %collective-permute-done.22.refs_2_, ...), custom_call_target="tpu_custom_call" | custom-call | flops 16000000000 | bytes 1048576 | tf_op jit(solution)/shard_map/chol_part/pallas_call | solution.py:132
  130.9 5.1 %panel_dot.3 = (f32[128,2048]{1,0:T(8,128)S(1)}, f32[128,2048]{1,0:T(8,128)S(1)}, f32[1024,256]{1,0:T(8,128)S(1)}) custom-call(s32[6]{0:T(128)S(1)} %stack.27.info_ref, bf16[1024,2048]{1,0:T(8,128)(2,1)S(1)} %copy-done.2, bf16[1024,2048]{1,0:T(8,128)(2,1)S(1)} %copy-done.4, f32[1024,256]{1,0:T(8,128)S(1)} %get-tuple-element.49.own_ref, ...), custom_call_target="tpu_custom_call" | custom-call | flops 3221225472 | bytes 1048576 | tf_op jit(solution)/shard_map/panel_dot/pallas_call | solution.py:301
  136.0 1.2 collective-permute-start.28
  137.4 1.2 collective-permute-start.33
  138.6 0.8 collective-permute-done.28
  140.1 1.0 collective-permute-start.31
  141.1 1.2 collective-permute-start.30
  142.4 6.6 %chol_part.4 = (f32[512,512]{1,0:T(8,128)S(1)}, f32[512,512]{1,0:T(8,128)S(1)}, f32[512,512]{1,0:T(8,128)S(1)}) custom-call(s32[6]{0:T(128)S(1)} %stack.27.info_ref, f32[512,512]{1,0:T(8,128)S(1)} %get-tuple-element.69.refs_0_, f32[512,512]{1,0:T(8,128)S(1)} %get-tuple-element.70.refs_1_, ...), custom_call_target="tpu_custom_call", output_to_operand_aliasing={{0}: (1, {}), {1}: (2, {}), {2}: (3, {})} | custom-call | flops 8000000000 | bytes 1048576 | tf_op jit(solution)/shard_map/chol_part/pallas_call | solution.py:132
  149.0 1.3 collective-permute-start.35
  150.5 2.0 collective-permute-start.32
  152.5 1.0 collective-permute-start.38
  153.5 3.8 %collective-permute-done.31 = f32[32,2048]{1,0:T(8,128)S(1)} collective-permute-done((f32[32,2048]{1,0:T(8,128)S(1)}, f32[32,2048]{1,0:T(8,128)S(1)}, u32[]{:S(2)}, u32[]{:S(2)}) %collective-permute-start.31) | collective-permute-done | bytes 262176 | tf_op jit(solution)/shard_map/ppermute | solution.py:360
  157.3 1.3 collective-permute-start.37
  158.6 3.2 %collective-permute-done.30 = f32[32,2048]{1,0:T(8,128)S(1)} collective-permute-done((f32[32,2048]{1,0:T(8,128)S(1)}, f32[32,2048]{1,0:T(8,128)S(1)}, u32[]{:S(2)}, u32[]{:S(2)}) %collective-permute-start.30) | collective-permute-done | bytes 262176 | tf_op jit(solution)/shard_map/ppermute | solution.py:360
  161.9 1.7 collective-permute-start.41
  163.5 1.2 collective-permute-start.40
  164.8 1.8 collective-permute-start.36
  166.7 2.8 %collective-permute-done.41.rest_11_ = f32[32,2048]{1,0:T(8,128)S(1)} collective-permute-done((f32[32,2048]{1,0:T(8,128)S(1)}, f32[32,2048]{1,0:T(8,128)S(1)}, u32[]{:S(2)}, u32[]{:S(2)}) %collective-permute-start.41) | collective-permute-done | bytes 262176 | tf_op jit(solution)/shard_map/ppermute | solution.py:365
  169.5 3.8 %collective-permute-start.45 = (f32[32,2048]{1,0:T(8,128)S(1)}, f32[32,2048]{1,0:T(8,128)S(1)}, u32[]{:S(2)}, u32[]{:S(2)}) collective-permute-start(f32[32,2048]{1,0:T(8,128)S(1)} %collective-permute-done.41.rest_11_), channel_id=1, source_target_pairs={{0,4},{4,0},{8,12},{12,8},{16,20},{20,16},{24,28},{28,24},{1,5},{5... | collective-permute-start | bytes 786440 | tf_op jit(solution)/shard_map/ppermute | solution.py:366
  173.3 3.4 %collective-permute-done.40.rest_10_ = f32[32,2048]{1,0:T(8,128)S(1)} collective-permute-done((f32[32,2048]{1,0:T(8,128)S(1)}, f32[32,2048]{1,0:T(8,128)S(1)}, u32[]{:S(2)}, u32[]{:S(2)}) %collective-permute-start.40) | collective-permute-done | bytes 262176 | tf_op jit(solution)/shard_map/ppermute | solution.py:365
  177.6 6.2 %chol_part.5 = (f32[512,512]{1,0:T(8,128)S(1)}, f32[512,512]{1,0:T(8,128)S(1)}, f32[512,512]{1,0:T(8,128)S(1)}) custom-call(s32[6]{0:T(128)S(1)} %stack.27.info_ref, f32[512,512]{1,0:T(8,128)S(1)} %get-tuple-element.75.refs_0_, f32[512,512]{1,0:T(8,128)S(1)} %get-tuple-element.76.refs_1_, ...), custom_call_target="tpu_custom_call", output_to_operand_aliasing={{0}: (1, {}), {1}: (2, {}), {2}: (3, {})} | custom-call | flops 8000000000 | bytes 1048576 | tf_op jit(solution)/shard_map/chol_part/pallas_call | solution.py:132
  183.8 2.7 %basis.1 = (f32[1024,512]{1,0:T(8,128)S(1)}, bf16[1024,1536]{1,0:T(8,128)(2,1)S(1)}, bf16[512,1536]{1,0:T(8,128)(2,1)S(1)}) custom-call(f32[1024,256]{1,0:T(8,128)S(1)} %copy-done.10, f32[1024,256]{1,0:T(8,128)S(1)} %get-tuple-element.66.refs_1_, f32[512,512]{1,0:T(8,128)S(1)} %get-tuple-element.78.refs_2_), custom_call_target="tpu_custom_call" | custom-call | flops 1610612736 | bytes 1048576 | tf_op jit(solution)/shard_map/basis/pallas_call | solution.py:183
  186.6 13.6 %finish.1 = (f32[1024,2048]{1,0:T(8,128)}, f32[512,2048]{1,0:T(8,128)}) custom-call(s32[6]{0:T(128)S(1)} %stack.27.info_ref, f32[1024,2048]{1,0:T(8,128)S(1)} %bitcast.7, f32[1024,512]{1,0:T(8,128)S(1)} %get-tuple-element.79.b_ref, bf16[1024,1536]{1,0:T(8,128)(2,1)S(1)} %get-tuple-element.80.b3_ref, bf16[512,1536]{1,0:T(8,128)(2,1)S(1)} %get-tuple-element.81.l3_ref, ...), custom_call_target="tpu_custom_call" | custom-call | flops 10000000000 | bytes 1048576 | tf_op jit(solution)/shard_map/finish/pallas_call | solution.py:242
  (93 shorter events, 4.7 us)
Async XLA Ops:
  6.4 6.2 %collective-permute-start.5 = (f32[256,512]{1,0:T(8,128)S(1)}, f32[256,512]{1,0:T(8,128)S(1)}, u32[]{:S(2)}, u32[]{:S(2)}) collective-permute-start(f32[256,512]{1,0:T(8,128)S(1)} %constant_dynamic-slice_fusion.9), channel_id=1, source_target_pairs={{0,4},{4,0},{8,12},{12,8},{16,20},{20,16},{24,28},{28,24},{1,5},{5... | collective-permute-start | bytes 1572872 | tf_op jit(solution)/shard_map/ppermute | solution.py:351
  9.2 12.8 %collective-permute-start.1 = (f32[344,256]{1,0:T(8,128)}, f32[344,256]{1,0:T(8,128)S(1)}, u32[]{:S(2)}, u32[]{:S(2)}) collective-permute-start(f32[344,256]{1,0:T(8,128)} %get-tuple-element.86), channel_id=1, source_target_pairs={{0,2},{4,6},{8,10},{12,14},{16,18},{20,22},{24,26},{28,30}} | collective-permute-start | bytes 1056776 | tf_op jit(solution)/shard_map/ppermute | solution.py:326
  10.5 12.8 %collective-permute-start.2 = (f32[344,256]{1,0:T(8,128)S(1)}, f32[344,256]{1,0:T(8,128)S(1)}, u32[]{:S(2)}, u32[]{:S(2)}) collective-permute-start(f32[344,256]{1,0:T(8,128)S(1)} %get-tuple-element.87), channel_id=1, source_target_pairs={{0,1},{4,5},{8,9},{12,13},{16,17},{20,21},{24,25},{28,29}} | collective-permute-start | bytes 1056776 | tf_op jit(solution)/shard_map/ppermute | solution.py:326
  11.2 12.1 %collective-permute-start = (f32[344,256]{1,0:T(8,128)S(1)}, f32[344,256]{1,0:T(8,128)}, u32[]{:S(2)}, u32[]{:S(2)}) collective-permute-start(f32[344,256]{1,0:T(8,128)S(1)} %get-tuple-element.88), channel_id=1, source_target_pairs={{0,3},{4,7},{8,11},{12,15},{16,19},{20,23},{24,27},{28,31}} | collective-permute-start | bytes 1056776 | tf_op jit(solution)/shard_map/ppermute | solution.py:326
  12.7 30.6 %collective-permute-start.6 = (f32[64,512]{1,0:T(8,128)S(1)}, f32[64,512]{1,0:T(8,128)S(1)}, u32[]{:S(2)}, u32[]{:S(2)}) collective-permute-start(f32[64,512]{1,0:T(8,128)S(1)} %get-tuple-element.98), channel_id=1, source_target_pairs={{0,8},{4,12},{8,0},{12,4},{16,24},{20,28},{24,16},{28,20},{1,9},{5... | collective-permute-start | bytes 393224 | tf_op jit(solution)/shard_map/ppermute | solution.py:360
  14.0 29.3 %collective-permute-start.8 = (f32[64,512]{1,0:T(8,128)S(1)}, f32[64,512]{1,0:T(8,128)S(1)}, u32[]{:S(2)}, u32[]{:S(2)}) collective-permute-start(f32[64,512]{1,0:T(8,128)S(1)} %get-tuple-element.99), channel_id=1, source_target_pairs={{0,24},{4,28},{8,16},{12,20},{16,8},{20,12},{24,0},{28,4},{1,25},{... | collective-permute-start | bytes 393224 | tf_op jit(solution)/shard_map/ppermute | solution.py:360
  22.0 21.3 %collective-permute-start.7 = (f32[64,512]{1,0:T(8,128)S(1)}, f32[64,512]{1,0:T(8,128)S(1)}, u32[]{:S(2)}, u32[]{:S(2)}) collective-permute-start(f32[64,512]{1,0:T(8,128)S(1)} %get-tuple-element.100), channel_id=1, source_target_pairs={{0,16},{4,20},{8,24},{12,28},{16,0},{20,4},{24,8},{28,12},{1,17},{... | collective-permute-start | bytes 393224 | tf_op jit(solution)/shard_map/ppermute | solution.py:360
  24.3 28.8 %collective-permute-start.4 = (f32[344,256]{1,0:T(8,128)S(1)}, f32[344,256]{1,0:T(8,128)S(1)}, u32[]{:S(2)}, u32[]{:S(2)}) collective-permute-start(f32[344,256]{1,0:T(8,128)S(1)} %add_add_fusion.1.rest_0_), channel_id=1, source_target_pairs={{1,3},{2,1},{3,2},{5,7},{6,5},{7,6},{9,11},{10,9},{11,10},{13,15},... | collective-permute-start | bytes 1056776 | tf_op jit(solution)/shard_map/ppermute | solution.py:334
  32.8 30.4 %collective-permute-start.3 = (f32[344,256]{1,0:T(8,128)S(1)}, f32[344,256]{1,0:T(8,128)S(1)}, u32[]{:S(2)}, u32[]{:S(2)}) collective-permute-start(f32[344,256]{1,0:T(8,128)S(1)} %add_add_fusion.1.rest_0_), channel_id=1, source_target_pairs={{1,2},{2,3},{3,1},{5,6},{6,7},{7,5},{9,10},{10,11},{11,9},{13,14},... | collective-permute-start | bytes 1056776 | tf_op jit(solution)/shard_map/ppermute | solution.py:334
  44.0 20.0 %collective-permute-start.11 = (f32[64,512]{1,0:T(8,128)}, f32[64,512]{1,0:T(8,128)S(1)}, u32[]{:S(2)}, u32[]{:S(2)}) collective-permute-start(f32[64,512]{1,0:T(8,128)} %add_add_fusion.4), channel_id=1, source_target_pairs={{0,1},{4,5},{8,9},{12,13},{16,17},{20,21},{24,25},{28,29}} | collective-permute-start | bytes 393224 | tf_op jit(solution)/shard_map/ppermute | solution.py:392
  44.7 19.3 %collective-permute-start.10 = (f32[64,512]{1,0:T(8,128)}, f32[64,512]{1,0:T(8,128)S(1)}, u32[]{:S(2)}, u32[]{:S(2)}) collective-permute-start(f32[64,512]{1,0:T(8,128)} %add_add_fusion.4), channel_id=1, source_target_pairs={{0,2},{4,6},{8,10},{12,14},{16,18},{20,22},{24,26},{28,30}} | collective-permute-start | bytes 393224 | tf_op jit(solution)/shard_map/ppermute | solution.py:392
  46.0 18.0 %collective-permute-start.9 = (f32[64,512]{1,0:T(8,128)}, f32[64,512]{1,0:T(8,128)S(1)}, u32[]{:S(2)}, u32[]{:S(2)}) collective-permute-start(f32[64,512]{1,0:T(8,128)} %add_add_fusion.4), channel_id=1, source_target_pairs={{0,3},{4,7},{8,11},{12,15},{16,19},{20,23},{24,27},{28,31}} | collective-permute-start | bytes 393224 | tf_op jit(solution)/shard_map/ppermute | solution.py:392
  48.5 3.4 %copy-start = (f32[1024,2048]{1,0:T(8,128)S(1)}, f32[1024,2048]{1,0:T(8,128)}, u32[]{:S(2)}) copy-start(f32[1024,2048]{1,0:T(8,128)} %s_ref.3) | copy-start | bytes 25165828
  53.1 19.7 %copy-start.1 = (bf16[1024,2048]{1,0:T(8,128)(2,1)}, bf16[1024,2048]{1,0:T(8,128)(2,1)S(1)}, u32[]{:S(2)}) copy-start(bf16[1024,2048]{1,0:T(8,128)(2,1)S(1)} %get-tuple-element.43.h_ref) | copy-start | bytes 12582916
  53.1 19.7 %copy-start.3 = (bf16[1024,2048]{1,0:T(8,128)(2,1)}, bf16[1024,2048]{1,0:T(8,128)(2,1)S(1)}, u32[]{:S(2)}) copy-start(bf16[1024,2048]{1,0:T(8,128)(2,1)S(1)} %get-tuple-element.44.l_ref) | copy-start | bytes 12582916
  53.1 0.8 copy-start.5
  63.2 0.7 copy-start.7
  64.0 0.7 copy-start.13
  64.0 0.7 copy-start.15
  64.7 1.0 copy-start.6
  65.7 1.0 copy-start.8
  66.7 7.8 %copy-start.12 = (f32[64,512]{1,0:T(8,128)S(1)}, f32[64,512]{1,0:T(8,128)}, u32[]{:S(2)}) copy-start(f32[64,512]{1,0:T(8,128)} %copy-done.11) | copy-start | bytes 393220
  66.7 7.8 %copy-start.14 = (f32[64,512]{1,0:T(8,128)S(1)}, f32[64,512]{1,0:T(8,128)}, u32[]{:S(2)}) copy-start(f32[64,512]{1,0:T(8,128)} %copy-done.13) | copy-start | bytes 393220
  66.7 7.8 %copy-start.16 = (f32[64,512]{1,0:T(8,128)S(1)}, f32[64,512]{1,0:T(8,128)}, u32[]{:S(2)}) copy-start(f32[64,512]{1,0:T(8,128)} %copy-done.15) | copy-start | bytes 393220
  72.8 13.9 %copy-start.9 = (f32[1024,256]{1,0:T(8,128)}, f32[1024,256]{1,0:T(8,128)S(1)}, u32[]{:S(2)}) copy-start(f32[1024,256]{1,0:T(8,128)S(1)} %get-tuple-element.48.refs_0_) | copy-start | bytes 3145732
  72.8 21.7 %collective-permute-start.17 = (f32[128,2048]{1,0:T(8,128)}, f32[128,2048]{1,0:T(8,128)}, u32[]{:S(2)}, u32[]{:S(2)}) collective-permute-start(f32[128,2048]{1,0:T(8,128)} %get-tuple-element.51), channel_id=1, source_target_pairs={{0,4},{4,0},{8,12},{12,8},{16,20},{20,16},{24,28},{28,24},{1,5},{5... | collective-permute-start | bytes 3145736 | tf_op jit(solution)/shard_map/ppermute | solution.py:351
  74.6 7.3 %collective-permute-start.23 = (f32[64,512]{1,0:T(8,128)S(1)}, f32[64,512]{1,0:T(8,128)S(1)}, u32[]{:S(2)}, u32[]{:S(2)}) collective-permute-start(f32[64,512]{1,0:T(8,128)S(1)} %add_select_fusion.refs_0_), channel_id=1, source_target_pairs={{0,24},{4,28},{8,16},{12,20},{16,8},{20,12},{24,0},{28,4},{1,25},{... | collective-permute-start | bytes 393224 | tf_op jit(solution)/shard_map/ppermute | solution.py:365
  77.7 15.0 %collective-permute-start.13 = (f32[344,256]{1,0:T(8,128)}, f32[344,256]{1,0:T(8,128)S(1)}, u32[]{:S(2)}, u32[]{:S(2)}) collective-permute-start(f32[344,256]{1,0:T(8,128)} %get-tuple-element.95), channel_id=1, source_target_pairs={{0,2},{4,6},{8,10},{12,14},{16,18},{20,22},{24,26},{28,30}} | collective-permute-start | bytes 1056776 | tf_op jit(solution)/shard_map/ppermute | solution.py:326
  79.0 13.7 %collective-permute-start.14 = (f32[344,256]{1,0:T(8,128)}, f32[344,256]{1,0:T(8,128)}, u32[]{:S(2)}, u32[]{:S(2)}) collective-permute-start(f32[344,256]{1,0:T(8,128)} %get-tuple-element.96), channel_id=1, source_target_pairs={{0,1},{4,5},{8,9},{12,13},{16,17},{20,21},{24,25},{28,29}} | collective-permute-start | bytes 1056776 | tf_op jit(solution)/shard_map/ppermute | solution.py:326
  80.4 12.8 %collective-permute-start.12 = (f32[344,256]{1,0:T(8,128)S(1)}, f32[344,256]{1,0:T(8,128)}, u32[]{:S(2)}, u32[]{:S(2)}) collective-permute-start(f32[344,256]{1,0:T(8,128)S(1)} %get-tuple-element.97), channel_id=1, source_target_pairs={{0,3},{4,7},{8,11},{12,15},{16,19},{20,23},{24,27},{28,31}} | collective-permute-start | bytes 1056776 | tf_op jit(solution)/shard_map/ppermute | solution.py:326
  81.8 4.8 %collective-permute-start.22 = (f32[64,512]{1,0:T(8,128)S(1)}, f32[64,512]{1,0:T(8,128)S(1)}, u32[]{:S(2)}, u32[]{:S(2)}) collective-permute-start(f32[64,512]{1,0:T(8,128)S(1)} %add_select_fusion.refs_0_), channel_id=1, source_target_pairs={{0,16},{4,20},{8,24},{12,28},{16,0},{20,4},{24,8},{28,12},{1,17},{... | collective-permute-start | bytes 393224 | tf_op jit(solution)/shard_map/ppermute | solution.py:365
  86.6 4.1 %collective-permute-start.21 = (f32[64,512]{1,0:T(8,128)S(1)}, f32[64,512]{1,0:T(8,128)S(1)}, u32[]{:S(2)}, u32[]{:S(2)}) collective-permute-start(f32[64,512]{1,0:T(8,128)S(1)} %add_select_fusion.refs_0_), channel_id=1, source_target_pairs={{0,8},{4,12},{8,0},{12,4},{16,24},{20,28},{24,16},{28,20},{1,9},{5... | collective-permute-start | bytes 393224 | tf_op jit(solution)/shard_map/ppermute | solution.py:365
  90.7 13.8 %collective-permute-start.24 = (f32[64,512]{1,0:T(8,128)S(1)}, f32[64,512]{1,0:T(8,128)S(1)}, u32[]{:S(2)}, u32[]{:S(2)}) collective-permute-start(f32[64,512]{1,0:T(8,128)S(1)} %add_select_fusion.refs_0_), channel_id=1, source_target_pairs={{0,4},{4,0},{8,12},{12,8},{16,20},{20,16},{24,28},{28,24},{1,5},{5... | collective-permute-start | bytes 393224 | tf_op jit(solution)/shard_map/ppermute | solution.py:366
  92.7 21.6 %collective-permute-start.27 = (f32[64,512]{1,0:T(8,128)S(1)}, f32[64,512]{1,0:T(8,128)S(1)}, u32[]{:S(2)}, u32[]{:S(2)}) collective-permute-start(f32[64,512]{1,0:T(8,128)S(1)} %collective-permute-done.23.refs_3_), channel_id=1, source_target_pairs={{0,4},{4,0},{8,12},{12,8},{16,20},{20,16},{24,28},{28,24},{1,5},{5... | collective-permute-start | bytes 393224 | tf_op jit(solution)/shard_map/ppermute | solution.py:366
  92.7 21.6 %collective-permute-start.26 = (f32[64,512]{1,0:T(8,128)S(1)}, f32[64,512]{1,0:T(8,128)S(1)}, u32[]{:S(2)}, u32[]{:S(2)}) collective-permute-start(f32[64,512]{1,0:T(8,128)S(1)} %collective-permute-done.22.refs_2_), channel_id=1, source_target_pairs={{0,4},{4,0},{8,12},{12,8},{16,20},{20,16},{24,28},{28,24},{1,5},{5... | collective-permute-start | bytes 393224 | tf_op jit(solution)/shard_map/ppermute | solution.py:366
  93.2 21.1 %collective-permute-start.25 = (f32[64,512]{1,0:T(8,128)S(1)}, f32[64,512]{1,0:T(8,128)S(1)}, u32[]{:S(2)}, u32[]{:S(2)}) collective-permute-start(f32[64,512]{1,0:T(8,128)S(1)} %collective-permute-done.21.refs_1_), channel_id=1, source_target_pairs={{0,4},{4,0},{8,12},{12,8},{16,20},{20,16},{24,28},{28,24},{1,5},{5... | collective-permute-start | bytes 393224 | tf_op jit(solution)/shard_map/ppermute | solution.py:366
  94.5 36.4 %collective-permute-start.16 = (f32[344,256]{1,0:T(8,128)S(1)}, f32[344,256]{1,0:T(8,128)S(1)}, u32[]{:S(2)}, u32[]{:S(2)}) collective-permute-start(f32[344,256]{1,0:T(8,128)S(1)} %add_add_fusion.rest_0_), channel_id=1, source_target_pairs={{1,3},{2,1},{3,2},{5,7},{6,5},{7,6},{9,11},{10,9},{11,10},{13,15},... | collective-permute-start | bytes 1056776 | tf_op jit(solution)/shard_map/ppermute | solution.py:334
  104.5 26.3 %collective-permute-start.15 = (f32[344,256]{1,0:T(8,128)S(1)}, f32[344,256]{1,0:T(8,128)S(1)}, u32[]{:S(2)}, u32[]{:S(2)}) collective-permute-start(f32[344,256]{1,0:T(8,128)S(1)} %add_add_fusion.rest_0_), channel_id=1, source_target_pairs={{1,2},{2,3},{3,1},{5,6},{6,7},{7,5},{9,10},{10,11},{11,9},{13,14},... | collective-permute-start | bytes 1056776 | tf_op jit(solution)/shard_map/ppermute | solution.py:334
  114.4 16.3 %collective-permute-start.18 = (f32[32,2048]{1,0:T(8,128)S(1)}, f32[32,2048]{1,0:T(8,128)S(1)}, u32[]{:S(2)}, u32[]{:S(2)}) collective-permute-start(f32[32,2048]{1,0:T(8,128)S(1)} %get-tuple-element.92), channel_id=1, source_target_pairs={{0,8},{4,12},{8,0},{12,4},{16,24},{20,28},{24,16},{28,20},{1,9},{5... | collective-permute-start | bytes 786440 | tf_op jit(solution)/shard_map/ppermute | solution.py:360
  114.8 16.0 %collective-permute-start.20 = (f32[32,2048]{1,0:T(8,128)S(1)}, f32[32,2048]{1,0:T(8,128)S(1)}, u32[]{:S(2)}, u32[]{:S(2)}) collective-permute-start(f32[32,2048]{1,0:T(8,128)S(1)} %get-tuple-element.93), channel_id=1, source_target_pairs={{0,24},{4,28},{8,16},{12,20},{16,8},{20,12},{24,0},{28,4},{1,25},{... | collective-permute-start | bytes 786440 | tf_op jit(solution)/shard_map/ppermute | solution.py:360
  115.9 14.9 %copy-start.2 = (bf16[1024,2048]{1,0:T(8,128)(2,1)S(1)}, bf16[1024,2048]{1,0:T(8,128)(2,1)}, u32[]{:S(2)}) copy-start(bf16[1024,2048]{1,0:T(8,128)(2,1)} %copy-done.1) | copy-start | bytes 12582916
  115.9 15.0 %copy-start.4 = (bf16[1024,2048]{1,0:T(8,128)(2,1)S(1)}, bf16[1024,2048]{1,0:T(8,128)(2,1)}, u32[]{:S(2)}) copy-start(bf16[1024,2048]{1,0:T(8,128)(2,1)} %copy-done.3) | copy-start | bytes 12582916
  115.9 14.8 %collective-permute-start.19 = (f32[32,2048]{1,0:T(8,128)S(1)}, f32[32,2048]{1,0:T(8,128)S(1)}, u32[]{:S(2)}, u32[]{:S(2)}) collective-permute-start(f32[32,2048]{1,0:T(8,128)S(1)} %get-tuple-element.94), channel_id=1, source_target_pairs={{0,16},{4,20},{8,24},{12,28},{16,0},{20,4},{24,8},{28,12},{1,17},{... | collective-permute-start | bytes 786440 | tf_op jit(solution)/shard_map/ppermute | solution.py:360
  136.0 3.5 %collective-permute-start.28 = (f32[128,2048]{1,0:T(8,128)S(1)}, f32[128,2048]{1,0:T(8,128)S(1)}, u32[]{:S(2)}, u32[]{:S(2)}) collective-permute-start(f32[128,2048]{1,0:T(8,128)S(1)} %get-tuple-element.68), channel_id=1, source_target_pairs={{0,4},{4,0},{8,12},{12,8},{16,20},{20,16},{24,28},{28,24},{1,5},{5... | collective-permute-start | bytes 3145736 | tf_op jit(solution)/shard_map/ppermute | solution.py:351
  137.2 11.8 %collective-permute-start.34 = (f32[32,2048]{1,0:T(8,128)S(1)}, f32[32,2048]{1,0:T(8,128)S(1)}, u32[]{:S(2)}, u32[]{:S(2)}) collective-permute-start(f32[32,2048]{1,0:T(8,128)S(1)} %add_add_fusion.3.rest_0_), channel_id=1, source_target_pairs={{0,24},{4,28},{8,16},{12,20},{16,8},{20,12},{24,0},{28,4},{1,25},{... | collective-permute-start | bytes 786440 | tf_op jit(solution)/shard_map/ppermute | solution.py:365
  137.4 13.2 %collective-permute-start.33 = (f32[32,2048]{1,0:T(8,128)S(1)}, f32[32,2048]{1,0:T(8,128)S(1)}, u32[]{:S(2)}, u32[]{:S(2)}) collective-permute-start(f32[32,2048]{1,0:T(8,128)S(1)} %add_add_fusion.3.rest_0_), channel_id=1, source_target_pairs={{0,16},{4,20},{8,24},{12,28},{16,0},{20,4},{24,8},{28,12},{1,17},{... | collective-permute-start | bytes 786440 | tf_op jit(solution)/shard_map/ppermute | solution.py:365
  139.7 12.9 %collective-permute-start.29 = (f32[32,2048]{1,0:T(8,128)S(1)}, f32[32,2048]{1,0:T(8,128)S(1)}, u32[]{:S(2)}, u32[]{:S(2)}) collective-permute-start(f32[32,2048]{1,0:T(8,128)S(1)} %get-tuple-element.89), channel_id=1, source_target_pairs={{0,8},{4,12},{8,0},{12,4},{16,24},{20,28},{24,16},{28,20},{1,9},{5... | collective-permute-start | bytes 786440 | tf_op jit(solution)/shard_map/ppermute | solution.py:360
  140.1 17.2 %collective-permute-start.31 = (f32[32,2048]{1,0:T(8,128)S(1)}, f32[32,2048]{1,0:T(8,128)S(1)}, u32[]{:S(2)}, u32[]{:S(2)}) collective-permute-start(f32[32,2048]{1,0:T(8,128)S(1)} %get-tuple-element.90), channel_id=1, source_target_pairs={{0,24},{4,28},{8,16},{12,20},{16,8},{20,12},{24,0},{28,4},{1,25},{... | collective-permute-start | bytes 786440 | tf_op jit(solution)/shard_map/ppermute | solution.py:360
  141.1 20.7 %collective-permute-start.30 = (f32[32,2048]{1,0:T(8,128)S(1)}, f32[32,2048]{1,0:T(8,128)S(1)}, u32[]{:S(2)}, u32[]{:S(2)}) collective-permute-start(f32[32,2048]{1,0:T(8,128)S(1)} %get-tuple-element.91), channel_id=1, source_target_pairs={{0,16},{4,20},{8,24},{12,28},{16,0},{20,4},{24,8},{28,12},{1,17},{... | collective-permute-start | bytes 786440 | tf_op jit(solution)/shard_map/ppermute | solution.py:360
  142.4 44.2 %slice-start = ((s8[8388608]{0:T(1024)(128)(4,1)}), s8[4194304]{0:T(1024)(128)(4,1)S(1)}, s32[]{:S(2)}) async-start(s8[8388608]{0:T(1024)(128)(4,1)} %bitcast.6), calls=%async_computation | async-start | bytes 8388608
  149.0 14.6 %collective-permute-start.35 = (f32[32,2048]{1,0:T(8,128)S(1)}, f32[32,2048]{1,0:T(8,128)S(1)}, u32[]{:S(2)}, u32[]{:S(2)}) collective-permute-start(f32[32,2048]{1,0:T(8,128)S(1)} %add_add_fusion.3.rest_0_), channel_id=1, source_target_pairs={{0,4},{4,0},{8,12},{12,8},{16,20},{20,16},{24,28},{28,24},{1,5},{5... | collective-permute-start | bytes 786440 | tf_op jit(solution)/shard_map/ppermute | solution.py:366
  150.5 14.2 %collective-permute-start.32 = (f32[32,2048]{1,0:T(8,128)S(1)}, f32[32,2048]{1,0:T(8,128)S(1)}, u32[]{:S(2)}, u32[]{:S(2)}) collective-permute-start(f32[32,2048]{1,0:T(8,128)S(1)} %add_add_fusion.3.rest_0_), channel_id=1, source_target_pairs={{0,8},{4,12},{8,0},{12,4},{16,24},{20,28},{24,16},{28,20},{1,9},{5... | collective-permute-start | bytes 786440 | tf_op jit(solution)/shard_map/ppermute | solution.py:365
  152.5 12.3 %collective-permute-start.38 = (f32[32,2048]{1,0:T(8,128)S(1)}, f32[32,2048]{1,0:T(8,128)S(1)}, u32[]{:S(2)}, u32[]{:S(2)}) collective-permute-start(f32[32,2048]{1,0:T(8,128)S(1)} %collective-permute-done.34.rest_3_), channel_id=1, source_target_pairs={{0,4},{4,0},{8,12},{12,8},{16,20},{20,16},{24,28},{28,24},{1,5},{5... | collective-permute-start | bytes 786440 | tf_op jit(solution)/shard_map/ppermute | solution.py:366
  157.3 9.3 %collective-permute-start.37 = (f32[32,2048]{1,0:T(8,128)S(1)}, f32[32,2048]{1,0:T(8,128)S(1)}, u32[]{:S(2)}, u32[]{:S(2)}) collective-permute-start(f32[32,2048]{1,0:T(8,128)S(1)} %collective-permute-done.33.rest_2_), channel_id=1, source_target_pairs={{0,4},{4,0},{8,12},{12,8},{16,20},{20,16},{24,28},{28,24},{1,5},{5... | collective-permute-start | bytes 786440 | tf_op jit(solution)/shard_map/ppermute | solution.py:366
  161.8 22.0 %copy-start.10 = (f32[1024,256]{1,0:T(8,128)S(1)}, f32[1024,256]{1,0:T(8,128)}, u32[]{:S(2)}) copy-start(f32[1024,256]{1,0:T(8,128)} %copy-done.9) | copy-start | bytes 3145732
  161.8 24.7 %slice-start.1 = ((s8[8388608]{0:T(1024)(128)(4,1)}), s8[4194304]{0:T(1024)(128)(4,1)S(1)}, s32[]{:S(2)}) async-start(s8[8388608]{0:T(1024)(128)(4,1)} %bitcast.6), calls=%async_computation.1 | async-start | bytes 8388608
  161.9 7.6 %collective-permute-start.41 = (f32[32,2048]{1,0:T(8,128)S(1)}, f32[32,2048]{1,0:T(8,128)S(1)}, u32[]{:S(2)}, u32[]{:S(2)}) collective-permute-start(f32[32,2048]{1,0:T(8,128)S(1)} %add_add_fusion.2.rest_8_), channel_id=1, source_target_pairs={{0,24},{4,28},{8,16},{12,20},{16,8},{20,12},{24,0},{28,4},{1,25},{... | collective-permute-start | bytes 786440 | tf_op jit(solution)/shard_map/ppermute | solution.py:365
  163.5 13.2 %collective-permute-start.40 = (f32[32,2048]{1,0:T(8,128)S(1)}, f32[32,2048]{1,0:T(8,128)S(1)}, u32[]{:S(2)}, u32[]{:S(2)}) collective-permute-start(f32[32,2048]{1,0:T(8,128)S(1)} %add_add_fusion.2.rest_8_), channel_id=1, source_target_pairs={{0,16},{4,20},{8,24},{12,28},{16,0},{20,4},{24,8},{28,12},{1,17},{... | collective-permute-start | bytes 786440 | tf_op jit(solution)/shard_map/ppermute | solution.py:365
  164.8 12.4 %collective-permute-start.39 = (f32[32,2048]{1,0:T(8,128)S(1)}, f32[32,2048]{1,0:T(8,128)S(1)}, u32[]{:S(2)}, u32[]{:S(2)}) collective-permute-start(f32[32,2048]{1,0:T(8,128)S(1)} %add_add_fusion.2.rest_8_), channel_id=1, source_target_pairs={{0,8},{4,12},{8,0},{12,4},{16,24},{20,28},{24,16},{28,20},{1,9},{5... | collective-permute-start | bytes 786440 | tf_op jit(solution)/shard_map/ppermute | solution.py:365
  164.8 21.7 %collective-permute-start.36 = (f32[32,2048]{1,0:T(8,128)S(1)}, f32[32,2048]{1,0:T(8,128)S(1)}, u32[]{:S(2)}, u32[]{:S(2)}) collective-permute-start(f32[32,2048]{1,0:T(8,128)S(1)} %collective-permute-done.32.rest_1_), channel_id=1, source_target_pairs={{0,4},{4,0},{8,12},{12,8},{16,20},{20,16},{24,28},{28,24},{1,5},{5... | collective-permute-start | bytes 786440 | tf_op jit(solution)/shard_map/ppermute | solution.py:366
  166.6 19.9 %collective-permute-start.42 = (f32[32,2048]{1,0:T(8,128)S(1)}, f32[32,2048]{1,0:T(8,128)S(1)}, u32[]{:S(2)}, u32[]{:S(2)}) collective-permute-start(f32[32,2048]{1,0:T(8,128)S(1)} %add_add_fusion.2.rest_8_), channel_id=1, source_target_pairs={{0,4},{4,0},{8,12},{12,8},{16,20},{20,16},{24,28},{28,24},{1,5},{5... | collective-permute-start | bytes 786440 | tf_op jit(solution)/shard_map/ppermute | solution.py:366
  169.5 17.0 %collective-permute-start.45 = (f32[32,2048]{1,0:T(8,128)S(1)}, f32[32,2048]{1,0:T(8,128)S(1)}, u32[]{:S(2)}, u32[]{:S(2)}) collective-permute-start(f32[32,2048]{1,0:T(8,128)S(1)} %collective-permute-done.41.rest_11_), channel_id=1, source_target_pairs={{0,4},{4,0},{8,12},{12,8},{16,20},{20,16},{24,28},{28,24},{1,5},{5... | collective-permute-start | bytes 786440 | tf_op jit(solution)/shard_map/ppermute | solution.py:366
  176.7 9.9 %collective-permute-start.44 = (f32[32,2048]{1,0:T(8,128)S(1)}, f32[32,2048]{1,0:T(8,128)S(1)}, u32[]{:S(2)}, u32[]{:S(2)}) collective-permute-start(f32[32,2048]{1,0:T(8,128)S(1)} %collective-permute-done.40.rest_10_), channel_id=1, source_target_pairs={{0,4},{4,0},{8,12},{12,8},{16,20},{20,16},{24,28},{28,24},{1,5},{5... | collective-permute-start | bytes 786440 | tf_op jit(solution)/shard_map/ppermute | solution.py:366
  177.2 9.4 %collective-permute-start.43 = (f32[32,2048]{1,0:T(8,128)S(1)}, f32[32,2048]{1,0:T(8,128)S(1)}, u32[]{:S(2)}, u32[]{:S(2)}) collective-permute-start(f32[32,2048]{1,0:T(8,128)S(1)} %collective-permute-done.39.rest_9_), channel_id=1, source_target_pairs={{0,4},{4,0},{8,12},{12,8},{16,20},{20,16},{24,28},{28,24},{1,5},{5... | collective-permute-start | bytes 786440 | tf_op jit(solution)/shard_map/ppermute | solution.py:366
  (1 other events, 0.7 us)

commit v8 on v7

--- a/solution.py
+++ b/solution.py
@@ -391,11 +391,11 @@
     share = scatter_chips(joined, n_rows)
     far = [lax.ppermute(share, "cols", [(0, k)]) for k in reversed(range(1, n_cols))]
     got_a = spread_round(mine_a, n_cols)
-    mine_b = spread_out(after(panel[:, half:], got_a), n_cols)
+    mine_b = spread_out(after(panel[:, half:], mine_a), n_cols)
     share = jnp.where(z == 0, share, sum(far, jnp.zeros_like(share)))
     grams, places = gather_rows(share, n_rows)
 
-    send, keep, panel_a = dot(after(got_a, far, high), 0)
+    send, keep, panel_a = dot(after(got_a, far, mine_b, high), 0)
     joined = join_cores(send, keep, n_rows)
     got_b = spread_round(mine_b, n_cols)
     own_a = scatter_chips(joined, n_rows)
@@ -404,9 +404,8 @@
     send, keep, panel_b = dot(after(got_b, own_a, state), half)
     joined = join_cores(send, keep, n_rows)
     own_b = scatter_chips(joined, n_rows)
-    state = chol_part(info, 2, 3, state=after(state, joined))
-    pieces_b, _ = gather_rows(after(own_b, state), n_rows)
-    _, factor, linv = chol_part(info, 3, 4, state=after(state, own_b))
+    _, factor, linv = chol_part(info, 2, 4, state=after(state, joined))
+    pieces_b, _ = gather_rows(after(own_b, linv), n_rows)
     b, b3, l3 = basis([panel_a, panel_b], linv)
     layout = [(base,) + w for base in (0, half) for w in where]
     return finish(info, snapshots, b, b3, l3, factor, pieces_a + pieces_b, layout)

time: 202 us -> 187 us (0.926)
  starting transfers between devices: 81.9 us -> 65.4 us
  other arithmetic: 4.67 us -> 6.97 us
    ppermute x4, starting transfers between devices: 37.4 us -> 23.8 us  [spread_round(): got.append(lax.ppermute(mine, 'cols', pairs))]
    ppermute x4, waiting for transfers between devices: 9.35 us -> 21.4 us  [spread_round(): got.append(lax.ppermute(mine, 'cols', pairs))]
    ppermute x6, waiting for transfers between devices: 6.84 us -> 0.02 us  [spread_out(): got.append(lax.ppermute(x[start:start + size], 'cols', [(0, k + 1)]))]
    ppermute x12, starting transfers between devices: 12.7 us -> 9.2 us  [gather_rows(): other = [lax.ppermute(g, 'rows', swap(n, 1)) for g in got]]
    ppermute x9, waiting for transfers between devices: 15.2 us -> 13.1 us  [gather_rows(): lax.ppermute(own, 'rows', swap(n, 2 * k))]
    unnamed x38 -> x34, local copies, waits for them, and re-layouts: 7.63 us -> 6.06 us
    pallas_call x3 -> x2, Pallas kernels: 26.3 us -> 25.9 us  [chol_part(): pl.pallas_call(kernel, out_shape=(shape, shape, shape), in_specs=[SMEM] +...]
  transfers between devices with their start and end apart: 46 -> 46, of which waited for: 10 -> 6; matrix products, arithmetic and copies ran while one was open for 5% -> 8% of each run, Pallas kernels for 15% -> 16%
where the time goes in v8:
time: 187 us; the launch traced here: 186 us
  starting transfers between devices  65.4 us (35%)
  Pallas kernels  55.1 us (29%)
  waiting for transfers between devices  39.5 us (21%)
  local copies, waits for them, and re-layouts  12 us (6%)
  other arithmetic  6.97 us (4%)
  matrix products  5.71 us (3%)
    pallas_call x2, Pallas kernels, chol_part(): pl.pallas_call(kernel, out_shape=(shape, shape, shape), in_specs=[SMEM] +...  25.9 us
    ppermute x4, starting transfers between devices, spread_round(): got.append(lax.ppermute(mine, 'cols', pairs))  23.8 us
    ppermute x4, waiting for transfers between devices, spread_round(): got.append(lax.ppermute(mine, 'cols', pairs))  21.4 us
    pallas_call x1, Pallas kernels, finish(): pl.pallas_call(kernel, out_shape=(jax.ShapeDtypeStruct((rows, cols), F32)...  13.8 us
    ppermute x9, waiting for transfers between devices, gather_rows(): lax.ppermute(own, 'rows', swap(n, 2 * k))  13.1 us
    pallas_call x2, Pallas kernels, panel_dot(): pl.pallas_call(kernel, out_shape=(out, out, jax.ShapeDtypeStruct((rows, w...  11.4 us
    ppermute x12, starting transfers between devices, gather_rows(): other = [lax.ppermute(g, 'rows', swap(n, 1)) for g in got]  9.2 us
    ppermute x9, starting transfers between devices, gather_rows(): lax.ppermute(own, 'rows', swap(n, 2 * k))  8.69 us
  transfers between devices with their start and end apart: 46, of which 6 were waited for; matrix products, arithmetic and copies ran while one was open for 8% of the time, Pallas kernels for 16%

profile of v8, /device:TPU:17, one launch (start us, length us, event | category | flops | bytes accessed | tf_op | source)
XLA Modules:
  0.0 186.0 jit_solution(4591345708810346559)
XLA Ops:
  0.6 2.2 %fusion.6 = (f32[344,256]{1,0:T(8,128)}, f32[344,256]{1,0:T(8,128)}, f32[344,256]{1,0:T(8,128)}) fusion(f32[1024,2048]{1,0:T(8,128)} %s_ref.3), kind=kLoop, calls=%fused_computation.21 | loop fusion | bytes 2113536 | tf_op jit(solution)/shard_map/slice | solution.py:326
  2.8 1.3 collective-permute-start.1
  4.1 1.4 collective-permute-start.2
  5.5 1.4 collective-permute-start
  6.9 5.7 %fusion.2 = f32[512,512]{1,0:T(8,128)S(1)} fusion(f32[1024,2048]{1,0:T(8,128)} %s_ref.3), kind=kOutput, calls=%fused_computation.2 | convolution fusion | flops 3221487616 | bytes 3145728 | tf_op jit(solution)/shard_map/dot_general | solution.py:31
  12.7 0.7 collective-permute-start.5
  13.6 1.8 fusion.5
  15.4 0.7 copy-done.11
  16.1 1.3 add_add_fusion.1.rest_0_
  17.5 0.7 constant_dynamic-slice_fusion.8
  18.3 1.2 collective-permute-start.6
  19.5 1.2 collective-permute-start.8
  20.9 1.0 fusion.7
  21.9 1.3 collective-permute-start.13
  23.2 1.4 collective-permute-start.14
  24.6 1.4 collective-permute-start.12
  26.1 3.4 %copy-done = f32[1024,2048]{1,0:T(8,128)S(1)} copy-done((f32[1024,2048]{1,0:T(8,128)S(1)}, f32[1024,2048]{1,0:T(8,128)}, u32[]{:S(2)}) %copy-start) | copy-done | bytes 8388632
  29.5 1.3 stage.1
  30.9 7.9 %collective-permute-start.4 = (f32[344,256]{1,0:T(8,128)S(1)}, f32[344,256]{1,0:T(8,128)S(1)}, u32[]{:S(2)}, u32[]{:S(2)}) collective-permute-start(f32[344,256]{1,0:T(8,128)S(1)} %add_add_fusion.1.rest_0_), channel_id=1, source_target_pairs={{1,3},{2,1},{3,2},{5,7},{6,5},{7,6},{9,11},{10,9},{11,10},{13,15},... | collective-permute-start | bytes 1056776 | tf_op jit(solution)/shard_map/ppermute | solution.py:334
  38.8 10.4 %collective-permute-start.3 = (f32[344,256]{1,0:T(8,128)S(1)}, f32[344,256]{1,0:T(8,128)S(1)}, u32[]{:S(2)}, u32[]{:S(2)}) collective-permute-start(f32[344,256]{1,0:T(8,128)S(1)} %add_add_fusion.1.rest_0_), channel_id=1, source_target_pairs={{1,2},{2,3},{3,1},{5,6},{6,7},{7,5},{9,10},{10,11},{11,9},{13,14},... | collective-permute-start | bytes 1056776 | tf_op jit(solution)/shard_map/ppermute | solution.py:334
  49.2 1.0 add_add_fusion.4
  50.3 0.7 collective-permute-start.11
  51.0 1.3 collective-permute-start.10
  52.3 0.7 collective-permute-start.9
  52.9 1.9 %add_add_fusion.rest_0_ = f32[344,256]{1,0:T(8,128)} fusion(f32[344,256]{1,0:T(8,128)} %collective-permute-done.14, f32[344,256]{1,0:T(8,128)} %collective-permute-done.12, f32[344,256]{1,0:T(8,128)S(1)} %collective-permute-done.13), kind=kLoop, calls=%fused_computation.4 | loop fusion | flops 176128 | bytes 1409024 | tf_op jit(solution)/shard_map/add | solution.py:327
  54.9 21.3 %collective-permute-done.3.rest_1_ = f32[344,256]{1,0:T(8,128)S(1)} collective-permute-done((f32[344,256]{1,0:T(8,128)S(1)}, f32[344,256]{1,0:T(8,128)S(1)}, u32[]{:S(2)}, u32[]{:S(2)}) %collective-permute-start.3) | collective-permute-done | bytes 352288 | tf_op jit(solution)/shard_map/ppermute | solution.py:334
  76.3 0.6 copy-done.12
  77.0 6.1 %panel_dot.2 = (f32[128,2048]{1,0:T(8,128)}, f32[128,2048]{1,0:T(8,128)S(1)}, f32[1024,256]{1,0:T(8,128)S(1)}) custom-call(s32[6]{0:T(128)S(1)} %stack.27.info_ref, bf16[1024,2048]{1,0:T(8,128)(2,1)S(1)} %get-tuple-element.37.h_ref, bf16[1024,2048]{1,0:T(8,128)(2,1)S(1)} %get-tuple-element.38.l_ref, f32[1024,256]{1,0:T(8,128)S(1)} %get-tuple-element.73.own_ref, ...), custom_call_target="tpu_custom_call" | custom-call | flops 3221225472 | bytes 1048576 | tf_op jit(solution)/shard_map/panel_dot/pallas_call | solution.py:301
  83.1 1.0 copy-done.6
  84.1 2.2 %collective-permute-start.17 = (f32[128,2048]{1,0:T(8,128)}, f32[128,2048]{1,0:T(8,128)}, u32[]{:S(2)}, u32[]{:S(2)}) collective-permute-start(f32[128,2048]{1,0:T(8,128)} %get-tuple-element.45), channel_id=1, source_target_pairs={{0,4},{4,0},{8,12},{12,8},{16,20},{20,16},{24,28},{28,24},{1,5},{5... | collective-permute-start | bytes 3145736 | tf_op jit(solution)/shard_map/ppermute | solution.py:351
  86.3 1.1 add_select_fusion.refs_0_
  87.3 2.2 %collective-permute-start.23 = (f32[64,512]{1,0:T(8,128)S(1)}, f32[64,512]{1,0:T(8,128)S(1)}, u32[]{:S(2)}, u32[]{:S(2)}) collective-permute-start(f32[64,512]{1,0:T(8,128)S(1)} %add_select_fusion.refs_0_), channel_id=1, source_target_pairs={{0,24},{4,28},{8,16},{12,20},{16,8},{20,12},{24,0},{28,4},{1,25},{... | collective-permute-start | bytes 393224 | tf_op jit(solution)/shard_map/ppermute | solution.py:365
  90.0 0.8 collective-permute-start.24
  90.9 2.5 %collective-permute-done.23.refs_3_ = f32[64,512]{1,0:T(8,128)S(1)} collective-permute-done((f32[64,512]{1,0:T(8,128)S(1)}, f32[64,512]{1,0:T(8,128)S(1)}, u32[]{:S(2)}, u32[]{:S(2)}) %collective-permute-start.23) | collective-permute-done | bytes 131104 | tf_op jit(solution)/shard_map/ppermute | solution.py:365
  93.4 1.1 collective-permute-start.27
  94.5 2.1 %collective-permute-done.22.refs_2_ = f32[64,512]{1,0:T(8,128)S(1)} collective-permute-done((f32[64,512]{1,0:T(8,128)S(1)}, f32[64,512]{1,0:T(8,128)S(1)}, u32[]{:S(2)}, u32[]{:S(2)}) %collective-permute-start.22) | collective-permute-done | bytes 131104 | tf_op jit(solution)/shard_map/ppermute | solution.py:365
  96.5 0.5 collective-permute-start.26
  97.1 1.9 %collective-permute-start.16 = (f32[344,256]{1,0:T(8,128)}, f32[344,256]{1,0:T(8,128)S(1)}, u32[]{:S(2)}, u32[]{:S(2)}) collective-permute-start(f32[344,256]{1,0:T(8,128)} %add_add_fusion.rest_0_), channel_id=1, source_target_pairs={{1,3},{2,1},{3,2},{5,7},{6,5},{7,6},{9,11},{10,9},{11,10},{13,15},... | collective-permute-start | bytes 1056776 | tf_op jit(solution)/shard_map/ppermute | solution.py:334
  99.0 1.3 add.122
  100.4 3.5 %collective-permute-start.15 = (f32[344,256]{1,0:T(8,128)}, f32[344,256]{1,0:T(8,128)S(1)}, u32[]{:S(2)}, u32[]{:S(2)}) collective-permute-start(f32[344,256]{1,0:T(8,128)} %add_add_fusion.rest_0_), channel_id=1, source_target_pairs={{1,2},{2,3},{3,1},{5,6},{6,7},{7,5},{9,10},{10,11},{11,9},{13,14},... | collective-permute-start | bytes 1056776 | tf_op jit(solution)/shard_map/ppermute | solution.py:334
  104.0 1.3 collective-permute-start.18
  105.3 1.2 collective-permute-start.20
  106.8 13.6 %chol_part.2 = (f32[512,512]{1,0:T(8,128)S(1)}, f32[512,512]{1,0:T(8,128)S(1)}, f32[512,512]{1,0:T(8,128)S(1)}) custom-call(s32[6]{0:T(128)S(1)} %stack.27.info_ref, f32[64,512]{1,0:T(8,128)S(1)} %add_select_fusion.refs_0_, f32[64,512]{1,0:T(8,128)S(1)} %collective-permute-done.21.refs_1_, f32[64,512]{1,0:T(8,128)S(1)} %collective-permute-done.22.refs_2_, ...), custom_call_target="tpu_custom_call" | custom-call | flops 16000000000 | bytes 1048576 | tf_op jit(solution)/shard_map/chol_part/pallas_call | solution.py:132
  120.5 5.3 %panel_dot.3 = (f32[128,2048]{1,0:T(8,128)S(1)}, f32[128,2048]{1,0:T(8,128)S(1)}, f32[1024,256]{1,0:T(8,128)S(1)}) custom-call(s32[6]{0:T(128)S(1)} %stack.27.info_ref, bf16[1024,2048]{1,0:T(8,128)(2,1)S(1)} %copy-done.3, bf16[1024,2048]{1,0:T(8,128)(2,1)S(1)} %copy-done.5, f32[1024,256]{1,0:T(8,128)S(1)} %get-tuple-element.39.own_ref, ...), custom_call_target="tpu_custom_call" | custom-call | flops 3221225472 | bytes 1048576 | tf_op jit(solution)/shard_map/panel_dot/pallas_call | solution.py:301
  125.9 1.9 %collective-permute-start.28 = (f32[128,2048]{1,0:T(8,128)S(1)}, f32[128,2048]{1,0:T(8,128)S(1)}, u32[]{:S(2)}, u32[]{:S(2)}) collective-permute-start(f32[128,2048]{1,0:T(8,128)S(1)} %get-tuple-element.62), channel_id=1, source_target_pairs={{0,4},{4,0},{8,12},{12,8},{16,20},{20,16},{24,28},{28,24},{1,5},{5... | collective-permute-start | bytes 3145736 | tf_op jit(solution)/shard_map/ppermute | solution.py:351
  127.7 1.5 collective-permute-start.31
  129.2 0.9 collective-permute-start.30
  130.4 1.2 collective-permute-start.36
  131.5 1.2 collective-permute-start.38
  132.7 0.4 collective-permute-start.37
  133.1 12.3 %chol_part.3 = (f32[512,512]{1,0:T(8,128)S(1)}, f32[512,512]{1,0:T(8,128)S(1)}, f32[512,512]{1,0:T(8,128)S(1)}) custom-call(s32[6]{0:T(128)S(1)} %stack.27.info_ref, f32[512,512]{1,0:T(8,128)S(1)} %get-tuple-element.63.refs_0_, f32[512,512]{1,0:T(8,128)S(1)} %get-tuple-element.64.refs_1_, ...), custom_call_target="tpu_custom_call", output_to_operand_aliasing={{0}: (1, {}), {1}: (2, {}), {2}: (3, {})} | custom-call | flops 16000000000 | bytes 1048576 | tf_op jit(solution)/shard_map/chol_part/pallas_call | solution.py:132
  145.4 1.5 collective-permute-start.32
  146.9 0.8 collective-permute-start.29
  148.1 0.6 collective-permute-start.34
  148.8 5.0 %collective-permute-done.37 = f32[32,2048]{1,0:T(8,128)S(1)} collective-permute-done((f32[32,2048]{1,0:T(8,128)S(1)}, f32[32,2048]{1,0:T(8,128)S(1)}, u32[]{:S(2)}, u32[]{:S(2)}) %collective-permute-start.37) | collective-permute-done | bytes 262176 | tf_op jit(solution)/shard_map/ppermute | solution.py:360
  153.8 1.5 collective-permute-start.41
  155.4 0.9 collective-permute-start.40
  156.5 1.3 collective-permute-start.33
  157.9 4.3 %collective-permute-done.41.rest_11_ = f32[32,2048]{1,0:T(8,128)S(1)} collective-permute-done((f32[32,2048]{1,0:T(8,128)S(1)}, f32[32,2048]{1,0:T(8,128)S(1)}, u32[]{:S(2)}, u32[]{:S(2)}) %collective-permute-start.41) | collective-permute-done | bytes 262176 | tf_op jit(solution)/shard_map/ppermute | solution.py:365
  162.2 2.2 %collective-permute-start.45 = (f32[32,2048]{1,0:T(8,128)S(1)}, f32[32,2048]{1,0:T(8,128)S(1)}, u32[]{:S(2)}, u32[]{:S(2)}) collective-permute-start(f32[32,2048]{1,0:T(8,128)S(1)} %collective-permute-done.41.rest_11_), channel_id=1, source_target_pairs={{0,4},{4,0},{8,12},{12,8},{16,20},{20,16},{24,28},{28,24},{1,5},{5... | collective-permute-start | bytes 786440 | tf_op jit(solution)/shard_map/ppermute | solution.py:366
  164.5 4.2 %collective-permute-done.40.rest_10_ = f32[32,2048]{1,0:T(8,128)S(1)} collective-permute-done((f32[32,2048]{1,0:T(8,128)S(1)}, f32[32,2048]{1,0:T(8,128)S(1)}, u32[]{:S(2)}, u32[]{:S(2)}) %collective-permute-start.40) | collective-permute-done | bytes 262176 | tf_op jit(solution)/shard_map/ppermute | solution.py:365
  168.6 0.5 collective-permute-start.44
  169.2 2.7 %basis.1 = (f32[1024,512]{1,0:T(8,128)S(1)}, bf16[1024,1536]{1,0:T(8,128)(2,1)S(1)}, bf16[512,1536]{1,0:T(8,128)(2,1)S(1)}) custom-call(f32[1024,256]{1,0:T(8,128)S(1)} %copy-done.7, f32[1024,256]{1,0:T(8,128)S(1)} %get-tuple-element.60.refs_1_, f32[512,512]{1,0:T(8,128)S(1)} %get-tuple-element.66.refs_2_), custom_call_target="tpu_custom_call" | custom-call | flops 1610612736 | bytes 1048576 | tf_op jit(solution)/shard_map/basis/pallas_call | solution.py:183
  172.0 13.8 %finish.1 = (f32[1024,2048]{1,0:T(8,128)}, f32[512,2048]{1,0:T(8,128)}) custom-call(s32[6]{0:T(128)S(1)} %stack.27.info_ref, f32[1024,2048]{1,0:T(8,128)S(1)} %bitcast.7, f32[1024,512]{1,0:T(8,128)S(1)} %get-tuple-element.67.b_ref, bf16[1024,1536]{1,0:T(8,128)(2,1)S(1)} %get-tuple-element.68.b3_ref, bf16[512,1536]{1,0:T(8,128)(2,1)S(1)} %get-tuple-element.69.l3_ref, ...), custom_call_target="tpu_custom_call" | custom-call | flops 10000000000 | bytes 1048576 | tf_op jit(solution)/shard_map/finish/pallas_call | solution.py:242
  (88 shorter events, 2.9 us)
Async XLA Ops:
  2.8 12.6 %collective-permute-start.1 = (f32[344,256]{1,0:T(8,128)}, f32[344,256]{1,0:T(8,128)S(1)}, u32[]{:S(2)}, u32[]{:S(2)}) collective-permute-start(f32[344,256]{1,0:T(8,128)} %get-tuple-element.74), channel_id=1, source_target_pairs={{0,2},{4,6},{8,10},{12,14},{16,18},{20,22},{24,26},{28,30}} | collective-permute-start | bytes 1056776 | tf_op jit(solution)/shard_map/ppermute | solution.py:326
  4.1 11.3 %collective-permute-start.2 = (f32[344,256]{1,0:T(8,128)}, f32[344,256]{1,0:T(8,128)}, u32[]{:S(2)}, u32[]{:S(2)}) collective-permute-start(f32[344,256]{1,0:T(8,128)} %get-tuple-element.75), channel_id=1, source_target_pairs={{0,1},{4,5},{8,9},{12,13},{16,17},{20,21},{24,25},{28,29}} | collective-permute-start | bytes 1056776 | tf_op jit(solution)/shard_map/ppermute | solution.py:326
  5.5 10.6 %collective-permute-start = (f32[344,256]{1,0:T(8,128)}, f32[344,256]{1,0:T(8,128)}, u32[]{:S(2)}, u32[]{:S(2)}) collective-permute-start(f32[344,256]{1,0:T(8,128)} %get-tuple-element.76), channel_id=1, source_target_pairs={{0,3},{4,7},{8,11},{12,15},{16,19},{20,23},{24,27},{28,31}} | collective-permute-start | bytes 1056776 | tf_op jit(solution)/shard_map/ppermute | solution.py:326
  12.6 1.0 copy-start.8
  12.7 4.7 %collective-permute-start.5 = (f32[256,512]{1,0:T(8,128)S(1)}, f32[256,512]{1,0:T(8,128)S(1)}, u32[]{:S(2)}, u32[]{:S(2)}) collective-permute-start(f32[256,512]{1,0:T(8,128)S(1)} %constant_dynamic-slice_fusion.9), channel_id=1, source_target_pairs={{0,4},{4,0},{8,12},{12,8},{16,20},{20,16},{24,28},{28,24},{1,5},{5... | collective-permute-start | bytes 1572872 | tf_op jit(solution)/shard_map/ppermute | solution.py:351
  13.6 3.8 %copy-start.9 = (f32[512,512]{1,0:T(8,128)S(1)}, f32[512,512]{1,0:T(8,128)}, u32[]{:S(2)}) copy-start(f32[512,512]{1,0:T(8,128)} %copy-done.8) | copy-start | bytes 3145732
  15.4 0.7 copy-start.11
  18.3 6.4 %collective-permute-start.6 = (f32[64,512]{1,0:T(8,128)S(1)}, f32[64,512]{1,0:T(8,128)S(1)}, u32[]{:S(2)}, u32[]{:S(2)}) collective-permute-start(f32[64,512]{1,0:T(8,128)S(1)} %get-tuple-element.86), channel_id=1, source_target_pairs={{0,8},{4,12},{8,0},{12,4},{16,24},{20,28},{24,16},{28,20},{1,9},{5... | collective-permute-start | bytes 393224 | tf_op jit(solution)/shard_map/ppermute | solution.py:360
  19.5 11.4 %collective-permute-start.8 = (f32[64,512]{1,0:T(8,128)}, f32[64,512]{1,0:T(8,128)}, u32[]{:S(2)}, u32[]{:S(2)}) collective-permute-start(f32[64,512]{1,0:T(8,128)} %get-tuple-element.87), channel_id=1, source_target_pairs={{0,24},{4,28},{8,16},{12,20},{16,8},{20,12},{24,0},{28,4},{1,25},{... | collective-permute-start | bytes 393224 | tf_op jit(solution)/shard_map/ppermute | solution.py:360
  20.7 18.1 %collective-permute-start.7 = (f32[64,512]{1,0:T(8,128)}, f32[64,512]{1,0:T(8,128)}, u32[]{:S(2)}, u32[]{:S(2)}) collective-permute-start(f32[64,512]{1,0:T(8,128)} %get-tuple-element.88), channel_id=1, source_target_pairs={{0,16},{4,20},{8,24},{12,28},{16,0},{20,4},{24,8},{28,12},{1,17},{... | collective-permute-start | bytes 393224 | tf_op jit(solution)/shard_map/ppermute | solution.py:360
  21.9 28.3 %collective-permute-start.13 = (f32[344,256]{1,0:T(8,128)}, f32[344,256]{1,0:T(8,128)S(1)}, u32[]{:S(2)}, u32[]{:S(2)}) collective-permute-start(f32[344,256]{1,0:T(8,128)} %get-tuple-element.83), channel_id=1, source_target_pairs={{0,2},{4,6},{8,10},{12,14},{16,18},{20,22},{24,26},{28,30}} | collective-permute-start | bytes 1056776 | tf_op jit(solution)/shard_map/ppermute | solution.py:326
  23.2 27.7 %collective-permute-start.14 = (f32[344,256]{1,0:T(8,128)}, f32[344,256]{1,0:T(8,128)}, u32[]{:S(2)}, u32[]{:S(2)}) collective-permute-start(f32[344,256]{1,0:T(8,128)} %get-tuple-element.84), channel_id=1, source_target_pairs={{0,1},{4,5},{8,9},{12,13},{16,17},{20,21},{24,25},{28,29}} | collective-permute-start | bytes 1056776 | tf_op jit(solution)/shard_map/ppermute | solution.py:326
  24.6 27.6 %collective-permute-start.12 = (f32[344,256]{1,0:T(8,128)}, f32[344,256]{1,0:T(8,128)}, u32[]{:S(2)}, u32[]{:S(2)}) collective-permute-start(f32[344,256]{1,0:T(8,128)} %get-tuple-element.85), channel_id=1, source_target_pairs={{0,3},{4,7},{8,11},{12,15},{16,19},{20,23},{24,27},{28,31}} | collective-permute-start | bytes 1056776 | tf_op jit(solution)/shard_map/ppermute | solution.py:326
  26.1 3.4 %copy-start = (f32[1024,2048]{1,0:T(8,128)S(1)}, f32[1024,2048]{1,0:T(8,128)}, u32[]{:S(2)}) copy-start(f32[1024,2048]{1,0:T(8,128)} %s_ref.3) | copy-start | bytes 25165828
  30.8 52.2 %copy-start.2 = (bf16[1024,2048]{1,0:T(8,128)(2,1)}, bf16[1024,2048]{1,0:T(8,128)(2,1)S(1)}, u32[]{:S(2)}) copy-start(bf16[1024,2048]{1,0:T(8,128)(2,1)S(1)} %get-tuple-element.37.h_ref) | copy-start | bytes 12582916
  30.8 52.2 %copy-start.4 = (bf16[1024,2048]{1,0:T(8,128)(2,1)}, bf16[1024,2048]{1,0:T(8,128)(2,1)S(1)}, u32[]{:S(2)}) copy-start(bf16[1024,2048]{1,0:T(8,128)(2,1)S(1)} %get-tuple-element.38.l_ref) | copy-start | bytes 12582916
  30.9 24.0 %collective-permute-start.4 = (f32[344,256]{1,0:T(8,128)S(1)}, f32[344,256]{1,0:T(8,128)S(1)}, u32[]{:S(2)}, u32[]{:S(2)}) collective-permute-start(f32[344,256]{1,0:T(8,128)S(1)} %add_add_fusion.1.rest_0_), channel_id=1, source_target_pairs={{1,3},{2,1},{3,2},{5,7},{6,5},{7,6},{9,11},{10,9},{11,10},{13,15},... | collective-permute-start | bytes 1056776 | tf_op jit(solution)/shard_map/ppermute | solution.py:334
  38.8 37.4 %collective-permute-start.3 = (f32[344,256]{1,0:T(8,128)S(1)}, f32[344,256]{1,0:T(8,128)S(1)}, u32[]{:S(2)}, u32[]{:S(2)}) collective-permute-start(f32[344,256]{1,0:T(8,128)S(1)} %add_add_fusion.1.rest_0_), channel_id=1, source_target_pairs={{1,2},{2,3},{3,1},{5,6},{6,7},{7,5},{9,10},{10,11},{11,9},{13,14},... | collective-permute-start | bytes 1056776 | tf_op jit(solution)/shard_map/ppermute | solution.py:334
  50.3 33.8 %copy-start.10 = (f32[64,512]{1,0:T(8,128)}, f32[64,512]{1,0:T(8,128)S(1)}, u32[]{:S(2)}) copy-start(f32[64,512]{1,0:T(8,128)S(1)} %add_add_fusion.4) | copy-start | bytes 393220
  50.3 25.9 %collective-permute-start.11 = (f32[64,512]{1,0:T(8,128)S(1)}, f32[64,512]{1,0:T(8,128)S(1)}, u32[]{:S(2)}, u32[]{:S(2)}) collective-permute-start(f32[64,512]{1,0:T(8,128)S(1)} %add_add_fusion.4), channel_id=1, source_target_pairs={{0,1},{4,5},{8,9},{12,13},{16,17},{20,21},{24,25},{28,29}} | collective-permute-start | bytes 393224 | tf_op jit(solution)/shard_map/ppermute | solution.py:392
  51.0 25.3 %collective-permute-start.10 = (f32[64,512]{1,0:T(8,128)S(1)}, f32[64,512]{1,0:T(8,128)S(1)}, u32[]{:S(2)}, u32[]{:S(2)}) collective-permute-start(f32[64,512]{1,0:T(8,128)S(1)} %add_add_fusion.4), channel_id=1, source_target_pairs={{0,2},{4,6},{8,10},{12,14},{16,18},{20,22},{24,26},{28,30}} | collective-permute-start | bytes 393224 | tf_op jit(solution)/shard_map/ppermute | solution.py:392
  52.3 24.0 %collective-permute-start.9 = (f32[64,512]{1,0:T(8,128)S(1)}, f32[64,512]{1,0:T(8,128)S(1)}, u32[]{:S(2)}, u32[]{:S(2)}) collective-permute-start(f32[64,512]{1,0:T(8,128)S(1)} %add_add_fusion.4), channel_id=1, source_target_pairs={{0,3},{4,7},{8,11},{12,15},{16,19},{20,23},{24,27},{28,31}} | collective-permute-start | bytes 393224 | tf_op jit(solution)/shard_map/ppermute | solution.py:392
  76.2 0.7 copy-start.12
  76.2 0.7 copy-start.13
  76.2 0.7 copy-start.14
  83.1 1.0 copy-start.6
  84.1 13.0 %collective-permute-start.17 = (f32[128,2048]{1,0:T(8,128)}, f32[128,2048]{1,0:T(8,128)}, u32[]{:S(2)}, u32[]{:S(2)}) collective-permute-start(f32[128,2048]{1,0:T(8,128)} %get-tuple-element.45), channel_id=1, source_target_pairs={{0,4},{4,0},{8,12},{12,8},{16,20},{20,16},{24,28},{28,24},{1,5},{5... | collective-permute-start | bytes 3145736 | tf_op jit(solution)/shard_map/ppermute | solution.py:351
  87.3 6.1 %collective-permute-start.23 = (f32[64,512]{1,0:T(8,128)S(1)}, f32[64,512]{1,0:T(8,128)S(1)}, u32[]{:S(2)}, u32[]{:S(2)}) collective-permute-start(f32[64,512]{1,0:T(8,128)S(1)} %add_select_fusion.refs_0_), channel_id=1, source_target_pairs={{0,24},{4,28},{8,16},{12,20},{16,8},{20,12},{24,0},{28,4},{1,25},{... | collective-permute-start | bytes 393224 | tf_op jit(solution)/shard_map/ppermute | solution.py:365
  89.6 7.0 %collective-permute-start.22 = (f32[64,512]{1,0:T(8,128)S(1)}, f32[64,512]{1,0:T(8,128)S(1)}, u32[]{:S(2)}, u32[]{:S(2)}) collective-permute-start(f32[64,512]{1,0:T(8,128)S(1)} %add_select_fusion.refs_0_), channel_id=1, source_target_pairs={{0,16},{4,20},{8,24},{12,28},{16,0},{20,4},{24,8},{28,12},{1,17},{... | collective-permute-start | bytes 393224 | tf_op jit(solution)/shard_map/ppermute | solution.py:365
  89.8 7.2 %collective-permute-start.21 = (f32[64,512]{1,0:T(8,128)S(1)}, f32[64,512]{1,0:T(8,128)S(1)}, u32[]{:S(2)}, u32[]{:S(2)}) collective-permute-start(f32[64,512]{1,0:T(8,128)S(1)} %add_select_fusion.refs_0_), channel_id=1, source_target_pairs={{0,8},{4,12},{8,0},{12,4},{16,24},{20,28},{24,16},{28,20},{1,9},{5... | collective-permute-start | bytes 393224 | tf_op jit(solution)/shard_map/ppermute | solution.py:365
  90.0 10.3 %collective-permute-start.24 = (f32[64,512]{1,0:T(8,128)S(1)}, f32[64,512]{1,0:T(8,128)S(1)}, u32[]{:S(2)}, u32[]{:S(2)}) collective-permute-start(f32[64,512]{1,0:T(8,128)S(1)} %add_select_fusion.refs_0_), channel_id=1, source_target_pairs={{0,4},{4,0},{8,12},{12,8},{16,20},{20,16},{24,28},{28,24},{1,5},{5... | collective-permute-start | bytes 393224 | tf_op jit(solution)/shard_map/ppermute | solution.py:366
  93.4 10.5 %collective-permute-start.27 = (f32[64,512]{1,0:T(8,128)S(1)}, f32[64,512]{1,0:T(8,128)S(1)}, u32[]{:S(2)}, u32[]{:S(2)}) collective-permute-start(f32[64,512]{1,0:T(8,128)S(1)} %collective-permute-done.23.refs_3_), channel_id=1, source_target_pairs={{0,4},{4,0},{8,12},{12,8},{16,20},{20,16},{24,28},{28,24},{1,5},{5... | collective-permute-start | bytes 393224 | tf_op jit(solution)/shard_map/ppermute | solution.py:366
  96.5 7.4 %collective-permute-start.26 = (f32[64,512]{1,0:T(8,128)S(1)}, f32[64,512]{1,0:T(8,128)S(1)}, u32[]{:S(2)}, u32[]{:S(2)}) collective-permute-start(f32[64,512]{1,0:T(8,128)S(1)} %collective-permute-done.22.refs_2_), channel_id=1, source_target_pairs={{0,4},{4,0},{8,12},{12,8},{16,20},{20,16},{24,28},{28,24},{1,5},{5... | collective-permute-start | bytes 393224 | tf_op jit(solution)/shard_map/ppermute | solution.py:366
  97.0 6.9 %collective-permute-start.25 = (f32[64,512]{1,0:T(8,128)S(1)}, f32[64,512]{1,0:T(8,128)S(1)}, u32[]{:S(2)}, u32[]{:S(2)}) collective-permute-start(f32[64,512]{1,0:T(8,128)S(1)} %collective-permute-done.21.refs_1_), channel_id=1, source_target_pairs={{0,4},{4,0},{8,12},{12,8},{16,20},{20,16},{24,28},{28,24},{1,5},{5... | collective-permute-start | bytes 393224 | tf_op jit(solution)/shard_map/ppermute | solution.py:366
  97.1 23.3 %collective-permute-start.16 = (f32[344,256]{1,0:T(8,128)}, f32[344,256]{1,0:T(8,128)S(1)}, u32[]{:S(2)}, u32[]{:S(2)}) collective-permute-start(f32[344,256]{1,0:T(8,128)} %add_add_fusion.rest_0_), channel_id=1, source_target_pairs={{1,3},{2,1},{3,2},{5,7},{6,5},{7,6},{9,11},{10,9},{11,10},{13,15},... | collective-permute-start | bytes 1056776 | tf_op jit(solution)/shard_map/ppermute | solution.py:334
  100.4 20.1 %collective-permute-start.15 = (f32[344,256]{1,0:T(8,128)}, f32[344,256]{1,0:T(8,128)S(1)}, u32[]{:S(2)}, u32[]{:S(2)}) collective-permute-start(f32[344,256]{1,0:T(8,128)} %add_add_fusion.rest_0_), channel_id=1, source_target_pairs={{1,2},{2,3},{3,1},{5,6},{6,7},{7,5},{9,10},{10,11},{11,9},{13,14},... | collective-permute-start | bytes 1056776 | tf_op jit(solution)/shard_map/ppermute | solution.py:334
  104.0 16.3 %collective-permute-start.18 = (f32[32,2048]{1,0:T(8,128)S(1)}, f32[32,2048]{1,0:T(8,128)S(1)}, u32[]{:S(2)}, u32[]{:S(2)}) collective-permute-start(f32[32,2048]{1,0:T(8,128)S(1)} %get-tuple-element.80), channel_id=1, source_target_pairs={{0,8},{4,12},{8,0},{12,4},{16,24},{20,28},{24,16},{28,20},{1,9},{5... | collective-permute-start | bytes 786440 | tf_op jit(solution)/shard_map/ppermute | solution.py:360
  105.3 15.0 %collective-permute-start.20 = (f32[32,2048]{1,0:T(8,128)S(1)}, f32[32,2048]{1,0:T(8,128)S(1)}, u32[]{:S(2)}, u32[]{:S(2)}) collective-permute-start(f32[32,2048]{1,0:T(8,128)S(1)} %get-tuple-element.81), channel_id=1, source_target_pairs={{0,24},{4,28},{8,16},{12,20},{16,8},{20,12},{24,0},{28,4},{1,25},{... | collective-permute-start | bytes 786440 | tf_op jit(solution)/shard_map/ppermute | solution.py:360
  106.5 14.0 %copy-start.1 = (f32[344,256]{1,0:T(8,128)S(1)}, f32[344,256]{1,0:T(8,128)}, u32[]{:S(2)}) copy-start(f32[344,256]{1,0:T(8,128)} %add_add_fusion.rest_0_) | copy-start | bytes 1056772
  106.5 14.0 %copy-start.3 = (bf16[1024,2048]{1,0:T(8,128)(2,1)S(1)}, bf16[1024,2048]{1,0:T(8,128)(2,1)}, u32[]{:S(2)}) copy-start(bf16[1024,2048]{1,0:T(8,128)(2,1)} %copy-done.2) | copy-start | bytes 12582916
  106.5 14.0 %copy-start.5 = (bf16[1024,2048]{1,0:T(8,128)(2,1)S(1)}, bf16[1024,2048]{1,0:T(8,128)(2,1)}, u32[]{:S(2)}) copy-start(bf16[1024,2048]{1,0:T(8,128)(2,1)} %copy-done.4) | copy-start | bytes 12582916
  106.5 13.9 %collective-permute-start.19 = (f32[32,2048]{1,0:T(8,128)S(1)}, f32[32,2048]{1,0:T(8,128)S(1)}, u32[]{:S(2)}, u32[]{:S(2)}) collective-permute-start(f32[32,2048]{1,0:T(8,128)S(1)} %get-tuple-element.82), channel_id=1, source_target_pairs={{0,16},{4,20},{8,24},{12,28},{16,0},{20,4},{24,8},{28,12},{1,17},{... | collective-permute-start | bytes 786440 | tf_op jit(solution)/shard_map/ppermute | solution.py:360
  125.9 4.3 %collective-permute-start.28 = (f32[128,2048]{1,0:T(8,128)S(1)}, f32[128,2048]{1,0:T(8,128)S(1)}, u32[]{:S(2)}, u32[]{:S(2)}) collective-permute-start(f32[128,2048]{1,0:T(8,128)S(1)} %get-tuple-element.62), channel_id=1, source_target_pairs={{0,4},{4,0},{8,12},{12,8},{16,20},{20,16},{24,28},{28,24},{1,5},{5... | collective-permute-start | bytes 3145736 | tf_op jit(solution)/shard_map/ppermute | solution.py:351
  127.7 17.6 %collective-permute-start.31 = (f32[32,2048]{1,0:T(8,128)S(1)}, f32[32,2048]{1,0:T(8,128)S(1)}, u32[]{:S(2)}, u32[]{:S(2)}) collective-permute-start(f32[32,2048]{1,0:T(8,128)S(1)} %add_add_fusion.3.rest_0_), channel_id=1, source_target_pairs={{0,24},{4,28},{8,16},{12,20},{16,8},{20,12},{24,0},{28,4},{1,25},{... | collective-permute-start | bytes 786440 | tf_op jit(solution)/shard_map/ppermute | solution.py:365
  129.2 17.7 %collective-permute-start.30 = (f32[32,2048]{1,0:T(8,128)S(1)}, f32[32,2048]{1,0:T(8,128)S(1)}, u32[]{:S(2)}, u32[]{:S(2)}) collective-permute-start(f32[32,2048]{1,0:T(8,128)S(1)} %add_add_fusion.3.rest_0_), channel_id=1, source_target_pairs={{0,16},{4,20},{8,24},{12,28},{16,0},{20,4},{24,8},{28,12},{1,17},{... | collective-permute-start | bytes 786440 | tf_op jit(solution)/shard_map/ppermute | solution.py:365
  130.4 17.4 %collective-permute-start.36 = (f32[32,2048]{1,0:T(8,128)S(1)}, f32[32,2048]{1,0:T(8,128)S(1)}, u32[]{:S(2)}, u32[]{:S(2)}) collective-permute-start(f32[32,2048]{1,0:T(8,128)S(1)} %get-tuple-element.77), channel_id=1, source_target_pairs={{0,8},{4,12},{8,0},{12,4},{16,24},{20,28},{24,16},{28,20},{1,9},{5... | collective-permute-start | bytes 786440 | tf_op jit(solution)/shard_map/ppermute | solution.py:360
  131.5 16.6 %collective-permute-start.38 = (f32[32,2048]{1,0:T(8,128)S(1)}, f32[32,2048]{1,0:T(8,128)S(1)}, u32[]{:S(2)}, u32[]{:S(2)}) collective-permute-start(f32[32,2048]{1,0:T(8,128)S(1)} %get-tuple-element.78), channel_id=1, source_target_pairs={{0,24},{4,28},{8,16},{12,20},{16,8},{20,12},{24,0},{28,4},{1,25},{... | collective-permute-start | bytes 786440 | tf_op jit(solution)/shard_map/ppermute | solution.py:360
  132.7 39.3 %slice-start = ((s8[8388608]{0:T(1024)(128)(4,1)}), s8[4194304]{0:T(1024)(128)(4,1)S(1)}, s32[]{:S(2)}) async-start(s8[8388608]{0:T(1024)(128)(4,1)} %bitcast.6), calls=%async_computation | async-start | bytes 8388608
  132.7 36.5 %copy-start.7 = (f32[1024,256]{1,0:T(8,128)S(1)}, f32[1024,256]{1,0:T(8,128)}, u32[]{:S(2)}) copy-start(f32[1024,256]{1,0:T(8,128)} %copy-done.6) | copy-start | bytes 3145732
  132.7 39.3 %slice-start.1 = ((s8[8388608]{0:T(1024)(128)(4,1)}), s8[4194304]{0:T(1024)(128)(4,1)S(1)}, s32[]{:S(2)}) async-start(s8[8388608]{0:T(1024)(128)(4,1)} %bitcast.6), calls=%async_computation.1 | async-start | bytes 8388608
  132.7 21.0 %collective-permute-start.37 = (f32[32,2048]{1,0:T(8,128)S(1)}, f32[32,2048]{1,0:T(8,128)S(1)}, u32[]{:S(2)}, u32[]{:S(2)}) collective-permute-start(f32[32,2048]{1,0:T(8,128)S(1)} %get-tuple-element.79), channel_id=1, source_target_pairs={{0,16},{4,20},{8,24},{12,28},{16,0},{20,4},{24,8},{28,12},{1,17},{... | collective-permute-start | bytes 786440 | tf_op jit(solution)/shard_map/ppermute | solution.py:360
  145.4 10.0 %collective-permute-start.32 = (f32[32,2048]{1,0:T(8,128)S(1)}, f32[32,2048]{1,0:T(8,128)S(1)}, u32[]{:S(2)}, u32[]{:S(2)}) collective-permute-start(f32[32,2048]{1,0:T(8,128)S(1)} %add_add_fusion.3.rest_0_), channel_id=1, source_target_pairs={{0,4},{4,0},{8,12},{12,8},{16,20},{20,16},{24,28},{28,24},{1,5},{5... | collective-permute-start | bytes 786440 | tf_op jit(solution)/shard_map/ppermute | solution.py:366
  146.9 9.4 %collective-permute-start.29 = (f32[32,2048]{1,0:T(8,128)S(1)}, f32[32,2048]{1,0:T(8,128)S(1)}, u32[]{:S(2)}, u32[]{:S(2)}) collective-permute-start(f32[32,2048]{1,0:T(8,128)S(1)} %add_add_fusion.3.rest_0_), channel_id=1, source_target_pairs={{0,8},{4,12},{8,0},{12,4},{16,24},{20,28},{24,16},{28,20},{1,9},{5... | collective-permute-start | bytes 786440 | tf_op jit(solution)/shard_map/ppermute | solution.py:365
  147.8 8.8 %collective-permute-start.35 = (f32[32,2048]{1,0:T(8,128)S(1)}, f32[32,2048]{1,0:T(8,128)S(1)}, u32[]{:S(2)}, u32[]{:S(2)}) collective-permute-start(f32[32,2048]{1,0:T(8,128)S(1)} %collective-permute-done.31.rest_3_), channel_id=1, source_target_pairs={{0,4},{4,0},{8,12},{12,8},{16,20},{20,16},{24,28},{28,24},{1,5},{5... | collective-permute-start | bytes 786440 | tf_op jit(solution)/shard_map/ppermute | solution.py:366
  148.1 9.7 %collective-permute-start.34 = (f32[32,2048]{1,0:T(8,128)S(1)}, f32[32,2048]{1,0:T(8,128)S(1)}, u32[]{:S(2)}, u32[]{:S(2)}) collective-permute-start(f32[32,2048]{1,0:T(8,128)S(1)} %collective-permute-done.30.rest_2_), channel_id=1, source_target_pairs={{0,4},{4,0},{8,12},{12,8},{16,20},{20,16},{24,28},{28,24},{1,5},{5... | collective-permute-start | bytes 786440 | tf_op jit(solution)/shard_map/ppermute | solution.py:366
  153.8 8.4 %collective-permute-start.41 = (f32[32,2048]{1,0:T(8,128)S(1)}, f32[32,2048]{1,0:T(8,128)S(1)}, u32[]{:S(2)}, u32[]{:S(2)}) collective-permute-start(f32[32,2048]{1,0:T(8,128)S(1)} %add_add_fusion.2.rest_8_), channel_id=1, source_target_pairs={{0,24},{4,28},{8,16},{12,20},{16,8},{20,12},{24,0},{28,4},{1,25},{... | collective-permute-start | bytes 786440 | tf_op jit(solution)/shard_map/ppermute | solution.py:365
  155.4 13.3 %collective-permute-start.40 = (f32[32,2048]{1,0:T(8,128)S(1)}, f32[32,2048]{1,0:T(8,128)S(1)}, u32[]{:S(2)}, u32[]{:S(2)}) collective-permute-start(f32[32,2048]{1,0:T(8,128)S(1)} %add_add_fusion.2.rest_8_), channel_id=1, source_target_pairs={{0,16},{4,20},{8,24},{12,28},{16,0},{20,4},{24,8},{28,12},{1,17},{... | collective-permute-start | bytes 786440 | tf_op jit(solution)/shard_map/ppermute | solution.py:365
  156.3 12.8 %collective-permute-start.39 = (f32[32,2048]{1,0:T(8,128)S(1)}, f32[32,2048]{1,0:T(8,128)S(1)}, u32[]{:S(2)}, u32[]{:S(2)}) collective-permute-start(f32[32,2048]{1,0:T(8,128)S(1)} %add_add_fusion.2.rest_8_), channel_id=1, source_target_pairs={{0,8},{4,12},{8,0},{12,4},{16,24},{20,28},{24,16},{28,20},{1,9},{5... | collective-permute-start | bytes 786440 | tf_op jit(solution)/shard_map/ppermute | solution.py:365
  156.5 15.4 %collective-permute-start.33 = (f32[32,2048]{1,0:T(8,128)S(1)}, f32[32,2048]{1,0:T(8,128)S(1)}, u32[]{:S(2)}, u32[]{:S(2)}) collective-permute-start(f32[32,2048]{1,0:T(8,128)S(1)} %collective-permute-done.29.rest_1_), channel_id=1, source_target_pairs={{0,4},{4,0},{8,12},{12,8},{16,20},{20,16},{24,28},{28,24},{1,5},{5... | collective-permute-start | bytes 786440 | tf_op jit(solution)/shard_map/ppermute | solution.py:366
  157.9 14.1 %collective-permute-start.42 = (f32[32,2048]{1,0:T(8,128)S(1)}, f32[32,2048]{1,0:T(8,128)S(1)}, u32[]{:S(2)}, u32[]{:S(2)}) collective-permute-start(f32[32,2048]{1,0:T(8,128)S(1)} %add_add_fusion.2.rest_8_), channel_id=1, source_target_pairs={{0,4},{4,0},{8,12},{12,8},{16,20},{20,16},{24,28},{28,24},{1,5},{5... | collective-permute-start | bytes 786440 | tf_op jit(solution)/shard_map/ppermute | solution.py:366
  162.2 9.7 %collective-permute-start.45 = (f32[32,2048]{1,0:T(8,128)S(1)}, f32[32,2048]{1,0:T(8,128)S(1)}, u32[]{:S(2)}, u32[]{:S(2)}) collective-permute-start(f32[32,2048]{1,0:T(8,128)S(1)} %collective-permute-done.41.rest_11_), channel_id=1, source_target_pairs={{0,4},{4,0},{8,12},{12,8},{16,20},{20,16},{24,28},{28,24},{1,5},{5... | collective-permute-start | bytes 786440 | tf_op jit(solution)/shard_map/ppermute | solution.py:366
  168.6 3.3 %collective-permute-start.44 = (f32[32,2048]{1,0:T(8,128)S(1)}, f32[32,2048]{1,0:T(8,128)S(1)}, u32[]{:S(2)}, u32[]{:S(2)}) collective-permute-start(f32[32,2048]{1,0:T(8,128)S(1)} %collective-permute-done.40.rest_10_), channel_id=1, source_target_pairs={{0,4},{4,0},{8,12},{12,8},{16,20},{20,16},{24,28},{28,24},{1,5},{5... | collective-permute-start | bytes 786440 | tf_op jit(solution)/shard_map/ppermute | solution.py:366
  169.1 2.8 %collective-permute-start.43 = (f32[32,2048]{1,0:T(8,128)S(1)}, f32[32,2048]{1,0:T(8,128)S(1)}, u32[]{:S(2)}, u32[]{:S(2)}) collective-permute-start(f32[32,2048]{1,0:T(8,128)S(1)} %collective-permute-done.39.rest_9_), channel_id=1, source_target_pairs={{0,4},{4,0},{8,12},{12,8},{16,20},{20,16},{24,28},{28,24},{1,5},{5... | collective-permute-start | bytes 786440 | tf_op jit(solution)/shard_map/ppermute | solution.py:366

commit v9 on v8

--- a/solution.py
+++ b/solution.py
@@ -361,9 +361,9 @@
     return own
 
 
-def gather_rows(own, n):
+def gather_rows(own, n, hold=()):
     got = [own] + [lax.ppermute(own, "rows", swap(n, 2 * k)) for k in range(1, n // 2)]
-    other = [lax.ppermute(g, "rows", swap(n, 1)) for g in got]
+    other = [lax.ppermute(after(g, hold), "rows", swap(n, 1)) for g in got]
     return got + other, [(0, k) for k in range(n // 2)] + [(1, k) for k in range(n // 2)]
 
 
@@ -405,8 +405,8 @@
     joined = join_cores(send, keep, n_rows)
     own_b = scatter_chips(joined, n_rows)
     _, factor, linv = chol_part(info, 2, 4, state=after(state, joined))
-    pieces_b, _ = gather_rows(after(own_b, linv), n_rows)
     b, b3, l3 = basis([panel_a, panel_b], linv)
+    pieces_b, _ = gather_rows(after(own_b, linv), n_rows, (b3,))
     layout = [(base,) + w for base in (0, half) for w in where]
     return finish(info, snapshots, b, b3, l3, factor, pieces_a + pieces_b, layout)
 

time: 187 us -> 186 us (level)
    ppermute x9, waiting for transfers between devices: 13.1 us -> 10.4 us  [gather_rows(): lax.ppermute(own, 'rows', swap(n, 2 * k))]
    ppermute x9, waiting for transfers between devices: 5.02 us -> 7.23 us  [scatter_chips(): lax.ppermute(take(mine, (chip ^ k) * piece, piece), 'rows', swap(n, 2 * k))]
  transfers between devices with their start and end apart: 46 -> 46, of which waited for: 6 -> 12; matrix products, arithmetic and copies ran while one was open for 8% -> 8% of each run, Pallas kernels for 16% -> 16%
where the time goes in v9:
time: 186 us
  starting transfers between devices  64.1 us (34%)
  Pallas kernels  55.1 us (30%)
  waiting for transfers between devices  40.6 us (22%)
  local copies, waits for them, and re-layouts  12 us (6%)
  other arithmetic  6.97 us (4%)
  matrix products  5.71 us (3%)
    pallas_call x2, Pallas kernels, chol_part(): pl.pallas_call(kernel, out_shape=(shape, shape, shape), in_specs=[SMEM] +...  25.9 us
    ppermute x4, starting transfers between devices, spread_round(): got.append(lax.ppermute(mine, 'cols', pairs))  23.8 us
    ppermute x4, waiting for transfers between devices, spread_round(): got.append(lax.ppermute(mine, 'cols', pairs))  21.4 us
    pallas_call x1, Pallas kernels, finish(): pl.pallas_call(kernel, out_shape=(jax.ShapeDtypeStruct((rows, cols), F32)...  13.8 us
    pallas_call x2, Pallas kernels, panel_dot(): pl.pallas_call(kernel, out_shape=(out, out, jax.ShapeDtypeStruct((rows, w...  11.4 us
    ppermute x9, waiting for transfers between devices, gather_rows(): lax.ppermute(own, 'rows', swap(n, 2 * k))  10.4 us
    ppermute x9, starting transfers between devices, gather_rows(): lax.ppermute(own, 'rows', swap(n, 2 * k))  8.98 us
    ppermute x6, starting transfers between devices, spread_out(): got.append(lax.ppermute(x[start:start + size], 'cols', [(0, k + 1)]))  8.17 us
  transfers between devices with their start and end apart: 46, of which 12 were waited for; matrix products, arithmetic and copies ran while one was open for 8% of the time, Pallas kernels for 16%

profile of v9, /device:TPU:17, one launch (start us, length us, event | category | flops | bytes accessed | tf_op | source)
XLA Modules:
  0.0 185.8 jit_solution(947085759225317824)
XLA Ops:
  0.6 2.2 %fusion.6 = (f32[344,256]{1,0:T(8,128)}, f32[344,256]{1,0:T(8,128)}, f32[344,256]{1,0:T(8,128)}) fusion(f32[1024,2048]{1,0:T(8,128)} %s_ref.3), kind=kLoop, calls=%fused_computation.21 | loop fusion | bytes 2113536 | tf_op jit(solution)/shard_map/slice | solution.py:326
  2.8 1.3 collective-permute-start.1
  4.1 1.4 collective-permute-start.2
  5.5 1.4 collective-permute-start
  6.9 5.7 %fusion.2 = f32[512,512]{1,0:T(8,128)S(1)} fusion(f32[1024,2048]{1,0:T(8,128)} %s_ref.3), kind=kOutput, calls=%fused_computation.2 | convolution fusion | flops 3221487616 | bytes 3145728 | tf_op jit(solution)/shard_map/dot_general | solution.py:31
  12.7 0.7 collective-permute-start.5
  13.6 1.8 fusion.5
  15.4 0.7 copy-done.11
  16.1 1.3 add_add_fusion.1.rest_0_
  17.5 0.7 constant_dynamic-slice_fusion.8
  18.3 1.2 collective-permute-start.6
  19.5 1.2 collective-permute-start.8
  20.9 1.0 fusion.7
  21.9 1.3 collective-permute-start.13
  23.2 1.4 collective-permute-start.14
  24.6 1.4 collective-permute-start.12
  26.1 3.4 %copy-done = f32[1024,2048]{1,0:T(8,128)S(1)} copy-done((f32[1024,2048]{1,0:T(8,128)S(1)}, f32[1024,2048]{1,0:T(8,128)}, u32[]{:S(2)}) %copy-start) | copy-done | bytes 8388632
  29.5 1.3 stage.1
  30.9 7.9 %collective-permute-start.4 = (f32[344,256]{1,0:T(8,128)S(1)}, f32[344,256]{1,0:T(8,128)S(1)}, u32[]{:S(2)}, u32[]{:S(2)}) collective-permute-start(f32[344,256]{1,0:T(8,128)S(1)} %add_add_fusion.1.rest_0_), channel_id=1, source_target_pairs={{1,3},{2,1},{3,2},{5,7},{6,5},{7,6},{9,11},{10,9},{11,10},{13,15},... | collective-permute-start | bytes 1056776 | tf_op jit(solution)/shard_map/ppermute | solution.py:334
  38.8 10.4 %collective-permute-start.3 = (f32[344,256]{1,0:T(8,128)S(1)}, f32[344,256]{1,0:T(8,128)S(1)}, u32[]{:S(2)}, u32[]{:S(2)}) collective-permute-start(f32[344,256]{1,0:T(8,128)S(1)} %add_add_fusion.1.rest_0_), channel_id=1, source_target_pairs={{1,2},{2,3},{3,1},{5,6},{6,7},{7,5},{9,10},{10,11},{11,9},{13,14},... | collective-permute-start | bytes 1056776 | tf_op jit(solution)/shard_map/ppermute | solution.py:334
  49.2 1.0 add_add_fusion.4
  50.3 0.7 collective-permute-start.11
  51.0 1.3 collective-permute-start.10
  52.3 0.7 collective-permute-start.9
  52.9 1.9 %add_add_fusion.rest_0_ = f32[344,256]{1,0:T(8,128)} fusion(f32[344,256]{1,0:T(8,128)} %collective-permute-done.14, f32[344,256]{1,0:T(8,128)} %collective-permute-done.12, f32[344,256]{1,0:T(8,128)S(1)} %collective-permute-done.13), kind=kLoop, calls=%fused_computation.4 | loop fusion | flops 176128 | bytes 1409024 | tf_op jit(solution)/shard_map/add | solution.py:327
  54.9 21.3 %collective-permute-done.3.rest_1_ = f32[344,256]{1,0:T(8,128)S(1)} collective-permute-done((f32[344,256]{1,0:T(8,128)S(1)}, f32[344,256]{1,0:T(8,128)S(1)}, u32[]{:S(2)}, u32[]{:S(2)}) %collective-permute-start.3) | collective-permute-done | bytes 352288 | tf_op jit(solution)/shard_map/ppermute | solution.py:334
  76.3 0.6 copy-done.12
  77.0 6.1 %panel_dot.2 = (f32[128,2048]{1,0:T(8,128)}, f32[128,2048]{1,0:T(8,128)S(1)}, f32[1024,256]{1,0:T(8,128)S(1)}) custom-call(s32[6]{0:T(128)S(1)} %stack.27.info_ref, bf16[1024,2048]{1,0:T(8,128)(2,1)S(1)} %get-tuple-element.41.h_ref, bf16[1024,2048]{1,0:T(8,128)(2,1)S(1)} %get-tuple-element.42.l_ref, f32[1024,256]{1,0:T(8,128)S(1)} %get-tuple-element.81.own_ref, ...), custom_call_target="tpu_custom_call" | custom-call | flops 3221225472 | bytes 1048576 | tf_op jit(solution)/shard_map/panel_dot/pallas_call | solution.py:301
  83.1 1.0 copy-done.6
  84.1 2.2 %collective-permute-start.17 = (f32[128,2048]{1,0:T(8,128)}, f32[128,2048]{1,0:T(8,128)}, u32[]{:S(2)}, u32[]{:S(2)}) collective-permute-start(f32[128,2048]{1,0:T(8,128)} %get-tuple-element.49), channel_id=1, source_target_pairs={{0,4},{4,0},{8,12},{12,8},{16,20},{20,16},{24,28},{28,24},{1,5},{5... | collective-permute-start | bytes 3145736 | tf_op jit(solution)/shard_map/ppermute | solution.py:351
  86.3 1.1 add_select_fusion.refs_0_
  87.3 2.2 %collective-permute-start.23 = (f32[64,512]{1,0:T(8,128)S(1)}, f32[64,512]{1,0:T(8,128)S(1)}, u32[]{:S(2)}, u32[]{:S(2)}) collective-permute-start(f32[64,512]{1,0:T(8,128)S(1)} %add_select_fusion.refs_0_), channel_id=1, source_target_pairs={{0,24},{4,28},{8,16},{12,20},{16,8},{20,12},{24,0},{28,4},{1,25},{... | collective-permute-start | bytes 393224 | tf_op jit(solution)/shard_map/ppermute | solution.py:365
  90.0 0.8 collective-permute-start.24
  90.9 2.5 %collective-permute-done.23.refs_3_ = f32[64,512]{1,0:T(8,128)S(1)} collective-permute-done((f32[64,512]{1,0:T(8,128)S(1)}, f32[64,512]{1,0:T(8,128)S(1)}, u32[]{:S(2)}, u32[]{:S(2)}) %collective-permute-start.23) | collective-permute-done | bytes 131104 | tf_op jit(solution)/shard_map/ppermute | solution.py:365
  93.4 1.1 collective-permute-start.27
  94.5 2.1 %collective-permute-done.22.refs_2_ = f32[64,512]{1,0:T(8,128)S(1)} collective-permute-done((f32[64,512]{1,0:T(8,128)S(1)}, f32[64,512]{1,0:T(8,128)S(1)}, u32[]{:S(2)}, u32[]{:S(2)}) %collective-permute-start.22) | collective-permute-done | bytes 131104 | tf_op jit(solution)/shard_map/ppermute | solution.py:365
  96.5 0.5 collective-permute-start.26
  97.1 1.9 %collective-permute-start.16 = (f32[344,256]{1,0:T(8,128)}, f32[344,256]{1,0:T(8,128)S(1)}, u32[]{:S(2)}, u32[]{:S(2)}) collective-permute-start(f32[344,256]{1,0:T(8,128)} %add_add_fusion.rest_0_), channel_id=1, source_target_pairs={{1,3},{2,1},{3,2},{5,7},{6,5},{7,6},{9,11},{10,9},{11,10},{13,15},... | collective-permute-start | bytes 1056776 | tf_op jit(solution)/shard_map/ppermute | solution.py:334
  99.0 1.3 add.122
  100.4 3.5 %collective-permute-start.15 = (f32[344,256]{1,0:T(8,128)}, f32[344,256]{1,0:T(8,128)S(1)}, u32[]{:S(2)}, u32[]{:S(2)}) collective-permute-start(f32[344,256]{1,0:T(8,128)} %add_add_fusion.rest_0_), channel_id=1, source_target_pairs={{1,2},{2,3},{3,1},{5,6},{6,7},{7,5},{9,10},{10,11},{11,9},{13,14},... | collective-permute-start | bytes 1056776 | tf_op jit(solution)/shard_map/ppermute | solution.py:334
  104.0 1.3 collective-permute-start.18
  105.3 1.2 collective-permute-start.20
  106.8 13.6 %chol_part.2 = (f32[512,512]{1,0:T(8,128)S(1)}, f32[512,512]{1,0:T(8,128)S(1)}, f32[512,512]{1,0:T(8,128)S(1)}) custom-call(s32[6]{0:T(128)S(1)} %stack.27.info_ref, f32[64,512]{1,0:T(8,128)S(1)} %add_select_fusion.refs_0_, f32[64,512]{1,0:T(8,128)S(1)} %collective-permute-done.21.refs_1_, f32[64,512]{1,0:T(8,128)S(1)} %collective-permute-done.22.refs_2_, ...), custom_call_target="tpu_custom_call" | custom-call | flops 16000000000 | bytes 1048576 | tf_op jit(solution)/shard_map/chol_part/pallas_call | solution.py:132
  120.5 5.3 %panel_dot.3 = (f32[128,2048]{1,0:T(8,128)S(1)}, f32[128,2048]{1,0:T(8,128)S(1)}, f32[1024,256]{1,0:T(8,128)S(1)}) custom-call(s32[6]{0:T(128)S(1)} %stack.27.info_ref, bf16[1024,2048]{1,0:T(8,128)(2,1)S(1)} %copy-done.3, bf16[1024,2048]{1,0:T(8,128)(2,1)S(1)} %copy-done.5, f32[1024,256]{1,0:T(8,128)S(1)} %get-tuple-element.43.own_ref, ...), custom_call_target="tpu_custom_call" | custom-call | flops 3221225472 | bytes 1048576 | tf_op jit(solution)/shard_map/panel_dot/pallas_call | solution.py:301
  125.8 1.9 %collective-permute-start.28 = (f32[128,2048]{1,0:T(8,128)S(1)}, f32[128,2048]{1,0:T(8,128)S(1)}, u32[]{:S(2)}, u32[]{:S(2)}) collective-permute-start(f32[128,2048]{1,0:T(8,128)S(1)} %get-tuple-element.66), channel_id=1, source_target_pairs={{0,4},{4,0},{8,12},{12,8},{16,20},{20,16},{24,28},{28,24},{1,5},{5... | collective-permute-start | bytes 3145736 | tf_op jit(solution)/shard_map/ppermute | solution.py:351
  127.7 1.5 collective-permute-start.31
  129.2 0.9 collective-permute-start.30
  130.3 1.2 collective-permute-start.36
  131.5 1.2 collective-permute-start.38
  133.1 12.3 %chol_part.3 = (f32[512,512]{1,0:T(8,128)S(1)}, f32[512,512]{1,0:T(8,128)S(1)}, f32[512,512]{1,0:T(8,128)S(1)}) custom-call(s32[6]{0:T(128)S(1)} %stack.27.info_ref, f32[512,512]{1,0:T(8,128)S(1)} %get-tuple-element.67.refs_0_, f32[512,512]{1,0:T(8,128)S(1)} %get-tuple-element.68.refs_1_, ...), custom_call_target="tpu_custom_call", output_to_operand_aliasing={{0}: (1, {}), {1}: (2, {}), {2}: (3, {})} | custom-call | flops 16000000000 | bytes 1048576 | tf_op jit(solution)/shard_map/chol_part/pallas_call | solution.py:132
  145.4 1.1 collective-permute-start.29
  146.5 1.3 collective-permute-done.38
  147.8 5.9 %collective-permute-done.37 = f32[32,2048]{1,0:T(8,128)S(1)} collective-permute-done((f32[32,2048]{1,0:T(8,128)S(1)}, f32[32,2048]{1,0:T(8,128)S(1)}, u32[]{:S(2)}, u32[]{:S(2)}) %collective-permute-start.37) | collective-permute-done | bytes 262176 | tf_op jit(solution)/shard_map/ppermute | solution.py:360
  153.8 1.5 collective-permute-start.41
  155.3 0.9 collective-permute-start.40
  156.5 1.3 collective-permute-start.32
  157.9 4.3 %collective-permute-done.41.rest_11_ = f32[32,2048]{1,0:T(8,128)S(1)} collective-permute-done((f32[32,2048]{1,0:T(8,128)S(1)}, f32[32,2048]{1,0:T(8,128)S(1)}, u32[]{:S(2)}, u32[]{:S(2)}) %collective-permute-start.41) | collective-permute-done | bytes 262176 | tf_op jit(solution)/shard_map/ppermute | solution.py:365
  162.2 2.2 %collective-permute-start.34 = (f32[32,2048]{1,0:T(8,128)S(1)}, f32[32,2048]{1,0:T(8,128)S(1)}, u32[]{:S(2)}, u32[]{:S(2)}) collective-permute-start(f32[32,2048]{1,0:T(8,128)S(1)} %collective-permute-done.30.rest_2_), channel_id=1, source_target_pairs={{0,4},{4,0},{8,12},{12,8},{16,20},{20,16},{24,28},{28,24},{1,5},{5... | collective-permute-start | bytes 786440 | tf_op jit(solution)/shard_map/ppermute | solution.py:366
  164.5 2.7 %basis.1 = (f32[1024,512]{1,0:T(8,128)S(1)}, bf16[1024,1536]{1,0:T(8,128)(2,1)S(1)}, bf16[512,1536]{1,0:T(8,128)(2,1)S(1)}) custom-call(f32[1024,256]{1,0:T(8,128)S(1)} %copy-done.7, f32[1024,256]{1,0:T(8,128)S(1)} %get-tuple-element.64.refs_1_, f32[512,512]{1,0:T(8,128)S(1)} %get-tuple-element.70.refs_2_), custom_call_target="tpu_custom_call" | custom-call | flops 1610612736 | bytes 1048576 | tf_op jit(solution)/shard_map/basis/pallas_call | solution.py:183
  167.1 1.5 collective-permute-done.40.rest_10_
  168.6 0.5 collective-permute-start.33
  169.2 0.4 collective-permute-start.43
  169.7 0.4 collective-permute-start.45
  171.8 13.8 %finish.1 = (f32[1024,2048]{1,0:T(8,128)}, f32[512,2048]{1,0:T(8,128)}) custom-call(s32[6]{0:T(128)S(1)} %stack.27.info_ref, f32[1024,2048]{1,0:T(8,128)S(1)} %bitcast.7, f32[1024,512]{1,0:T(8,128)S(1)} %get-tuple-element.71.b_ref, bf16[1024,1536]{1,0:T(8,128)(2,1)S(1)} %get-tuple-element.72.b3_ref, bf16[512,1536]{1,0:T(8,128)(2,1)S(1)} %get-tuple-element.73.l3_ref, ...), custom_call_target="tpu_custom_call" | custom-call | flops 10000000000 | bytes 1048576 | tf_op jit(solution)/shard_map/finish/pallas_call | solution.py:242
  (88 shorter events, 4.6 us)
Async XLA Ops:
  2.8 12.6 %collective-permute-start.1 = (f32[344,256]{1,0:T(8,128)}, f32[344,256]{1,0:T(8,128)S(1)}, u32[]{:S(2)}, u32[]{:S(2)}) collective-permute-start(f32[344,256]{1,0:T(8,128)} %get-tuple-element.82), channel_id=1, source_target_pairs={{0,2},{4,6},{8,10},{12,14},{16,18},{20,22},{24,26},{28,30}} | collective-permute-start | bytes 1056776 | tf_op jit(solution)/shard_map/ppermute | solution.py:326
  4.1 11.3 %collective-permute-start.2 = (f32[344,256]{1,0:T(8,128)}, f32[344,256]{1,0:T(8,128)}, u32[]{:S(2)}, u32[]{:S(2)}) collective-permute-start(f32[344,256]{1,0:T(8,128)} %get-tuple-element.83), channel_id=1, source_target_pairs={{0,1},{4,5},{8,9},{12,13},{16,17},{20,21},{24,25},{28,29}} | collective-permute-start | bytes 1056776 | tf_op jit(solution)/shard_map/ppermute | solution.py:326
  5.5 10.6 %collective-permute-start = (f32[344,256]{1,0:T(8,128)}, f32[344,256]{1,0:T(8,128)}, u32[]{:S(2)}, u32[]{:S(2)}) collective-permute-start(f32[344,256]{1,0:T(8,128)} %get-tuple-element.84), channel_id=1, source_target_pairs={{0,3},{4,7},{8,11},{12,15},{16,19},{20,23},{24,27},{28,31}} | collective-permute-start | bytes 1056776 | tf_op jit(solution)/shard_map/ppermute | solution.py:326
  12.6 1.0 copy-start.8
  12.7 4.7 %collective-permute-start.5 = (f32[256,512]{1,0:T(8,128)S(1)}, f32[256,512]{1,0:T(8,128)S(1)}, u32[]{:S(2)}, u32[]{:S(2)}) collective-permute-start(f32[256,512]{1,0:T(8,128)S(1)} %constant_dynamic-slice_fusion.9), channel_id=1, source_target_pairs={{0,4},{4,0},{8,12},{12,8},{16,20},{20,16},{24,28},{28,24},{1,5},{5... | collective-permute-start | bytes 1572872 | tf_op jit(solution)/shard_map/ppermute | solution.py:351
  13.6 3.8 %copy-start.9 = (f32[512,512]{1,0:T(8,128)S(1)}, f32[512,512]{1,0:T(8,128)}, u32[]{:S(2)}) copy-start(f32[512,512]{1,0:T(8,128)} %copy-done.8) | copy-start | bytes 3145732
  15.4 0.7 copy-start.11
  18.3 6.4 %collective-permute-start.6 = (f32[64,512]{1,0:T(8,128)S(1)}, f32[64,512]{1,0:T(8,128)S(1)}, u32[]{:S(2)}, u32[]{:S(2)}) collective-permute-start(f32[64,512]{1,0:T(8,128)S(1)} %get-tuple-element.94), channel_id=1, source_target_pairs={{0,8},{4,12},{8,0},{12,4},{16,24},{20,28},{24,16},{28,20},{1,9},{5... | collective-permute-start | bytes 393224 | tf_op jit(solution)/shard_map/ppermute | solution.py:360
  19.5 11.4 %collective-permute-start.8 = (f32[64,512]{1,0:T(8,128)}, f32[64,512]{1,0:T(8,128)}, u32[]{:S(2)}, u32[]{:S(2)}) collective-permute-start(f32[64,512]{1,0:T(8,128)} %get-tuple-element.95), channel_id=1, source_target_pairs={{0,24},{4,28},{8,16},{12,20},{16,8},{20,12},{24,0},{28,4},{1,25},{... | collective-permute-start | bytes 393224 | tf_op jit(solution)/shard_map/ppermute | solution.py:360
  20.7 18.1 %collective-permute-start.7 = (f32[64,512]{1,0:T(8,128)}, f32[64,512]{1,0:T(8,128)}, u32[]{:S(2)}, u32[]{:S(2)}) collective-permute-start(f32[64,512]{1,0:T(8,128)} %get-tuple-element.96), channel_id=1, source_target_pairs={{0,16},{4,20},{8,24},{12,28},{16,0},{20,4},{24,8},{28,12},{1,17},{... | collective-permute-start | bytes 393224 | tf_op jit(solution)/shard_map/ppermute | solution.py:360
  21.9 28.3 %collective-permute-start.13 = (f32[344,256]{1,0:T(8,128)}, f32[344,256]{1,0:T(8,128)S(1)}, u32[]{:S(2)}, u32[]{:S(2)}) collective-permute-start(f32[344,256]{1,0:T(8,128)} %get-tuple-element.91), channel_id=1, source_target_pairs={{0,2},{4,6},{8,10},{12,14},{16,18},{20,22},{24,26},{28,30}} | collective-permute-start | bytes 1056776 | tf_op jit(solution)/shard_map/ppermute | solution.py:326
  23.2 27.7 %collective-permute-start.14 = (f32[344,256]{1,0:T(8,128)}, f32[344,256]{1,0:T(8,128)}, u32[]{:S(2)}, u32[]{:S(2)}) collective-permute-start(f32[344,256]{1,0:T(8,128)} %get-tuple-element.92), channel_id=1, source_target_pairs={{0,1},{4,5},{8,9},{12,13},{16,17},{20,21},{24,25},{28,29}} | collective-permute-start | bytes 1056776 | tf_op jit(solution)/shard_map/ppermute | solution.py:326
  24.6 27.6 %collective-permute-start.12 = (f32[344,256]{1,0:T(8,128)}, f32[344,256]{1,0:T(8,128)}, u32[]{:S(2)}, u32[]{:S(2)}) collective-permute-start(f32[344,256]{1,0:T(8,128)} %get-tuple-element.93), channel_id=1, source_target_pairs={{0,3},{4,7},{8,11},{12,15},{16,19},{20,23},{24,27},{28,31}} | collective-permute-start | bytes 1056776 | tf_op jit(solution)/shard_map/ppermute | solution.py:326
  26.1 3.4 %copy-start = (f32[1024,2048]{1,0:T(8,128)S(1)}, f32[1024,2048]{1,0:T(8,128)}, u32[]{:S(2)}) copy-start(f32[1024,2048]{1,0:T(8,128)} %s_ref.3) | copy-start | bytes 25165828
  30.8 52.2 %copy-start.2 = (bf16[1024,2048]{1,0:T(8,128)(2,1)}, bf16[1024,2048]{1,0:T(8,128)(2,1)S(1)}, u32[]{:S(2)}) copy-start(bf16[1024,2048]{1,0:T(8,128)(2,1)S(1)} %get-tuple-element.41.h_ref) | copy-start | bytes 12582916
  30.8 52.2 %copy-start.4 = (bf16[1024,2048]{1,0:T(8,128)(2,1)}, bf16[1024,2048]{1,0:T(8,128)(2,1)S(1)}, u32[]{:S(2)}) copy-start(bf16[1024,2048]{1,0:T(8,128)(2,1)S(1)} %get-tuple-element.42.l_ref) | copy-start | bytes 12582916
  30.9 24.0 %collective-permute-start.4 = (f32[344,256]{1,0:T(8,128)S(1)}, f32[344,256]{1,0:T(8,128)S(1)}, u32[]{:S(2)}, u32[]{:S(2)}) collective-permute-start(f32[344,256]{1,0:T(8,128)S(1)} %add_add_fusion.1.rest_0_), channel_id=1, source_target_pairs={{1,3},{2,1},{3,2},{5,7},{6,5},{7,6},{9,11},{10,9},{11,10},{13,15},... | collective-permute-start | bytes 1056776 | tf_op jit(solution)/shard_map/ppermute | solution.py:334
  38.8 37.4 %collective-permute-start.3 = (f32[344,256]{1,0:T(8,128)S(1)}, f32[344,256]{1,0:T(8,128)S(1)}, u32[]{:S(2)}, u32[]{:S(2)}) collective-permute-start(f32[344,256]{1,0:T(8,128)S(1)} %add_add_fusion.1.rest_0_), channel_id=1, source_target_pairs={{1,2},{2,3},{3,1},{5,6},{6,7},{7,5},{9,10},{10,11},{11,9},{13,14},... | collective-permute-start | bytes 1056776 | tf_op jit(solution)/shard_map/ppermute | solution.py:334
  50.3 33.8 %copy-start.10 = (f32[64,512]{1,0:T(8,128)}, f32[64,512]{1,0:T(8,128)S(1)}, u32[]{:S(2)}) copy-start(f32[64,512]{1,0:T(8,128)S(1)} %add_add_fusion.4) | copy-start | bytes 393220
  50.3 25.9 %collective-permute-start.11 = (f32[64,512]{1,0:T(8,128)S(1)}, f32[64,512]{1,0:T(8,128)S(1)}, u32[]{:S(2)}, u32[]{:S(2)}) collective-permute-start(f32[64,512]{1,0:T(8,128)S(1)} %add_add_fusion.4), channel_id=1, source_target_pairs={{0,1},{4,5},{8,9},{12,13},{16,17},{20,21},{24,25},{28,29}} | collective-permute-start | bytes 393224 | tf_op jit(solution)/shard_map/ppermute | solution.py:392
  51.0 25.3 %collective-permute-start.10 = (f32[64,512]{1,0:T(8,128)S(1)}, f32[64,512]{1,0:T(8,128)S(1)}, u32[]{:S(2)}, u32[]{:S(2)}) collective-permute-start(f32[64,512]{1,0:T(8,128)S(1)} %add_add_fusion.4), channel_id=1, source_target_pairs={{0,2},{4,6},{8,10},{12,14},{16,18},{20,22},{24,26},{28,30}} | collective-permute-start | bytes 393224 | tf_op jit(solution)/shard_map/ppermute | solution.py:392
  52.3 24.0 %collective-permute-start.9 = (f32[64,512]{1,0:T(8,128)S(1)}, f32[64,512]{1,0:T(8,128)S(1)}, u32[]{:S(2)}, u32[]{:S(2)}) collective-permute-start(f32[64,512]{1,0:T(8,128)S(1)} %add_add_fusion.4), channel_id=1, source_target_pairs={{0,3},{4,7},{8,11},{12,15},{16,19},{20,23},{24,27},{28,31}} | collective-permute-start | bytes 393224 | tf_op jit(solution)/shard_map/ppermute | solution.py:392
  76.2 0.7 copy-start.12
  76.2 0.7 copy-start.13
  76.2 0.7 copy-start.14
  83.1 1.0 copy-start.6
  84.1 13.0 %collective-permute-start.17 = (f32[128,2048]{1,0:T(8,128)}, f32[128,2048]{1,0:T(8,128)}, u32[]{:S(2)}, u32[]{:S(2)}) collective-permute-start(f32[128,2048]{1,0:T(8,128)} %get-tuple-element.49), channel_id=1, source_target_pairs={{0,4},{4,0},{8,12},{12,8},{16,20},{20,16},{24,28},{28,24},{1,5},{5... | collective-permute-start | bytes 3145736 | tf_op jit(solution)/shard_map/ppermute | solution.py:351
  87.3 6.1 %collective-permute-start.23 = (f32[64,512]{1,0:T(8,128)S(1)}, f32[64,512]{1,0:T(8,128)S(1)}, u32[]{:S(2)}, u32[]{:S(2)}) collective-permute-start(f32[64,512]{1,0:T(8,128)S(1)} %add_select_fusion.refs_0_), channel_id=1, source_target_pairs={{0,24},{4,28},{8,16},{12,20},{16,8},{20,12},{24,0},{28,4},{1,25},{... | collective-permute-start | bytes 393224 | tf_op jit(solution)/shard_map/ppermute | solution.py:365
  89.6 7.0 %collective-permute-start.22 = (f32[64,512]{1,0:T(8,128)S(1)}, f32[64,512]{1,0:T(8,128)S(1)}, u32[]{:S(2)}, u32[]{:S(2)}) collective-permute-start(f32[64,512]{1,0:T(8,128)S(1)} %add_select_fusion.refs_0_), channel_id=1, source_target_pairs={{0,16},{4,20},{8,24},{12,28},{16,0},{20,4},{24,8},{28,12},{1,17},{... | collective-permute-start | bytes 393224 | tf_op jit(solution)/shard_map/ppermute | solution.py:365
  89.8 7.2 %collective-permute-start.21 = (f32[64,512]{1,0:T(8,128)S(1)}, f32[64,512]{1,0:T(8,128)S(1)}, u32[]{:S(2)}, u32[]{:S(2)}) collective-permute-start(f32[64,512]{1,0:T(8,128)S(1)} %add_select_fusion.refs_0_), channel_id=1, source_target_pairs={{0,8},{4,12},{8,0},{12,4},{16,24},{20,28},{24,16},{28,20},{1,9},{5... | collective-permute-start | bytes 393224 | tf_op jit(solution)/shard_map/ppermute | solution.py:365
  90.0 10.3 %collective-permute-start.24 = (f32[64,512]{1,0:T(8,128)S(1)}, f32[64,512]{1,0:T(8,128)S(1)}, u32[]{:S(2)}, u32[]{:S(2)}) collective-permute-start(f32[64,512]{1,0:T(8,128)S(1)} %add_select_fusion.refs_0_), channel_id=1, source_target_pairs={{0,4},{4,0},{8,12},{12,8},{16,20},{20,16},{24,28},{28,24},{1,5},{5... | collective-permute-start | bytes 393224 | tf_op jit(solution)/shard_map/ppermute | solution.py:366
  93.4 10.5 %collective-permute-start.27 = (f32[64,512]{1,0:T(8,128)S(1)}, f32[64,512]{1,0:T(8,128)S(1)}, u32[]{:S(2)}, u32[]{:S(2)}) collective-permute-start(f32[64,512]{1,0:T(8,128)S(1)} %collective-permute-done.23.refs_3_), channel_id=1, source_target_pairs={{0,4},{4,0},{8,12},{12,8},{16,20},{20,16},{24,28},{28,24},{1,5},{5... | collective-permute-start | bytes 393224 | tf_op jit(solution)/shard_map/ppermute | solution.py:366
  96.5 7.4 %collective-permute-start.26 = (f32[64,512]{1,0:T(8,128)S(1)}, f32[64,512]{1,0:T(8,128)S(1)}, u32[]{:S(2)}, u32[]{:S(2)}) collective-permute-start(f32[64,512]{1,0:T(8,128)S(1)} %collective-permute-done.22.refs_2_), channel_id=1, source_target_pairs={{0,4},{4,0},{8,12},{12,8},{16,20},{20,16},{24,28},{28,24},{1,5},{5... | collective-permute-start | bytes 393224 | tf_op jit(solution)/shard_map/ppermute | solution.py:366
  97.0 6.9 %collective-permute-start.25 = (f32[64,512]{1,0:T(8,128)S(1)}, f32[64,512]{1,0:T(8,128)S(1)}, u32[]{:S(2)}, u32[]{:S(2)}) collective-permute-start(f32[64,512]{1,0:T(8,128)S(1)} %collective-permute-done.21.refs_1_), channel_id=1, source_target_pairs={{0,4},{4,0},{8,12},{12,8},{16,20},{20,16},{24,28},{28,24},{1,5},{5... | collective-permute-start | bytes 393224 | tf_op jit(solution)/shard_map/ppermute | solution.py:366
  97.1 23.3 %collective-permute-start.16 = (f32[344,256]{1,0:T(8,128)}, f32[344,256]{1,0:T(8,128)S(1)}, u32[]{:S(2)}, u32[]{:S(2)}) collective-permute-start(f32[344,256]{1,0:T(8,128)} %add_add_fusion.rest_0_), channel_id=1, source_target_pairs={{1,3},{2,1},{3,2},{5,7},{6,5},{7,6},{9,11},{10,9},{11,10},{13,15},... | collective-permute-start | bytes 1056776 | tf_op jit(solution)/shard_map/ppermute | solution.py:334
  100.4 20.1 %collective-permute-start.15 = (f32[344,256]{1,0:T(8,128)}, f32[344,256]{1,0:T(8,128)S(1)}, u32[]{:S(2)}, u32[]{:S(2)}) collective-permute-start(f32[344,256]{1,0:T(8,128)} %add_add_fusion.rest_0_), channel_id=1, source_target_pairs={{1,2},{2,3},{3,1},{5,6},{6,7},{7,5},{9,10},{10,11},{11,9},{13,14},... | collective-permute-start | bytes 1056776 | tf_op jit(solution)/shard_map/ppermute | solution.py:334
  104.0 16.3 %collective-permute-start.18 = (f32[32,2048]{1,0:T(8,128)S(1)}, f32[32,2048]{1,0:T(8,128)S(1)}, u32[]{:S(2)}, u32[]{:S(2)}) collective-permute-start(f32[32,2048]{1,0:T(8,128)S(1)} %get-tuple-element.88), channel_id=1, source_target_pairs={{0,8},{4,12},{8,0},{12,4},{16,24},{20,28},{24,16},{28,20},{1,9},{5... | collective-permute-start | bytes 786440 | tf_op jit(solution)/shard_map/ppermute | solution.py:360
  105.3 15.0 %collective-permute-start.20 = (f32[32,2048]{1,0:T(8,128)S(1)}, f32[32,2048]{1,0:T(8,128)S(1)}, u32[]{:S(2)}, u32[]{:S(2)}) collective-permute-start(f32[32,2048]{1,0:T(8,128)S(1)} %get-tuple-element.89), channel_id=1, source_target_pairs={{0,24},{4,28},{8,16},{12,20},{16,8},{20,12},{24,0},{28,4},{1,25},{... | collective-permute-start | bytes 786440 | tf_op jit(solution)/shard_map/ppermute | solution.py:360
  106.5 14.0 %copy-start.1 = (f32[344,256]{1,0:T(8,128)S(1)}, f32[344,256]{1,0:T(8,128)}, u32[]{:S(2)}) copy-start(f32[344,256]{1,0:T(8,128)} %add_add_fusion.rest_0_) | copy-start | bytes 1056772
  106.5 14.0 %copy-start.3 = (bf16[1024,2048]{1,0:T(8,128)(2,1)S(1)}, bf16[1024,2048]{1,0:T(8,128)(2,1)}, u32[]{:S(2)}) copy-start(bf16[1024,2048]{1,0:T(8,128)(2,1)} %copy-done.2) | copy-start | bytes 12582916
  106.5 14.0 %copy-start.5 = (bf16[1024,2048]{1,0:T(8,128)(2,1)S(1)}, bf16[1024,2048]{1,0:T(8,128)(2,1)}, u32[]{:S(2)}) copy-start(bf16[1024,2048]{1,0:T(8,128)(2,1)} %copy-done.4) | copy-start | bytes 12582916
  106.5 13.9 %collective-permute-start.19 = (f32[32,2048]{1,0:T(8,128)S(1)}, f32[32,2048]{1,0:T(8,128)S(1)}, u32[]{:S(2)}, u32[]{:S(2)}) collective-permute-start(f32[32,2048]{1,0:T(8,128)S(1)} %get-tuple-element.90), channel_id=1, source_target_pairs={{0,16},{4,20},{8,24},{12,28},{16,0},{20,4},{24,8},{28,12},{1,17},{... | collective-permute-start | bytes 786440 | tf_op jit(solution)/shard_map/ppermute | solution.py:360
  125.8 4.3 %collective-permute-start.28 = (f32[128,2048]{1,0:T(8,128)S(1)}, f32[128,2048]{1,0:T(8,128)S(1)}, u32[]{:S(2)}, u32[]{:S(2)}) collective-permute-start(f32[128,2048]{1,0:T(8,128)S(1)} %get-tuple-element.66), channel_id=1, source_target_pairs={{0,4},{4,0},{8,12},{12,8},{16,20},{20,16},{24,28},{28,24},{1,5},{5... | collective-permute-start | bytes 3145736 | tf_op jit(solution)/shard_map/ppermute | solution.py:351
  127.7 28.5 %collective-permute-start.31 = (f32[32,2048]{1,0:T(8,128)S(1)}, f32[32,2048]{1,0:T(8,128)S(1)}, u32[]{:S(2)}, u32[]{:S(2)}) collective-permute-start(f32[32,2048]{1,0:T(8,128)S(1)} %add_add_fusion.3.rest_0_), channel_id=1, source_target_pairs={{0,24},{4,28},{8,16},{12,20},{16,8},{20,12},{24,0},{28,4},{1,25},{... | collective-permute-start | bytes 786440 | tf_op jit(solution)/shard_map/ppermute | solution.py:365
  129.2 27.3 %collective-permute-start.30 = (f32[32,2048]{1,0:T(8,128)S(1)}, f32[32,2048]{1,0:T(8,128)S(1)}, u32[]{:S(2)}, u32[]{:S(2)}) collective-permute-start(f32[32,2048]{1,0:T(8,128)S(1)} %add_add_fusion.3.rest_0_), channel_id=1, source_target_pairs={{0,16},{4,20},{8,24},{12,28},{16,0},{20,4},{24,8},{28,12},{1,17},{... | collective-permute-start | bytes 786440 | tf_op jit(solution)/shard_map/ppermute | solution.py:365
  130.3 15.0 %collective-permute-start.36 = (f32[32,2048]{1,0:T(8,128)S(1)}, f32[32,2048]{1,0:T(8,128)S(1)}, u32[]{:S(2)}, u32[]{:S(2)}) collective-permute-start(f32[32,2048]{1,0:T(8,128)S(1)} %get-tuple-element.85), channel_id=1, source_target_pairs={{0,8},{4,12},{8,0},{12,4},{16,24},{20,28},{24,16},{28,20},{1,9},{5... | collective-permute-start | bytes 786440 | tf_op jit(solution)/shard_map/ppermute | solution.py:360
  131.5 16.3 %collective-permute-start.38 = (f32[32,2048]{1,0:T(8,128)S(1)}, f32[32,2048]{1,0:T(8,128)S(1)}, u32[]{:S(2)}, u32[]{:S(2)}) collective-permute-start(f32[32,2048]{1,0:T(8,128)S(1)} %get-tuple-element.86), channel_id=1, source_target_pairs={{0,24},{4,28},{8,16},{12,20},{16,8},{20,12},{24,0},{28,4},{1,25},{... | collective-permute-start | bytes 786440 | tf_op jit(solution)/shard_map/ppermute | solution.py:360
  132.7 39.1 %slice-start = ((s8[8388608]{0:T(1024)(128)(4,1)}), s8[4194304]{0:T(1024)(128)(4,1)S(1)}, s32[]{:S(2)}) async-start(s8[8388608]{0:T(1024)(128)(4,1)} %bitcast.6), calls=%async_computation | async-start | bytes 8388608
  132.7 31.7 %copy-start.7 = (f32[1024,256]{1,0:T(8,128)S(1)}, f32[1024,256]{1,0:T(8,128)}, u32[]{:S(2)}) copy-start(f32[1024,256]{1,0:T(8,128)} %copy-done.6) | copy-start | bytes 3145732
  132.7 39.1 %slice-start.1 = ((s8[8388608]{0:T(1024)(128)(4,1)}), s8[4194304]{0:T(1024)(128)(4,1)S(1)}, s32[]{:S(2)}) async-start(s8[8388608]{0:T(1024)(128)(4,1)} %bitcast.6), calls=%async_computation.1 | async-start | bytes 8388608
  132.7 21.0 %collective-permute-start.37 = (f32[32,2048]{1,0:T(8,128)S(1)}, f32[32,2048]{1,0:T(8,128)S(1)}, u32[]{:S(2)}, u32[]{:S(2)}) collective-permute-start(f32[32,2048]{1,0:T(8,128)S(1)} %get-tuple-element.87), channel_id=1, source_target_pairs={{0,16},{4,20},{8,24},{12,28},{16,0},{20,4},{24,8},{28,12},{1,17},{... | collective-permute-start | bytes 786440 | tf_op jit(solution)/shard_map/ppermute | solution.py:360
  145.4 12.5 %collective-permute-start.29 = (f32[32,2048]{1,0:T(8,128)S(1)}, f32[32,2048]{1,0:T(8,128)S(1)}, u32[]{:S(2)}, u32[]{:S(2)}) collective-permute-start(f32[32,2048]{1,0:T(8,128)S(1)} %add_add_fusion.3.rest_0_), channel_id=1, source_target_pairs={{0,8},{4,12},{8,0},{12,4},{16,24},{20,28},{24,16},{28,20},{1,9},{5... | collective-permute-start | bytes 786440 | tf_op jit(solution)/shard_map/ppermute | solution.py:365
  153.8 8.4 %collective-permute-start.41 = (f32[32,2048]{1,0:T(8,128)S(1)}, f32[32,2048]{1,0:T(8,128)S(1)}, u32[]{:S(2)}, u32[]{:S(2)}) collective-permute-start(f32[32,2048]{1,0:T(8,128)S(1)} %add_add_fusion.2.rest_8_), channel_id=1, source_target_pairs={{0,24},{4,28},{8,16},{12,20},{16,8},{20,12},{24,0},{28,4},{1,25},{... | collective-permute-start | bytes 786440 | tf_op jit(solution)/shard_map/ppermute | solution.py:365
  155.3 13.3 %collective-permute-start.40 = (f32[32,2048]{1,0:T(8,128)S(1)}, f32[32,2048]{1,0:T(8,128)S(1)}, u32[]{:S(2)}, u32[]{:S(2)}) collective-permute-start(f32[32,2048]{1,0:T(8,128)S(1)} %add_add_fusion.2.rest_8_), channel_id=1, source_target_pairs={{0,16},{4,20},{8,24},{12,28},{16,0},{20,4},{24,8},{28,12},{1,17},{... | collective-permute-start | bytes 786440 | tf_op jit(solution)/shard_map/ppermute | solution.py:365
  156.3 12.8 %collective-permute-start.39 = (f32[32,2048]{1,0:T(8,128)S(1)}, f32[32,2048]{1,0:T(8,128)S(1)}, u32[]{:S(2)}, u32[]{:S(2)}) collective-permute-start(f32[32,2048]{1,0:T(8,128)S(1)} %add_add_fusion.2.rest_8_), channel_id=1, source_target_pairs={{0,8},{4,12},{8,0},{12,4},{16,24},{20,28},{24,16},{28,20},{1,9},{5... | collective-permute-start | bytes 786440 | tf_op jit(solution)/shard_map/ppermute | solution.py:365
  156.5 12.7 %collective-permute-start.32 = (f32[32,2048]{1,0:T(8,128)S(1)}, f32[32,2048]{1,0:T(8,128)S(1)}, u32[]{:S(2)}, u32[]{:S(2)}) collective-permute-start(f32[32,2048]{1,0:T(8,128)S(1)} %add_add_fusion.3.rest_0_), channel_id=1, source_target_pairs={{0,4},{4,0},{8,12},{12,8},{16,20},{20,16},{24,28},{28,24},{1,5},{5... | collective-permute-start | bytes 786440 | tf_op jit(solution)/shard_map/ppermute | solution.py:366
  157.8 11.8 %collective-permute-start.35 = (f32[32,2048]{1,0:T(8,128)S(1)}, f32[32,2048]{1,0:T(8,128)S(1)}, u32[]{:S(2)}, u32[]{:S(2)}) collective-permute-start(f32[32,2048]{1,0:T(8,128)S(1)} %collective-permute-done.31.rest_3_), channel_id=1, source_target_pairs={{0,4},{4,0},{8,12},{12,8},{16,20},{20,16},{24,28},{28,24},{1,5},{5... | collective-permute-start | bytes 786440 | tf_op jit(solution)/shard_map/ppermute | solution.py:366
  162.2 7.5 %collective-permute-start.34 = (f32[32,2048]{1,0:T(8,128)S(1)}, f32[32,2048]{1,0:T(8,128)S(1)}, u32[]{:S(2)}, u32[]{:S(2)}) collective-permute-start(f32[32,2048]{1,0:T(8,128)S(1)} %collective-permute-done.30.rest_2_), channel_id=1, source_target_pairs={{0,4},{4,0},{8,12},{12,8},{16,20},{20,16},{24,28},{28,24},{1,5},{5... | collective-permute-start | bytes 786440 | tf_op jit(solution)/shard_map/ppermute | solution.py:366
  168.6 1.7 collective-permute-start.33
  169.1 1.5 collective-permute-start.42
  169.2 1.8 collective-permute-start.43
  169.6 1.8 collective-permute-start.44
  169.7 2.0 %collective-permute-start.45 = (f32[32,2048]{1,0:T(8,128)S(1)}, f32[32,2048]{1,0:T(8,128)S(1)}, u32[]{:S(2)}, u32[]{:S(2)}) collective-permute-start(f32[32,2048]{1,0:T(8,128)S(1)} %collective-permute-done.41.rest_11_), channel_id=1, source_target_pairs={{0,4},{4,0},{8,12},{12,8},{16,20},{20,16},{24,28},{28,24},{1,5},{5... | collective-permute-start | bytes 786440 | tf_op jit(solution)/shard_map/ppermute | solution.py:366
